TPU v7x, 32 devices: a whole 2x2x4 slice. The times are simulated.
32 devices in a mesh: dp: 4 (over y, core), fsdp: 8 (over z, x).
Axes of the slice: x: 2, y: 2, z: 4, core: 2. Of those that a mesh axis runs over, the one named last changes fastest.
Arguments:
- tokens: bfloat16 [43520, 1024], P(('dp', 'fsdp')), may hold values from -6 to 6
- cond: bfloat16 [64, 1024], P(('dp', 'fsdp')), may hold values from -6 to 6
- stop_scale: int32 [64], P(('dp', 'fsdp')), may hold values from 5 to 9
- w_ada: bfloat16 [1024, 6144], P('fsdp'), may hold values from -0.1875 to 0.1875
- w_qkv: bfloat16 [1024, 3072], P('fsdp'), may hold values from -0.1875 to 0.1875
- w_proj: bfloat16 [1024, 1024], P('fsdp'), may hold values from -0.5 to 0.5
- w_fc1: bfloat16 [1024, 4096], P('fsdp'), may hold values from -0.1875 to 0.1875
- w_fc2: bfloat16 [4096, 1024], P('fsdp'), may hold values from -0.125 to 0.125
- head_log_scale: float32 [16], replicated, may hold values from 1.9 to 2.5
- cotangent: bfloat16 [43520, 1024], P(('dp', 'fsdp')), may hold values from -6 to 6
Outputs:
- out: bfloat16 [43520, 1024], P(('dp', 'fsdp'))
- grad_tokens: bfloat16 [43520, 1024], P(('dp', 'fsdp'))
- grad_cond: bfloat16 [64, 1024], P(('dp', 'fsdp'))
- grad_w_ada: float32 [1024, 6144], P('fsdp')
- grad_w_qkv: float32 [1024, 3072], P('fsdp')
- grad_w_proj: float32 [1024, 1024], P('fsdp')
- grad_w_fc1: float32 [1024, 4096], P('fsdp')
- grad_w_fc2: float32 [4096, 1024], P('fsdp')
- grad_head_log_scale: float32 [16], replicated
- rms: float32 [64, 3], P(('dp', 'fsdp'))
Inputs may be any that keep to these rules, and one draw needn't show every extreme that they name: `stop_scale`: index of the last scale that holds real tokens of each item.
All inputs are finite; a program needn't handle non-finite values.
Results may differ from a plain program's by a relative error of at most 0.018.
Values may be sent and summed in bfloat16 or wider, within the bound.
No kernel may reach another device: no remote copies, remote signals or barrier semaphores. Data moves between devices by JAX's collectives and lax.ppermute only.
A program may use at most 384 MiB of HBM per device.

v0:
```python
import jax
import jax.numpy as jnp
import numpy as np
from jax import lax
from jax.sharding import PartitionSpec as P

SCALES = 10


PATCHES = (1, 2, 3, 4, 5, 6, 8, 10, 13, 16)
EPS = 1e-06
GELU_COEF = 0.7978845608028654


def scale_table(scale_total):
    labels = []
    for scale_index in range(scale_total):
        labels = labels + [scale_index] * (PATCHES[scale_index] * PATCHES[scale_index])
    return jnp.asarray(np.array(labels, dtype=np.int32))


def silu_act(values):
    return values * jax.nn.sigmoid(values)


def gelu_act(values):
    return (
        0.5 * values * (1.0 + jnp.tanh(GELU_COEF * (values + 0.044715 * values * values * values)))
    )


def layer_norm(values):
    centred = values - jnp.mean(values, -1, keepdims=True)
    return centred * lax.rsqrt(jnp.mean(centred * centred, -1, keepdims=True) + EPS)


def modulate(values, scale_term, shift_term):
    return layer_norm(values) * (1.0 + scale_term) + shift_term


def unit_rows(values):
    return values * lax.rsqrt(jnp.sum(values * values, -1, keepdims=True) + EPS)


def shards(tokens, cond, stop_scale, w_ada, w_qkv, w_proj, w_fc1, w_fc2, head_log_scale, cotangent):
    item_count = cond.shape[0]
    feature_width = cond.shape[1]
    length = tokens.shape[0] // item_count
    head_count = head_log_scale.shape[0]
    head_size = feature_width // head_count
    half_heads = head_count // 2
    scale_ids = scale_table(SCALES)
    low_type = jnp.bfloat16
    full_ada, full_qkv, full_proj, full_fc1, full_fc2 = (
        lax.all_gather(w_ada, "fsdp", axis=0, tiled=True),
        lax.all_gather(w_qkv, "fsdp", axis=0, tiled=True),
        lax.all_gather(w_proj, "fsdp", axis=0, tiled=True),
        lax.all_gather(w_fc1, "fsdp", axis=0, tiled=True),
        lax.all_gather(w_fc2, "fsdp", axis=0, tiled=True),
    )
    valid = (scale_ids[None, :] <= stop_scale[:, None]).astype(jnp.float32)[:, :, None]
    residual = tokens.astype(jnp.float32).reshape(item_count, length, feature_width)
    cond_float = cond.astype(jnp.float32)
    silu_cond = silu_act(cond_float).astype(low_type)
    modulation = jnp.dot(silu_cond, full_ada, preferred_element_type=jnp.float32)
    blocks = [
        modulation[:, None, portion * feature_width : (portion + 1) * feature_width]
        for portion in range(6)
    ]
    gamma_one, gamma_two, scale_one, scale_two, shift_one, shift_two = blocks
    normed_one = modulate(residual, scale_one, shift_one).astype(low_type)
    projected = jnp.einsum("ind,de->ine", normed_one, full_qkv, preferred_element_type=jnp.float32)
    split_heads = projected.reshape(item_count, length, 3, head_count, head_size)
    value_rows = split_heads[:, :, 2].astype(low_type)

    def normalize_pair(query_in, key_in, log_scale):
        return (unit_rows(query_in) * jnp.exp(log_scale)[:, None], unit_rows(key_in))

    (query_float, key_float), normalize_pull = jax.vjp(
        normalize_pair, split_heads[:, :, 0], split_heads[:, :, 1], head_log_scale
    )
    query_rows = query_float.astype(low_type)
    key_rows = key_float.astype(low_type)

    def key_mask(stop_index):
        return (scale_ids[None, :] <= scale_ids[:, None]) & (scale_ids[None, :] <= stop_index)

    def attend_item(operands):
        query_item, key_item, value_item, stop_index = operands
        allowed = key_mask(stop_index)
        outputs = []
        totals = []
        for head_start in (0, half_heads):
            head_span = slice(head_start, head_start + half_heads)
            scores = jnp.einsum(
                "qhc,khc->hqk",
                query_item[:, head_span],
                key_item[:, head_span],
                preferred_element_type=jnp.float32,
            )
            log_total = jnp.log(jnp.sum(jnp.where(allowed, jnp.exp(scores), 0.0), -1))
            weights_low = jnp.where(allowed, jnp.exp(scores - log_total[:, :, None]), 0.0).astype(
                low_type
            )
            outputs.append(
                jnp.einsum(
                    "hqk,khc->qhc",
                    weights_low,
                    value_item[:, head_span],
                    preferred_element_type=jnp.float32,
                )
            )
            totals.append(log_total)
        return (jnp.concatenate(outputs, 1), jnp.concatenate(totals, 0))

    attended, log_totals = lax.map(attend_item, (query_rows, key_rows, value_rows, stop_scale))
    attended_low = attended.astype(low_type).reshape(item_count, length, feature_width)
    attn_out = jnp.einsum(
        "ind,de->ine", attended_low, full_proj, preferred_element_type=jnp.float32
    )
    branch_one = valid * gamma_one * attn_out
    middle = residual + branch_one
    normed_two = modulate(middle, scale_two, shift_two).astype(low_type)
    hidden = jnp.einsum("ind,df->inf", normed_two, full_fc1, preferred_element_type=jnp.float32)
    activated, gelu_pull = jax.vjp(gelu_act, hidden)
    activated = activated.astype(low_type)
    mlp_out = jnp.einsum("inf,fd->ind", activated, full_fc2, preferred_element_type=jnp.float32)
    branch_two = valid * gamma_two * mlp_out
    stream = middle + branch_two
    result = stream.astype(low_type).reshape(tokens.shape)
    counted = jnp.sum(valid[:, :, 0], 1) * feature_width

    def root_mean(field_rows):
        return jnp.sqrt(jnp.sum(valid * field_rows * field_rows, (1, 2)) / counted + EPS)

    rms_rows = jnp.stack([root_mean(stream), root_mean(branch_one), root_mean(branch_two)], 1)
    back_ada, back_qkv, back_proj, back_fc1, back_fc2 = (
        lax.all_gather(w_ada, "fsdp", axis=0, tiled=True),
        lax.all_gather(w_qkv, "fsdp", axis=0, tiled=True),
        lax.all_gather(w_proj, "fsdp", axis=0, tiled=True),
        lax.all_gather(w_fc1, "fsdp", axis=0, tiled=True),
        lax.all_gather(w_fc2, "fsdp", axis=0, tiled=True),
    )
    upstream = cotangent.astype(jnp.float32).reshape(item_count, length, feature_width)
    grad_mlp = (valid * gamma_two * upstream).astype(low_type)
    grad_gamma_two = jnp.sum(valid * mlp_out * upstream, 1)
    term_fc2 = jnp.einsum("inf,ind->fd", activated, grad_mlp, preferred_element_type=jnp.float32)
    grad_act = jnp.einsum("ind,fd->inf", grad_mlp, back_fc2, preferred_element_type=jnp.float32)
    grad_hidden = gelu_pull(grad_act)[0].astype(low_type)
    term_fc1 = jnp.einsum(
        "ind,inf->df", normed_two, grad_hidden, preferred_element_type=jnp.float32
    )
    grad_normed_two = jnp.einsum(
        "inf,df->ind", grad_hidden, back_fc1, preferred_element_type=jnp.float32
    )
    _, second_pull = jax.vjp(modulate, middle, scale_two, shift_two)
    grad_middle, grad_scale_two, grad_shift_two = second_pull(grad_normed_two)
    grad_middle = grad_middle + upstream
    grad_attn = (valid * gamma_one * grad_middle).astype(low_type)
    grad_gamma_one = jnp.sum(valid * attn_out * grad_middle, 1)
    term_proj = jnp.einsum(
        "ind,ine->de", attended_low, grad_attn, preferred_element_type=jnp.float32
    )
    grad_attended = jnp.einsum(
        "ine,de->ind", grad_attn, back_proj, preferred_element_type=jnp.float32
    )
    grad_attended = grad_attended.astype(low_type).reshape(
        item_count, length, head_count, head_size
    )

    def attend_back(operands):
        query_item, key_item, value_item, grad_item, total_item, stop_index = operands
        allowed = key_mask(stop_index)
        grad_queries = []
        grad_keys = []
        grad_values = []
        for head_start in (0, half_heads):
            head_span = slice(head_start, head_start + half_heads)
            scores = jnp.einsum(
                "qhc,khc->hqk",
                query_item[:, head_span],
                key_item[:, head_span],
                preferred_element_type=jnp.float32,
            )
            probs_float = jnp.where(
                allowed, jnp.exp(scores - total_item[head_span][:, :, None]), 0.0
            )
            grad_probs = jnp.einsum(
                "qhc,khc->hqk",
                grad_item[:, head_span],
                value_item[:, head_span],
                preferred_element_type=jnp.float32,
            )
            centre = jnp.sum(probs_float * grad_probs, -1, keepdims=True)
            grad_scores = (probs_float * (grad_probs - centre)).astype(low_type)
            grad_queries.append(
                jnp.einsum(
                    "hqk,khc->qhc",
                    grad_scores,
                    key_item[:, head_span],
                    preferred_element_type=jnp.float32,
                )
            )
            grad_keys.append(
                jnp.einsum(
                    "hqk,qhc->khc",
                    grad_scores,
                    query_item[:, head_span],
                    preferred_element_type=jnp.float32,
                )
            )
            grad_values.append(
                jnp.einsum(
                    "hqk,qhc->khc",
                    probs_float.astype(low_type),
                    grad_item[:, head_span],
                    preferred_element_type=jnp.float32,
                )
            )
        return (
            jnp.concatenate(grad_queries, 1),
            jnp.concatenate(grad_keys, 1),
            jnp.concatenate(grad_values, 1),
        )

    grad_query, grad_key, grad_value = lax.map(
        attend_back, (query_rows, key_rows, value_rows, grad_attended, log_totals, stop_scale)
    )
    grad_raw_query, grad_raw_key, grad_log_scale = normalize_pull((grad_query, grad_key))
    grad_projected = jnp.stack([grad_raw_query, grad_raw_key, grad_value], 2)
    grad_projected = grad_projected.reshape(item_count, length, 3 * feature_width).astype(low_type)
    term_qkv = jnp.einsum(
        "ind,ine->de", normed_one, grad_projected, preferred_element_type=jnp.float32
    )
    grad_normed_one = jnp.einsum(
        "ine,de->ind", grad_projected, back_qkv, preferred_element_type=jnp.float32
    )
    _, first_pull = jax.vjp(modulate, residual, scale_one, shift_one)
    grad_residual, grad_scale_one, grad_shift_one = first_pull(grad_normed_one)
    grad_tokens = (grad_residual + grad_middle).astype(low_type).reshape(tokens.shape)
    grad_modulation = jnp.concatenate(
        [
            grad_gamma_one,
            grad_gamma_two,
            grad_scale_one[:, 0],
            grad_scale_two[:, 0],
            grad_shift_one[:, 0],
            grad_shift_two[:, 0],
        ],
        1,
    ).astype(low_type)
    fsdp_count = lax.axis_size("fsdp")
    term_ada = jnp.dot(silu_cond.T, grad_modulation, preferred_element_type=jnp.float32)
    grad_silu = jnp.dot(grad_modulation, back_ada.T, preferred_element_type=jnp.float32)
    wide_term = jnp.concatenate([term_ada, term_qkv, term_proj, term_fc1], 1)
    _, silu_pull = jax.vjp(silu_act, cond_float)
    grad_cond = silu_pull(grad_silu)[0].astype(low_type)
    head_term = jnp.broadcast_to(grad_log_scale[None, :], (fsdp_count, head_count))
    reduced = (
        lax.psum_scatter(wide_term, "fsdp", scatter_dimension=0, tiled=True),
        lax.psum_scatter(term_fc2, "fsdp", scatter_dimension=0, tiled=True),
        lax.psum_scatter(head_term, "fsdp", scatter_dimension=0, tiled=True),
    )
    reduced = (
        lax.psum(reduced[0].astype(jnp.bfloat16), "dp").astype(jnp.float32),
        lax.psum(reduced[1].astype(jnp.bfloat16), "dp").astype(jnp.float32),
        lax.psum(reduced[2].astype(jnp.bfloat16), "dp").astype(jnp.float32),
    )
    wide_reduced = reduced[0]
    grad_ada_rows = wide_reduced[:, : 6 * feature_width]
    remaining = wide_reduced[:, 6 * feature_width :]
    grad_qkv_rows = remaining[:, : 3 * feature_width]
    grad_proj_rows = remaining[:, 3 * feature_width : 4 * feature_width]
    grad_fc1_rows = remaining[:, 4 * feature_width :]
    return (
        result,
        grad_tokens,
        grad_cond,
        grad_ada_rows,
        grad_qkv_rows,
        grad_proj_rows,
        grad_fc1_rows,
        reduced[1],
        reduced[2].reshape(head_count),
        rms_rows,
    )


def solution(mesh):
    return jax.shard_map(
        shards,
        mesh=mesh,
        in_specs=(
            P(("dp", "fsdp"), None),
            P(("dp", "fsdp"), None),
            P(("dp", "fsdp")),
            P("fsdp", None),
            P("fsdp", None),
            P("fsdp", None),
            P("fsdp", None),
            P("fsdp", None),
            P(),
            P(("dp", "fsdp"), None),
        ),
        out_specs=(
            P(("dp", "fsdp"), None),
            P(("dp", "fsdp"), None),
            P(("dp", "fsdp"), None),
            P("fsdp", None),
            P("fsdp", None),
            P("fsdp", None),
            P("fsdp", None),
            P("fsdp", None),
            P(),
            P(("dp", "fsdp"), None),
        ),
        check_vma=False,
    )
```

profile of v0, /device:TPU:9, one launch (start us, length us, event | category | flops | bytes accessed | tf_op | source)
XLA Modules:
  0.0 2128.6 jit_solution(14700864105759745068)
XLA Ops:
  15.4 4.0 copy.94
  20.0 88.1 %all-gather.8.cloned.1.call-done = bf16[1024,3072]{1,0:T(8,128)(2,1)} async-done(((bf16[128,3072]{1,0:T(8,128)(2,1)}), bf16[1024,3072]{1,0:T(8,128)(2,1)}) %all-gather.8.cloned.1.call-update) | async-done | bytes 6291472 | tf_op jit(solution)/shard_map/all_gather | solution.py:56
  108.1 9.2 copy.62
  117.3 167.7 %all-gather.6.cloned.1.call-done = bf16[1024,6144]{1,0:T(8,128)(2,1)} async-done(((bf16[128,6144]{1,0:T(8,128)(2,1)}), bf16[1024,6144]{1,0:T(8,128)(2,1)}) %all-gather.6.cloned.1.call-update) | async-done | bytes 12582928 | tf_op jit(solution)/shard_map/all_gather | solution.py:55
  285.0 6.3 fusion.148
  294.5 13.7 fusion.158
  318.7 90.4 %while.28 = (s32[]{:T(128)}, bf16[2,680,16,64]{1,3,2,0:T(8,128)(2,1)}, f32[2,16,680]{2,1,0:T(8,128)S(1)}, bf16[2,680,16,64]{1,3,2,0:T(8,128)(2,1)}, s32[2]{0:T(1...) while((s32[]{:T(128)}, ...), condition=%wide.region_7.8_spmd.clone, body=%wide.region_4.7_spmd.sunk.clone.sunk | while | flops 1934693120 | bytes 136050640 | solution.py:116
  320.7 9.4 fusion.220
  330.1 13.3 select_reduce_fusion.3
  343.4 9.7 fusion.221
  353.1 8.8 fusion.222
  365.7 9.4 fusion.220
  375.1 13.3 select_reduce_fusion.3
  388.4 9.7 fusion.221
  398.1 8.8 fusion.222
  409.1 12.7 fusion.154
  425.0 35.3 %all-gather.12.cloned.1.call-done = bf16[1024,4096]{1,0:T(8,128)(2,1)} async-done(((bf16[128,4096]{1,0:T(8,128)(2,1)}), bf16[1024,4096]{1,0:T(8,128)(2,1)}) %all-gather.12.cloned.1.call-update) | async-done | bytes 8388624 | tf_op jit(solution)/shard_map/all_gather | solution.py:58
  460.3 21.2 fusion.112
  481.5 26.4 %convolution_bitcast_fusion.2 = f32[4096,1024]{1,0:T(8,128)} fusion(bf16[2,680,1024]{2,1,0:T(8,128)(2,1)S(1)} %bitcast.297, f32[2,1024]{1,0:T(2,128)S(1)} %copy-done.63, f32[2,680]{1,0:T(2,128)S(1)} %copy-done.45, f32[2,680,4096]{2,1,0:T(8,128)} %fusion.112), kind=kOutput, calls=%fused_computation.124 | convolution fusion | flops 11464212480 | bytes 41858368 | tf_op jit(solution)/shard_map/inf,ind->fd/dot_general | solution.py:147
  507.9 77.4 %all-gather.14.cloned.1.call-done = bf16[4096,1024]{1,0:T(8,128)(2,1)} async-done(((bf16[512,1024]{1,0:T(8,128)(2,1)}), bf16[4096,1024]{1,0:T(8,128)(2,1)}) %all-gather.14.cloned.1.call-update) | async-done | bytes 8388624 | tf_op jit(solution)/shard_map/all_gather | solution.py:59
  585.3 33.5 %fusion.104 = bf16[2,680,4096]{2,1,0:T(8,128)(2,1)} fusion(f32[2,680,4096]{2,1,0:T(8,128)} %fusion.112, bf16[4096,1024]{1,0:T(8,128)(2,1)} %all-gather.14.cloned.1.call-done, bf16[2,680,1024]{2,1,0:T(8,128)(2,1)S(1)} %bitcast.298, f32[2,1024]{1,0:T(2,128)S(1)} %copy-done.63, f32[2,680]{1,0:T(2,128)S(1)} %copy-done.45), kind=kOutput, calls=%fused_computation.117 | convolution fusion | flops 11547770880 | bytes 44610880 | tf_op jit(solution)/shard_map/ind,fd->inf/dot_general | solution.py:148
  618.9 18.5 fusion.110
  637.3 27.7 %fusion.119 = (f32[2]{0:T(128)}, f32[2]{0:T(128)}, bf16[2,1024]{1,0:T(2,128)(2,1)}, f32[2,680]{1,0:T(2,128)S(1)}, bf16[2,1024]{1,0:T(2,128)(2,1)}, /*index=5*/bf16[2,1024]{1,0:T(2,128)(2,1)}, bf16[2,680,1024]{2,1,0:T(8,128)(2,1)}) fusion(f32[2,680]{1,0:T(2,128)S(1)} %copy-done.45, f32[2,680,1024]{2,1,0:T(8,128)} %copy-done.8, ...), kind=kOutput, calls=%fused_computation.160 | convolution fusion | flops 11489272832 | bytes 47432976 | tf_op jit(solution)/shard_map/inf,fd->ind/dot_general | solution.py:127
  665.1 6.5 fusion.153
  672.4 6.4 fusion.120
  680.3 3.4 convolution_convert_fusion
  686.5 3.3 broadcast.233.clone
  689.9 3.4 broadcast.233
  693.3 255.9 %while.29 = (s32[]{:T(128)}, f32[2,680,16,64]{1,3,2,0:T(8,128)}, f32[2,680,16,64]{1,3,2,0:T(8,128)}, bf16[2,680,16,64]{1,3,2,0:T(8,128)(2,1)}, bf16[2,680,16,64]...) while((s32[]{:T(128)}, f32[2,680,16,64]{1,3,2,0:T(8,128)}, ...), condition=%wide.region_15.16_spmd.clone, body=%wide.region_12.15_spmd.sunk.clone.sunk | while | flops 4828849152 | bytes 467244864 | solution.py:226
  697.8 8.1 fusion.245
  706.0 8.0 fusion.249
  714.0 8.1 fusion.243
  722.1 7.7 fusion.250
  731.1 8.1 fusion.244
  739.2 26.1 %multiply_reduce_fusion.15 = (f32[8,680]{1,0:T(8,128)S(1)}, f32[8,680]{1,0:T(8,128)S(1)}, f32[8,680,680]{1,2,0:T(8,128)}) fusion(f32[8,680,680]{1,2,0:T(8,128)} %fusion.243, f32[8,680]{1,0:T(8,128)S(1)} %get-tuple-element.430, pred[680,680]{0,1:T(8,128)(4,1)S(1)} %compare_and_fusion.5, f32[8,680,680]{1,2,0:T(8,128)} %fusion.244, ...), kind=kOutput, calls=%fused_computation.43.clone.1 | convolution fusion | flops 503080320 | bytes 67906048 | tf_op jit(solution)/shard_map/while/body/eval_jaxpr/qhc,khc->hqk/dot_general | solution.py:188
  765.3 29.9 %multiply_convert_fusion.8 = (bf16[8,680,680]{1,2,0:T(8,128)(2,1)}, bf16[8,680,680]{1,2,0:T(8,128)(2,1)}) fusion(f32[8,680,680]{1,2,0:T(8,128)} %get-tuple-element.432, f32[8,680,680]{1,2,0:T(8,128)} %fusion.243, f32[8,680]{1,0:T(8,128)S(1)} %get-tuple-element.433, f32[8,680]{1,0:T(8,128)S(1)} %get-tuple-element.430, ...), kind=kLoop, calls=%fused_computation.42.clone.1 | loop fusion | flops 36992000 | bytes 74533440 | tf_op jit(solution)/shard_map/while/body/eval_jaxpr/convert_element_type | solution.py:195
  795.2 6.5 fusion.246
  808.5 5.3 fusion.247
  826.1 8.1 fusion.245
  834.3 7.6 fusion.249
  841.9 8.1 fusion.243
  850.0 7.6 fusion.250
  858.9 8.1 fusion.244
  867.0 25.6 %multiply_reduce_fusion.15 = (f32[8,680]{1,0:T(8,128)S(1)}, f32[8,680]{1,0:T(8,128)S(1)}, f32[8,680,680]{1,2,0:T(8,128)}) fusion(f32[8,680,680]{1,2,0:T(8,128)} %fusion.243, f32[8,680]{1,0:T(8,128)S(1)} %get-tuple-element.430, pred[680,680]{0,1:T(8,128)(4,1)S(1)} %compare_and_fusion.5, f32[8,680,680]{1,2,0:T(8,128)} %fusion.244, ...), kind=kOutput, calls=%fused_computation.43.clone.1 | convolution fusion | flops 503080320 | bytes 67906048 | tf_op jit(solution)/shard_map/while/body/eval_jaxpr/qhc,khc->hqk/dot_general | solution.py:188
  892.6 29.7 %multiply_convert_fusion.8 = (bf16[8,680,680]{1,2,0:T(8,128)(2,1)}, bf16[8,680,680]{1,2,0:T(8,128)(2,1)}) fusion(f32[8,680,680]{1,2,0:T(8,128)} %get-tuple-element.432, f32[8,680,680]{1,2,0:T(8,128)} %fusion.243, f32[8,680]{1,0:T(8,128)S(1)} %get-tuple-element.433, f32[8,680]{1,0:T(8,128)S(1)} %get-tuple-element.430, ...), kind=kLoop, calls=%fused_computation.42.clone.1 | loop fusion | flops 36992000 | bytes 74533440 | tf_op jit(solution)/shard_map/while/body/eval_jaxpr/convert_element_type | solution.py:195
  922.4 6.5 fusion.246
  935.5 5.4 fusion.247
  949.3 10.3 multiply_reduce_fusion.2
  963.1 8.8 fusion.114
  971.8 8.6 maximum_convert_fusion
  980.5 8.7 copy.66
  989.3 15.9 fusion.152
  1009.9 5.0 convolution_bitcast_fusion.5
  1015.0 20.5 convolution_bitcast_fusion.3
  1035.6 10.3 fusion.146
  1045.9 13.1 convolution_bitcast_fusion.4
  1059.0 38.8 %pad_maximum_fusion = f32[1024,14336]{1,0:T(8,128)} fusion(f32[1024,4096]{1,0:T(8,128)} %convolution_bitcast_fusion.3, f32[1024,1024]{1,0:T(8,128)} %convolution_bitcast_fusion.5, f32[1024,3072]{1,0:T(8,128)} %convolution_bitcast_fusion.4, f32[1024,6144]{1,0:T(8,128)} %fusion.146), kind=kLoop, calls=%fused_computation.109 | loop fusion | flops 44040192 | bytes 117440512 | tf_op jit(solution)/shard_map/concatenate | solution.py:255
  1099.1 14.9 all-reduce
  1114.8 10.2 psum.23
  1127.7 883.8 %reduce-scatter.3.cloned.1.call-done = f32[128,14336]{1,0:T(8,128)} async-done(((f32[1024,14336]{1,0:T(8,128)}), f32[128,14336]{1,0:T(8,128)}) %reduce-scatter.3.cloned.1.call-update) | async-done | bytes 7340048 | tf_op jit(solution)/shard_map/reduce_scatter | solution.py:260
  2011.5 5.3 convert_element_type.133
  2018.1 8.7 fusion.141
  2026.8 6.6 add_convert_fusion
  2033.5 78.6 %all-reduce.4.cloned.1.call-done = (bf16[128,14336]{1,0:T(8,128)(2,1)}, bf16[512,1024]{1,0:T(8,128)(2,1)}) async-done(((bf16[128,14336]{1,0:T(8,128)(2,1)}, bf16[512,1024]{1,0:T(8,128)(2,1)}), (bf16[128,14336]{1,0:T(8,128)(2,1)}, bf16[512,1024]{1,0:T(8,128)(2,1)})) %all-reduce.4.cloned.1.call-update) | async-done | bytes 4718608 | tf_op jit(solution)/shard_map/psum | solution.py:265
  (322 shorter events, 102.1 us)
Async XLA Ops:
  7.2 100.9 %all-gather.8.cloned.1.call-start = ((), (), s32[]{:S(2)}) async-start(), calls=%async_computation.3 | async-start | bytes 7077888 | tf_op jit(solution)/shard_map/all_gather | solution.py:56
  7.9 277.1 %all-gather.6.cloned.1.call-start = ((), (), s32[]{:S(2)}) async-start(), calls=%async_computation.2 | async-start | bytes 14155776 | tf_op jit(solution)/shard_map/all_gather | solution.py:55
  8.7 400.4 %all-gather.10.cloned.1.call-start = ((), (), s32[]{:S(2)}) async-start(), calls=%async_computation.4 | async-start | bytes 2359296 | tf_op jit(solution)/shard_map/all_gather | solution.py:57
  9.4 450.8 %all-gather.12.cloned.1.call-start = ((), (), s32[]{:S(2)}) async-start(), calls=%async_computation.5 | async-start | bytes 9437184 | tf_op jit(solution)/shard_map/all_gather | solution.py:58
  10.0 575.3 %all-gather.14.cloned.1.call-start = ((), (), s32[]{:S(2)}) async-start(), calls=%async_computation.6 | async-start | bytes 9437184 | tf_op jit(solution)/shard_map/all_gather | solution.py:59
  10.6 1114.3 %reduce-scatter.5.cloned.1.call-start = ((), (), s32[]{:S(2)}) async-start(), calls=%async_computation.8 | async-start | bytes 18874368 | tf_op jit(solution)/shard_map/reduce_scatter | solution.py:261
  14.7 297.9 %copy-start.64 = (f32[16]{0:T(128)}, f32[16]{0:T(128)S(1)}, u32[]{:S(2)}) copy-start(f32[16]{0:T(128)S(1)} %exp.26) | copy-start | bytes 196
  108.1 176.9 %copy-start.53 = (bf16[2,1024]{1,0:T(2,128)(2,1)S(1)}, bf16[2,1024]{1,0:T(2,128)(2,1)}, u32[]{:S(2)}) copy-start(bf16[2,1024]{1,0:T(2,128)(2,1)} %param.16) | copy-start | bytes 12292
  291.9 16.3 copy-start.41
  294.5 13.8 copy-start.25
  309.8 8.9 copy-start.33
  309.8 8.9 copy-start.35
  318.7 90.4 %copy-start.43 = (f32[2,1024]{1,0:T(2,128)S(1)}, f32[2,1024]{1,0:T(2,128)}, u32[]{:S(2)}) copy-start(f32[2,1024]{1,0:T(2,128)} %get-tuple-element.299) | copy-start | bytes 24580
  318.7 90.4 %copy-start.45 = (f32[2,680]{1,0:T(2,128)S(1)}, f32[2,680]{1,0:T(2,128)}, u32[]{:S(2)}) copy-start(f32[2,680]{1,0:T(2,128)} %compare_convert_fusion) | copy-start | bytes 16324
  320.6 9.4 copy-start.23
  330.1 13.3 copy-start.12
  353.1 8.8 copy-start.16
  365.7 9.4 copy-start.23
  375.1 13.3 copy-start.12
  398.1 8.8 copy-start.16
  409.0 12.7 copy-start.4
  409.1 12.7 copy-start.39
  421.8 38.4 %copy-start.55 = (f32[2,1024]{1,0:T(2,128)S(1)}, f32[2,1024]{1,0:T(2,128)}, u32[]{:S(2)}) copy-start(f32[2,1024]{1,0:T(2,128)} %get-tuple-element.296) | copy-start | bytes 24580
  421.8 38.4 %copy-start.61 = (f32[2,1024]{1,0:T(2,128)S(1)}, f32[2,1024]{1,0:T(2,128)}, u32[]{:S(2)}) copy-start(f32[2,1024]{1,0:T(2,128)} %get-tuple-element.295) | copy-start | bytes 24580
  421.8 243.2 %copy-start.49 = (f32[2,680]{1,0:T(2,128)}, f32[2,680]{1,0:T(2,128)S(1)}, u32[]{:S(2)}) copy-start(f32[2,680]{1,0:T(2,128)S(1)} %broadcast_multiply_fusion.1) | copy-start | bytes 16324
  424.9 56.6 %copy-start.51 = (f32[2,680]{1,0:T(2,128)}, f32[2,680]{1,0:T(2,128)S(1)}, u32[]{:S(2)}) copy-start(f32[2,680]{1,0:T(2,128)S(1)} %multiply_reduce_fusion.12) | copy-start | bytes 16324
  425.0 240.1 %copy-start.57 = (f32[2,680]{1,0:T(2,128)}, f32[2,680]{1,0:T(2,128)S(1)}, u32[]{:S(2)}) copy-start(f32[2,680]{1,0:T(2,128)S(1)} %fusion.142) | copy-start | bytes 16324
  460.2 21.2 copy-start.19
  460.3 21.2 copy-start.63
  637.3 27.7 %copy-start.52 = (f32[2,680]{1,0:T(2,128)S(1)}, f32[2,680]{1,0:T(2,128)}, u32[]{:S(2)}) copy-start(f32[2,680]{1,0:T(2,128)} %copy-done.51) | copy-start | bytes 16324
  671.7 1339.8 %reduce-scatter.3.cloned.1.call-start = ((), (), s32[]{:S(2)}) async-start(), calls=%async_computation.7 | async-start | bytes 66060288 | tf_op jit(solution)/shard_map/reduce_scatter | solution.py:260
  693.3 255.9 %copy-start.31 = (f32[2,680,16]{1,2,0:T(8,128)S(1)}, f32[2,680,16]{1,2,0:T(8,128)}, u32[]{:S(2)}) copy-start(f32[2,680,16]{1,2,0:T(8,128)} %copy-done.30) | copy-start | bytes 261124
  693.3 255.9 %copy-start.65 = (f32[16]{0:T(128)S(1)}, f32[16]{0:T(128)}, u32[]{:S(2)}) copy-start(f32[16]{0:T(128)} %copy-done.64) | copy-start | bytes 196
  695.7 18.3 copy-start.10
  697.8 8.1 copy-start.13
  824.0 17.9 copy-start.10
  826.1 8.1 copy-start.13
  932.8 8.1 slice-start
  932.8 8.1 slice-start.2
  949.3 10.4 copy-start.34
  949.3 10.4 copy-start.36
  949.3 13.8 copy-start.3
  949.3 13.8 copy-start.38
  980.5 8.7 copy-start.60
  980.5 8.7 copy-start.68
  980.5 8.8 copy-start.42
  980.5 8.8 copy-start.46
  980.5 24.7 %slice-start.4 = ((s8[5570560]{0:T(1024)(128)(4,1)}), s8[1376256]{0:T(1024)(128)(4,1)S(1)}, s32[]{:S(2)}) async-start(s8[5570560]{0:T(1024)(128)(4,1)} %bitcast.287), calls=%async_computation.14 | async-start | bytes 2752512
  989.2 15.9 copy-start.59
  989.3 16.0 slice-start.5
  1005.3 9.7 slice-start.6
  1015.0 20.6 copy-start.54
  1015.0 30.9 %slice-start.10 = ((s8[9437184]{0:T(1024)(128)(4,1)}), s8[1048576]{0:T(1024)(128)(4,1)S(1)}, s32[]{:S(2)}) async-start(s8[9437184]{0:T(1024)(128)(4,1)} %bitcast.303), calls=%async_computation.20 | async-start | bytes 2097152
  1015.0 30.9 %slice-start.11 = ((s8[9437184]{0:T(1024)(128)(4,1)}), s8[4194304]{0:T(1024)(128)(4,1)S(1)}, s32[]{:S(2)}) async-start(s8[9437184]{0:T(1024)(128)(4,1)} %bitcast.303), calls=%async_computation.21 | async-start | bytes 8388608
  1035.6 10.3 slice-start.12
  1035.6 10.3 copy-start.26
  1097.8 1014.2 %all-reduce.4.cloned.1.call-start = ((), (), s32[]{:S(2)}) async-start(), calls=%async_computation.9 | async-start | bytes 9437184 | tf_op jit(solution)/shard_map/psum | solution.py:265
  1127.7 889.2 %copy-start.69 = (f32[2]{0:T(128)S(1)}, f32[2]{0:T(128)}, u32[]{:S(2)}) copy-start(f32[2]{0:T(128)} %get-tuple-element.230) | copy-start | bytes 28
  1127.7 889.2 %copy-start.72 = (f32[2]{0:T(128)S(1)}, f32[2]{0:T(128)}, u32[]{:S(2)}) copy-start(f32[2]{0:T(128)} %get-tuple-element.227) | copy-start | bytes 28
  1127.7 889.2 %copy-start.73 = (f32[2]{0:T(128)S(1)}, f32[2]{0:T(128)}, u32[]{:S(2)}) copy-start(f32[2]{0:T(128)} %get-tuple-element.228) | copy-start | bytes 28
  2016.9 10.0 slice-start.8
  2018.1 8.7 slice-start.9
  2018.1 8.7 copy-start.20
  2018.1 8.7 copy-start.48
  (50 other events, 231.5 us)
Sparse Core Ops, SparseCore 0:
  10.2 97.8 all-gather.7
  110.3 174.6 all-gather.5
  287.1 49.0 all-gather.9
  338.2 122.0 all-gather.11
  462.2 123.0 all-gather.13
  671.8 281.7 reduce-scatter.4
  1098.0 913.5 reduce-scatter.2
  2017.0 94.9 all-reduce.3
where the time goes:
time: 2130 us
  waiting for transfers between devices  1330 us (62%)
  matrix products  485 us (23%)
  other arithmetic  186 us (9%)
  local copies, waits for them, and re-layouts  81.6 us (4%)
  blocking collectives  25 us (1%)
    reduce_scatter x1, waiting for transfers between devices, shards(): lax.psum_scatter(wide_term, 'fsdp', scatter_dimension=0, tiled=True)  884 us
    all_gather x1, waiting for transfers between devices, shards(): lax.all_gather(w_ada, 'fsdp', axis=0, tiled=True)  168 us
    all_gather x1, waiting for transfers between devices, shards(): lax.all_gather(w_qkv, 'fsdp', axis=0, tiled=True)  88.1 us
    psum x1, waiting for transfers between devices, shards(): lax.psum(reduced[0].astype(jnp.bfloat16), 'dp').astype(jnp.float32)  78.6 us
    all_gather x1, waiting for transfers between devices, shards(): lax.all_gather(w_fc2, 'fsdp', axis=0, tiled=True)  77.4 us
    dot_general x4, matrix products, attend_back(): jnp.einsum('qhc,khc->hqk', grad_item[:, head_span], value_item[:, head_sp...  68 us
    convert_element_type x2, other arithmetic, attend_back(): grad_scores = (probs_float * (grad_probs - centre)).astype(low_type)  59.6 us
    dot_general x4, matrix products, attend_item(): jnp.einsum('qhc,khc->hqk', query_item[:, head_span], key_item[:, head_spa...  45.4 us
  transfers between devices with their start and end apart: 8, of which 6 were waited for; matrix products, arithmetic and copies ran while one was open for 29% of the time, Pallas kernels for 0%

commit v1 on v0

v1 whole, which is shorter than its diff:
```python
import functools

import jax
import jax.numpy as jnp
import numpy as np
from jax import lax
from jax.experimental import pallas as pl
from jax.experimental.pallas import tpu as pltpu
from jax.sharding import PartitionSpec as P

PATCHES = (1, 2, 3, 4, 5, 6, 8, 10, 13, 16)
EPS = 1e-06
GELU_COEF = 0.7978845608028654
AXES = ("dp", "fsdp")
LOW = jnp.bfloat16
WIDE = jnp.float32
NN = (((1,), (0,)), ((), ()))
NT = (((1,), (1,)), ((), ()))
TN = (((0,), (0,)), ((), ()))
VMEM_LIMIT = 56 << 20
BLOCKED = -30000.0


def dot(left, right, dims=NN):
    return lax.dot_general(left, right, dims, preferred_element_type=WIDE)


def two_parts(values):
    high = values.astype(LOW)
    return high, (values - high.astype(WIDE)).astype(LOW)


def split_dot(values, table):
    high, rest = two_parts(values)
    return dot(high, table) + dot(rest, table)


class Place:
    def __init__(self, dp_count, fsdp_count):
        self.grouped = dp_count == 4 and fsdp_count == 8
        self.dp_count = dp_count
        self.fsdp_count = fsdp_count
        dp_index = lax.axis_index("dp")
        fsdp_index = lax.axis_index("fsdp")
        self.dp_index, self.fsdp_index = dp_index, fsdp_index
        self.y, self.c = dp_index // 2, dp_index % 2
        self.z, self.x = fsdp_index // 2, fsdp_index % 2
        self.table = jnp.stack([self.y, self.c, self.z, self.x]).astype(jnp.int32)


def hop(values, dy=0, dc=0, dz=0, dx=0):
    pairs = [
        (d * 8 + f, (d ^ (2 * dy + dc)) * 8 + (f ^ (2 * dz + dx)))
        for d in range(4)
        for f in range(8)
    ]
    return lax.ppermute(values, AXES, pairs)


def gather_parts(place, shard, order, after=None):
    if not place.grouped:
        return [lax.all_gather(shard, "fsdp", axis=0, tiled=True)], None
    rows, columns = shard.shape
    quarter = columns // 4
    own = lax.dynamic_slice(shard, (0, (place.c * 2 + place.y) * quarter), (rows, quarter))
    if after is not None:
        own, _ = lax.optimization_barrier((own, after))
    stack = jnp.concatenate([own] + [hop(own, dz=k) for k in (1, 2, 3)], 0)
    if order == "xy":
        over_x = hop(stack, dx=1)
        over_y = hop(stack, dy=1)
        over_both = hop(over_x, dy=1)
    else:
        over_y = hop(stack, dy=1)
        over_x = hop(stack, dx=1)
        over_both = hop(over_y, dx=1)
    half = [stack, over_x, over_y, over_both]
    return half + [hop(piece, dc=1) for piece in half], stack


def load_weight(place_ref, pieces, buffer, sems):
    copies = []
    if len(pieces) == 1:
        copies.append(pltpu.make_async_copy(pieces[0], buffer, sems.at[0]))
    else:
        rows = pieces[0].shape[0] // 4
        quarter = pieces[0].shape[1]
        for number, piece in enumerate(pieces):
            core, side, across = number // 4, (number // 2) % 2, number % 2
            column = ((place_ref[1] ^ core) * 2 + (place_ref[0] ^ side)) * quarter
            for k in range(4):
                row = ((place_ref[2] ^ k) * 2 + (place_ref[3] ^ across)) * rows
                copies.append(
                    pltpu.make_async_copy(
                        piece.at[pl.ds(k * rows, rows), :],
                        buffer.at[
                            pl.ds(pl.multiple_of(row, 128), rows),
                            pl.ds(pl.multiple_of(column, 128), quarter),
                        ],
                        sems.at[number * 4 + k],
                    )
                )
    for copy in copies:
        copy.start()
    for copy in copies:
        copy.wait()


def add(left, right):
    return left.astype(WIDE) + right.astype(WIDE)


def reduce_rows(place, keep, send, rows, order):
    if not place.grouped:
        flip = place.c == 1
        full = jnp.concatenate([jnp.where(flip, send, keep), jnp.where(flip, keep, send)], 1)
        part = lax.psum_scatter(full, "fsdp", scatter_dimension=0, tiled=True)
        return lax.psum(part, "dp").astype(WIDE)
    quarter = keep.shape[1] // 2
    y, z, x = place.y, place.z, place.x

    def over_y(values):
        count = values.shape[0]
        mine = lax.dynamic_slice(values, (0, y * quarter), (count, quarter))
        other = lax.dynamic_slice(values, (0, (1 - y) * quarter), (count, quarter))
        return add(mine, hop(other, dy=1)).astype(LOW)

    def over_x(values):
        width = values.shape[1]
        values = values.reshape(4, 2, rows, width)
        size = (4, 1, rows, width)
        mine = lax.dynamic_slice(values, (0, x, 0, 0), size).reshape(4 * rows, width)
        other = lax.dynamic_slice(values, (0, 1 - x, 0, 0), size).reshape(4 * rows, width)
        return add(mine, hop(other, dx=1)).astype(LOW)

    values = add(keep, hop(send, dc=1)).astype(LOW)
    values = over_x(over_y(values)) if order == "yx" else over_y(over_x(values))
    total = lax.dynamic_slice(values, (z * rows, 0), (rows, quarter)).astype(WIDE)
    for k in (1, 2, 3):
        piece = lax.dynamic_slice(values, ((z ^ k) * rows, 0), (rows, quarter))
        total = total + hop(piece, dz=k).astype(WIDE)
    own = total.astype(LOW)
    from_y = hop(own, dy=1)
    from_c = hop(own, dc=1)
    from_both = hop(from_y, dc=1)
    here = place.c * 2 + y

    def pick(index):
        apart = index ^ here
        return jnp.where(
            apart == 0, own, jnp.where(apart == 1, from_y, jnp.where(apart == 2, from_c, from_both))
        )

    return jnp.concatenate([pick(index) for index in range(4)], 1).astype(WIDE)


def reorder(stack, count, flip):
    return jnp.concatenate(
        [lax.dynamic_slice_in_dim(stack, i ^ flip, 1, axis=0) for i in range(count)], 0
    )


def gather_small(place, values, whole):
    if not place.grouped:
        return lax.all_gather(values, AXES if whole else "fsdp", axis=0, tiled=True)
    count = values.shape[0]
    stack = jnp.stack([values] + [hop(values, dz=k) for k in (1, 2, 3)])
    stack = jnp.stack([stack, hop(stack, dx=1)], 1)
    stack = stack.reshape((8,) + values.shape)
    ordered = reorder(stack, 8, place.fsdp_index)
    ordered = ordered.reshape((8 * count,) + values.shape[1:])
    if not whole:
        return ordered
    stack = jnp.stack([ordered, hop(ordered, dc=1)])
    stack = jnp.concatenate([stack, hop(stack, dy=1)], 0)
    ordered = reorder(stack, 4, place.dp_index)
    return ordered.reshape((32 * count,) + values.shape[1:])


def scatter_small(place, values):
    if not place.grouped:
        return lax.psum_scatter(values, "fsdp", scatter_dimension=0, tiled=True)
    count = values.shape[0] // 8
    tail = values.shape[1:]
    values = values.reshape((4, 2, count) + tail)
    mine = lax.dynamic_index_in_dim(values, place.x, 1, keepdims=False)
    other = lax.dynamic_index_in_dim(values, 1 - place.x, 1, keepdims=False)
    values = mine + hop(other, dx=1)
    total = lax.dynamic_index_in_dim(values, place.z, 0, keepdims=False)
    for k in (1, 2, 3):
        total = total + hop(
            lax.dynamic_index_in_dim(values, place.z ^ k, 0, keepdims=False), dz=k
        )
    return total


def mask_tables(length):
    scale_ids = np.concatenate([np.full(side * side, i) for i, side in enumerate(PATCHES)])
    spare = np.arange(128) & 63
    slot = spare[None, :] - 2
    scale_column = scale_ids[:, None]
    later = (slot >= 0) & (slot < len(PATCHES)) & (slot > scale_column)
    query_side = np.where(later, BLOCKED, 0.0)
    key_side = np.where(slot == scale_column, 1.0, 0.0) + np.where(spare[None, :] < 2, 1.0, 0.0)
    return jnp.asarray(query_side, LOW), jnp.asarray(key_side, LOW)


FORWARD_BLOCKS = ((0, 240, 256), (240, 416, 512), (416, 680, 680))
BACKWARD_BLOCKS = ((424, 680, 680), (240, 424, 432), (0, 240, 256))


def attend_kernel(q_ref, k_ref, v_ref, qm_ref, km_ref, out_ref, extra_ref):
    query, key, value = q_ref[0], k_ref[0], v_ref[0]
    query_mask, key_mask = qm_ref[...], km_ref[...]
    lane = lax.broadcasted_iota(jnp.int32, query.shape, 1)
    even = lane < 64
    ones = jnp.ones_like(value)
    heads = (
        (jnp.where(even, query, query_mask), jnp.where(even, key, key_mask), jnp.where(even, value, ones)),
        (jnp.where(even, query_mask, query), jnp.where(even, key_mask, key), jnp.where(even, ones, value)),
    )
    for start, stop, keys in FORWARD_BLOCKS:
        sums = []
        for query_head, key_head, value_head in heads:
            scores = dot(query_head[start:stop], key_head[:keys], NT)
            sums.append(dot(jnp.exp(scores).astype(LOW), value_head[:keys]))
        side = even[start:stop]
        chosen = jnp.where(side, sums[0], sums[1])
        totals = jnp.where(side, sums[1], sums[0])
        out_ref[0, start:stop, :] = (chosen / pltpu.roll(totals, 64, 1)).astype(LOW)
        high, rest = two_parts(-jnp.log(totals))
        spare = lane[start:stop] & 63
        extra_ref[0, start:stop, :] = jnp.where(
            spare == 0, high, jnp.where(spare == 1, rest, query_mask[start:stop])
        )


def attend(query, key, value, query_mask, key_mask):
    items, length, width = query.shape
    pairs = width // 128
    block = pl.BlockSpec((1, length, 128), lambda i, p: (i, 0, p))
    table = pl.BlockSpec((length, 128), lambda i, p: (0, 0))
    return pl.pallas_call(
        attend_kernel,
        grid=(items, pairs),
        in_specs=[block, block, block, table, table],
        out_specs=[block, block],
        out_shape=[jax.ShapeDtypeStruct(query.shape, LOW)] * 2,
        compiler_params=pltpu.CompilerParams(vmem_limit_bytes=VMEM_LIMIT),
        cost_estimate=pl.CostEstimate(
            flops=items * pairs * length * length * 128 * 10,
            transcendentals=items * pairs * 2 * length * length,
            bytes_accessed=items * length * width * 10,
        ),
        name="attend",
    )(query, key, value, query_mask, key_mask)


def side_table(cross):
    first = lax.broadcasted_iota(jnp.int32, (128, 128), 0) < 64
    second = lax.broadcasted_iota(jnp.int32, (128, 128), 1) < 64
    return jnp.where((first != second) if cross else (first == second), 1.0, 0.0).astype(LOW)


def attend_back_kernel(
    q_ref, k_ref, v_ref, extra_ref, km_ref, out_ref, grad_ref, rq_ref, rk_ref, gain_ref,
    dq_ref, dk_ref, dv_ref, head_ref, value_sum, key_sum, query_sum,
):
    query, key, value, extra = q_ref[0], k_ref[0], v_ref[0], extra_ref[0]
    key_mask, grad = km_ref[...], grad_ref[0]
    lane = lax.broadcasted_iota(jnp.int32, query.shape, 1)
    even = lane < 64
    spare = lane & 63
    centre = split_dot(grad.astype(WIDE) * out_ref[0].astype(WIDE), side_table(True))
    high, rest = two_parts(-centre)
    grad_extra = jnp.where(spare == 0, high, jnp.where(spare == 1, rest, jnp.zeros_like(high)))
    ones = jnp.ones_like(value)
    key_rows = key.astype(WIDE).T.astype(LOW)
    heads = (
        (jnp.where(even, query, extra), jnp.where(even, key, key_mask),
         jnp.where(even, value, ones), jnp.where(even, grad, grad_extra)),
        (jnp.where(even, extra, query), jnp.where(even, key_mask, key),
         jnp.where(even, ones, value), jnp.where(even, grad_extra, grad)),
    )
    for head, (query_head, key_head, value_head, grad_head) in enumerate(heads):
        head_rows = key_rows[64 * head : 64 * head + 64]
        for number, (start, stop, keys) in enumerate(BACKWARD_BLOCKS):
            probs = jnp.exp(dot(key_head[:keys], query_head[start:stop], NT))
            grad_probs = dot(value_head[:keys], grad_head[start:stop], NT)
            grad_scores = (probs * grad_probs).astype(LOW)
            value_part = dot(probs.astype(LOW), grad[start:stop])
            key_part = dot(grad_scores, query[start:stop])
            if number == 0:
                value_sum[head] = value_part
                key_sum[head] = key_part
            else:
                value_sum[head, :keys] += value_part
                key_sum[head, :keys] += key_part
            query_sum[start:stop, 64 * head : 64 * head + 64] = dot(head_rows[:, :keys], grad_scores).T
    head_count = rq_ref.shape[2]
    head_row = lax.broadcasted_iota(jnp.int32, (head_count, 128), 0)
    head_lane = lax.broadcasted_iota(jnp.int32, (head_count, 128), 1)
    wanted = 2 * pl.program_id(1) + jnp.where(head_lane >= 64, 1, 0)
    table = jnp.where(head_row == wanted, 1.0, 0.0).astype(LOW)
    same = side_table(False)
    gain = gain_ref[...]
    grad_query = query_sum[...] * gain
    unit_query = query.astype(WIDE) / gain
    product = unit_query * grad_query
    head_ref[0] = jnp.sum(product, 0, keepdims=True)
    dq_ref[0] = (
        split_dot(rq_ref[0], table) * (grad_query - unit_query * split_dot(product, same))
    ).astype(LOW)
    grad_key = jnp.where(even, key_sum[0], key_sum[1])
    unit_key = key.astype(WIDE)
    dk_ref[0] = (
        split_dot(rk_ref[0], table) * (grad_key - unit_key * split_dot(unit_key * grad_key, same))
    ).astype(LOW)
    dv_ref[0] = jnp.where(even, value_sum[0], value_sum[1]).astype(LOW)


def attend_back(query, key, value, extra, key_mask, out, grad, rq, rk, gain):
    items, length, width = query.shape
    pairs = width // 128
    block = pl.BlockSpec((1, length, 128), lambda i, p: (i, 0, p))
    table = pl.BlockSpec((length, 128), lambda i, p: (0, 0))
    rows = pl.BlockSpec((1, length, rq.shape[2]), lambda i, p: (i, 0, 0))
    return pl.pallas_call(
        attend_back_kernel,
        grid=(items, pairs),
        in_specs=[block] * 4 + [table, block, block, rows, rows, pl.BlockSpec((1, 128), lambda i, p: (0, p))],
        out_specs=[block] * 3 + [pl.BlockSpec((1, 1, 128), lambda i, p: (i, 0, p))],
        out_shape=[jax.ShapeDtypeStruct(query.shape, LOW)] * 3
        + [jax.ShapeDtypeStruct((items, 1, width), WIDE)],
        scratch_shapes=[
            pltpu.VMEM((2, length, 128), WIDE),
            pltpu.VMEM((2, length, 128), WIDE),
            pltpu.VMEM((length, 128), WIDE),
        ],
        compiler_params=pltpu.CompilerParams(vmem_limit_bytes=VMEM_LIMIT),
        cost_estimate=pl.CostEstimate(
            flops=items * pairs * length * length * 128 * 26,
            transcendentals=items * pairs * 2 * length * length,
            bytes_accessed=items * length * width * 22,
        ),
        name="attend_back",
    )(query, key, value, extra, key_mask, out, grad, rq, rk, gain)


def row_facts(lengths_ref, block_rows, length):
    row = pl.program_id(0) * block_rows + lax.broadcasted_iota(jnp.int32, (block_rows, 1), 0)
    second = row >= length
    end = jnp.where(second, length + lengths_ref[1], lengths_ref[0])
    return second, row < end


def per_row(ref, second):
    return jnp.where(second, ref[1:2, :], ref[0:1, :])


def add_sums(ref, start, second, values):
    ref[start : start + 1, :] += jnp.sum(jnp.where(second, 0.0, values), 0, keepdims=True)
    ref[start + 1 : start + 2, :] += jnp.sum(jnp.where(second, values, 0.0), 0, keepdims=True)


def normalize(values):
    centred = values - jnp.mean(values, -1, keepdims=True)
    scale = lax.rsqrt(jnp.mean(centred * centred, -1, keepdims=True) + EPS)
    return centred * scale, scale


def token_call(kernel, place, rows, length, lengths, blocked, full, weights, outs, sums, flops, name, scratch=()):
    block_rows = 2 * length // 5
    grid = rows // block_rows
    parts = [part for pieces in weights for part in pieces[0]]
    counts = [len(pieces[0]) for pieces in weights]
    shapes = [pieces[1] for pieces in weights]
    blocked_count, full_count, out_count = len(blocked), len(full), len(outs)

    def body(place_ref, lengths_ref, *refs):
        refs = list(refs)
        token_refs = refs[:blocked_count]
        full_refs = refs[blocked_count : blocked_count + full_count]
        cursor = blocked_count + full_count
        groups = []
        for count in counts:
            groups.append(refs[cursor : cursor + count])
            cursor += count
        out_refs = refs[cursor : cursor + out_count]
        cursor += out_count
        sum_refs = refs[cursor : cursor + sums]
        cursor += sums
        buffers = refs[cursor : cursor + len(counts)]
        cursor += len(counts)
        sems = refs[cursor : cursor + len(counts)]
        cursor += len(counts)

        @pl.when(pl.program_id(0) == 0)
        def _():
            for ref in sum_refs:
                ref[...] = jnp.zeros_like(ref)
            for pieces, buffer, sem in zip(groups, buffers, sems):
                load_weight(place_ref, pieces, buffer, sem)

        second, real = row_facts(lengths_ref, block_rows, length)
        kernel(second, real, token_refs, full_refs, buffers, out_refs, sum_refs, *refs[cursor:])

    any_space = pl.BlockSpec(memory_space=pl.ANY)
    smem = pl.BlockSpec(memory_space=pltpu.SMEM)
    moved = sum(v.size * v.dtype.itemsize for v in blocked) + sum(
        rows * width * jnp.dtype(kind).itemsize for width, kind in outs
    )
    return pl.pallas_call(
        body,
        grid=(grid,),
        in_specs=[smem, smem]
        + [pl.BlockSpec((block_rows, v.shape[1]), lambda i: (i, 0)) for v in blocked]
        + [pl.BlockSpec(v.shape, lambda i: (0, 0)) for v in full]
        + [any_space] * len(parts),
        out_specs=[pl.BlockSpec((block_rows, width), lambda i: (i, 0)) for width, _ in outs]
        + [pl.BlockSpec((8, 1024), lambda i: (0, 0))] * sums,
        out_shape=[jax.ShapeDtypeStruct((rows, width), kind) for width, kind in outs]
        + [jax.ShapeDtypeStruct((8, 1024), WIDE)] * sums,
        scratch_shapes=[pltpu.VMEM(shape, LOW) for shape in shapes]
        + [pltpu.SemaphoreType.DMA((32,))] * len(shapes)
        + list(scratch),
        compiler_params=pltpu.CompilerParams(vmem_limit_bytes=VMEM_LIMIT),
        cost_estimate=pl.CostEstimate(
            flops=flops, transcendentals=0,
            bytes_accessed=moved + sum(2 * a * b for a, b in shapes),
        ),
        name=name,
    )(place.table, lengths, *blocked, *full, *parts)


def project_kernel(second, real, tokens, full, weights, outs, sums):
    (x_ref,) = tokens
    scale, shift, gain, spread, collect = full
    (weight,) = weights
    h_ref, q_ref, k_ref, v_ref, rq_ref, rk_ref = outs
    unit, _ = normalize(x_ref[...].astype(WIDE))
    hidden = (unit * (1.0 + per_row(scale, second)) + per_row(shift, second)).astype(LOW)
    h_ref[...] = hidden
    width = hidden.shape[1]
    for number, (ref, root_ref) in enumerate(((q_ref, rq_ref), (k_ref, rk_ref))):
        raw = dot(hidden, weight[:, number * width : (number + 1) * width])
        root = lax.rsqrt(split_dot(raw * raw, collect[...]) + EPS)
        root_ref[...] = root
        rows = raw * split_dot(root, spread[...])
        if number == 0:
            rows = rows * gain[...]
        ref[...] = rows.astype(LOW)
    v_ref[...] = dot(hidden, weight[:, 2 * width :]).astype(LOW)


def branch_kernel(second, real, tokens, full, weights, outs, sums):
    attended_ref, x_ref = tokens
    gamma, scale, shift = full
    proj, fc1 = weights
    attn_ref, h_ref, act_ref, slope_ref = outs
    (sum_ref,) = sums
    attn = dot(attended_ref[...], proj[...]).astype(LOW)
    attn_ref[...] = attn
    branch = jnp.where(real, per_row(gamma, second) * attn.astype(WIDE), 0.0)
    add_sums(sum_ref, 0, second, branch * branch)
    unit, _ = normalize(x_ref[...].astype(WIDE) + branch)
    hidden = (unit * (1.0 + per_row(scale, second)) + per_row(shift, second)).astype(LOW)
    h_ref[...] = hidden
    width = hidden.shape[1]
    for start in range(0, fc1.shape[1], width):
        span = slice(start, start + width)
        wide = dot(hidden, fc1[:, span])
        square = wide * wide
        bend = jnp.tanh(GELU_COEF * wide * (1.0 + 0.044715 * square))
        lift = 0.5 * (1.0 + bend)
        act_ref[:, span] = (wide * lift).astype(LOW)
        slope = lift + 0.5 * wide * (1.0 - bend * bend) * (
            GELU_COEF * (1.0 + 3.0 * 0.044715 * square)
        )
        slope_ref[:, span] = slope.astype(LOW)


def stream_kernel(second, real, tokens, full, weights, outs, sums):
    act_ref, x_ref, attn_ref, cot_ref = tokens
    gamma_one, gamma_two = full
    (fc2,) = weights
    out_ref, grad_ref = outs
    (sum_ref,) = sums
    mlp = dot(act_ref[...], fc2[...])
    branch_one = jnp.where(real, per_row(gamma_one, second) * attn_ref[...].astype(WIDE), 0.0)
    gate = per_row(gamma_two, second)
    branch_two = jnp.where(real, gate * mlp, 0.0)
    stream = x_ref[...].astype(WIDE) + branch_one + branch_two
    out_ref[...] = stream.astype(LOW)
    upstream = cot_ref[...].astype(WIDE)
    grad_ref[...] = jnp.where(real, gate * upstream, 0.0).astype(LOW)
    add_sums(sum_ref, 0, second, jnp.where(real, stream * stream, 0.0))
    add_sums(sum_ref, 2, second, branch_two * branch_two)
    add_sums(sum_ref, 4, second, jnp.where(real, mlp * upstream, 0.0))


def hidden_back_kernel(second, real, tokens, full, weights, outs, sums):
    grad_ref, slope_ref = tokens
    (fc2,) = weights
    (out_ref,) = outs
    grad = grad_ref[...]
    width = grad.shape[1]
    for start in range(0, fc2.shape[0], width):
        span = slice(start, start + width)
        out_ref[:, span] = (
            dot(grad, fc2[span, :], NT) * slope_ref[:, span].astype(WIDE)
        ).astype(LOW)


def middle_back_kernel(second, real, tokens, full, weights, outs, sums):
    grad_ref, x_ref, attn_ref, cot_ref = tokens
    gamma, scale = full
    fc1, proj = weights
    middle_ref, attn_grad_ref, attended_grad_ref = outs
    (sum_ref,) = sums
    grad = dot(grad_ref[...], fc1[...], NT)
    attn = attn_ref[...].astype(WIDE)
    gate = per_row(gamma, second)
    unit, root = normalize(x_ref[...].astype(WIDE) + jnp.where(real, gate * attn, 0.0))
    add_sums(sum_ref, 0, second, grad * unit)
    add_sums(sum_ref, 2, second, grad)
    scaled = grad * (1.0 + per_row(scale, second))
    middle = cot_ref[...].astype(WIDE) + root * (
        scaled - jnp.mean(scaled, -1, keepdims=True) - unit * jnp.mean(scaled * unit, -1, keepdims=True)
    )
    middle_ref[...] = middle.astype(LOW)
    add_sums(sum_ref, 4, second, jnp.where(real, attn * middle, 0.0))
    attn_grad = jnp.where(real, gate * middle, 0.0).astype(LOW)
    attn_grad_ref[...] = attn_grad
    attended_grad_ref[...] = dot(attn_grad, proj[...], NT).astype(LOW)


def token_back_kernel(second, real, tokens, full, weights, outs, sums):
    dq_ref, dk_ref, dv_ref, x_ref, middle_ref = tokens
    (scale,) = full
    (weight,) = weights
    (out_ref,) = outs
    (sum_ref,) = sums
    width = x_ref.shape[1]
    grad = dot(dq_ref[...], weight[:, :width], NT)
    grad = grad + dot(dk_ref[...], weight[:, width : 2 * width], NT)
    grad = grad + dot(dv_ref[...], weight[:, 2 * width :], NT)
    unit, root = normalize(x_ref[...].astype(WIDE))
    add_sums(sum_ref, 0, second, grad * unit)
    add_sums(sum_ref, 2, second, grad)
    scaled = grad * (1.0 + per_row(scale, second))
    total = middle_ref[...].astype(WIDE) + root * (
        scaled - jnp.mean(scaled, -1, keepdims=True) - unit * jnp.mean(scaled * unit, -1, keepdims=True)
    )
    out_ref[...] = total.astype(LOW)


def weight_grad(place, left, rights, own_half):
    half = place.c if own_half else 1 - place.c
    parts = []
    for right in rights:
        width = right.shape[1] // 2
        piece = lax.dynamic_slice(right, (0, half * width), (right.shape[0], width))
        parts.append(dot(left, piece, TN).astype(LOW))
    return parts[0] if len(parts) == 1 else jnp.concatenate(parts, 1)


def shards(place_counts, tokens, cond, stop_scale, w_ada, w_qkv, w_proj, w_fc1, w_fc2, head_log_scale, cotangent):
    place = Place(*place_counts)
    items, width = cond.shape
    rows = tokens.shape[0]
    length = rows // items
    heads = head_log_scale.shape[0]
    ends = jnp.asarray(np.cumsum([side * side for side in PATCHES]).astype(np.int32))
    lengths = jnp.sum(jnp.where(jnp.arange(len(PATCHES))[None, :] == stop_scale[:, None], ends[None, :], 0), 1)

    cond_wide = cond.astype(WIDE)
    silu_cond = (cond_wide * jax.nn.sigmoid(cond_wide)).astype(LOW)
    ada_rows = w_ada.shape[0]
    group_cond = gather_small(place, silu_cond, False)
    ada_columns = (0, place.fsdp_index * ada_rows)
    group_slice = lax.dynamic_slice(group_cond, ada_columns, (group_cond.shape[0], ada_rows))
    modulation = scatter_small(place, dot(group_slice, w_ada))
    gamma_one, gamma_two, scale_one, scale_two, shift_one, shift_two = [
        modulation[:, n * width : (n + 1) * width] for n in range(6)
    ]

    qkv_parts, mark = gather_parts(place, w_qkv, "xy")
    proj_parts, mark = gather_parts(place, w_proj, "yx", mark)
    fc1_parts, mark = gather_parts(place, w_fc1, "xy", mark)
    fc2_parts, mark = gather_parts(place, w_fc2, "yx", mark)
    qkv_weight = (qkv_parts, (width, 3 * width))
    proj_weight = (proj_parts, (width, width))
    fc1_weight = (fc1_parts, (width, w_fc1.shape[1]))
    fc2_weight = (fc2_parts, (w_fc1.shape[1], width))

    hidden_width = w_fc1.shape[1]
    base = 2 * rows * width * width
    gain = jnp.repeat(jnp.exp(head_log_scale), width // heads)[None, :]
    head_of = np.arange(width) // (width // heads)
    spread = jnp.asarray((np.arange(heads)[:, None] == head_of[None, :]).astype(np.float32), LOW)
    collect = jnp.asarray((head_of[:, None] == np.arange(heads)[None, :]).astype(np.float32), LOW)
    normed_one, query, key, value, root_query, root_key = token_call(
        project_kernel, place, rows, length, lengths, [tokens],
        [scale_one, shift_one, gain, spread, collect], [qkv_weight],
        [(width, LOW)] * 4 + [(heads, WIDE)] * 2, 0, 3 * base, "project",
    )
    cube = (items, length, width)
    query, key, value = query.reshape(cube), key.reshape(cube), value.reshape(cube)
    query_mask, key_mask = mask_tables(length)
    attended, extra = attend(query, key, value, query_mask, key_mask)

    attn, normed_two, act, slope, sum_one = token_call(
        branch_kernel, place, rows, length, lengths,
        [attended.reshape(rows, width), tokens], [gamma_one, scale_two, shift_two],
        [proj_weight, fc1_weight],
        [(width, LOW), (width, LOW), (hidden_width, LOW), (hidden_width, LOW)], 1, 5 * base, "branch",
    )
    result, grad_mlp, sum_two = token_call(
        stream_kernel, place, rows, length, lengths,
        [act, tokens, attn, cotangent], [gamma_one, gamma_two], [fc2_weight],
        [(width, LOW), (width, LOW)], 1, 4 * base, "stream",
    )
    fc2_send = weight_grad(place, act, [grad_mlp], False)
    fc2_keep = weight_grad(place, act, [grad_mlp], True)
    grad_fc2 = reduce_rows(place, fc2_keep, fc2_send, w_fc2.shape[0], "yx")
    (grad_hidden,) = token_call(
        hidden_back_kernel, place, rows, length, lengths, [grad_mlp, slope], [], [fc2_weight],
        [(hidden_width, LOW)], 0, 4 * base, "hidden_back",
    )
    fc1_send = weight_grad(place, normed_two, [grad_hidden], False)
    fc1_keep = weight_grad(place, normed_two, [grad_hidden], True)
    grad_fc1 = reduce_rows(place, fc1_keep, fc1_send, w_fc1.shape[0], "xy")
    grad_middle, grad_attn, grad_attended, sum_three = token_call(
        middle_back_kernel, place, rows, length, lengths,
        [grad_hidden, tokens, attn, cotangent], [gamma_one, scale_two], [fc1_weight, proj_weight],
        [(width, LOW)] * 3, 1, 5 * base, "middle_back",
    )
    flat_attended = attended.reshape(rows, width)
    proj_send = weight_grad(place, flat_attended, [grad_attn], False)
    proj_keep = weight_grad(place, flat_attended, [grad_attn], True)
    grad_proj = reduce_rows(place, proj_keep, proj_send, w_proj.shape[0], "yx")

    grad_query, grad_key, grad_value, head_sums = attend_back(
        query, key, value, extra, key_mask, attended, grad_attended.reshape(cube),
        root_query.reshape(items, length, heads), root_key.reshape(items, length, heads), gain,
    )
    grad_query, grad_key, grad_value = (
        v.reshape(rows, width) for v in (grad_query, grad_key, grad_value)
    )
    joined = jnp.concatenate([grad_query, grad_key, grad_value], 1)
    qkv_send = weight_grad(place, normed_one, [joined], False)
    qkv_keep = weight_grad(place, normed_one, [joined], True)
    grad_qkv = reduce_rows(place, qkv_keep, qkv_send, w_qkv.shape[0], "xy")

    grad_tokens, sum_four = token_call(
        token_back_kernel, place, rows, length, lengths,
        [grad_query, grad_key, grad_value, tokens, grad_middle], [scale_one], [qkv_weight],
        [(width, LOW)], 1, 3 * base, "token_back",
    )

    grad_modulation = jnp.concatenate(
        [sum_three[4:6], sum_two[4:6], sum_four[0:2], sum_three[0:2], sum_four[2:4], sum_three[2:4]], 1
    ).astype(LOW)
    all_cond = gather_small(place, silu_cond, True)
    all_slice = lax.dynamic_slice(all_cond, ada_columns, (all_cond.shape[0], ada_rows))
    all_modulation = gather_small(place, grad_modulation, True)
    grad_ada = dot(all_slice, all_modulation, TN)
    group_count = group_cond.shape[0]
    group_modulation = lax.dynamic_slice(
        all_modulation, (place.dp_index * group_count, 0), (group_count, all_modulation.shape[1])
    )
    grad_columns = dot(group_modulation, w_ada, NT)
    grad_parts = gather_small(place, grad_columns[None], False)
    own_items = lax.dynamic_slice(
        grad_parts, (0, place.fsdp_index * items, 0), (grad_parts.shape[0], items, ada_rows)
    )
    grad_silu = jnp.swapaxes(own_items, 0, 1).reshape(items, width)
    gate = jax.nn.sigmoid(cond_wide)
    grad_cond = (grad_silu * gate * (1.0 + cond_wide * (1.0 - gate))).astype(LOW)

    grad_head = lax.psum(head_sums.reshape(items, heads, width // heads).sum((0, 2)), AXES)

    counted = (lengths * width).astype(WIDE)
    squares = jnp.stack(
        [sum_two[0:2].sum(1), sum_one[0:2].sum(1), sum_two[2:4].sum(1)], 1
    )
    rms_rows = jnp.sqrt(squares / counted[:, None] + EPS)
    return (
        result, grad_tokens, grad_cond, grad_ada, grad_qkv, grad_proj, grad_fc1, grad_fc2,
        grad_head, rms_rows,
    )


def solution(mesh):
    both = P(("dp", "fsdp"), None)
    rows = P("fsdp", None)
    return jax.shard_map(
        functools.partial(shards, (mesh.shape["dp"], mesh.shape["fsdp"])),
        mesh=mesh,
        in_specs=(both, both, P(("dp", "fsdp")), rows, rows, rows, rows, rows, P(), both),
        out_specs=(both, both, both, rows, rows, rows, rows, rows, P(), both),
        check_vma=False,
    )
```

time: 2130 us -> 800 us (0.38)
  waiting for transfers between devices: 1330 us -> 262 us
  matrix products: 485 us -> 72 us
  Pallas kernels: 0 us -> 250 us
  other arithmetic: 186 us -> 36.4 us
  starting transfers between devices: 0.31 us -> 107 us
  local copies, waits for them, and re-layouts: 81.6 us -> 24.1 us
    reduce_scatter x2 -> x0, waiting for transfers between devices: 884 us -> none  [the longest x1 884 us: shards(): lax.psum_scatter(wide_term, 'fsdp', scatter_dimension=0, tiled=True)]
    dot_general x43 -> x11, matrix products: 485 us -> 72 us  [dot(): return lax.dot_general(left, right, dims, preferred_element_type=WIDE)]
    all_gather x5 -> x0, waiting for transfers between devices: 368 us -> none  [the longest x1 168 us: shards(): lax.all_gather(w_ada, 'fsdp', axis=0, tiled=True)]
    ppermute x0 -> x96, waiting for transfers between devices: none -> 262 us  [hop(): return lax.ppermute(values, AXES, pairs)]
    pallas_call x0 -> x8, Pallas kernels: none -> 250 us  [the longest x6 159 us: token_call(): pl.pallas_call(body, grid=(grid,), in_specs=[smem, smem] + [pl.BlockSpec(...]
    ppermute x0 -> x96, starting transfers between devices: none -> 107 us  [hop(): return lax.ppermute(values, AXES, pairs)]
    psum x1 -> x0, waiting for transfers between devices: 78.6 us -> none  [shards(): lax.psum(reduced[0].astype(jnp.bfloat16), 'dp').astype(jnp.float32)]
    convert_element_type x10 -> x23, other arithmetic: 90.7 us -> 21 us  [the longest x4 8.8 us: reduce_rows(): values = add(keep, hop(send, dc=1)).astype(LOW)]
  transfers between devices with their start and end apart: 8 -> 96, of which waited for: 6 -> 34; matrix products, arithmetic and copies ran while one was open for 29% -> 15% of each run, Pallas kernels for 0% -> 11%
where the time goes in v1:
time: 800 us; the launch traced here: 793 us
  waiting for transfers between devices  262 us (33%)
  Pallas kernels  250 us (31%)
  starting transfers between devices  107 us (13%)
  matrix products  72 us (9%)
  blocking collectives  40.9 us (5%)
  other arithmetic  36.4 us (5%)
  local copies, waits for them, and re-layouts  24.1 us (3%)
    ppermute x96, waiting for transfers between devices, hop(): return lax.ppermute(values, AXES, pairs)  262 us
    pallas_call x6, Pallas kernels, token_call(): pl.pallas_call(body, grid=(grid,), in_specs=[smem, smem] + [pl.BlockSpec(...  159 us
    ppermute x96, starting transfers between devices, hop(): return lax.ppermute(values, AXES, pairs)  107 us
    dot_general x11, matrix products, dot(): return lax.dot_general(left, right, dims, preferred_element_type=WIDE)  72 us
    pallas_call x1, Pallas kernels, attend_back(): pl.pallas_call(attend_back_kernel, grid=(items, pairs), in_specs=[block]...  64.2 us
    psum x1, blocking collectives, shards(): lax.psum(head_sums.reshape(items, heads, width // heads).sum((0, 2)), AXES)  40.9 us
    pallas_call x1, Pallas kernels, attend(): pl.pallas_call(attend_kernel, grid=(items, pairs), in_specs=[block, block...  26.2 us
  transfers between devices with their start and end apart: 96, of which 34 were waited for; matrix products, arithmetic and copies ran while one was open for 15% of the time, Pallas kernels for 11%

profile of v1, /device:TPU:9, one launch (start us, length us, event | category | flops | bytes accessed | tf_op | source)
XLA Modules:
  0.0 793.5 jit_solution(6864214309651792044)
XLA Ops:
  3.1 2.2 collective-permute-start.8
  6.4 2.3 collective-permute-start.2
  17.9 3.0 collective-permute-start.58
  31.3 2.8 collective-permute-done.19
  40.2 4.0 collective-permute-done.28
  45.7 3.3 collective-permute-start.11
  49.9 11.5 %collective-permute-done.6 = f32[2,6144]{1,0:T(2,128)S(1)} collective-permute-done((f32[2,6144]{1,0:T(2,128)S(1)}, f32[2,6144]{1,0:T(2,128)S(1)}, u32[]{:S(2)}, u32[]{:S(2)}) %collective-permute-start.6) | collective-permute-done | bytes 49184 | tf_op jit(solution)/shard_map/ppermute | solution.py:57
  61.4 2.7 collective-permute-start.24
  66.4 2.0 collective-permute-done.7
  68.4 4.4 collective-permute-start.38
  75.9 4.5 collective-permute-done.38
  80.4 2.6 collective-permute-start.23
  83.0 7.4 collective-permute-done.39
  90.4 3.6 collective-permute-start.25
  94.0 4.1 collective-permute-done.40
  109.1 16.4 %collective-permute-done.31.refs_14_.refs_7_ = bf16[512,1024]{1,0:T(8,128)(2,1)} collective-permute-done((bf16[512,1024]{1,0:T(8,128)(2,1)}, bf16[512,1024]{1,0:T(8,128)(2,1)}, u32[]{:S(2)}, u32[]{:S(2)}) %collective-permute-start.31) | collective-permute-done | bytes 1048608 | tf_op jit(solution)/shard_map/ppermute | solution.py:57
  128.7 14.3 %collective-permute-done.13.refs_9_ = bf16[512,768]{1,0:T(8,128)(2,1)S(1)} collective-permute-done((bf16[512,768]{1,0:T(8,128)(2,1)}, bf16[512,768]{1,0:T(8,128)(2,1)S(1)}, u32[]{:S(2)}, u32[]{:S(2)}) %collective-permute-start.13) | collective-permute-done | bytes 786464 | tf_op jit(solution)/shard_map/ppermute | solution.py:57
  143.0 2.0 collective-permute-start.17
  147.5 18.1 %collective-permute-done.42.refs_8_.refs_4_ = bf16[2048,256]{1,0:T(8,128)(2,1)S(1)} collective-permute-done((bf16[2048,256]{1,0:T(8,128)(2,1)S(1)}, bf16[2048,256]{1,0:T(8,128)(2,1)S(1)}, u32[]{:S(2)}, u32[]{:S(2)}) %collective-permute-start.42) | collective-permute-done | bytes 1048608 | tf_op jit(solution)/shard_map/ppermute | solution.py:57
  168.8 19.2 %collective-permute-done.33.refs_16_.refs_9_ = bf16[512,1024]{1,0:T(8,128)(2,1)S(1)} collective-permute-done((bf16[512,1024]{1,0:T(8,128)(2,1)}, bf16[512,1024]{1,0:T(8,128)(2,1)S(1)}, u32[]{:S(2)}, u32[]{:S(2)}) %collective-permute-start.33) | collective-permute-done | bytes 1048608 | tf_op jit(solution)/shard_map/ppermute | solution.py:57
  189.1 23.6 %project.1 = (bf16[1360,1024]{1,0:T(8,128)(2,1)}, bf16[1360,1024]{1,0:T(8,128)(2,1)}, bf16[1360,1024]{1,0:T(8,128)(2,1)}, bf16[1360,1024]{1,0:T(8,128)(2,1)}, f32[1360,16]{1,0:T(8,128)}, /*index=5*/f32[1360,16]{1,0:T(8,128)}) custom-call(s32[4]{0:T(128)} %pad_add_fusion.place_ref, s32[2]{0:T(128)} %copy-done.28, bf16[1360,1024]{1,0:T(8,128)(2,1)} %refs_3_.5, ...), custom_call_target="tpu_custom_call" | custom-call | flops 8556380160 | bytes 20391936 | tf_op jit(solution)/shard_map/project/pallas_call | solution.py:413
  212.8 26.2 %attend.1 = (bf16[2,680,1024]{2,1,0:T(8,128)(2,1)}, bf16[2,680,1024]{2,1,0:T(8,128)(2,1)}) custom-call(bf16[2,680,1024]{2,1,0:T(8,128)(2,1)} %bitcast.188, bf16[2,680,1024]{2,1,0:T(8,128)(2,1)} %bitcast.190, bf16[2,680,1024]{2,1,0:T(8,128)(2,1)} %bitcast.192, bf16[680,128]{1,0:T(8,128)(2,1)} %constant.117.clone.qm_ref, bf16[680,128]{1,0:T(8,128)(2,1)} %constant.118.clone.km_ref), custom_call_target="tpu_custom_call" | custom-call | flops 9469952000 | bytes 13926400 | tf_op jit(solution)/shard_map/attend/pallas_call | solution.py:243
  241.1 39.2 %branch.1 = (bf16[1360,1024]{1,0:T(8,128)(2,1)}, bf16[1360,1024]{1,0:T(8,128)(2,1)}, bf16[1360,4096]{1,0:T(8,128)(2,1)}, bf16[1360,4096]{1,0:T(8,128)(2,1)}, f32[8,1024]{1,0:T(8,128)}) custom-call(s32[4]{0:T(128)} %pad_add_fusion.place_ref, s32[2]{0:T(128)} %copy-done.28, bf16[1360,1024]{1,0:T(8,128)(2,1)} %bitcast.185, bf16[1360,1024]{1,0:T(8,128)(2,1)} %refs_3_.5, ...), custom_call_target="tpu_custom_call" | custom-call | flops 14260633600 | bytes 43909120 | tf_op jit(solution)/shard_map/branch/pallas_call | solution.py:413
  281.3 25.0 %stream.1 = (bf16[1360,1024]{1,0:T(8,128)(2,1)}, bf16[1360,1024]{1,0:T(8,128)(2,1)}, f32[8,1024]{1,0:T(8,128)}) custom-call(s32[4]{0:T(128)} %pad_add_fusion.place_ref, s32[2]{0:T(128)} %copy-done.28, bf16[1360,4096]{1,0:T(8,128)(2,1)} %get-tuple-element.45.refs_0_, bf16[1360,1024]{1,0:T(8,128)(2,1)} %refs_3_.5, ...), custom_call_target="tpu_custom_call" | custom-call | flops 11408506880 | bytes 33456128 | tf_op jit(solution)/shard_map/stream/pallas_call | solution.py:413
  306.4 19.7 %hidden_back.1.refs_0_ = bf16[1360,4096]{1,0:T(8,128)(2,1)} custom-call(s32[4]{0:T(128)} %pad_add_fusion.place_ref, s32[2]{0:T(128)} %copy-done.28, bf16[1360,1024]{1,0:T(8,128)(2,1)} %get-tuple-element.50.refs_0_, bf16[1360,4096]{1,0:T(8,128)(2,1)} %get-tuple-element.51.refs_1_, bf16[2048,256]{1,0:T(8,128)(2,1)} %copy-done.6, ...), custom_call_target="tpu_custom_call" | custom-call | flops 11408506880 | bytes 33456128 | tf_op jit(solution)/shard_map/hidden_back/pallas_call | solution.py:413
  326.1 31.4 %middle_back.1 = (bf16[1360,1024]{1,0:T(8,128)(2,1)}, bf16[1360,1024]{1,0:T(8,128)(2,1)}, bf16[1360,1024]{1,0:T(8,128)(2,1)}, f32[8,1024]{1,0:T(8,128)}) custom-call(s32[4]{0:T(128)} %pad_add_fusion.place_ref, s32[2]{0:T(128)} %copy-done.28, bf16[1360,4096]{1,0:T(8,128)(2,1)} %hidden_back.1.refs_0_, bf16[1360,1024]{1,0:T(8,128)(2,1)} %refs_3_.5, ...), custom_call_target="tpu_custom_call" | custom-call | flops 14260633600 | bytes 38338560 | tf_op jit(solution)/shard_map/middle_back/pallas_call | solution.py:413
  359.1 64.2 %attend_back.1 = (bf16[2,680,1024]{2,1,0:T(8,128)(2,1)}, bf16[2,680,1024]{2,1,0:T(8,128)(2,1)}, bf16[2,680,1024]{2,1,0:T(8,128)(2,1)}, f32[2,1,1024]{2,1,0:T(1,128)}) custom-call(bf16[2,680,1024]{2,1,0:T(8,128)(2,1)} %bitcast.189, bf16[2,680,1024]{2,1,0:T(8,128)(2,1)} %bitcast.191, bf16[2,680,1024]{2,1,0:T(8,128)(2,1)} %bitcast.193, ...), custom_call_target="tpu_custom_call" | custom-call | flops 24621875200 | bytes 30638080 | tf_op jit(solution)/shard_map/attend_back/pallas_call | solution.py:328
  423.3 7.1 pad_maximum_fusion
  430.4 20.2 %token_back.1 = (bf16[1360,1024]{1,0:T(8,128)(2,1)}, f32[8,1024]{1,0:T(8,128)}) custom-call(s32[4]{0:T(128)} %pad_add_fusion.place_ref, s32[2]{0:T(128)} %copy-done.28, bf16[1360,1024]{1,0:T(8,128)(2,1)} %bitcast.123, bf16[1360,1024]{1,0:T(8,128)(2,1)} %bitcast.125, bf16[1360,1024]{1,0:T(8,128)(2,1)} %bitcast.127, bf16[1360,1024]{1,0:T(8,128)(2,1)} %refs_3_.5, ...), custom_call_target="tpu_custom_call" | custom-call | flops 8556380160 | bytes 23003136 | tf_op jit(solution)/shard_map/token_back/pallas_call | solution.py:413
  454.9 13.0 %convolution_convert_fusion = bf16[4096,512]{1,0:T(8,128)(2,1)} fusion(bf16[1360,4096]{1,0:T(8,128)(2,1)} %get-tuple-element.45.refs_0_, bf16[1360,1024]{1,0:T(8,128)(2,1)S(1)} %copy-done.31, s32[]{:T(128)S(6)} %select_n.565), kind=kOutput, calls=%fused_computation.4 | convolution fusion | flops 5706350592 | bytes 16728068 | tf_op jit(solution)/shard_map/dot_general | solution.py:25
  468.9 13.5 %convolution_convert_fusion.1 = bf16[4096,512]{1,0:T(8,128)(2,1)} fusion(bf16[1360,4096]{1,0:T(8,128)(2,1)} %get-tuple-element.45.refs_0_, bf16[1360,1024]{1,0:T(8,128)(2,1)S(1)} %copy-done.31, s32[]{:T(128)S(6)} %select_n.564), kind=kOutput, calls=%fused_computation.5 | convolution fusion | flops 5706350592 | bytes 16728068 | tf_op jit(solution)/shard_map/dot_general | solution.py:25
  482.5 8.6 %fusion.9 = bf16[1024,2048]{1,0:T(8,128)(2,1)} fusion(bf16[1360,1024]{1,0:T(8,128)(2,1)S(1)} %copy-done.32, bf16[1360,4096]{1,0:T(8,128)(2,1)S(1)} %bitcast.198, s32[]{:T(128)S(6)} %select_n.593), kind=kOutput, calls=%fused_computation.17 | convolution fusion | flops 5706350592 | bytes 12550148 | tf_op jit(solution)/shard_map/dot_general | solution.py:25
  491.1 8.6 %fusion.2 = bf16[1024,2048]{1,0:T(8,128)(2,1)} fusion(bf16[1360,1024]{1,0:T(8,128)(2,1)S(1)} %copy-done.32, bf16[1360,4096]{1,0:T(8,128)(2,1)S(1)} %bitcast.198, s32[]{:T(128)S(6)} %select_n.592), kind=kOutput, calls=%fused_computation.8 | convolution fusion | flops 5704253440 | bytes 12550148 | tf_op jit(solution)/shard_map/dot_general | solution.py:25
  499.8 2.8 convolution_convert_fusion.2
  504.2 6.9 fusion.12
  512.4 2.8 collective-permute-done.51
  517.4 9.0 %fusion.15 = bf16[1024,1536]{1,0:T(8,128)(2,1)} fusion(bf16[1360,1024]{1,0:T(8,128)(2,1)} %get-tuple-element.63, bf16[1360,3072]{1,0:T(8,128)(2,1)} %pad_maximum_fusion, s32[]{:T(128)S(6)} %select_n.533), kind=kOutput, calls=%fused_computation.19 | convolution fusion | flops 4279762944 | bytes 10108932 | tf_op jit(solution)/shard_map/dot_general | solution.py:25
  526.7 5.0 convolution_convert_fusion.3
  531.7 5.1 collective-permute-done.53
  540.8 40.9 %psum.7 = f32[16]{0:T(128)} all-reduce(f32[16]{0:T(128)S(1)} %reduce_sum.55), channel_id=1, replica_groups=mesh['dp'=4,'fsdp'=8] {'dp','fsdp'}, use_global_device_ids=true, to_apply=%region_3.4 | all-reduce | flops 16 | bytes 128 | tf_op jit(solution)/shard_map/psum | solution.py:682
  583.8 2.1 collective-permute-start.57
  585.9 3.0 fusion.38
  590.2 12.3 %collective-permute-done.70 = bf16[1024,256]{1,0:T(8,128)(2,1)S(1)} collective-permute-done((bf16[1024,256]{1,0:T(8,128)(2,1)S(1)}, bf16[1024,256]{1,0:T(8,128)(2,1)S(1)}, u32[]{:S(2)}, u32[]{:S(2)}) %collective-permute-start.70) | collective-permute-done | bytes 524320 | tf_op jit(solution)/shard_map/ppermute | solution.py:57
  602.9 6.6 collective-permute-done.71
  609.7 2.7 add_convert_fusion.2
  615.2 3.5 add_convert_fusion
  621.6 2.3 add_convert_fusion.1
  623.9 23.9 %collective-permute-done.61 = bf16[512,1536]{1,0:T(8,128)(2,1)} collective-permute-done((bf16[512,1536]{1,0:T(8,128)(2,1)}, bf16[512,1536]{1,0:T(8,128)(2,1)}, u32[]{:S(2)}, u32[]{:S(2)}) %collective-permute-start.61) | collective-permute-done | bytes 1572896 | tf_op jit(solution)/shard_map/ppermute | solution.py:57
  652.0 2.1 collective-permute-start.73
  656.1 2.3 collective-permute-done.74
  658.6 23.6 %collective-permute-done.62 = bf16[512,768]{1,0:T(8,128)(2,1)S(1)} collective-permute-done((bf16[512,768]{1,0:T(8,128)(2,1)S(1)}, bf16[512,768]{1,0:T(8,128)(2,1)S(1)}, u32[]{:S(2)}, u32[]{:S(2)}) %collective-permute-start.62) | collective-permute-done | bytes 786464 | tf_op jit(solution)/shard_map/ppermute | solution.py:57
  685.9 8.7 %collective-permute-done.79 = bf16[512,2048]{1,0:T(8,128)(2,1)S(1)} collective-permute-done((bf16[512,2048]{1,0:T(8,128)(2,1)S(1)}, bf16[512,2048]{1,0:T(8,128)(2,1)S(1)}, u32[]{:S(2)}, u32[]{:S(2)}) %collective-permute-start.79) | collective-permute-done | bytes 2097184 | tf_op jit(solution)/shard_map/ppermute | solution.py:57
  695.9 6.1 collective-permute-start.76
  705.8 24.8 %collective-permute-done.66 = bf16[128,768]{1,0:T(8,128)(2,1)S(1)} collective-permute-done((bf16[128,768]{1,0:T(8,128)(2,1)S(1)}, bf16[128,768]{1,0:T(8,128)(2,1)S(1)}, u32[]{:S(2)}, u32[]{:S(2)}) %collective-permute-start.66) | collective-permute-done | bytes 196640 | tf_op jit(solution)/shard_map/ppermute | solution.py:57
  735.6 9.1 %collective-permute-done.90 = bf16[512,256]{1,0:T(8,128)(2,1)S(1)} collective-permute-done((bf16[512,256]{1,0:T(8,128)(2,1)S(1)}, bf16[512,256]{1,0:T(8,128)(2,1)S(1)}, u32[]{:S(2)}, u32[]{:S(2)}) %collective-permute-start.90) | collective-permute-done | bytes 262176 | tf_op jit(solution)/shard_map/ppermute | solution.py:57
  744.7 2.2 collective-permute-start.81
  746.9 4.2 collective-permute-done.91
  751.1 3.5 collective-permute-start.82
  754.6 13.6 %collective-permute-done.92 = bf16[512,256]{1,0:T(8,128)(2,1)S(1)} collective-permute-done((bf16[512,256]{1,0:T(8,128)(2,1)S(1)}, bf16[512,256]{1,0:T(8,128)(2,1)S(1)}, u32[]{:S(2)}, u32[]{:S(2)}) %collective-permute-start.92) | collective-permute-done | bytes 262176 | tf_op jit(solution)/shard_map/ppermute | solution.py:57
  768.2 2.3 collective-permute-start.83
  771.1 2.3 collective-permute-start.94
  774.0 6.7 collective-permute-done.83
  783.8 3.9 collective-permute-done.84
  787.7 2.0 collective-permute-start.86
  (363 shorter events, 114.2 us)
Async XLA Ops:
  1.7 24.6 %collective-permute-start.10 = (bf16[128,768]{1,0:T(8,128)(2,1)S(1)}, bf16[128,768]{1,0:T(8,128)(2,1)S(1)}, u32[]{:S(2)}, u32[]{:S(2)}) collective-permute-start(bf16[128,768]{1,0:T(8,128)(2,1)S(1)} %constant_dynamic-slice_fusion.45), channel_id=1, source_target_pairs={{0,6},{1,7},{2,4},{3,5},{4,2},{5,3},{6,0},{7,1},{8,14},{9,15},{10,... | collective-permute-start | bytes 589832 | tf_op jit(solution)/shard_map/ppermute | solution.py:57
  3.1 23.2 %collective-permute-start.8 = (bf16[128,768]{1,0:T(8,128)(2,1)S(1)}, bf16[128,768]{1,0:T(8,128)(2,1)S(1)}, u32[]{:S(2)}, u32[]{:S(2)}) collective-permute-start(bf16[128,768]{1,0:T(8,128)(2,1)S(1)} %constant_dynamic-slice_fusion.45), channel_id=1, source_target_pairs={{0,2},{1,3},{2,0},{3,1},{4,6},{5,7},{6,4},{7,5},{8,10},{9,11},{10,... | collective-permute-start | bytes 589832 | tf_op jit(solution)/shard_map/ppermute | solution.py:57
  14.0 12.3 %collective-permute-start.9 = (bf16[128,768]{1,0:T(8,128)(2,1)S(1)}, bf16[128,768]{1,0:T(8,128)(2,1)}, u32[]{:S(2)}, u32[]{:S(2)}) collective-permute-start(bf16[128,768]{1,0:T(8,128)(2,1)S(1)} %constant_dynamic-slice_fusion.45), channel_id=1, source_target_pairs={{0,4},{1,5},{2,6},{3,7},{4,0},{5,1},{6,2},{7,3},{8,12},{9,13},{10,... | collective-permute-start | bytes 589832 | tf_op jit(solution)/shard_map/ppermute | solution.py:57
  25.1 20.6 %collective-permute-start.59 = (bf16[2,16,1024]{2,1,0:T(8,128)(2,1)S(1)}, bf16[2,16,1024]{2,1,0:T(8,128)(2,1)S(1)}, u32[]{:S(2)}, u32[]{:S(2)}) collective-permute-start(bf16[2,16,1024]{2,1,0:T(8,128)(2,1)S(1)} %pad_maximum_fusion.10), channel_id=1, source_target_pairs={{0,16},{1,17},{2,18},{3,19},{4,20},{5,21},{6,22},{7,23},{8,24},{9,... | collective-permute-start | bytes 196616 | tf_op jit(solution)/shard_map/ppermute | solution.py:57
  36.7 24.7 %collective-permute-start.29 = (bf16[128,1024]{1,0:T(8,128)(2,1)S(1)}, bf16[128,1024]{1,0:T(8,128)(2,1)S(1)}, u32[]{:S(2)}, u32[]{:S(2)}) collective-permute-start(bf16[128,1024]{1,0:T(8,128)(2,1)S(1)} %constant_dynamic-slice_fusion.43), channel_id=1, source_target_pairs={{0,4},{1,5},{2,6},{3,7},{4,0},{5,1},{6,2},{7,3},{8,12},{9,13},{10,... | collective-permute-start | bytes 786440 | tf_op jit(solution)/shard_map/ppermute | solution.py:57
  38.6 26.3 %collective-permute-start.30 = (bf16[128,1024]{1,0:T(8,128)(2,1)S(1)}, bf16[128,1024]{1,0:T(8,128)(2,1)S(1)}, u32[]{:S(2)}, u32[]{:S(2)}) collective-permute-start(bf16[128,1024]{1,0:T(8,128)(2,1)S(1)} %constant_dynamic-slice_fusion.43), channel_id=1, source_target_pairs={{0,6},{1,7},{2,4},{3,5},{4,2},{5,3},{6,0},{7,1},{8,14},{9,15},{10,... | collective-permute-start | bytes 786440 | tf_op jit(solution)/shard_map/ppermute | solution.py:57
  44.2 17.3 %collective-permute-start.6 = (f32[2,6144]{1,0:T(2,128)S(1)}, f32[2,6144]{1,0:T(2,128)S(1)}, u32[]{:S(2)}, u32[]{:S(2)}) collective-permute-start(f32[2,6144]{1,0:T(2,128)S(1)} %get-tuple-element.152), channel_id=1, source_target_pairs={{0,4},{1,5},{2,6},{3,7},{4,0},{5,1},{6,2},{7,3},{8,12},{9,13},{10,... | collective-permute-start | bytes 147464 | tf_op jit(solution)/shard_map/ppermute | solution.py:57
  45.7 55.9 %collective-permute-start.11 = (bf16[512,768]{1,0:T(8,128)(2,1)}, bf16[512,768]{1,0:T(8,128)(2,1)}, u32[]{:S(2)}, u32[]{:S(2)}) collective-permute-start(bf16[512,768]{1,0:T(8,128)(2,1)} %pad_maximum_fusion.1.refs_6_), channel_id=1, source_target_pairs={{0,1},{1,0},{2,3},{3,2},{4,5},{5,4},{6,7},{7,6},{8,9},{9,8},{10,11... | collective-permute-start | bytes 2359304 | tf_op jit(solution)/shard_map/ppermute | solution.py:57
  49.0 23.8 %collective-permute-start.22 = (bf16[512,256]{1,0:T(8,128)(2,1)S(1)}, bf16[512,256]{1,0:T(8,128)(2,1)}, u32[]{:S(2)}, u32[]{:S(2)}) collective-permute-start(bf16[512,256]{1,0:T(8,128)(2,1)S(1)} %constant_dynamic-update-slice_fusion.8.refs_5_.refs_14_), channel_id=1, source_target_pairs={{0,16},{1,17},{2,18},{3,19},{4,20},{5,21},{6,22},{7,23},{8,24},{9,... | collective-permute-start | bytes 786440 | tf_op jit(solution)/shard_map/ppermute | solution.py:57
  61.4 13.3 %collective-permute-start.21 = (bf16[512,256]{1,0:T(8,128)(2,1)S(1)}, bf16[512,256]{1,0:T(8,128)(2,1)}, u32[]{:S(2)}, u32[]{:S(2)}) collective-permute-start(bf16[512,256]{1,0:T(8,128)(2,1)S(1)} %constant_dynamic-update-slice_fusion.8.refs_5_.refs_14_), channel_id=1, source_target_pairs={{0,1},{1,0},{2,3},{3,2},{4,5},{5,4},{6,7},{7,6},{8,9},{9,8},{10,11... | collective-permute-start | bytes 786440 | tf_op jit(solution)/shard_map/ppermute | solution.py:57
  61.4 13.3 %collective-permute-start.24 = (bf16[512,256]{1,0:T(8,128)(2,1)S(1)}, bf16[512,256]{1,0:T(8,128)(2,1)}, u32[]{:S(2)}, u32[]{:S(2)}) collective-permute-start(bf16[512,256]{1,0:T(8,128)(2,1)S(1)} %constant_dynamic-update-slice_fusion.8.refs_5_.refs_14_), channel_id=1, source_target_pairs={{0,8},{1,9},{2,10},{3,11},{4,12},{5,13},{6,14},{7,15},{8,0},{9,1},... | collective-permute-start | bytes 786440 | tf_op jit(solution)/shard_map/ppermute | solution.py:57
  72.8 31.1 %collective-permute-start.12 = (bf16[512,768]{1,0:T(8,128)(2,1)}, bf16[512,768]{1,0:T(8,128)(2,1)}, u32[]{:S(2)}, u32[]{:S(2)}) collective-permute-start(bf16[512,768]{1,0:T(8,128)(2,1)} %pad_maximum_fusion.1.refs_6_), channel_id=1, source_target_pairs={{0,16},{1,17},{2,18},{3,19},{4,20},{5,21},{6,22},{7,23},{8,24},{9,... | collective-permute-start | bytes 2359304 | tf_op jit(solution)/shard_map/ppermute | solution.py:57
  74.7 15.7 %collective-permute-start.39 = (bf16[512,256]{1,0:T(8,128)(2,1)S(1)}, bf16[512,256]{1,0:T(8,128)(2,1)S(1)}, u32[]{:S(2)}, u32[]{:S(2)}) collective-permute-start(bf16[512,256]{1,0:T(8,128)(2,1)S(1)} %constant_dynamic-slice_fusion.42), channel_id=1, source_target_pairs={{0,4},{1,5},{2,6},{3,7},{4,0},{5,1},{6,2},{7,3},{8,12},{9,13},{10,... | collective-permute-start | bytes 786440 | tf_op jit(solution)/shard_map/ppermute | solution.py:57
  74.7 23.4 %collective-permute-start.40 = (bf16[512,256]{1,0:T(8,128)(2,1)S(1)}, bf16[512,256]{1,0:T(8,128)(2,1)S(1)}, u32[]{:S(2)}, u32[]{:S(2)}) collective-permute-start(bf16[512,256]{1,0:T(8,128)(2,1)S(1)} %constant_dynamic-slice_fusion.42), channel_id=1, source_target_pairs={{0,6},{1,7},{2,4},{3,5},{4,2},{5,3},{6,0},{7,1},{8,14},{9,15},{10,... | collective-permute-start | bytes 786440 | tf_op jit(solution)/shard_map/ppermute | solution.py:57
  80.4 19.8 %collective-permute-start.23 = (bf16[512,256]{1,0:T(8,128)(2,1)}, bf16[512,256]{1,0:T(8,128)(2,1)}, u32[]{:S(2)}, u32[]{:S(2)}) collective-permute-start(bf16[512,256]{1,0:T(8,128)(2,1)} %collective-permute-done.22.refs_7_.refs_16_), channel_id=1, source_target_pairs={{0,1},{1,0},{2,3},{3,2},{4,5},{5,4},{6,7},{7,6},{8,9},{9,8},{10,11... | collective-permute-start | bytes 786440 | tf_op jit(solution)/shard_map/ppermute | solution.py:57
  100.9 24.6 %collective-permute-start.31 = (bf16[512,1024]{1,0:T(8,128)(2,1)}, bf16[512,1024]{1,0:T(8,128)(2,1)}, u32[]{:S(2)}, u32[]{:S(2)}) collective-permute-start(bf16[512,1024]{1,0:T(8,128)(2,1)} %constant_dynamic-update-slice_fusion.12.refs_13_.refs_6_), channel_id=1, source_target_pairs={{0,1},{1,0},{2,3},{3,2},{4,5},{5,4},{6,7},{7,6},{8,9},{9,8},{10,11... | collective-permute-start | bytes 3145736 | tf_op jit(solution)/shard_map/ppermute | solution.py:57
  101.6 25.3 %collective-permute-start.32 = (bf16[512,1024]{1,0:T(8,128)(2,1)}, bf16[512,1024]{1,0:T(8,128)(2,1)}, u32[]{:S(2)}, u32[]{:S(2)}) collective-permute-start(bf16[512,1024]{1,0:T(8,128)(2,1)} %constant_dynamic-update-slice_fusion.12.refs_13_.refs_6_), channel_id=1, source_target_pairs={{0,16},{1,17},{2,18},{3,19},{4,20},{5,21},{6,22},{7,23},{8,24},{9,... | collective-permute-start | bytes 3145736 | tf_op jit(solution)/shard_map/ppermute | solution.py:57
  101.6 26.6 %collective-permute-start.34 = (bf16[512,1024]{1,0:T(8,128)(2,1)}, bf16[512,1024]{1,0:T(8,128)(2,1)}, u32[]{:S(2)}, u32[]{:S(2)}) collective-permute-start(bf16[512,1024]{1,0:T(8,128)(2,1)} %constant_dynamic-update-slice_fusion.12.refs_13_.refs_6_), channel_id=1, source_target_pairs={{0,8},{1,9},{2,10},{3,11},{4,12},{5,13},{6,14},{7,15},{8,0},{9,1},... | collective-permute-start | bytes 3145736 | tf_op jit(solution)/shard_map/ppermute | solution.py:57
  103.9 39.1 %collective-permute-start.13 = (bf16[512,768]{1,0:T(8,128)(2,1)}, bf16[512,768]{1,0:T(8,128)(2,1)S(1)}, u32[]{:S(2)}, u32[]{:S(2)}) collective-permute-start(bf16[512,768]{1,0:T(8,128)(2,1)} %collective-permute-done.11.refs_7_), channel_id=1, source_target_pairs={{0,16},{1,17},{2,18},{3,19},{4,20},{5,21},{6,22},{7,23},{8,24},{9,... | collective-permute-start | bytes 2359304 | tf_op jit(solution)/shard_map/ppermute | solution.py:57
  108.4 57.2 %collective-permute-start.42 = (bf16[2048,256]{1,0:T(8,128)(2,1)S(1)}, bf16[2048,256]{1,0:T(8,128)(2,1)S(1)}, u32[]{:S(2)}, u32[]{:S(2)}) collective-permute-start(bf16[2048,256]{1,0:T(8,128)(2,1)S(1)} %constant_dynamic-update-slice_fusion.16.refs_6_.refs_2_), channel_id=1, source_target_pairs={{0,16},{1,17},{2,18},{3,19},{4,20},{5,21},{6,22},{7,23},{8,24},{9,... | collective-permute-start | bytes 3145736 | tf_op jit(solution)/shard_map/ppermute | solution.py:57
  125.5 20.2 %collective-permute-start.15 = (bf16[512,768]{1,0:T(8,128)(2,1)}, bf16[512,768]{1,0:T(8,128)(2,1)S(1)}, u32[]{:S(2)}, u32[]{:S(2)}) collective-permute-start(bf16[512,768]{1,0:T(8,128)(2,1)} %collective-permute-done.11.refs_7_), channel_id=1, source_target_pairs={{0,8},{1,9},{2,10},{3,11},{4,12},{5,13},{6,14},{7,15},{8,0},{9,1},... | collective-permute-start | bytes 2359304 | tf_op jit(solution)/shard_map/ppermute | solution.py:57
  126.8 20.3 %collective-permute-start.16 = (bf16[512,768]{1,0:T(8,128)(2,1)}, bf16[512,768]{1,0:T(8,128)(2,1)}, u32[]{:S(2)}, u32[]{:S(2)}) collective-permute-start(bf16[512,768]{1,0:T(8,128)(2,1)} %collective-permute-done.12.refs_8_), channel_id=1, source_target_pairs={{0,8},{1,9},{2,10},{3,11},{4,12},{5,13},{6,14},{7,15},{8,0},{9,1},... | collective-permute-start | bytes 2359304 | tf_op jit(solution)/shard_map/ppermute | solution.py:57
  128.2 59.8 %collective-permute-start.33 = (bf16[512,1024]{1,0:T(8,128)(2,1)}, bf16[512,1024]{1,0:T(8,128)(2,1)S(1)}, u32[]{:S(2)}, u32[]{:S(2)}) collective-permute-start(bf16[512,1024]{1,0:T(8,128)(2,1)} %collective-permute-done.31.refs_14_.refs_7_), channel_id=1, source_target_pairs={{0,16},{1,17},{2,18},{3,19},{4,20},{5,21},{6,22},{7,23},{8,24},{9,... | collective-permute-start | bytes 3145736 | tf_op jit(solution)/shard_map/ppermute | solution.py:57
  143.0 24.5 %collective-permute-start.17 = (bf16[512,768]{1,0:T(8,128)(2,1)S(1)}, bf16[512,768]{1,0:T(8,128)(2,1)S(1)}, u32[]{:S(2)}, u32[]{:S(2)}) collective-permute-start(bf16[512,768]{1,0:T(8,128)(2,1)S(1)} %collective-permute-done.13.refs_9_), channel_id=1, source_target_pairs={{0,8},{1,9},{2,10},{3,11},{4,12},{5,13},{6,14},{7,15},{8,0},{9,1},... | collective-permute-start | bytes 2359304 | tf_op jit(solution)/shard_map/ppermute | solution.py:57
  145.7 93.3 %collective-permute-start.41 = (bf16[2048,256]{1,0:T(8,128)(2,1)S(1)}, bf16[2048,256]{1,0:T(8,128)(2,1)}, u32[]{:S(2)}, u32[]{:S(2)}) collective-permute-start(bf16[2048,256]{1,0:T(8,128)(2,1)S(1)} %constant_dynamic-update-slice_fusion.16.refs_6_.refs_2_), channel_id=1, source_target_pairs={{0,1},{1,0},{2,3},{3,2},{4,5},{5,4},{6,7},{7,6},{8,9},{9,8},{10,11... | collective-permute-start | bytes 3145736 | tf_op jit(solution)/shard_map/ppermute | solution.py:57
  147.1 92.1 %collective-permute-start.35 = (bf16[512,1024]{1,0:T(8,128)(2,1)}, bf16[512,1024]{1,0:T(8,128)(2,1)S(1)}, u32[]{:S(2)}, u32[]{:S(2)}) collective-permute-start(bf16[512,1024]{1,0:T(8,128)(2,1)} %collective-permute-done.31.refs_14_.refs_7_), channel_id=1, source_target_pairs={{0,8},{1,9},{2,10},{3,11},{4,12},{5,13},{6,14},{7,15},{8,0},{9,1},... | collective-permute-start | bytes 3145736 | tf_op jit(solution)/shard_map/ppermute | solution.py:57
  165.6 74.0 %collective-permute-start.36 = (bf16[512,1024]{1,0:T(8,128)(2,1)}, bf16[512,1024]{1,0:T(8,128)(2,1)S(1)}, u32[]{:S(2)}, u32[]{:S(2)}) collective-permute-start(bf16[512,1024]{1,0:T(8,128)(2,1)} %collective-permute-done.32.refs_15_.refs_8_), channel_id=1, source_target_pairs={{0,8},{1,9},{2,10},{3,11},{4,12},{5,13},{6,14},{7,15},{8,0},{9,1},... | collective-permute-start | bytes 3145736 | tf_op jit(solution)/shard_map/ppermute | solution.py:57
  167.5 72.3 %collective-permute-start.43 = (bf16[2048,256]{1,0:T(8,128)(2,1)S(1)}, bf16[2048,256]{1,0:T(8,128)(2,1)}, u32[]{:S(2)}, u32[]{:S(2)}) collective-permute-start(bf16[2048,256]{1,0:T(8,128)(2,1)S(1)} %collective-permute-done.42.refs_8_.refs_4_), channel_id=1, source_target_pairs={{0,1},{1,0},{2,3},{3,2},{4,5},{5,4},{6,7},{7,6},{8,9},{9,8},{10,11... | collective-permute-start | bytes 3145736 | tf_op jit(solution)/shard_map/ppermute | solution.py:57
  188.0 52.1 %collective-permute-start.37 = (bf16[512,1024]{1,0:T(8,128)(2,1)S(1)}, bf16[512,1024]{1,0:T(8,128)(2,1)S(1)}, u32[]{:S(2)}, u32[]{:S(2)}) collective-permute-start(bf16[512,1024]{1,0:T(8,128)(2,1)S(1)} %collective-permute-done.33.refs_16_.refs_9_), channel_id=1, source_target_pairs={{0,8},{1,9},{2,10},{3,11},{4,12},{5,13},{6,14},{7,15},{8,0},{9,1},... | collective-permute-start | bytes 3145736 | tf_op jit(solution)/shard_map/ppermute | solution.py:57
  239.0 42.3 %collective-permute-start.44 = (bf16[2048,256]{1,0:T(8,128)(2,1)S(1)}, bf16[2048,256]{1,0:T(8,128)(2,1)}, u32[]{:S(2)}, u32[]{:S(2)}) collective-permute-start(bf16[2048,256]{1,0:T(8,128)(2,1)S(1)} %constant_dynamic-update-slice_fusion.16.refs_6_.refs_2_), channel_id=1, source_target_pairs={{0,8},{1,9},{2,10},{3,11},{4,12},{5,13},{6,14},{7,15},{8,0},{9,1},... | collective-permute-start | bytes 3145736 | tf_op jit(solution)/shard_map/ppermute | solution.py:57
  239.2 42.1 %collective-permute-start.46 = (bf16[2048,256]{1,0:T(8,128)(2,1)S(1)}, bf16[2048,256]{1,0:T(8,128)(2,1)}, u32[]{:S(2)}, u32[]{:S(2)}) collective-permute-start(bf16[2048,256]{1,0:T(8,128)(2,1)S(1)} %collective-permute-done.42.refs_8_.refs_4_), channel_id=1, source_target_pairs={{0,8},{1,9},{2,10},{3,11},{4,12},{5,13},{6,14},{7,15},{8,0},{9,1},... | collective-permute-start | bytes 3145736 | tf_op jit(solution)/shard_map/ppermute | solution.py:57
  239.6 41.7 %collective-permute-start.45 = (bf16[2048,256]{1,0:T(8,128)(2,1)}, bf16[2048,256]{1,0:T(8,128)(2,1)}, u32[]{:S(2)}, u32[]{:S(2)}) collective-permute-start(bf16[2048,256]{1,0:T(8,128)(2,1)} %collective-permute-done.41.refs_7_.refs_3_), channel_id=1, source_target_pairs={{0,8},{1,9},{2,10},{3,11},{4,12},{5,13},{6,14},{7,15},{8,0},{9,1},... | collective-permute-start | bytes 3145736 | tf_op jit(solution)/shard_map/ppermute | solution.py:57
  239.8 41.5 %collective-permute-start.47 = (bf16[2048,256]{1,0:T(8,128)(2,1)}, bf16[2048,256]{1,0:T(8,128)(2,1)}, u32[]{:S(2)}, u32[]{:S(2)}) collective-permute-start(bf16[2048,256]{1,0:T(8,128)(2,1)} %collective-permute-done.43.refs_9_.refs_5_), channel_id=1, source_target_pairs={{0,8},{1,9},{2,10},{3,11},{4,12},{5,13},{6,14},{7,15},{8,0},{9,1},... | collective-permute-start | bytes 3145736 | tf_op jit(solution)/shard_map/ppermute | solution.py:57
  452.2 58.9 %collective-permute-start.48 = (bf16[2,6144]{1,0:T(2,128)(2,1)S(1)}, bf16[2,6144]{1,0:T(2,128)(2,1)S(1)}, u32[]{:S(2)}, u32[]{:S(2)}) collective-permute-start(bf16[2,6144]{1,0:T(2,128)(2,1)S(1)} %constant_dynamic-update-slice_fusion.26), channel_id=1, source_target_pairs={{0,2},{1,3},{2,0},{3,1},{4,6},{5,7},{6,4},{7,5},{8,10},{9,11},{10,... | collective-permute-start | bytes 73736 | tf_op jit(solution)/shard_map/ppermute | solution.py:57
  452.2 58.8 %collective-permute-start.49 = (bf16[2,6144]{1,0:T(2,128)(2,1)S(1)}, bf16[2,6144]{1,0:T(2,128)(2,1)S(1)}, u32[]{:S(2)}, u32[]{:S(2)}) collective-permute-start(bf16[2,6144]{1,0:T(2,128)(2,1)S(1)} %constant_dynamic-update-slice_fusion.26), channel_id=1, source_target_pairs={{0,4},{1,5},{2,6},{3,7},{4,0},{5,1},{6,2},{7,3},{8,12},{9,13},{10,... | collective-permute-start | bytes 73736 | tf_op jit(solution)/shard_map/ppermute | solution.py:57
  453.7 57.4 %collective-permute-start.50 = (bf16[2,6144]{1,0:T(2,128)(2,1)S(1)}, bf16[2,6144]{1,0:T(2,128)(2,1)S(1)}, u32[]{:S(2)}, u32[]{:S(2)}) collective-permute-start(bf16[2,6144]{1,0:T(2,128)(2,1)S(1)} %constant_dynamic-update-slice_fusion.26), channel_id=1, source_target_pairs={{0,6},{1,7},{2,4},{3,5},{4,2},{5,3},{6,0},{7,1},{8,14},{9,15},{10,... | collective-permute-start | bytes 73736 | tf_op jit(solution)/shard_map/ppermute | solution.py:57
  467.9 145.9 %collective-permute-start.87 = (bf16[4096,512]{1,0:T(8,128)(2,1)}, bf16[4096,512]{1,0:T(8,128)(2,1)}, u32[]{:S(2)}, u32[]{:S(2)}) collective-permute-start(bf16[4096,512]{1,0:T(8,128)(2,1)} %convolution_convert_fusion), channel_id=1, source_target_pairs={{0,8},{1,9},{2,10},{3,11},{4,12},{5,13},{6,14},{7,15},{8,0},{9,1},... | collective-permute-start | bytes 12582920 | tf_op jit(solution)/shard_map/ppermute | solution.py:57
  502.6 86.3 %collective-permute-start.69 = (bf16[1024,512]{1,0:T(8,128)(2,1)}, bf16[1024,512]{1,0:T(8,128)(2,1)S(1)}, u32[]{:S(2)}, u32[]{:S(2)}) collective-permute-start(bf16[1024,512]{1,0:T(8,128)(2,1)} %convolution_convert_fusion.2), channel_id=1, source_target_pairs={{0,8},{1,9},{2,10},{3,11},{4,12},{5,13},{6,14},{7,15},{8,0},{9,1},... | collective-permute-start | bytes 3145736 | tf_op jit(solution)/shard_map/ppermute | solution.py:57
  526.4 83.3 %collective-permute-start.60 = (bf16[1024,1536]{1,0:T(8,128)(2,1)}, bf16[1024,1536]{1,0:T(8,128)(2,1)}, u32[]{:S(2)}, u32[]{:S(2)}) collective-permute-start(bf16[1024,1536]{1,0:T(8,128)(2,1)} %fusion.15), channel_id=1, source_target_pairs={{0,8},{1,9},{2,10},{3,11},{4,12},{5,13},{6,14},{7,15},{8,0},{9,1},... | collective-permute-start | bytes 9437192 | tf_op jit(solution)/shard_map/ppermute | solution.py:57
  538.7 43.6 %collective-permute-start.55 = (f32[1,16,128]{2,1,0:T(8,128)S(1)}, f32[1,16,128]{2,1,0:T(8,128)S(1)}, u32[]{:S(2)}, u32[]{:S(2)}) collective-permute-start(f32[1,16,128]{2,1,0:T(8,128)S(1)} %bitcast.167), channel_id=1, source_target_pairs={{0,4},{1,5},{2,6},{3,7},{4,0},{5,1},{6,2},{7,3},{8,12},{9,13},{10,... | collective-permute-start | bytes 24584 | tf_op jit(solution)/shard_map/ppermute | solution.py:57
  540.2 43.6 %collective-permute-start.56 = (f32[1,16,128]{2,1,0:T(8,128)S(1)}, f32[1,16,128]{2,1,0:T(8,128)S(1)}, u32[]{:S(2)}, u32[]{:S(2)}) collective-permute-start(f32[1,16,128]{2,1,0:T(8,128)S(1)} %bitcast.168), channel_id=1, source_target_pairs={{0,6},{1,7},{2,4},{3,5},{4,2},{5,3},{6,0},{7,1},{8,14},{9,15},{10,... | collective-permute-start | bytes 24584 | tf_op jit(solution)/shard_map/ppermute | solution.py:57
  582.3 38.7 %collective-permute-start.78 = (bf16[1024,2048]{1,0:T(8,128)(2,1)}, bf16[1024,2048]{1,0:T(8,128)(2,1)S(1)}, u32[]{:S(2)}, u32[]{:S(2)}) collective-permute-start(bf16[1024,2048]{1,0:T(8,128)(2,1)} %fusion.9), channel_id=1, source_target_pairs={{0,8},{1,9},{2,10},{3,11},{4,12},{5,13},{6,14},{7,15},{8,0},{9,1},... | collective-permute-start | bytes 12582920 | tf_op jit(solution)/shard_map/ppermute | solution.py:57
  589.2 13.3 %collective-permute-start.70 = (bf16[1024,256]{1,0:T(8,128)(2,1)S(1)}, bf16[1024,256]{1,0:T(8,128)(2,1)S(1)}, u32[]{:S(2)}, u32[]{:S(2)}) collective-permute-start(bf16[1024,256]{1,0:T(8,128)(2,1)S(1)} %constant_dynamic-slice_fusion.17), channel_id=1, source_target_pairs={{0,16},{1,17},{2,18},{3,19},{4,20},{5,21},{6,22},{7,23},{8,24},{9,... | collective-permute-start | bytes 1572872 | tf_op jit(solution)/shard_map/ppermute | solution.py:57
  609.6 44.6 %collective-permute-start.72 = (bf16[128,256]{1,0:T(8,128)(2,1)S(1)}, bf16[128,256]{1,0:T(8,128)(2,1)S(1)}, u32[]{:S(2)}, u32[]{:S(2)}) collective-permute-start(bf16[128,256]{1,0:T(8,128)(2,1)S(1)} %get-tuple-element.147), channel_id=1, source_target_pairs={{0,2},{1,3},{2,0},{3,1},{4,6},{5,7},{6,4},{7,5},{8,10},{9,11},{10,... | collective-permute-start | bytes 196616 | tf_op jit(solution)/shard_map/ppermute | solution.py:57
  613.8 34.0 %collective-permute-start.61 = (bf16[512,1536]{1,0:T(8,128)(2,1)}, bf16[512,1536]{1,0:T(8,128)(2,1)}, u32[]{:S(2)}, u32[]{:S(2)}) collective-permute-start(bf16[512,1536]{1,0:T(8,128)(2,1)} %bitcast.55), channel_id=1, source_target_pairs={{0,1},{1,0},{2,3},{3,2},{4,5},{5,4},{6,7},{7,6},{8,9},{9,8},{10,11... | collective-permute-start | bytes 4718600 | tf_op jit(solution)/shard_map/ppermute | solution.py:57
  620.2 64.6 %collective-permute-start.88 = (bf16[4096,256]{1,0:T(8,128)(2,1)}, bf16[4096,256]{1,0:T(8,128)(2,1)S(1)}, u32[]{:S(2)}, u32[]{:S(2)}) collective-permute-start(bf16[4096,256]{1,0:T(8,128)(2,1)} %constant_dynamic-slice_fusion.5), channel_id=1, source_target_pairs={{0,16},{1,17},{2,18},{3,19},{4,20},{5,21},{6,22},{7,23},{8,24},{9,... | collective-permute-start | bytes 6291464 | tf_op jit(solution)/shard_map/ppermute | solution.py:57
  649.6 32.5 %collective-permute-start.62 = (bf16[512,768]{1,0:T(8,128)(2,1)S(1)}, bf16[512,768]{1,0:T(8,128)(2,1)S(1)}, u32[]{:S(2)}, u32[]{:S(2)}) collective-permute-start(bf16[512,768]{1,0:T(8,128)(2,1)S(1)} %constant_dynamic-slice_fusion.21), channel_id=1, source_target_pairs={{0,16},{1,17},{2,18},{3,19},{4,20},{5,21},{6,22},{7,23},{8,24},{9,... | collective-permute-start | bytes 2359304 | tf_op jit(solution)/shard_map/ppermute | solution.py:57
  650.9 43.7 %collective-permute-start.79 = (bf16[512,2048]{1,0:T(8,128)(2,1)S(1)}, bf16[512,2048]{1,0:T(8,128)(2,1)S(1)}, u32[]{:S(2)}, u32[]{:S(2)}) collective-permute-start(bf16[512,2048]{1,0:T(8,128)(2,1)S(1)} %bitcast.128), channel_id=1, source_target_pairs={{0,1},{1,0},{2,3},{3,2},{4,5},{5,4},{6,7},{7,6},{8,9},{9,8},{10,11... | collective-permute-start | bytes 6291464 | tf_op jit(solution)/shard_map/ppermute | solution.py:57
  658.5 37.4 %collective-permute-start.75 = (bf16[128,256]{1,0:T(8,128)(2,1)S(1)}, bf16[128,256]{1,0:T(8,128)(2,1)S(1)}, u32[]{:S(2)}, u32[]{:S(2)}) collective-permute-start(bf16[128,256]{1,0:T(8,128)(2,1)S(1)} %add_convert_fusion.11), channel_id=1, source_target_pairs={{0,16},{1,17},{2,18},{3,19},{4,20},{5,21},{6,22},{7,23},{8,24},{9,... | collective-permute-start | bytes 196616 | tf_op jit(solution)/shard_map/ppermute | solution.py:57
  682.4 19.6 %collective-permute-start.63 = (bf16[128,768]{1,0:T(8,128)(2,1)S(1)}, bf16[128,768]{1,0:T(8,128)(2,1)S(1)}, u32[]{:S(2)}, u32[]{:S(2)}) collective-permute-start(bf16[128,768]{1,0:T(8,128)(2,1)S(1)} %get-tuple-element.134), channel_id=1, source_target_pairs={{0,2},{1,3},{2,0},{3,1},{4,6},{5,7},{6,4},{7,5},{8,10},{9,11},{10,... | collective-permute-start | bytes 589832 | tf_op jit(solution)/shard_map/ppermute | solution.py:57
  683.8 18.3 %collective-permute-start.64 = (bf16[128,768]{1,0:T(8,128)(2,1)S(1)}, bf16[128,768]{1,0:T(8,128)(2,1)S(1)}, u32[]{:S(2)}, u32[]{:S(2)}) collective-permute-start(bf16[128,768]{1,0:T(8,128)(2,1)S(1)} %get-tuple-element.136), channel_id=1, source_target_pairs={{0,4},{1,5},{2,6},{3,7},{4,0},{5,1},{6,2},{7,3},{8,12},{9,13},{10,... | collective-permute-start | bytes 589832 | tf_op jit(solution)/shard_map/ppermute | solution.py:57
  684.8 17.5 %collective-permute-start.65 = (bf16[128,768]{1,0:T(8,128)(2,1)S(1)}, bf16[128,768]{1,0:T(8,128)(2,1)S(1)}, u32[]{:S(2)}, u32[]{:S(2)}) collective-permute-start(bf16[128,768]{1,0:T(8,128)(2,1)S(1)} %get-tuple-element.135), channel_id=1, source_target_pairs={{0,6},{1,7},{2,4},{3,5},{4,2},{5,3},{6,0},{7,1},{8,14},{9,15},{10,... | collective-permute-start | bytes 589832 | tf_op jit(solution)/shard_map/ppermute | solution.py:57
  694.6 37.2 %collective-permute-start.89 = (bf16[2048,256]{1,0:T(8,128)(2,1)S(1)}, bf16[2048,256]{1,0:T(8,128)(2,1)S(1)}, u32[]{:S(2)}, u32[]{:S(2)}) collective-permute-start(bf16[2048,256]{1,0:T(8,128)(2,1)S(1)} %bitcast.130), channel_id=1, source_target_pairs={{0,1},{1,0},{2,3},{3,2},{4,5},{5,4},{6,7},{7,6},{8,9},{9,8},{10,11... | collective-permute-start | bytes 3145736 | tf_op jit(solution)/shard_map/ppermute | solution.py:57
  702.0 32.7 %collective-permute-start.80 = (bf16[512,1024]{1,0:T(8,128)(2,1)S(1)}, bf16[512,1024]{1,0:T(8,128)(2,1)S(1)}, u32[]{:S(2)}, u32[]{:S(2)}) collective-permute-start(bf16[512,1024]{1,0:T(8,128)(2,1)S(1)} %constant_dynamic-slice_fusion.9), channel_id=1, source_target_pairs={{0,16},{1,17},{2,18},{3,19},{4,20},{5,21},{6,22},{7,23},{8,24},{9,... | collective-permute-start | bytes 3145736 | tf_op jit(solution)/shard_map/ppermute | solution.py:57
  702.4 28.2 %collective-permute-start.66 = (bf16[128,768]{1,0:T(8,128)(2,1)S(1)}, bf16[128,768]{1,0:T(8,128)(2,1)S(1)}, u32[]{:S(2)}, u32[]{:S(2)}) collective-permute-start(bf16[128,768]{1,0:T(8,128)(2,1)S(1)} %add_convert_fusion.10), channel_id=1, source_target_pairs={{0,16},{1,17},{2,18},{3,19},{4,20},{5,21},{6,22},{7,23},{8,24},{9,... | collective-permute-start | bytes 589832 | tf_op jit(solution)/shard_map/ppermute | solution.py:57
  704.6 66.1 %collective-permute-start.67 = (bf16[128,768]{1,0:T(8,128)(2,1)S(1)}, bf16[128,768]{1,0:T(8,128)(2,1)S(1)}, u32[]{:S(2)}, u32[]{:S(2)}) collective-permute-start(bf16[128,768]{1,0:T(8,128)(2,1)S(1)} %add_convert_fusion.10), channel_id=1, source_target_pairs={{0,8},{1,9},{2,10},{3,11},{4,12},{5,13},{6,14},{7,15},{8,0},{9,1},... | collective-permute-start | bytes 589832 | tf_op jit(solution)/shard_map/ppermute | solution.py:57
  730.6 40.4 %collective-permute-start.68 = (bf16[128,768]{1,0:T(8,128)(2,1)S(1)}, bf16[128,768]{1,0:T(8,128)(2,1)S(1)}, u32[]{:S(2)}, u32[]{:S(2)}) collective-permute-start(bf16[128,768]{1,0:T(8,128)(2,1)S(1)} %collective-permute-done.66), channel_id=1, source_target_pairs={{0,8},{1,9},{2,10},{3,11},{4,12},{5,13},{6,14},{7,15},{8,0},{9,1},... | collective-permute-start | bytes 589832 | tf_op jit(solution)/shard_map/ppermute | solution.py:57
  732.3 12.3 %collective-permute-start.90 = (bf16[512,256]{1,0:T(8,128)(2,1)S(1)}, bf16[512,256]{1,0:T(8,128)(2,1)S(1)}, u32[]{:S(2)}, u32[]{:S(2)}) collective-permute-start(bf16[512,256]{1,0:T(8,128)(2,1)S(1)} %get-tuple-element.120), channel_id=1, source_target_pairs={{0,2},{1,3},{2,0},{3,1},{4,6},{5,7},{6,4},{7,5},{8,10},{9,11},{10,... | collective-permute-start | bytes 786440 | tf_op jit(solution)/shard_map/ppermute | solution.py:57
  733.8 17.3 %collective-permute-start.91 = (bf16[512,256]{1,0:T(8,128)(2,1)S(1)}, bf16[512,256]{1,0:T(8,128)(2,1)S(1)}, u32[]{:S(2)}, u32[]{:S(2)}) collective-permute-start(bf16[512,256]{1,0:T(8,128)(2,1)S(1)} %get-tuple-element.122), channel_id=1, source_target_pairs={{0,4},{1,5},{2,6},{3,7},{4,0},{5,1},{6,2},{7,3},{8,12},{9,13},{10,... | collective-permute-start | bytes 786440 | tf_op jit(solution)/shard_map/ppermute | solution.py:57
  734.7 33.5 %collective-permute-start.92 = (bf16[512,256]{1,0:T(8,128)(2,1)S(1)}, bf16[512,256]{1,0:T(8,128)(2,1)S(1)}, u32[]{:S(2)}, u32[]{:S(2)}) collective-permute-start(bf16[512,256]{1,0:T(8,128)(2,1)S(1)} %get-tuple-element.121), channel_id=1, source_target_pairs={{0,6},{1,7},{2,4},{3,5},{4,2},{5,3},{6,0},{7,1},{8,14},{9,15},{10,... | collective-permute-start | bytes 786440 | tf_op jit(solution)/shard_map/ppermute | solution.py:57
  744.7 28.8 %collective-permute-start.81 = (bf16[128,1024]{1,0:T(8,128)(2,1)S(1)}, bf16[128,1024]{1,0:T(8,128)(2,1)S(1)}, u32[]{:S(2)}, u32[]{:S(2)}) collective-permute-start(bf16[128,1024]{1,0:T(8,128)(2,1)S(1)} %get-tuple-element.127), channel_id=1, source_target_pairs={{0,2},{1,3},{2,0},{3,1},{4,6},{5,7},{6,4},{7,5},{8,10},{9,11},{10,... | collective-permute-start | bytes 786440 | tf_op jit(solution)/shard_map/ppermute | solution.py:57
  751.1 22.9 %collective-permute-start.82 = (bf16[128,1024]{1,0:T(8,128)(2,1)S(1)}, bf16[128,1024]{1,0:T(8,128)(2,1)S(1)}, u32[]{:S(2)}, u32[]{:S(2)}) collective-permute-start(bf16[128,1024]{1,0:T(8,128)(2,1)S(1)} %get-tuple-element.129), channel_id=1, source_target_pairs={{0,4},{1,5},{2,6},{3,7},{4,0},{5,1},{6,2},{7,3},{8,12},{9,13},{10,... | collective-permute-start | bytes 786440 | tf_op jit(solution)/shard_map/ppermute | solution.py:57
  768.2 12.5 %collective-permute-start.83 = (bf16[128,1024]{1,0:T(8,128)(2,1)S(1)}, bf16[128,1024]{1,0:T(8,128)(2,1)S(1)}, u32[]{:S(2)}, u32[]{:S(2)}) collective-permute-start(bf16[128,1024]{1,0:T(8,128)(2,1)S(1)} %get-tuple-element.128), channel_id=1, source_target_pairs={{0,6},{1,7},{2,4},{3,5},{4,2},{5,3},{6,0},{7,1},{8,14},{9,15},{10,... | collective-permute-start | bytes 786440 | tf_op jit(solution)/shard_map/ppermute | solution.py:57
  771.1 18.6 %collective-permute-start.94 = (bf16[512,256]{1,0:T(8,128)(2,1)S(1)}, bf16[512,256]{1,0:T(8,128)(2,1)S(1)}, u32[]{:S(2)}, u32[]{:S(2)}) collective-permute-start(bf16[512,256]{1,0:T(8,128)(2,1)S(1)} %add_convert_fusion.8), channel_id=1, source_target_pairs={{0,8},{1,9},{2,10},{3,11},{4,12},{5,13},{6,14},{7,15},{8,0},{9,1},... | collective-permute-start | bytes 786440 | tf_op jit(solution)/shard_map/ppermute | solution.py:57
  (70 other events, 1307.1 us)

commit v2 on v1

v2 whole, which is shorter than its diff:
```python
import functools

import jax
import jax.numpy as jnp
import numpy as np
from jax import lax
from jax.experimental import pallas as pl
from jax.experimental.pallas import tpu as pltpu
from jax.sharding import PartitionSpec as P

PATCHES = (1, 2, 3, 4, 5, 6, 8, 10, 13, 16)
EPS = 1e-06
GELU_COEF = 0.7978845608028654
AXES = ("dp", "fsdp")
LOW = jnp.bfloat16
WIDE = jnp.float32
NN = (((1,), (0,)), ((), ()))
NT = (((1,), (1,)), ((), ()))
TN = (((0,), (0,)), ((), ()))
VMEM_LIMIT = 56 << 20
BLOCKED = -30000.0
LIGHT = pl.CostEstimate(flops=1024, transcendentals=0, bytes_accessed=1024)


def dot(left, right, dims=NN):
    return lax.dot_general(left, right, dims, preferred_element_type=WIDE)


def two_parts(values):
    high = values.astype(LOW)
    return high, (values - high.astype(WIDE)).astype(LOW)


def split_dot(values, table):
    high, rest = two_parts(values)
    return dot(high, table) + dot(rest, table)


class Place:
    def __init__(self, dp_count, fsdp_count):
        self.grouped = dp_count == 4 and fsdp_count == 8
        self.dp_count = dp_count
        self.fsdp_count = fsdp_count
        dp_index = lax.axis_index("dp")
        fsdp_index = lax.axis_index("fsdp")
        self.dp_index, self.fsdp_index = dp_index, fsdp_index
        self.y, self.c = dp_index // 2, dp_index % 2
        self.z, self.x = fsdp_index // 2, fsdp_index % 2
        self.table = jnp.stack([self.y, self.c, self.z, self.x]).astype(jnp.int32)


def hop(values, dy=0, dc=0, dz=0, dx=0):
    pairs = [
        (d * 8 + f, (d ^ (2 * dy + dc)) * 8 + (f ^ (2 * dz + dx)))
        for d in range(4)
        for f in range(8)
    ]
    return lax.ppermute(values, AXES, pairs)


def tie(*values):
    return lax.optimization_barrier(values)


class Gather:
    def __init__(self, own):
        self.own = own

    def over_z(self):
        self.stack = jnp.concatenate([self.own] + [hop(self.own, dz=k) for k in (1, 2, 3)], 0)

    def over_xy(self):
        self.from_x, self.from_y = hop(self.stack, dx=1), hop(self.stack, dy=1)

    def over_both(self):
        half = self.stack.shape[0] // 2
        self.from_both = [hop(self.from_x[:half], dy=1), hop(self.from_y[half:], dx=1)]

    def over_core_first(self):
        self.first = [self.stack, self.from_x, self.from_y]
        self.first_core = [hop(piece, dc=1) for piece in self.first]

    def over_core(self):
        self.last_core = [hop(piece, dc=1) for piece in self.from_both]
        return self.first + self.from_both + self.first_core + self.last_core


def own_quarter(place, shard):
    rows, columns = shard.shape
    quarter = columns // 4
    return lax.dynamic_slice(shard, (0, (place.c * 2 + place.y) * quarter), (rows, quarter))


def weight_copies(place_ref, pieces, sources, buffer, sem):
    copies = []
    if sources is None:
        return [pltpu.make_async_copy(pieces[0], buffer, sem.at[0])]
    for column_from, quarter, rows, column_to in sources:
        for number in range(10):
            core, kind = number // 5, number % 5
            across, side = (0, 1, 0, 1, 1)[kind], (0, 0, 1, 1, 1)[kind]
            column = column_to + ((place_ref[1] ^ core) * 2 + (place_ref[0] ^ side)) * quarter
            members = range(4) if kind < 3 else range(2 * (kind - 3), 2 * (kind - 3) + 2)
            for place_in, k in enumerate(members):
                row = ((place_ref[2] ^ k) * 2 + (place_ref[3] ^ across)) * rows
                copies.append(
                    pltpu.make_async_copy(
                        pieces[number].at[pl.ds(place_in * rows, rows), pl.ds(column_from, quarter)],
                        buffer.at[
                            pl.ds(pl.multiple_of(row, 128), rows),
                            pl.ds(pl.multiple_of(column, 128), quarter),
                        ],
                        sem.at[len(copies)],
                    )
                )
    return copies


def add(left, right):
    return left.astype(WIDE) + right.astype(WIDE)


def add_blocks(place, steps, block, outs, name):
    arrays, specs, plan = [], [], []
    for _, _, terms in outs:
        entry = []
        for array, where, when in terms:
            entry.append((len(arrays), when))
            arrays.append(array)
            specs.append(pl.BlockSpec(block, functools.partial(lambda where, n, p: where(n, p), where)))
        plan.append(entry)

    def body(place_ref, *refs):
        step = pl.program_id(0)
        for entry, out_ref in zip(plan, refs[len(arrays) :]):
            total = None
            for number, when in entry:
                value = refs[number][...].astype(WIDE)
                if when is not None:
                    value = jnp.where(when(step, place_ref), value, 0.0)
                total = value if total is None else total + value
            out_ref[...] = total.astype(LOW)

    return pl.pallas_call(
        body,
        grid_spec=pltpu.PrefetchScalarGridSpec(
            num_scalar_prefetch=1,
            grid=(steps,),
            in_specs=specs,
            out_specs=[
                pl.BlockSpec(block, functools.partial(lambda where, n, p: where(n, p), where))
                for _, where, _ in outs
            ],
        ),
        out_shape=[
            jax.ShapeDtypeStruct((blocks[0] * block[0], blocks[1] * block[1]), LOW) for blocks, _, _ in outs
        ],
        compiler_params=pltpu.CompilerParams(vmem_limit_bytes=VMEM_LIMIT),
        cost_estimate=LIGHT,
        name=name,
    )(place.table, *arrays)


class RowSum:
    def __init__(self, place, keep, arrived, rows, order):
        self.place, self.base = place, [keep, arrived]
        self.block = (rows, keep.shape[1] // 2)
        self.streams = (
            [{"z": 0, "count": 2, "order": "yx"}, {"z": 2, "count": 2, "order": "xy"}]
            if order == "mixed"
            else [{"z": 0, "count": 4, "order": order}]
        )

    def first(self):
        outs, steps = [], 2 * self.streams[0]["count"]
        for stream in self.streams:
            start, count = stream["z"], stream["count"]
            if stream["order"] == "yx":
                where = lambda n, p, start=start: (2 * start + n, 1 - p[0])
                outs.append(((2 * count, 1), lambda n, p: (n, 0), [(t, where, None) for t in self.base]))
            else:
                where = lambda n, p, start=start: (2 * (start + n // 2) + 1 - p[3], n % 2)
                outs.append(((count, 2), lambda n, p: (n // 2, n % 2), [(t, where, None) for t in self.base]))
        sent = add_blocks(self.place, steps, self.block, outs, "first_sums")
        return [(v, {"d" + s["order"][0]: 1}) for v, s in zip(sent, self.streams)]

    def second(self, arrived):
        outs, steps = [], self.streams[0]["count"]
        for stream, value in zip(self.streams, arrived):
            stream["first"] = value
            start, count = stream["z"], stream["count"]
            if stream["order"] == "yx":
                where = lambda n, p, start=start: (2 * (start + n) + 1 - p[3], p[0])
                terms = [(value, lambda n, p: (2 * n + 1 - p[3], 0), None)]
            else:
                where = lambda n, p, start=start: (2 * (start + n) + p[3], 1 - p[0])
                terms = [(value, lambda n, p: (n, 1 - p[0]), None)]
            outs.append(((count, 1), lambda n, p: (n, 0), [(t, where, None) for t in self.base] + terms))
        sent = add_blocks(self.place, steps, self.block, outs, "second_sums")
        return [(v, {"d" + s["order"][1]: 1}) for v, s in zip(sent, self.streams)]

    def terms(self, flip):
        out = [(t, lambda n, p: (2 * (p[2] ^ flip) + p[3], p[0]), None) for t in self.base]
        for stream in self.streams:
            mask = stream["count"] - 1
            when = None
            if stream["count"] == 2:
                when = lambda n, p, start=stream["z"]: (p[2] ^ flip) // 2 == start // 2
            if stream["order"] == "yx":
                first = lambda n, p, mask=mask: (2 * ((p[2] ^ flip) & mask) + p[3], 0)
            else:
                first = lambda n, p, mask=mask: ((p[2] ^ flip) & mask, p[0])
            out.append((stream["first"], first, when))
            out.append((stream["second"], lambda n, p, mask=mask: ((p[2] ^ flip) & mask, 0), when))
        return out

    def third(self, arrived):
        for stream, value in zip(self.streams, arrived):
            stream["second"] = value
        outs = [((1, 1), lambda n, p: (0, 0), self.terms(k)) for k in (1, 2, 3)]
        sent = add_blocks(self.place, 1, self.block, outs, "third_sums")
        return [(v, {"dz": k}) for v, k in zip(sent, (1, 2, 3))]

    def finish(self, arrived):
        terms = self.terms(0) + [(v, lambda n, p: (0, 0), None) for v in arrived]
        return add_blocks(self.place, 1, self.block, [((1, 1), lambda n, p: (0, 0), terms)], "last_sums")[0]


def beside(kernel, operand, moves):
    out = tie(operand, *(value for value, _ in moves))
    arrived = [hop(value, **axes) for value, (_, axes) in zip(out[1:], moves)]
    results = kernel(out[0])
    results = list(results) if isinstance(results, (list, tuple)) else [results]
    out = tie(*results, *arrived)
    results, arrived = list(out[: len(results)]), list(out[len(results) :])
    return (results[0] if len(results) == 1 else results), arrived


def lay_out_kernel(layout, place_ref, *refs):
    quarters, outs = refs[:4], refs[4:]
    here = place_ref[1] * 2 + place_ref[0]
    for apart, ref in enumerate(quarters):
        index = here ^ apart
        for number, column, width, row, to, stride in layout:
            rows = ref.shape[0]
            start = pl.multiple_of(to + index * stride, 128)
            outs[number][pl.ds(row, rows), pl.ds(start, width)] = ref[:, column : column + width].astype(WIDE)


def lay_out(place, quarters, layout, shapes, name):
    vmem = pl.BlockSpec(memory_space=pltpu.VMEM)
    return pl.pallas_call(
        functools.partial(lay_out_kernel, layout),
        in_specs=[pl.BlockSpec(memory_space=pltpu.SMEM)] + [vmem] * 4,
        out_specs=[vmem] * len(shapes),
        out_shape=[jax.ShapeDtypeStruct(shape, WIDE) for shape in shapes],
        compiler_params=pltpu.CompilerParams(vmem_limit_bytes=VMEM_LIMIT),
        cost_estimate=LIGHT,
        name=name,
    )(place.table, *quarters)


def spread(own):
    return [own, hop(own, dy=1), hop(own, dc=1), hop(own, dy=1, dc=1)]


def reorder(stack, count, flip):
    return jnp.concatenate(
        [lax.dynamic_slice_in_dim(stack, i ^ flip, 1, axis=0) for i in range(count)], 0
    )


def small_over_z(values):
    return jnp.stack([values] + [hop(values, dz=k) for k in (1, 2, 3)])


def small_over_x(place, stack):
    count, tail = stack.shape[1], stack.shape[2:]
    stack = jnp.stack([stack, hop(stack, dx=1)], 1).reshape((8, count) + tail)
    return reorder(stack, 8, place.fsdp_index).reshape((8 * count,) + tail)


def gather_small(place, values, whole):
    if not place.grouped:
        return lax.all_gather(values, AXES if whole else "fsdp", axis=0, tiled=True)
    ordered = small_over_x(place, small_over_z(values))
    return over_dp(place, ordered) if whole else ordered


def over_dp(place, values):
    if not place.grouped:
        return lax.all_gather(values, "dp", axis=0, tiled=True)
    stack = jnp.stack([values, hop(values, dc=1), hop(values, dy=1), hop(values, dy=1, dc=1)])
    return reorder(stack, 4, place.dp_index).reshape((4 * values.shape[0],) + values.shape[1:])


def scatter_over_x(place, values):
    values = values.reshape((4, 2, values.shape[0] // 8) + values.shape[1:])
    mine = lax.dynamic_index_in_dim(values, place.x, 1, keepdims=False)
    other = lax.dynamic_index_in_dim(values, 1 - place.x, 1, keepdims=False)
    return mine + hop(other, dx=1)


def scatter_over_z(place, values):
    total = lax.dynamic_index_in_dim(values, place.z, 0, keepdims=False)
    for k in (1, 2, 3):
        total = total + hop(
            lax.dynamic_index_in_dim(values, place.z ^ k, 0, keepdims=False), dz=k
        )
    return total


def mask_tables(length):
    scale_ids = np.concatenate([np.full(side * side, i) for i, side in enumerate(PATCHES)])
    spare = np.arange(128) & 63
    slot = spare[None, :] - 2
    scale_column = scale_ids[:, None]
    later = (slot >= 0) & (slot < len(PATCHES)) & (slot > scale_column)
    query_side = np.where(later, BLOCKED, 0.0)
    key_side = np.where(slot == scale_column, 1.0, 0.0) + np.where(spare[None, :] < 2, 1.0, 0.0)
    return jnp.asarray(query_side, LOW), jnp.asarray(key_side, LOW)


FORWARD_BLOCKS = ((0, 240, 256), (240, 416, 512), (416, 680, 680))
BACKWARD_BLOCKS = ((424, 680, 680), (240, 424, 432), (0, 240, 256))


def attend_kernel(qkv_ref, qm_ref, km_ref, out_ref, extra_ref):
    query, key, value = (qkv_ref[0, :, 128 * n : 128 * n + 128] for n in range(3))
    query_mask, key_mask = qm_ref[...], km_ref[...]
    lane = lax.broadcasted_iota(jnp.int32, query.shape, 1)
    even = lane < 64
    ones = jnp.ones_like(value)
    heads = (
        (jnp.where(even, query, query_mask), jnp.where(even, key, key_mask), jnp.where(even, value, ones)),
        (jnp.where(even, query_mask, query), jnp.where(even, key_mask, key), jnp.where(even, ones, value)),
    )
    for start, stop, keys in FORWARD_BLOCKS:
        sums = []
        for query_head, key_head, value_head in heads:
            scores = dot(query_head[start:stop], key_head[:keys], NT)
            sums.append(dot(jnp.exp(scores).astype(LOW), value_head[:keys]))
        side = even[start:stop]
        chosen = jnp.where(side, sums[0], sums[1])
        totals = jnp.where(side, sums[1], sums[0])
        out_ref[0, start:stop, :] = (chosen / pltpu.roll(totals, 64, 1)).astype(LOW)
        high, rest = two_parts(-jnp.log(totals))
        spare = lane[start:stop] & 63
        extra_ref[0, start:stop, :] = jnp.where(
            spare == 0, high, jnp.where(spare == 1, rest, query_mask[start:stop])
        )


def attend(qkv, query_mask, key_mask):
    items, length, triple = qkv.shape
    pairs = triple // 384
    block = pl.BlockSpec((1, length, 128), lambda i, p: (i, 0, p))
    table = pl.BlockSpec((length, 128), lambda i, p: (0, 0))
    return pl.pallas_call(
        attend_kernel,
        grid=(items, pairs),
        in_specs=[pl.BlockSpec((1, length, 384), lambda i, p: (i, 0, p)), table, table],
        out_specs=[block, block],
        out_shape=[jax.ShapeDtypeStruct((items, length, 128 * pairs), LOW)] * 2,
        compiler_params=pltpu.CompilerParams(vmem_limit_bytes=VMEM_LIMIT),
        cost_estimate=LIGHT,
        name="attend",
    )(qkv, query_mask, key_mask)


def side_table(cross, size=128):
    first = lax.broadcasted_iota(jnp.int32, (size, size), 0) // 64
    second = lax.broadcasted_iota(jnp.int32, (size, size), 1) // 64
    return jnp.where((first != second) if cross else (first == second), 1.0, 0.0).astype(LOW)


def attend_back_kernel(
    qkv_ref, extra_ref, km_ref, out_ref, grad_ref, root_ref, gain_ref,
    grad_qkv_ref, head_ref, value_sum, key_sum, query_sum,
):
    query, key, value = (qkv_ref[0, :, 128 * n : 128 * n + 128] for n in range(3))
    key_mask, grad, extra = km_ref[...], grad_ref[0], extra_ref[0]
    lane = lax.broadcasted_iota(jnp.int32, query.shape, 1)
    even = lane < 64
    spare = lane & 63
    centre = split_dot(grad.astype(WIDE) * out_ref[0].astype(WIDE), side_table(True))
    high, rest = two_parts(-centre)
    grad_extra = jnp.where(spare == 0, high, jnp.where(spare == 1, rest, jnp.zeros_like(high)))
    ones = jnp.ones_like(value)
    key_rows = key.astype(WIDE).T.astype(LOW)
    heads = (
        (jnp.where(even, query, extra), jnp.where(even, key, key_mask),
         jnp.where(even, value, ones), jnp.where(even, grad, grad_extra)),
        (jnp.where(even, extra, query), jnp.where(even, key_mask, key),
         jnp.where(even, ones, value), jnp.where(even, grad_extra, grad)),
    )
    for head, (query_head, key_head, value_head, grad_head) in enumerate(heads):
        head_rows = key_rows[64 * head : 64 * head + 64]
        for number, (start, stop, keys) in enumerate(BACKWARD_BLOCKS):
            probs = jnp.exp(dot(key_head[:keys], query_head[start:stop], NT))
            grad_probs = dot(value_head[:keys], grad_head[start:stop], NT)
            grad_scores = (probs * grad_probs).astype(LOW)
            value_part = dot(probs.astype(LOW), grad[start:stop])
            key_part = dot(grad_scores, query[start:stop])
            if number == 0:
                value_sum[head] = value_part
                key_sum[head] = key_part
            else:
                value_sum[head, :keys] += value_part
                key_sum[head, :keys] += key_part
            query_sum[start:stop, 64 * head : 64 * head + 64] = dot(head_rows[:, :keys], grad_scores).T
    row = lax.broadcasted_iota(jnp.int32, (128, 128), 0)
    wanted = jnp.where(lax.broadcasted_iota(jnp.int32, (128, 128), 1) >= 64, 64, 0)
    roots = root_ref[0]
    root_query = dot(roots, jnp.where(row == wanted, 1.0, 0.0).astype(LOW))
    root_key = dot(roots, jnp.where(row == wanted + 32, 1.0, 0.0).astype(LOW))
    same = side_table(False)
    gain = gain_ref[...]
    grad_query = query_sum[...] * gain
    unit_query = query.astype(WIDE) / gain
    product = unit_query * grad_query
    head_ref[0] = jnp.sum(product, 0, keepdims=True)
    grad_qkv_ref[0, :, :128] = (
        root_query * (grad_query - unit_query * split_dot(product, same))
    ).astype(LOW)
    grad_key = jnp.where(even, key_sum[0], key_sum[1])
    unit_key = key.astype(WIDE)
    grad_qkv_ref[0, :, 128:256] = (
        root_key * (grad_key - unit_key * split_dot(unit_key * grad_key, same))
    ).astype(LOW)
    grad_qkv_ref[0, :, 256:] = jnp.where(even, value_sum[0], value_sum[1]).astype(LOW)


def attend_back(qkv, extra, key_mask, out, grad, roots, gain, first, pairs):
    items, length, _ = qkv.shape
    block = pl.BlockSpec((1, length, 128), lambda i, p: (i, 0, p + first))
    table = pl.BlockSpec((length, 128), lambda i, p: (0, 0))
    return pl.pallas_call(
        attend_back_kernel,
        grid=(items, pairs),
        in_specs=[pl.BlockSpec((1, length, 384), lambda i, p: (i, 0, p + first))]
        + [block, table, block, block, block, pl.BlockSpec((1, 128), lambda i, p: (0, p + first))],
        out_specs=[
            pl.BlockSpec((1, length, 384), lambda i, p: (i, 0, p)),
            pl.BlockSpec((1, 1, 128), lambda i, p: (i, 0, p)),
        ],
        out_shape=[
            jax.ShapeDtypeStruct((items, length, 384 * pairs), LOW),
            jax.ShapeDtypeStruct((items, 1, 128 * pairs), WIDE),
        ],
        scratch_shapes=[
            pltpu.VMEM((2, length, 128), WIDE),
            pltpu.VMEM((2, length, 128), WIDE),
            pltpu.VMEM((length, 128), WIDE),
        ],
        compiler_params=pltpu.CompilerParams(vmem_limit_bytes=VMEM_LIMIT),
        cost_estimate=LIGHT,
        name="attend_back",
    )(qkv, extra, key_mask, out, grad, roots, gain)


def row_facts(lengths_ref, block_rows, length):
    row = pl.program_id(0) * block_rows + lax.broadcasted_iota(jnp.int32, (block_rows, 1), 0)
    second = row >= length
    end = jnp.where(second, length + lengths_ref[1], lengths_ref[0])
    return second, row < end


def per_row(ref, second):
    return jnp.where(second, ref[1:2, :], ref[0:1, :])


def add_sums(ref, start, second, values):
    ref[start : start + 1, :] += jnp.sum(jnp.where(second, 0.0, values), 0, keepdims=True)
    ref[start + 1 : start + 2, :] += jnp.sum(jnp.where(second, values, 0.0), 0, keepdims=True)


def normalize(values):
    centred = values - jnp.mean(values, -1, keepdims=True)
    scale = lax.rsqrt(jnp.mean(centred * centred, -1, keepdims=True) + EPS)
    return centred * scale, scale


def token_call(kernel, place, rows, length, lengths, blocked, full, weights, outs, sums, name):
    block_rows = 2 * length // 5
    grid = rows // block_rows
    parts, where = [], []
    for pieces, sources, _ in weights:
        start = len(parts)
        parts.extend(pieces)
        where.append((start, len(pieces), sources))
    shapes = [weight[2] for weight in weights]
    counts = [1 if sources is None else 32 * len(sources) for _, _, sources in where]
    blocked_count, full_count, out_count, weight_count = len(blocked), len(full), len(outs), len(weights)

    def body(place_ref, lengths_ref, *refs):
        cursor = 0

        def take(count):
            nonlocal cursor
            cursor += count
            return refs[cursor - count : cursor]

        token_refs, full_refs, part_refs = take(blocked_count), take(full_count), take(len(parts))
        out_refs, sum_refs = take(out_count), take(sums)
        buffers, sems = take(weight_count), take(weight_count)
        first = pl.program_id(0) == 0

        def copies(number):
            start, count, sources = where[number]
            return weight_copies(
                place_ref, part_refs[start : start + count], sources, buffers[number], sems[number]
            )

        @pl.when(first)
        def _():
            for number in range(weight_count):
                for copy in copies(number):
                    copy.start()
            for ref in sum_refs:
                ref[...] = jnp.zeros_like(ref)

        def ready(number):
            @pl.when(first)
            def _():
                for copy in copies(number):
                    copy.wait()

            return buffers[number]

        second, real = row_facts(lengths_ref, block_rows, length)
        kernel(second, real, token_refs, full_refs, ready, out_refs, sum_refs)

    any_space = pl.BlockSpec(memory_space=pl.ANY)
    smem = pl.BlockSpec(memory_space=pltpu.SMEM)
    return pl.pallas_call(
        body,
        grid=(grid,),
        in_specs=[smem, smem]
        + [pl.BlockSpec((block_rows, v.shape[1]), lambda i: (i, 0)) for v in blocked]
        + [pl.BlockSpec(v.shape, lambda i: (0, 0)) for v in full]
        + [any_space] * len(parts),
        out_specs=[pl.BlockSpec((block_rows, width), lambda i: (i, 0)) for width, _ in outs]
        + [pl.BlockSpec((8, 1024), lambda i: (0, 0))] * sums,
        out_shape=[jax.ShapeDtypeStruct((rows, width), kind) for width, kind in outs]
        + [jax.ShapeDtypeStruct((8, 1024), WIDE)] * sums,
        scratch_shapes=[pltpu.VMEM(shape, LOW) for shape in shapes]
        + [pltpu.SemaphoreType.DMA((count,)) for count in counts],
        compiler_params=pltpu.CompilerParams(vmem_limit_bytes=VMEM_LIMIT),
        cost_estimate=LIGHT,
        name=name,
    )(place.table, lengths, *blocked, *full, *parts)


def project_kernel(second, real, tokens, full, ready, outs, sums):
    (x_ref,) = tokens
    scale, shift, gain = full
    h_ref, qkv_ref, root_ref = outs
    unit, _ = normalize(x_ref[...].astype(WIDE))
    hidden = (unit * (1.0 + per_row(scale, second)) + per_row(shift, second)).astype(LOW)
    h_ref[...] = hidden
    same = side_table(False, 256)
    first_half = (lax.broadcasted_iota(jnp.int32, (hidden.shape[0], 128), 1) & 32) == 0
    weight = ready(0)
    for pair in range(weight.shape[1] // 384):
        start = 384 * pair
        raw = dot(hidden, weight[:, start : start + 384])
        both = raw[:, :256]
        root = lax.rsqrt(dot((both * both).astype(LOW), same) + EPS)
        root_ref[:, 128 * pair : 128 * pair + 128] = jnp.where(
            first_half, root[:, :128], root[:, 128:]
        ).astype(LOW)
        query = raw[:, :128] * (root[:, :128] * gain[:, 128 * pair : 128 * pair + 128])
        qkv_ref[:, start : start + 128] = query.astype(LOW)
        qkv_ref[:, start + 128 : start + 256] = (raw[:, 128:256] * root[:, 128:]).astype(LOW)
        qkv_ref[:, start + 256 : start + 384] = raw[:, 256:].astype(LOW)


def branch_kernel(second, real, tokens, full, ready, outs, sums):
    attended_ref, x_ref = tokens
    gamma, scale, shift = full
    attn_ref, h_ref, act_ref, slope_ref = outs
    (sum_ref,) = sums
    attn = dot(attended_ref[...], ready(0)[...]).astype(LOW)
    attn_ref[...] = attn
    branch = jnp.where(real, per_row(gamma, second) * attn.astype(WIDE), 0.0)
    add_sums(sum_ref, 0, second, branch * branch)
    unit, _ = normalize(x_ref[...].astype(WIDE) + branch)
    hidden = (unit * (1.0 + per_row(scale, second)) + per_row(shift, second)).astype(LOW)
    h_ref[...] = hidden
    width = 512
    fc1 = ready(1)
    for start in range(0, fc1.shape[1], width):
        span = slice(start, start + width)
        wide = dot(hidden, fc1[:, span])
        square = wide * wide
        lift = 0.5 + 0.5 * jnp.tanh(wide * (GELU_COEF + (GELU_COEF * 0.044715) * square))
        act_ref[:, span] = (wide * lift).astype(LOW)
        bend = wide * (2.0 * GELU_COEF + (6.0 * 0.044715 * GELU_COEF) * square)
        slope_ref[:, span] = (lift * (1.0 + bend * (1.0 - lift))).astype(LOW)


def stream_kernel(second, real, tokens, full, ready, outs, sums):
    act_ref, x_ref, attn_ref, cot_ref = tokens
    gamma_one, gamma_two = full
    out_ref, grad_ref = outs
    (sum_ref,) = sums
    mlp = dot(act_ref[...], ready(0)[...])
    branch_one = jnp.where(real, per_row(gamma_one, second) * attn_ref[...].astype(WIDE), 0.0)
    gate = per_row(gamma_two, second)
    branch_two = jnp.where(real, gate * mlp, 0.0)
    stream = x_ref[...].astype(WIDE) + branch_one + branch_two
    out_ref[...] = stream.astype(LOW)
    upstream = cot_ref[...].astype(WIDE)
    grad_ref[...] = jnp.where(real, gate * upstream, 0.0).astype(LOW)
    add_sums(sum_ref, 0, second, jnp.where(real, stream * stream, 0.0))
    add_sums(sum_ref, 2, second, branch_two * branch_two)
    add_sums(sum_ref, 4, second, jnp.where(real, mlp * upstream, 0.0))


def hidden_back_kernel(second, real, tokens, full, ready, outs, sums):
    grad_ref, slope_ref = tokens
    (out_ref,) = outs
    grad = grad_ref[...]
    width = 512
    fc2 = ready(0)
    for start in range(0, fc2.shape[0], width):
        span = slice(start, start + width)
        out_ref[:, span] = (
            dot(grad, fc2[span, :], NT) * slope_ref[:, span].astype(WIDE)
        ).astype(LOW)


def middle_back_kernel(second, real, tokens, full, ready, outs, sums):
    grad_ref, x_ref, attn_ref, cot_ref = tokens
    gamma, scale = full
    middle_ref, attn_grad_ref, attended_grad_ref = outs
    (sum_ref,) = sums
    grad = dot(grad_ref[...], ready(0)[...], NT)
    attn = attn_ref[...].astype(WIDE)
    gate = per_row(gamma, second)
    unit, root = normalize(x_ref[...].astype(WIDE) + jnp.where(real, gate * attn, 0.0))
    add_sums(sum_ref, 0, second, grad * unit)
    add_sums(sum_ref, 2, second, grad)
    scaled = grad * (1.0 + per_row(scale, second))
    middle = cot_ref[...].astype(WIDE) + root * (
        scaled - jnp.mean(scaled, -1, keepdims=True) - unit * jnp.mean(scaled * unit, -1, keepdims=True)
    )
    middle_ref[...] = middle.astype(LOW)
    add_sums(sum_ref, 4, second, jnp.where(real, attn * middle, 0.0))
    attn_grad = jnp.where(real, gate * middle, 0.0).astype(LOW)
    attn_grad_ref[...] = attn_grad
    attended_grad_ref[...] = dot(attn_grad, ready(1)[...], NT).astype(LOW)


def token_back_kernel(second, real, tokens, full, ready, outs, sums):
    *grad_refs, x_ref, middle_ref = tokens
    (scale,) = full
    (out_ref,) = outs
    (sum_ref,) = sums
    weight = ready(0)
    grad, column = 0.0, 0
    for ref in grad_refs:
        grad = grad + dot(ref[...], weight[:, column : column + ref.shape[1]], NT)
        column += ref.shape[1]
    unit, root = normalize(x_ref[...].astype(WIDE))
    add_sums(sum_ref, 0, second, grad * unit)
    add_sums(sum_ref, 2, second, grad)
    scaled = grad * (1.0 + per_row(scale, second))
    total = middle_ref[...].astype(WIDE) + root * (
        scaled - jnp.mean(scaled, -1, keepdims=True) - unit * jnp.mean(scaled * unit, -1, keepdims=True)
    )
    out_ref[...] = total.astype(LOW)


def outer_kernel(half_ref, left_ref, right_ref, out_ref):
    out_ref[...] = dot(left_ref[...], right_ref[...], TN).astype(LOW)


def outer(left, right, half=None):
    count, height = left.shape
    width = right.shape[1] if half is None else right.shape[1] // 2
    half = jnp.zeros((1,), jnp.int32) if half is None else half.reshape(1).astype(jnp.int32)
    tall = min(height, 1024)
    wide = min(width, 1024 if width % 1024 == 0 else 768 if width % 768 == 0 else 512)
    steps = width // wide
    return pl.pallas_call(
        outer_kernel,
        grid_spec=pltpu.PrefetchScalarGridSpec(
            num_scalar_prefetch=1,
            grid=(height // tall, steps),
            in_specs=[
                pl.BlockSpec((count, tall), lambda i, j, h: (0, i)),
                pl.BlockSpec((count, wide), lambda i, j, h: (0, h[0] * steps + j)),
            ],
            out_specs=pl.BlockSpec((tall, wide), lambda i, j, h: (i, j)),
        ),
        out_shape=jax.ShapeDtypeStruct((height, width), LOW),
        compiler_params=pltpu.CompilerParams(vmem_limit_bytes=VMEM_LIMIT),
        cost_estimate=LIGHT,
        name="outer",
    )(half, left, right)


def plain_sum(place, keep, send):
    flip = place.c == 1
    full = jnp.concatenate([jnp.where(flip, send, keep), jnp.where(flip, keep, send)], 1)
    part = lax.psum_scatter(full, "fsdp", scatter_dimension=0, tiled=True)
    return lax.psum(part, "dp").astype(WIDE)


def shards(place_counts, tokens, cond, stop_scale, w_ada, w_qkv, w_proj, w_fc1, w_fc2, head_log_scale, cotangent):
    place = Place(*place_counts)
    items, width = cond.shape
    rows = tokens.shape[0]
    length = rows // items
    heads = head_log_scale.shape[0]
    pairs = heads // 2
    hidden_width = w_fc1.shape[1]
    ends = jnp.asarray(np.cumsum([side * side for side in PATCHES]).astype(np.int32))
    lengths = jnp.sum(jnp.where(jnp.arange(len(PATCHES))[None, :] == stop_scale[:, None], ends[None, :], 0), 1)

    def by_pair(matrix):
        return jnp.swapaxes(matrix.reshape(matrix.shape[0], 3, pairs, 128), 1, 2).reshape(matrix.shape)

    def from_pair(matrix):
        return jnp.swapaxes(matrix.reshape(matrix.shape[0], pairs, 3, 128), 1, 2).reshape(matrix.shape)

    paired = by_pair(w_qkv)
    half = paired.shape[1] // 2
    cond_wide = cond.astype(WIDE)
    silu_cond = (cond_wide * jax.nn.sigmoid(cond_wide)).astype(LOW)
    ada_rows = w_ada.shape[0]
    group_count = items * place.fsdp_count
    ada_columns = (0, place.fsdp_index * ada_rows)

    def part_modulation(group_cond):
        return dot(lax.dynamic_slice(group_cond, ada_columns, (group_count, ada_rows)), w_ada)

    if place.grouped:
        unit_rows = w_qkv.shape[0]
        cond_stack = small_over_z(silu_cond)
        own_qkv, cond_stack = tie(own_quarter(place, paired), cond_stack)
        qkv = Gather(own_qkv)
        qkv.over_z()
        mixed = scatter_over_x(place, part_modulation(small_over_x(place, cond_stack)))
        qkv.stack, mixed = tie(qkv.stack, mixed)
        qkv.over_xy()
        modulation = scatter_over_z(place, mixed)
        own_rest = jnp.concatenate([own_quarter(place, w_proj), own_quarter(place, w_fc1)], 1)
        own_rest, modulation = tie(own_rest, modulation)
        rest = Gather(own_rest)
        rest.over_z()
        qkv.over_both()
        qkv.over_core_first()
        out = tie(rest.stack, *qkv.from_both)
        rest.stack, qkv.from_both = out[0], list(out[1:])
        rest.over_xy()
        qkv_parts = qkv.over_core()
        piece = w_fc2.shape[0] // place.dp_count
        fc2_piece = lax.dynamic_slice(w_fc2, (place.dp_index * piece, 0), (piece, width))
        fc2_piece, qkv_parts[-1] = tie(fc2_piece, qkv_parts[-1])
        fc2_full = lax.all_gather(fc2_piece, ("fsdp", "dp"), axis=0, tiled=True)
        quarter = half // 2
        qkv_weight = (qkv_parts, [(0, quarter, unit_rows, 0)], (width, 2 * half))
        fc2_weight = ([fc2_full], None, (hidden_width, width))
    else:
        qkv_weight, proj_weight, fc1_weight, fc2_weight = (
            ([lax.all_gather(w, "fsdp", axis=0, tiled=True)], None, (w.shape[0] * place.fsdp_count, w.shape[1]))
            for w in (paired, w_proj, w_fc1, w_fc2)
        )
        modulation = lax.psum_scatter(
            part_modulation(gather_small(place, silu_cond, False)), "fsdp", scatter_dimension=0, tiled=True
        )
    gamma_one, gamma_two, scale_one, scale_two, shift_one, shift_two = [
        modulation[:, n * width : (n + 1) * width] for n in range(6)
    ]

    gain = jnp.repeat(jnp.exp(head_log_scale), width // heads)[None, :]
    normed_one, projected, roots = token_call(
        project_kernel, place, rows, length, lengths, [tokens], [scale_one, shift_one, gain],
        [qkv_weight], [(width, LOW), (3 * width, LOW), (width, LOW)], 0, "project",
    )
    if place.grouped:
        rest.from_x, rest.from_y, projected = tie(rest.from_x, rest.from_y, projected)
        rest.over_both()
        rest.over_core_first()
    cube = (items, length, width)
    projected, roots = projected.reshape(items, length, 3 * width), roots.reshape(cube)
    query_mask, key_mask = mask_tables(length)
    attended, extra = attend(projected, query_mask, key_mask)
    if place.grouped:
        out = tie(attended, *rest.from_both)
        attended, rest.from_both = out[0], list(out[1:])
        rest_parts = rest.over_core()
        proj_weight = (rest_parts, [(0, width // 4, unit_rows, 0)], (width, width))
        fc1_weight = (
            rest_parts, [(width // 4, hidden_width // 4, unit_rows, 0)], (width, hidden_width)
        )
    flat_attended = attended.reshape(rows, width)
    attn, normed_two, act, slope, sum_one = token_call(
        branch_kernel, place, rows, length, lengths, [flat_attended, tokens],
        [gamma_one, scale_two, shift_two], [proj_weight, fc1_weight],
        [(width, LOW), (width, LOW), (hidden_width, LOW), (hidden_width, LOW)], 1, "branch",
    )
    result, grad_mlp, sum_two = token_call(
        stream_kernel, place, rows, length, lengths, [act, tokens, attn, cotangent],
        [gamma_one, gamma_two], [fc2_weight], [(width, LOW), (width, LOW)], 1, "stream",
    )

    def send_part(left, right):
        return outer(left, right, 1 - place.c)

    def keep_part(left, right):
        return outer(left, right, place.c)

    def hidden_back(grad):
        return token_call(
            hidden_back_kernel, place, rows, length, lengths, [grad, slope], [], [fc2_weight],
            [(hidden_width, LOW)], 0, "hidden_back",
        )[0]

    def middle_back(grad):
        return token_call(
            middle_back_kernel, place, rows, length, lengths, [grad, tokens, attn, cotangent],
            [gamma_one, scale_two], [fc1_weight, proj_weight], [(width, LOW)] * 3, 1, "middle_back",
        )

    def heads_back(grad, first):
        out, sums = attend_back(
            projected, extra, key_mask, attended, grad.reshape(cube), roots, gain, first, pairs // 2
        )
        return out.reshape(rows, half), sums

    def token_back(first, second):
        return token_call(
            token_back_kernel, place, rows, length, lengths, [first, second, tokens, grad_middle],
            [scale_one], [qkv_weight], [(width, LOW)], 1, "token_back",
        )

    if place.grouped:
        fc2_rows = w_fc2.shape[0]
        fc2_send = send_part(act, grad_mlp)
        fc2_keep, arrived = beside(lambda g: keep_part(act, g), grad_mlp, [(fc2_send, {"dc": 1})])
        fc2_sum = RowSum(place, fc2_keep, arrived[0], fc2_rows, "mixed")
        grad_hidden, arrived = beside(hidden_back, grad_mlp, fc2_sum.first())
        fc1_send, arrived = beside(lambda g: send_part(normed_two, g), grad_hidden, fc2_sum.second(arrived))
        fc2_moves = fc2_sum.third(arrived)
        fc1_keep, arrived = beside(lambda g: keep_part(normed_two, g), grad_hidden, [(fc1_send, {"dc": 1})])
        fc1_sum = RowSum(place, fc1_keep, arrived[0], unit_rows, "mixed")
        out, arrived = beside(middle_back, grad_hidden, fc1_sum.first() + fc2_moves)
        grad_middle, grad_attn, grad_attended, sum_three = out
        fc2_own = fc2_sum.finish(arrived[2:])
        fc1_moves = fc1_sum.second(arrived[:2])
        grad_attn, *tied = tie(grad_attn, fc2_own, *(v for v, _ in fc1_moves))
        fc2_own, fc1_moves = tied[0], [(v, axes) for v, (_, axes) in zip(tied[1:], fc1_moves)]
        proj_send = send_part(flat_attended, grad_attn)
        proj_keep, arrived = beside(lambda g: keep_part(flat_attended, g), grad_attn, [(proj_send, {"dc": 1})])
        proj_sum = RowSum(place, proj_keep, arrived[0], unit_rows, "yx")
        out, arrived = beside(
            lambda g: heads_back(g, 0), grad_attended, fc1_moves + proj_sum.first() + [(fc2_own, {"dy": 1})]
        )
        grad_first, heads_first = out
        fc1_moves = fc1_sum.third(arrived[:2])
        proj_moves = proj_sum.second(arrived[2:3])
        fc2_y = arrived[3]
        first_send, fc2_core = beside(
            lambda g: send_part(normed_one, g), grad_first, [(fc2_own, {"dc": 1}), (fc2_y, {"dc": 1})]
        )
        first_keep, arrived = beside(lambda g: keep_part(normed_one, g), grad_first, [(first_send, {"dc": 1})])
        first_sum = RowSum(place, first_keep, arrived[0], unit_rows, "yx")
        out, arrived = beside(
            lambda g: heads_back(g, pairs // 2), grad_attended, fc1_moves + first_sum.first() + proj_moves
        )
        grad_second, heads_second = out
        fc1_own = fc1_sum.finish(arrived[:3])
        first_moves = first_sum.second(arrived[3:4])
        proj_moves = proj_sum.third(arrived[4:])
        second_send, arrived = beside(
            lambda g: send_part(normed_one, g), grad_second, proj_moves + first_moves
        )
        proj_own = proj_sum.finish(arrived[:3])
        first_moves = first_sum.third(arrived[3:])
        second_keep, arrived = beside(
            lambda g: keep_part(normed_one, g), grad_second, [(second_send, {"dc": 1}), (fc1_own, {"dy": 1})]
        )
        fc1_y = arrived[1]
        second_sum = RowSum(place, second_keep, arrived[0], unit_rows, "xy")
        out, arrived = beside(
            lambda g: token_back(grad_first, g), grad_second, second_sum.first() + first_moves
        )
        grad_tokens, sum_four = out
        second_moves = second_sum.second(arrived[:1])
        first_own = first_sum.finish(arrived[1:])
        second_moves = second_sum.third([hop(v, **axes) for v, axes in second_moves])
        second_own = second_sum.finish([hop(v, **axes) for v, axes in second_moves])
        quarter = width // 4
        (grad_fc2,) = lay_out(
            place, [fc2_own, fc2_y] + fc2_core, [(0, 0, quarter, 0, 0, quarter)], [w_fc2.shape], "lay_out_fc2"
        )
        (grad_fc1,) = lay_out(
            place, [fc1_own, fc1_y, hop(fc1_own, dc=1), hop(fc1_y, dc=1)],
            [(0, 0, hidden_width // 4, 0, 0, hidden_width // 4)], [w_fc1.shape], "lay_out_fc1",
        )
        late = spread(jnp.concatenate([first_own, second_own, proj_own], 1))
        layout = [
            (0, 384 * side + 128 * n, 128, 0, n * width + 512 * side, 128) for side in range(2) for n in range(3)
        ]
        layout.append((1, 768, quarter, 0, 0, quarter))
        grad_qkv, grad_proj = lay_out(place, late, layout, [w_qkv.shape, w_proj.shape], "lay_out_late")
    else:
        def whole_sum(left, right):
            return plain_sum(place, keep_part(left, right), send_part(left, right))

        grad_fc2 = whole_sum(act, grad_mlp)
        grad_hidden = hidden_back(grad_mlp)
        grad_fc1 = whole_sum(normed_two, grad_hidden)
        grad_middle, grad_attn, grad_attended, sum_three = middle_back(grad_hidden)
        grad_proj = whole_sum(flat_attended, grad_attn)
        grad_first, heads_first = heads_back(grad_attended, 0)
        grad_second, heads_second = heads_back(grad_attended, pairs // 2)
        grad_qkv = from_pair(
            jnp.concatenate([whole_sum(normed_one, grad_first), whole_sum(normed_one, grad_second)], 1)
        )
        grad_tokens, sum_four = token_back(grad_first, grad_second)

    head_terms = jnp.concatenate([heads_first, heads_second], 2).reshape(items, heads, width // heads).sum(2)
    head_parts = jnp.concatenate([*two_parts(head_terms), jnp.zeros((items, 128 - 2 * heads), LOW)], 1)
    grad_modulation = jnp.concatenate(
        [sum_three[4:6], sum_two[4:6], sum_four[0:2], sum_three[0:2], sum_four[2:4], sum_three[2:4]], 1
    ).astype(LOW)
    group = gather_small(place, jnp.concatenate([grad_modulation, head_parts, silu_cond], 1), False)
    grad_columns = dot(group[:, : 6 * width], w_ada, NT)
    everything = over_dp(place, group)
    all_heads = everything[:, 6 * width : 6 * width + 2 * heads].astype(WIDE)
    grad_head = jnp.sum(all_heads[:, :heads] + all_heads[:, heads:], 0)
    all_slice = lax.dynamic_slice(
        everything, (0, 6 * width + 128 + place.fsdp_index * ada_rows), (everything.shape[0], ada_rows)
    )
    grad_ada = dot(all_slice, everything[:, : 6 * width], TN)
    grad_parts = gather_small(place, grad_columns[None], False)
    own_items = lax.dynamic_slice(
        grad_parts, (0, place.fsdp_index * items, 0), (grad_parts.shape[0], items, ada_rows)
    )
    grad_silu = jnp.swapaxes(own_items, 0, 1).reshape(items, width)
    gate = jax.nn.sigmoid(cond_wide)
    grad_cond = (grad_silu * gate * (1.0 + cond_wide * (1.0 - gate))).astype(LOW)

    counted = (lengths * width).astype(WIDE)
    squares = jnp.stack(
        [sum_two[0:2].sum(1), sum_one[0:2].sum(1), sum_two[2:4].sum(1)], 1
    )
    rms_rows = jnp.sqrt(squares / counted[:, None] + EPS)
    return (
        result, grad_tokens, grad_cond, grad_ada, grad_qkv, grad_proj, grad_fc1, grad_fc2,
        grad_head, rms_rows,
    )


def solution(mesh):
    both = P(("dp", "fsdp"), None)
    rows = P("fsdp", None)
    return jax.shard_map(
        functools.partial(shards, (mesh.shape["dp"], mesh.shape["fsdp"])),
        mesh=mesh,
        in_specs=(both, both, P(("dp", "fsdp")), rows, rows, rows, rows, rows, P(), both),
        out_specs=(both, both, both, rows, rows, rows, rows, rows, P(), both),
        check_vma=False,
    )
```

time: 800 us -> 652 us (0.81)
  waiting for transfers between devices: 262 us -> 78.1 us
  Pallas kernels: 250 us -> 413 us
  matrix products: 72 us -> 3.09 us
  blocking collectives: 40.9 us -> 0 us
  other arithmetic: 36.4 us -> 11.6 us
  between operations: 2.12 us -> 15.8 us
  starting transfers between devices: 107 us -> 97.1 us
    ppermute x96 -> x86, waiting for transfers between devices: 262 us -> 78.1 us  [hop(): return lax.ppermute(values, AXES, pairs)]
    pallas_call x2 -> x36, Pallas kernels: 90.4 us -> 251 us  [the longest x10 78.9 us: outer(): pl.pallas_call(outer_kernel, grid_spec=pltpu.PrefetchScalarGridSpec(num_s...]
    dot_general x11 -> x3, matrix products: 72 us -> 3.09 us  [dot(): return lax.dot_general(left, right, dims, preferred_element_type=WIDE)]
    psum x1 -> x0, blocking collectives: 40.9 us -> none  [shards(): lax.psum(head_sums.reshape(items, heads, width // heads).sum((0, 2)), AXES)]
    convert_element_type x20 -> x2, other arithmetic: 19.2 us -> 0.01 us  [the longest x1 0.01 us: shards(): all_heads = everything[:, 6 * width:6 * width + 2 * heads].astype(WIDE)]
    ppermute x96 -> x86, starting transfers between devices: 107 us -> 97.1 us  [hop(): return lax.ppermute(values, AXES, pairs)]
    unnamed x117 -> x185, local copies, waits for them, and re-layouts: 11.4 us -> 17.4 us
  transfers between devices with their start and end apart: 96 -> 87, of which waited for: 34 -> 24; matrix products, arithmetic and copies ran while one was open for 15% -> 3% of each run, Pallas kernels for 11% -> 49%
where the time goes in v2:
time: 652 us; the launch traced here: 644 us
  Pallas kernels  413 us (63%)
  starting transfers between devices  97.1 us (15%)
  waiting for transfers between devices  78.1 us (12%)
  local copies, waits for them, and re-layouts  25.9 us (4%)
  between operations  15.8 us (2%)
  other arithmetic  11.6 us (2%)
    pallas_call x6, Pallas kernels, token_call(): pl.pallas_call(body, grid=(grid,), in_specs=[smem, smem] + [pl.BlockSpec(...  161 us
    ppermute x86, starting transfers between devices, hop(): return lax.ppermute(values, AXES, pairs)  97.1 us
    pallas_call x10, Pallas kernels, outer(): pl.pallas_call(outer_kernel, grid_spec=pltpu.PrefetchScalarGridSpec(num_s...  78.9 us
    pallas_call x20, Pallas kernels, add_blocks(): pl.pallas_call(body, grid_spec=pltpu.PrefetchScalarGridSpec(num_scalar_pr...  78.5 us
    ppermute x86, waiting for transfers between devices, hop(): return lax.ppermute(values, AXES, pairs)  78.1 us
    pallas_call x2, Pallas kernels, attend_back(): pl.pallas_call(attend_back_kernel, grid=(items, pairs), in_specs=[pl.Bloc...  59.9 us
    pallas_call x1, Pallas kernels, attend(): pl.pallas_call(attend_kernel, grid=(items, pairs), in_specs=[pl.BlockSpec...  25.9 us
    unnamed x185, local copies, waits for them, and re-layouts  17.4 us
  transfers between devices with their start and end apart: 87, of which 24 were waited for; matrix products, arithmetic and copies ran while one was open for 3% of the time, Pallas kernels for 49%

profile of v2, /device:TPU:9, one launch (start us, length us, event | category | flops | bytes accessed | tf_op | source)
XLA Modules:
  0.0 644.4 jit_solution(11036125164842213745)
XLA Ops:
  22.2 6.5 %collective-permute-done.5 = bf16[128,768]{1,0:T(8,128)(2,1)S(1)} collective-permute-done((bf16[128,768]{1,0:T(8,128)(2,1)S(1)}, bf16[128,768]{1,0:T(8,128)(2,1)S(1)}, u32[]{:S(2)}, u32[]{:S(2)}) %collective-permute-start.5) | collective-permute-done | bytes 196640 | tf_op jit(solution)/shard_map/ppermute | solution.py:58
  28.7 4.3 collective-permute-done.4
  34.9 2.9 collective-permute-start.8
  43.3 2.5 collective-permute-start.12
  45.9 10.7 %collective-permute-done.16.refs_6_.refs_7_ = bf16[512,768]{1,0:T(8,128)(2,1)S(1)} collective-permute-done((bf16[512,768]{1,0:T(8,128)(2,1)S(1)}, bf16[512,768]{1,0:T(8,128)(2,1)S(1)}, u32[]{:S(2)}, u32[]{:S(2)}) %collective-permute-start.16) | collective-permute-done | bytes 786464 | tf_op jit(solution)/shard_map/ppermute | solution.py:58
  58.3 7.4 %collective-permute-done.13 = bf16[128,1280]{1,0:T(8,128)(2,1)S(1)} collective-permute-done((bf16[128,1280]{1,0:T(8,128)(2,1)S(1)}, bf16[128,1280]{1,0:T(8,128)(2,1)S(1)}, u32[]{:S(2)}, u32[]{:S(2)}) %collective-permute-start.13) | collective-permute-done | bytes 327712 | tf_op jit(solution)/shard_map/ppermute | solution.py:58
  65.7 5.1 collective-permute-done.12
  83.4 23.7 %project.1 = (bf16[1360,1024]{1,0:T(8,128)(2,1)}, bf16[1360,3072]{1,0:T(8,128)(2,1)}, bf16[1360,1024]{1,0:T(8,128)(2,1)}) custom-call(s32[4]{0:T(128)} %pad_add_fusion.place_ref, s32[2]{0:T(128)} %fusion.19.lengths_ref, bf16[1360,1024]{1,0:T(8,128)(2,1)} %refs_2_.1, f32[2,1024]{1,0:T(2,128)} %get-tuple-element.404.refs_1_.refs_4_, ...), custom_call_target="tpu_custom_call" | custom-call | flops 1024 | bytes 1024 | tf_op jit(solution)/shard_map/project/pallas_call | solution.py:536
  113.4 3.4 collective-permute-start.27
  117.3 25.9 %attend.1 = (bf16[2,680,1024]{2,1,0:T(8,128)(2,1)}, bf16[2,680,1024]{2,1,0:T(8,128)(2,1)}) custom-call(bf16[2,680,3072]{2,1,0:T(8,128)(2,1)} %bitcast.76, bf16[680,128]{1,0:T(8,128)(2,1)} %constant.112.clone.qm_ref, bf16[680,128]{1,0:T(8,128)(2,1)} %constant.113.clone.km_ref), custom_call_target="tpu_custom_call" | custom-call | flops 1024 | bytes 1024 | tf_op jit(solution)/shard_map/attend/pallas_call | solution.py:359
  146.6 39.3 %branch.1 = (bf16[1360,1024]{1,0:T(8,128)(2,1)}, bf16[1360,1024]{1,0:T(8,128)(2,1)}, bf16[1360,4096]{1,0:T(8,128)(2,1)}, bf16[1360,4096]{1,0:T(8,128)(2,1)}, f32[8,1024]{1,0:T(8,128)}) custom-call(s32[4]{0:T(128)} %pad_add_fusion.place_ref, s32[2]{0:T(128)} %fusion.19.lengths_ref, bf16[1360,1024]{1,0:T(8,128)(2,1)} %bitcast.79, bf16[1360,1024]{1,0:T(8,128)(2,1)} %refs_2_.1, ...), custom_call_target="tpu_custom_call" | custom-call | flops 1024 | bytes 1024 | tf_op jit(solution)/shard_map/branch/pallas_call | solution.py:536
  185.9 25.8 %stream.1 = (bf16[1360,1024]{1,0:T(8,128)(2,1)}, bf16[1360,1024]{1,0:T(8,128)(2,1)}, f32[8,1024]{1,0:T(8,128)}) custom-call(s32[4]{0:T(128)} %pad_add_fusion.place_ref, s32[2]{0:T(128)} %fusion.19.lengths_ref, bf16[1360,4096]{1,0:T(8,128)(2,1)} %get-tuple-element.197.refs_0_.left_ref, bf16[1360,1024]{1,0:T(8,128)(2,1)} %refs_2_.1, ...), custom_call_target="tpu_custom_call" | custom-call | flops 1024 | bytes 1024 | tf_op jit(solution)/shard_map/stream/pallas_call | solution.py:536
  211.7 11.0 %outer.10 = bf16[4096,512]{1,0:T(8,128)(2,1)} custom-call(s32[1]{0:T(128)} %bitcast.22.half_ref, bf16[1360,4096]{1,0:T(8,128)(2,1)} %get-tuple-element.197.refs_0_.left_ref, bf16[1360,1024]{1,0:T(8,128)(2,1)} %get-tuple-element.209.right_ref.refs_0_), custom_call_target="tpu_custom_call" | custom-call | flops 1024 | bytes 1024 | tf_op jit(solution)/shard_map/outer/pallas_call | solution.py:687
  222.7 10.9 %outer.11.refs_0_.refs_2_.refs_3_.refs_6_.refs_12_ = bf16[4096,512]{1,0:T(8,128)(2,1)} custom-call(s32[1]{0:T(128)} %bitcast.1.half_ref, bf16[1360,4096]{1,0:T(8,128)(2,1)} %get-tuple-element.197.refs_0_.left_ref, bf16[1360,1024]{1,0:T(8,128)(2,1)} %get-tuple-element.209.right_ref.refs_0_), custom_call_target="tpu_custom_call" | custom-call | flops 1024 | bytes 1024 | tf_op jit(solution)/shard_map/outer/pallas_call | solution.py:687
  235.6 4.8 first_sums.5
  243.3 19.7 %hidden_back.1.right_ref.refs_0_ = bf16[1360,4096]{1,0:T(8,128)(2,1)} custom-call(s32[4]{0:T(128)} %pad_add_fusion.place_ref, s32[2]{0:T(128)} %fusion.19.lengths_ref, bf16[1360,1024]{1,0:T(8,128)(2,1)} %get-tuple-element.209.right_ref.refs_0_, bf16[1360,4096]{1,0:T(8,128)(2,1)} %get-tuple-element.210.refs_1_, ...), custom_call_target="tpu_custom_call" | custom-call | flops 1024 | bytes 1024 | tf_op jit(solution)/shard_map/hidden_back/pallas_call | solution.py:536
  263.0 2.4 collective-permute-done.33.refs_2_.refs_8_.refs_14_
  267.4 3.4 second_sums.5
  273.2 10.9 %outer.12 = bf16[1024,2048]{1,0:T(8,128)(2,1)} custom-call(s32[1]{0:T(128)} %bitcast.22.half_ref, bf16[1360,1024]{1,0:T(8,128)(2,1)} %get-tuple-element.214.left_ref, bf16[1360,4096]{1,0:T(8,128)(2,1)} %hidden_back.1.right_ref.refs_0_), custom_call_target="tpu_custom_call" | custom-call | flops 1024 | bytes 1024 | tf_op jit(solution)/shard_map/outer/pallas_call | solution.py:687
  286.5 11.1 %outer.13.refs_0_.refs_2_.refs_3_.refs_6_.refs_12_ = bf16[1024,2048]{1,0:T(8,128)(2,1)} custom-call(s32[1]{0:T(128)} %bitcast.1.half_ref, bf16[1360,1024]{1,0:T(8,128)(2,1)} %get-tuple-element.214.left_ref, bf16[1360,4096]{1,0:T(8,128)(2,1)} %hidden_back.1.right_ref.refs_0_), custom_call_target="tpu_custom_call" | custom-call | flops 1024 | bytes 1024 | tf_op jit(solution)/shard_map/outer/pallas_call | solution.py:687
  297.6 4.5 third_sums.5
  304.1 4.8 first_sums.6
  310.6 6.9 %collective-permute-start.40 = (bf16[512,256]{1,0:T(8,128)(2,1)S(1)}, bf16[512,256]{1,0:T(8,128)(2,1)S(1)}, u32[]{:S(2)}, u32[]{:S(2)}) collective-permute-start(bf16[512,256]{1,0:T(8,128)(2,1)S(1)} %copy-done.69), channel_id=1, source_target_pairs={{0,2},{1,3},{2,0},{3,1},{4,6},{5,7},{6,4},{7,5},{8,10},{9,11},{10,... | collective-permute-start | bytes 786440 | tf_op jit(solution)/shard_map/ppermute | solution.py:58
  318.8 32.9 %middle_back.1 = (bf16[1360,1024]{1,0:T(8,128)(2,1)}, bf16[1360,1024]{1,0:T(8,128)(2,1)}, bf16[1360,1024]{1,0:T(8,128)(2,1)}, f32[8,1024]{1,0:T(8,128)}) custom-call(s32[4]{0:T(128)} %pad_add_fusion.place_ref, s32[2]{0:T(128)} %fusion.19.lengths_ref, bf16[1360,4096]{1,0:T(8,128)(2,1)} %hidden_back.1.right_ref.refs_0_, bf16[1360,1024]{1,0:T(8,128)(2,1)} %refs_2_.1, ...), custom_call_target="tpu_custom_call" | custom-call | flops 1024 | bytes 1024 | tf_op jit(solution)/shard_map/middle_back/pallas_call | solution.py:536
  353.1 3.4 second_sums.6
  356.6 3.4 last_sums.5.refs_0_
  360.0 5.0 outer.14
  366.1 5.0 outer.15.refs_0_.refs_4_.refs_8_
  372.1 5.8 first_sums.7
  380.8 30.0 %attend_back.2 = (bf16[2,680,1536]{2,1,0:T(8,128)(2,1)}, f32[2,1,512]{2,1,0:T(1,128)}) custom-call(bf16[2,680,3072]{2,1,0:T(8,128)(2,1)} %bitcast.77, bf16[2,680,1024]{2,1,0:T(8,128)(2,1)} %get-tuple-element.201.extra_ref, bf16[680,128]{1,0:T(8,128)(2,1)} %constant.113.clone.km_ref, bf16[2,680,1024]{2,1,0:T(8,128)(2,1)} %get-tuple-element.194.out_ref, ...), custom_call_target="tpu_custom_call" | custom-call | flops 1024 | bytes 1024 | tf_op jit(solution)/shard_map/attend_back/pallas_call | solution.py:438
  412.1 6.3 outer.16
  419.0 3.8 second_sums.7
  422.8 4.5 third_sums.6
  427.3 6.3 outer.17.refs_0_.refs_4_.refs_8_
  434.8 6.0 first_sums.8
  442.0 2.6 collective-permute-start.51
  446.2 30.0 %attend_back.3 = (bf16[2,680,1536]{2,1,0:T(8,128)(2,1)}, f32[2,1,512]{2,1,0:T(1,128)}) custom-call(bf16[2,680,3072]{2,1,0:T(8,128)(2,1)} %bitcast.78, bf16[2,680,1024]{2,1,0:T(8,128)(2,1)} %get-tuple-element.201.extra_ref, bf16[680,128]{1,0:T(8,128)(2,1)} %constant.113.clone.km_ref, bf16[2,680,1024]{2,1,0:T(8,128)(2,1)} %get-tuple-element.194.out_ref, ...), custom_call_target="tpu_custom_call" | custom-call | flops 1024 | bytes 1024 | tf_op jit(solution)/shard_map/attend_back/pallas_call | solution.py:438
  477.1 2.6 third_sums.7
  479.7 4.6 second_sums.8
  489.0 6.3 outer.18
  495.3 3.5 last_sums.6.refs_0_
  500.0 2.4 collective-permute-start.60
  502.7 6.3 outer.19.refs_0_.refs_4_.refs_8_
  508.9 2.8 third_sums.8
  513.0 6.0 first_sums.9
  520.2 2.6 collective-permute-start.63
  524.0 20.1 %token_back.1 = (bf16[1360,1024]{1,0:T(8,128)(2,1)}, f32[8,1024]{1,0:T(8,128)}) custom-call(s32[4]{0:T(128)} %pad_add_fusion.place_ref, s32[2]{0:T(128)} %fusion.19.lengths_ref, bf16[1360,1536]{1,0:T(8,128)(2,1)} %bitcast.84, bf16[1360,1536]{1,0:T(8,128)(2,1)} %bitcast.87, bf16[1360,1024]{1,0:T(8,128)(2,1)} %refs_2_.1, ...), custom_call_target="tpu_custom_call" | custom-call | flops 1024 | bytes 1024 | tf_op jit(solution)/shard_map/token_back/pallas_call | solution.py:536
  545.6 4.1 collective-permute-start.67
  554.0 2.4 collective-permute-done.69
  560.6 5.2 collective-permute-start.84
  568.4 2.7 lay_out_fc2.1
  571.1 2.4 last_sums.9
  573.5 2.7 lay_out_fc1.1
  576.1 4.2 second_sums.9
  581.7 2.6 last_sums.7
  584.3 2.9 collective-permute-start.76
  589.3 9.2 %collective-permute-done.76 = bf16[16,7296]{1,0:T(8,128)(2,1)S(1)} collective-permute-done((bf16[16,7296]{1,0:T(8,128)(2,1)S(1)}, bf16[16,7296]{1,0:T(8,128)(2,1)S(1)}, u32[]{:S(2)}, u32[]{:S(2)}) %collective-permute-start.76) | collective-permute-done | bytes 233504 | tf_op jit(solution)/shard_map/ppermute | solution.py:58
  600.9 2.8 third_sums.9
  609.7 4.8 collective-permute-done.80.refs_6_
  615.1 2.6 last_sums.8
  618.7 2.7 collective-permute-start.83
  624.5 3.5 collective-permute-done.83.refs_3_
  628.1 5.8 collective-permute-done.81.refs_1_
  634.6 2.8 lay_out_late.1
  (406 shorter events, 115.5 us)
Async XLA Ops:
  7.2 178.7 %all-gather.2.cloned.1.call-start = ((), (), s32[]{:S(2)}) async-start(), calls=%async_computation | async-start | bytes 8650752 | tf_op jit(solution)/shard_map/all_gather | solution.py:763
  16.6 12.2 %collective-permute-start.5 = (bf16[128,768]{1,0:T(8,128)(2,1)S(1)}, bf16[128,768]{1,0:T(8,128)(2,1)S(1)}, u32[]{:S(2)}, u32[]{:S(2)}) collective-permute-start(bf16[128,768]{1,0:T(8,128)(2,1)S(1)} %copy.46), channel_id=1, source_target_pairs={{0,6},{1,7},{2,4},{3,5},{4,2},{5,3},{6,0},{7,1},{8,14},{9,15},{10,... | collective-permute-start | bytes 589832 | tf_op jit(solution)/shard_map/ppermute | solution.py:58
  17.8 15.2 %collective-permute-start.4 = (bf16[128,768]{1,0:T(8,128)(2,1)S(1)}, bf16[128,768]{1,0:T(8,128)(2,1)S(1)}, u32[]{:S(2)}, u32[]{:S(2)}) collective-permute-start(bf16[128,768]{1,0:T(8,128)(2,1)S(1)} %copy.46), channel_id=1, source_target_pairs={{0,4},{1,5},{2,6},{3,7},{4,0},{5,1},{6,2},{7,3},{8,12},{9,13},{10,... | collective-permute-start | bytes 589832 | tf_op jit(solution)/shard_map/ppermute | solution.py:58
  19.5 14.2 %collective-permute-start.3 = (bf16[128,768]{1,0:T(8,128)(2,1)S(1)}, bf16[128,768]{1,0:T(8,128)(2,1)}, u32[]{:S(2)}, u32[]{:S(2)}) collective-permute-start(bf16[128,768]{1,0:T(8,128)(2,1)S(1)} %copy.46), channel_id=1, source_target_pairs={{0,2},{1,3},{2,0},{3,1},{4,6},{5,7},{6,4},{7,5},{8,10},{9,11},{10,... | collective-permute-start | bytes 589832 | tf_op jit(solution)/shard_map/ppermute | solution.py:58
  21.1 13.7 %collective-permute-start.7 = (f32[4,2,6144]{2,1,0:T(2,128)S(1)}, f32[4,2,6144]{2,1,0:T(2,128)S(1)}, u32[]{:S(2)}, u32[]{:S(2)}) collective-permute-start(f32[4,2,6144]{2,1,0:T(2,128)S(1)} %dynamic-slice_bitcast_fusion), channel_id=1, source_target_pairs={{0,1},{1,0},{2,3},{3,2},{4,5},{5,4},{6,7},{7,6},{8,9},{9,8},{10,11... | collective-permute-start | bytes 589832 | tf_op jit(solution)/shard_map/ppermute | solution.py:58
  34.9 6.7 %collective-permute-start.8 = (f32[2,6144]{1,0:T(2,128)S(1)}, f32[2,6144]{1,0:T(2,128)S(1)}, u32[]{:S(2)}, u32[]{:S(2)}) collective-permute-start(f32[2,6144]{1,0:T(2,128)S(1)} %get-tuple-element.396), channel_id=1, source_target_pairs={{0,2},{1,3},{2,0},{3,1},{4,6},{5,7},{6,4},{7,5},{8,10},{9,11},{10,... | collective-permute-start | bytes 147464 | tf_op jit(solution)/shard_map/ppermute | solution.py:58
  40.0 16.6 %collective-permute-start.16 = (bf16[512,768]{1,0:T(8,128)(2,1)S(1)}, bf16[512,768]{1,0:T(8,128)(2,1)S(1)}, u32[]{:S(2)}, u32[]{:S(2)}) collective-permute-start(bf16[512,768]{1,0:T(8,128)(2,1)S(1)} %pad_maximum_fusion.3.refs_4_.refs_5_), channel_id=1, source_target_pairs={{0,16},{1,17},{2,18},{3,19},{4,20},{5,21},{6,22},{7,23},{8,24},{9,... | collective-permute-start | bytes 2359304 | tf_op jit(solution)/shard_map/ppermute | solution.py:58
  41.4 16.2 %collective-permute-start.14 = (bf16[512,768]{1,0:T(8,128)(2,1)S(1)}, bf16[512,768]{1,0:T(8,128)(2,1)S(1)}, u32[]{:S(2)}, u32[]{:S(2)}) collective-permute-start(bf16[512,768]{1,0:T(8,128)(2,1)S(1)} %pad_maximum_fusion.3.refs_4_.refs_5_), channel_id=1, source_target_pairs={{0,1},{1,0},{2,3},{3,2},{4,5},{5,4},{6,7},{7,6},{8,9},{9,8},{10,11... | collective-permute-start | bytes 2359304 | tf_op jit(solution)/shard_map/ppermute | solution.py:58
  42.1 23.5 %collective-permute-start.13 = (bf16[128,1280]{1,0:T(8,128)(2,1)S(1)}, bf16[128,1280]{1,0:T(8,128)(2,1)S(1)}, u32[]{:S(2)}, u32[]{:S(2)}) collective-permute-start(bf16[128,1280]{1,0:T(8,128)(2,1)S(1)} %pad_maximum_fusion.4), channel_id=1, source_target_pairs={{0,6},{1,7},{2,4},{3,5},{4,2},{5,3},{6,0},{7,1},{8,14},{9,15},{10,... | collective-permute-start | bytes 983048 | tf_op jit(solution)/shard_map/ppermute | solution.py:58
  43.3 27.4 %collective-permute-start.12 = (bf16[128,1280]{1,0:T(8,128)(2,1)S(1)}, bf16[128,1280]{1,0:T(8,128)(2,1)S(1)}, u32[]{:S(2)}, u32[]{:S(2)}) collective-permute-start(bf16[128,1280]{1,0:T(8,128)(2,1)S(1)} %pad_maximum_fusion.4), channel_id=1, source_target_pairs={{0,4},{1,5},{2,6},{3,7},{4,0},{5,1},{6,2},{7,3},{8,12},{9,13},{10,... | collective-permute-start | bytes 983048 | tf_op jit(solution)/shard_map/ppermute | solution.py:58
  45.9 24.9 %collective-permute-start.11 = (bf16[128,1280]{1,0:T(8,128)(2,1)S(1)}, bf16[128,1280]{1,0:T(8,128)(2,1)S(1)}, u32[]{:S(2)}, u32[]{:S(2)}) collective-permute-start(bf16[128,1280]{1,0:T(8,128)(2,1)S(1)} %pad_maximum_fusion.4), channel_id=1, source_target_pairs={{0,2},{1,3},{2,0},{3,1},{4,6},{5,7},{6,4},{7,5},{8,10},{9,11},{10,... | collective-permute-start | bytes 983048 | tf_op jit(solution)/shard_map/ppermute | solution.py:58
  56.7 15.2 %collective-permute-start.17 = (bf16[256,768]{1,0:T(8,128)(2,1)S(1)}, bf16[256,768]{1,0:T(8,128)(2,1)S(1)}, u32[]{:S(2)}, u32[]{:S(2)}) collective-permute-start(bf16[256,768]{1,0:T(8,128)(2,1)S(1)} %slice.103), channel_id=1, source_target_pairs={{0,1},{1,0},{2,3},{3,2},{4,5},{5,4},{6,7},{7,6},{8,9},{9,8},{10,11... | collective-permute-start | bytes 1179656 | tf_op jit(solution)/shard_map/ppermute | solution.py:58
  57.6 14.3 %collective-permute-start.15 = (bf16[256,768]{1,0:T(8,128)(2,1)S(1)}, bf16[256,768]{1,0:T(8,128)(2,1)}, u32[]{:S(2)}, u32[]{:S(2)}) collective-permute-start(bf16[256,768]{1,0:T(8,128)(2,1)S(1)} %slice.102), channel_id=1, source_target_pairs={{0,16},{1,17},{2,18},{3,19},{4,20},{5,21},{6,22},{7,23},{8,24},{9,... | collective-permute-start | bytes 1179656 | tf_op jit(solution)/shard_map/ppermute | solution.py:58
  75.7 33.1 %collective-permute-start.19 = (bf16[512,1280]{1,0:T(8,128)(2,1)S(1)}, bf16[512,1280]{1,0:T(8,128)(2,1)}, u32[]{:S(2)}, u32[]{:S(2)}) collective-permute-start(bf16[512,1280]{1,0:T(8,128)(2,1)S(1)} %pad_maximum_fusion.refs_5_.refs_15_.refs_6_.refs_16_), channel_id=1, source_target_pairs={{0,16},{1,17},{2,18},{3,19},{4,20},{5,21},{6,22},{7,23},{8,24},{9,... | collective-permute-start | bytes 3932168 | tf_op jit(solution)/shard_map/ppermute | solution.py:58
  77.0 33.6 %collective-permute-start.18 = (bf16[512,1280]{1,0:T(8,128)(2,1)S(1)}, bf16[512,1280]{1,0:T(8,128)(2,1)}, u32[]{:S(2)}, u32[]{:S(2)}) collective-permute-start(bf16[512,1280]{1,0:T(8,128)(2,1)S(1)} %pad_maximum_fusion.refs_5_.refs_15_.refs_6_.refs_16_), channel_id=1, source_target_pairs={{0,1},{1,0},{2,3},{3,2},{4,5},{5,4},{6,7},{7,6},{8,9},{9,8},{10,11... | collective-permute-start | bytes 3932168 | tf_op jit(solution)/shard_map/ppermute | solution.py:58
  112.9 30.3 %collective-permute-start.26 = (bf16[256,1280]{1,0:T(8,128)(2,1)S(1)}, bf16[256,1280]{1,0:T(8,128)(2,1)S(1)}, u32[]{:S(2)}, u32[]{:S(2)}) collective-permute-start(bf16[256,1280]{1,0:T(8,128)(2,1)S(1)} %slice.83), channel_id=1, source_target_pairs={{0,1},{1,0},{2,3},{3,2},{4,5},{5,4},{6,7},{7,6},{8,9},{9,8},{10,11... | collective-permute-start | bytes 1966088 | tf_op jit(solution)/shard_map/ppermute | solution.py:58
  113.2 30.0 %collective-permute-start.25 = (bf16[256,1280]{1,0:T(8,128)(2,1)S(1)}, bf16[256,1280]{1,0:T(8,128)(2,1)}, u32[]{:S(2)}, u32[]{:S(2)}) collective-permute-start(bf16[256,1280]{1,0:T(8,128)(2,1)S(1)} %slice.82), channel_id=1, source_target_pairs={{0,16},{1,17},{2,18},{3,19},{4,20},{5,21},{6,22},{7,23},{8,24},{9,... | collective-permute-start | bytes 1966088 | tf_op jit(solution)/shard_map/ppermute | solution.py:58
  113.4 30.4 %collective-permute-start.27 = (bf16[512,1280]{1,0:T(8,128)(2,1)S(1)}, bf16[512,1280]{1,0:T(8,128)(2,1)}, u32[]{:S(2)}, u32[]{:S(2)}) collective-permute-start(bf16[512,1280]{1,0:T(8,128)(2,1)S(1)} %pad_maximum_fusion.refs_5_.refs_15_.refs_6_.refs_16_), channel_id=1, source_target_pairs={{0,8},{1,9},{2,10},{3,11},{4,12},{5,13},{6,14},{7,15},{8,0},{9,1},... | collective-permute-start | bytes 3932168 | tf_op jit(solution)/shard_map/ppermute | solution.py:58
  116.8 27.0 %collective-permute-start.28 = (bf16[512,1280]{1,0:T(8,128)(2,1)}, bf16[512,1280]{1,0:T(8,128)(2,1)}, u32[]{:S(2)}, u32[]{:S(2)}) collective-permute-start(bf16[512,1280]{1,0:T(8,128)(2,1)} %collective-permute-done.18.refs_6_.refs_16_.refs_7_.refs_17_), channel_id=1, source_target_pairs={{0,8},{1,9},{2,10},{3,11},{4,12},{5,13},{6,14},{7,15},{8,0},{9,1},... | collective-permute-start | bytes 3932168 | tf_op jit(solution)/shard_map/ppermute | solution.py:58
  116.9 26.9 %collective-permute-start.29 = (bf16[512,1280]{1,0:T(8,128)(2,1)}, bf16[512,1280]{1,0:T(8,128)(2,1)}, u32[]{:S(2)}, u32[]{:S(2)}) collective-permute-start(bf16[512,1280]{1,0:T(8,128)(2,1)} %collective-permute-done.19.refs_7_.refs_17_.refs_8_.refs_18_), channel_id=1, source_target_pairs={{0,8},{1,9},{2,10},{3,11},{4,12},{5,13},{6,14},{7,15},{8,0},{9,1},... | collective-permute-start | bytes 3932168 | tf_op jit(solution)/shard_map/ppermute | solution.py:58
  222.7 11.0 %collective-permute-start.32 = (bf16[4096,512]{1,0:T(8,128)(2,1)}, bf16[4096,512]{1,0:T(8,128)(2,1)S(1)}, u32[]{:S(2)}, u32[]{:S(2)}) collective-permute-start(bf16[4096,512]{1,0:T(8,128)(2,1)} %outer.10), channel_id=1, source_target_pairs={{0,8},{1,9},{2,10},{3,11},{4,12},{5,13},{6,14},{7,15},{8,0},{9,1},... | collective-permute-start | bytes 12582920 | tf_op jit(solution)/shard_map/ppermute | solution.py:58
  240.4 25.0 %collective-permute-start.33 = (bf16[2048,256]{1,0:T(8,128)(2,1)}, bf16[2048,256]{1,0:T(8,128)(2,1)S(1)}, u32[]{:S(2)}, u32[]{:S(2)}) collective-permute-start(bf16[2048,256]{1,0:T(8,128)(2,1)} %get-tuple-element.211), channel_id=1, source_target_pairs={{0,16},{1,17},{2,18},{3,19},{4,20},{5,21},{6,22},{7,23},{8,24},{9,... | collective-permute-start | bytes 3145736 | tf_op jit(solution)/shard_map/ppermute | solution.py:58
  242.1 24.2 %collective-permute-start.34 = (bf16[1024,512]{1,0:T(8,128)(2,1)}, bf16[1024,512]{1,0:T(8,128)(2,1)S(1)}, u32[]{:S(2)}, u32[]{:S(2)}) collective-permute-start(bf16[1024,512]{1,0:T(8,128)(2,1)} %get-tuple-element.212), channel_id=1, source_target_pairs={{0,1},{1,0},{2,3},{3,2},{4,5},{5,4},{6,7},{7,6},{8,9},{9,8},{10,11... | collective-permute-start | bytes 3145736 | tf_op jit(solution)/shard_map/ppermute | solution.py:58
  270.8 13.4 %collective-permute-start.35 = (bf16[1024,256]{1,0:T(8,128)(2,1)}, bf16[1024,256]{1,0:T(8,128)(2,1)S(1)}, u32[]{:S(2)}, u32[]{:S(2)}) collective-permute-start(bf16[1024,256]{1,0:T(8,128)(2,1)} %get-tuple-element.220), channel_id=1, source_target_pairs={{0,1},{1,0},{2,3},{3,2},{4,5},{5,4},{6,7},{7,6},{8,9},{9,8},{10,11... | collective-permute-start | bytes 1572872 | tf_op jit(solution)/shard_map/ppermute | solution.py:58
  271.9 12.3 %collective-permute-start.36 = (bf16[1024,256]{1,0:T(8,128)(2,1)}, bf16[1024,256]{1,0:T(8,128)(2,1)S(1)}, u32[]{:S(2)}, u32[]{:S(2)}) collective-permute-start(bf16[1024,256]{1,0:T(8,128)(2,1)} %get-tuple-element.221), channel_id=1, source_target_pairs={{0,16},{1,17},{2,18},{3,19},{4,20},{5,21},{6,22},{7,23},{8,24},{9,... | collective-permute-start | bytes 1572872 | tf_op jit(solution)/shard_map/ppermute | solution.py:58
  284.2 17.9 %collective-permute-start.37 = (bf16[1024,2048]{1,0:T(8,128)(2,1)}, bf16[1024,2048]{1,0:T(8,128)(2,1)S(1)}, u32[]{:S(2)}, u32[]{:S(2)}) collective-permute-start(bf16[1024,2048]{1,0:T(8,128)(2,1)} %outer.12), channel_id=1, source_target_pairs={{0,8},{1,9},{2,10},{3,11},{4,12},{5,13},{6,14},{7,15},{8,0},{9,1},... | collective-permute-start | bytes 12582920 | tf_op jit(solution)/shard_map/ppermute | solution.py:58
  309.0 42.8 %collective-permute-start.38 = (bf16[512,1024]{1,0:T(8,128)(2,1)}, bf16[512,1024]{1,0:T(8,128)(2,1)S(1)}, u32[]{:S(2)}, u32[]{:S(2)}) collective-permute-start(bf16[512,1024]{1,0:T(8,128)(2,1)} %get-tuple-element.239), channel_id=1, source_target_pairs={{0,16},{1,17},{2,18},{3,19},{4,20},{5,21},{6,22},{7,23},{8,24},{9,... | collective-permute-start | bytes 3145736 | tf_op jit(solution)/shard_map/ppermute | solution.py:58
  310.2 41.5 %collective-permute-start.39 = (bf16[256,2048]{1,0:T(8,128)(2,1)}, bf16[256,2048]{1,0:T(8,128)(2,1)S(1)}, u32[]{:S(2)}, u32[]{:S(2)}) collective-permute-start(bf16[256,2048]{1,0:T(8,128)(2,1)} %get-tuple-element.240), channel_id=1, source_target_pairs={{0,1},{1,0},{2,3},{3,2},{4,5},{5,4},{6,7},{7,6},{8,9},{9,8},{10,11... | collective-permute-start | bytes 3145736 | tf_op jit(solution)/shard_map/ppermute | solution.py:58
  310.6 41.1 %collective-permute-start.40 = (bf16[512,256]{1,0:T(8,128)(2,1)S(1)}, bf16[512,256]{1,0:T(8,128)(2,1)S(1)}, u32[]{:S(2)}, u32[]{:S(2)}) collective-permute-start(bf16[512,256]{1,0:T(8,128)(2,1)S(1)} %copy-done.69), channel_id=1, source_target_pairs={{0,2},{1,3},{2,0},{3,1},{4,6},{5,7},{6,4},{7,5},{8,10},{9,11},{10,... | collective-permute-start | bytes 786440 | tf_op jit(solution)/shard_map/ppermute | solution.py:58
  317.5 34.2 %collective-permute-start.41 = (bf16[512,256]{1,0:T(8,128)(2,1)S(1)}, bf16[512,256]{1,0:T(8,128)(2,1)S(1)}, u32[]{:S(2)}, u32[]{:S(2)}) collective-permute-start(bf16[512,256]{1,0:T(8,128)(2,1)S(1)} %copy-done.68), channel_id=1, source_target_pairs={{0,4},{1,5},{2,6},{3,7},{4,0},{5,1},{6,2},{7,3},{8,12},{9,13},{10,... | collective-permute-start | bytes 786440 | tf_op jit(solution)/shard_map/ppermute | solution.py:58
  317.6 34.2 %collective-permute-start.42 = (bf16[512,256]{1,0:T(8,128)(2,1)S(1)}, bf16[512,256]{1,0:T(8,128)(2,1)S(1)}, u32[]{:S(2)}, u32[]{:S(2)}) collective-permute-start(bf16[512,256]{1,0:T(8,128)(2,1)S(1)} %copy-done.67), channel_id=1, source_target_pairs={{0,6},{1,7},{2,4},{3,5},{4,2},{5,3},{6,0},{7,1},{8,14},{9,15},{10,... | collective-permute-start | bytes 786440 | tf_op jit(solution)/shard_map/ppermute | solution.py:58
  378.0 32.8 %collective-permute-start.44 = (bf16[256,1024]{1,0:T(8,128)(2,1)S(1)}, bf16[256,1024]{1,0:T(8,128)(2,1)S(1)}, u32[]{:S(2)}, u32[]{:S(2)}) collective-permute-start(bf16[256,1024]{1,0:T(8,128)(2,1)S(1)} %copy-done.66), channel_id=1, source_target_pairs={{0,1},{1,0},{2,3},{3,2},{4,5},{5,4},{6,7},{7,6},{8,9},{9,8},{10,11... | collective-permute-start | bytes 1572872 | tf_op jit(solution)/shard_map/ppermute | solution.py:58
  379.1 31.7 %collective-permute-start.45 = (bf16[256,1024]{1,0:T(8,128)(2,1)S(1)}, bf16[256,1024]{1,0:T(8,128)(2,1)S(1)}, u32[]{:S(2)}, u32[]{:S(2)}) collective-permute-start(bf16[256,1024]{1,0:T(8,128)(2,1)S(1)} %copy-done.65), channel_id=1, source_target_pairs={{0,16},{1,17},{2,18},{3,19},{4,20},{5,21},{6,22},{7,23},{8,24},{9,... | collective-permute-start | bytes 1572872 | tf_op jit(solution)/shard_map/ppermute | solution.py:58
  379.4 31.5 %collective-permute-start.46 = (bf16[1024,256]{1,0:T(8,128)(2,1)}, bf16[1024,256]{1,0:T(8,128)(2,1)S(1)}, u32[]{:S(2)}, u32[]{:S(2)}) collective-permute-start(bf16[1024,256]{1,0:T(8,128)(2,1)} %first_sums.7), channel_id=1, source_target_pairs={{0,16},{1,17},{2,18},{3,19},{4,20},{5,21},{6,22},{7,23},{8,24},{9,... | collective-permute-start | bytes 1572872 | tf_op jit(solution)/shard_map/ppermute | solution.py:58
  380.6 30.2 %collective-permute-start.47 = (bf16[512,256]{1,0:T(8,128)(2,1)S(1)}, bf16[512,256]{1,0:T(8,128)(2,1)S(1)}, u32[]{:S(2)}, u32[]{:S(2)}) collective-permute-start(bf16[512,256]{1,0:T(8,128)(2,1)S(1)} %copy-done.29), channel_id=1, source_target_pairs={{0,16},{1,17},{2,18},{3,19},{4,20},{5,21},{6,22},{7,23},{8,24},{9,... | collective-permute-start | bytes 786440 | tf_op jit(solution)/shard_map/ppermute | solution.py:58
  410.9 7.5 %collective-permute-start.48 = (bf16[512,256]{1,0:T(8,128)(2,1)S(1)}, bf16[512,256]{1,0:T(8,128)(2,1)S(1)}, u32[]{:S(2)}, u32[]{:S(2)}) collective-permute-start(bf16[512,256]{1,0:T(8,128)(2,1)S(1)} %copy-done.29), channel_id=1, source_target_pairs={{0,8},{1,9},{2,10},{3,11},{4,12},{5,13},{6,14},{7,15},{8,0},{9,1},... | collective-permute-start | bytes 786440 | tf_op jit(solution)/shard_map/ppermute | solution.py:58
  418.5 15.2 %collective-permute-start.50 = (bf16[1024,768]{1,0:T(8,128)(2,1)}, bf16[1024,768]{1,0:T(8,128)(2,1)S(1)}, u32[]{:S(2)}, u32[]{:S(2)}) collective-permute-start(bf16[1024,768]{1,0:T(8,128)(2,1)} %outer.16), channel_id=1, source_target_pairs={{0,8},{1,9},{2,10},{3,11},{4,12},{5,13},{6,14},{7,15},{8,0},{9,1},... | collective-permute-start | bytes 4718600 | tf_op jit(solution)/shard_map/ppermute | solution.py:58
  440.8 35.4 %collective-permute-start.54 = (bf16[1024,384]{1,0:T(8,128)(2,1)}, bf16[1024,384]{1,0:T(8,128)(2,1)S(1)}, u32[]{:S(2)}, u32[]{:S(2)}) collective-permute-start(bf16[1024,384]{1,0:T(8,128)(2,1)} %first_sums.8), channel_id=1, source_target_pairs={{0,16},{1,17},{2,18},{3,19},{4,20},{5,21},{6,22},{7,23},{8,24},{9,... | collective-permute-start | bytes 2359304 | tf_op jit(solution)/shard_map/ppermute | solution.py:58
  442.0 34.2 %collective-permute-start.51 = (bf16[128,1024]{1,0:T(8,128)(2,1)S(1)}, bf16[128,1024]{1,0:T(8,128)(2,1)S(1)}, u32[]{:S(2)}, u32[]{:S(2)}) collective-permute-start(bf16[128,1024]{1,0:T(8,128)(2,1)S(1)} %copy-done.72), channel_id=1, source_target_pairs={{0,2},{1,3},{2,0},{3,1},{4,6},{5,7},{6,4},{7,5},{8,10},{9,11},{10,... | collective-permute-start | bytes 786440 | tf_op jit(solution)/shard_map/ppermute | solution.py:58
  444.6 31.6 %collective-permute-start.52 = (bf16[128,1024]{1,0:T(8,128)(2,1)S(1)}, bf16[128,1024]{1,0:T(8,128)(2,1)S(1)}, u32[]{:S(2)}, u32[]{:S(2)}) collective-permute-start(bf16[128,1024]{1,0:T(8,128)(2,1)S(1)} %copy-done.71), channel_id=1, source_target_pairs={{0,4},{1,5},{2,6},{3,7},{4,0},{5,1},{6,2},{7,3},{8,12},{9,13},{10,... | collective-permute-start | bytes 786440 | tf_op jit(solution)/shard_map/ppermute | solution.py:58
  444.6 31.6 %collective-permute-start.53 = (bf16[128,1024]{1,0:T(8,128)(2,1)S(1)}, bf16[128,1024]{1,0:T(8,128)(2,1)S(1)}, u32[]{:S(2)}, u32[]{:S(2)}) collective-permute-start(bf16[128,1024]{1,0:T(8,128)(2,1)S(1)} %copy-done.70), channel_id=1, source_target_pairs={{0,6},{1,7},{2,4},{3,5},{4,2},{5,3},{6,0},{7,1},{8,14},{9,15},{10,... | collective-permute-start | bytes 786440 | tf_op jit(solution)/shard_map/ppermute | solution.py:58
  445.8 30.4 %collective-permute-start.55 = (bf16[512,256]{1,0:T(8,128)(2,1)S(1)}, bf16[512,256]{1,0:T(8,128)(2,1)S(1)}, u32[]{:S(2)}, u32[]{:S(2)}) collective-permute-start(bf16[512,256]{1,0:T(8,128)(2,1)S(1)} %copy-done.37), channel_id=1, source_target_pairs={{0,1},{1,0},{2,3},{3,2},{4,5},{5,4},{6,7},{7,6},{8,9},{9,8},{10,11... | collective-permute-start | bytes 786440 | tf_op jit(solution)/shard_map/ppermute | solution.py:58
  484.3 15.8 %collective-permute-start.59 = (bf16[512,384]{1,0:T(8,128)(2,1)}, bf16[512,384]{1,0:T(8,128)(2,1)S(1)}, u32[]{:S(2)}, u32[]{:S(2)}) collective-permute-start(bf16[512,384]{1,0:T(8,128)(2,1)} %second_sums.8), channel_id=1, source_target_pairs={{0,1},{1,0},{2,3},{3,2},{4,5},{5,4},{6,7},{7,6},{8,9},{9,8},{10,11... | collective-permute-start | bytes 1179656 | tf_op jit(solution)/shard_map/ppermute | solution.py:58
  485.4 13.3 %collective-permute-start.56 = (bf16[128,256]{1,0:T(8,128)(2,1)S(1)}, bf16[128,256]{1,0:T(8,128)(2,1)S(1)}, u32[]{:S(2)}, u32[]{:S(2)}) collective-permute-start(bf16[128,256]{1,0:T(8,128)(2,1)S(1)} %copy-done.77), channel_id=1, source_target_pairs={{0,2},{1,3},{2,0},{3,1},{4,6},{5,7},{6,4},{7,5},{8,10},{9,11},{10,... | collective-permute-start | bytes 196616 | tf_op jit(solution)/shard_map/ppermute | solution.py:58
  487.7 11.0 %collective-permute-start.57 = (bf16[128,256]{1,0:T(8,128)(2,1)S(1)}, bf16[128,256]{1,0:T(8,128)(2,1)S(1)}, u32[]{:S(2)}, u32[]{:S(2)}) collective-permute-start(bf16[128,256]{1,0:T(8,128)(2,1)S(1)} %copy-done.76), channel_id=1, source_target_pairs={{0,4},{1,5},{2,6},{3,7},{4,0},{5,1},{6,2},{7,3},{8,12},{9,13},{10,... | collective-permute-start | bytes 196616 | tf_op jit(solution)/shard_map/ppermute | solution.py:58
  487.7 11.0 %collective-permute-start.58 = (bf16[128,256]{1,0:T(8,128)(2,1)S(1)}, bf16[128,256]{1,0:T(8,128)(2,1)S(1)}, u32[]{:S(2)}, u32[]{:S(2)}) collective-permute-start(bf16[128,256]{1,0:T(8,128)(2,1)S(1)} %copy-done.75), channel_id=1, source_target_pairs={{0,6},{1,7},{2,4},{3,5},{4,2},{5,3},{6,0},{7,1},{8,14},{9,15},{10,... | collective-permute-start | bytes 196616 | tf_op jit(solution)/shard_map/ppermute | solution.py:58
  500.0 11.8 %collective-permute-start.60 = (bf16[1024,768]{1,0:T(8,128)(2,1)S(1)}, bf16[1024,768]{1,0:T(8,128)(2,1)S(1)}, u32[]{:S(2)}, u32[]{:S(2)}) collective-permute-start(bf16[1024,768]{1,0:T(8,128)(2,1)S(1)} %copy-done.25), channel_id=1, source_target_pairs={{0,8},{1,9},{2,10},{3,11},{4,12},{5,13},{6,14},{7,15},{8,0},{9,1},... | collective-permute-start | bytes 4718600 | tf_op jit(solution)/shard_map/ppermute | solution.py:58
  502.4 9.4 %collective-permute-start.61 = (bf16[128,1024]{1,0:T(8,128)(2,1)}, bf16[128,1024]{1,0:T(8,128)(2,1)S(1)}, u32[]{:S(2)}, u32[]{:S(2)}) collective-permute-start(bf16[128,1024]{1,0:T(8,128)(2,1)} %last_sums.6.refs_0_), channel_id=1, source_target_pairs={{0,16},{1,17},{2,18},{3,19},{4,20},{5,21},{6,22},{7,23},{8,24},{9,... | collective-permute-start | bytes 786440 | tf_op jit(solution)/shard_map/ppermute | solution.py:58
  519.0 25.2 %collective-permute-start.62 = (bf16[512,768]{1,0:T(8,128)(2,1)}, bf16[512,768]{1,0:T(8,128)(2,1)S(1)}, u32[]{:S(2)}, u32[]{:S(2)}) collective-permute-start(bf16[512,768]{1,0:T(8,128)(2,1)} %first_sums.9), channel_id=1, source_target_pairs={{0,1},{1,0},{2,3},{3,2},{4,5},{5,4},{6,7},{7,6},{8,9},{9,8},{10,11... | collective-permute-start | bytes 2359304 | tf_op jit(solution)/shard_map/ppermute | solution.py:58
  520.2 24.0 %collective-permute-start.63 = (bf16[128,384]{1,0:T(8,128)(2,1)}, bf16[128,384]{1,0:T(8,128)(2,1)S(1)}, u32[]{:S(2)}, u32[]{:S(2)}) collective-permute-start(bf16[128,384]{1,0:T(8,128)(2,1)} %get-tuple-element.323), channel_id=1, source_target_pairs={{0,2},{1,3},{2,0},{3,1},{4,6},{5,7},{6,4},{7,5},{8,10},{9,11},{10,... | collective-permute-start | bytes 294920 | tf_op jit(solution)/shard_map/ppermute | solution.py:58
  522.7 21.4 %collective-permute-start.64 = (bf16[128,384]{1,0:T(8,128)(2,1)S(1)}, bf16[128,384]{1,0:T(8,128)(2,1)S(1)}, u32[]{:S(2)}, u32[]{:S(2)}) collective-permute-start(bf16[128,384]{1,0:T(8,128)(2,1)S(1)} %copy-done.74), channel_id=1, source_target_pairs={{0,4},{1,5},{2,6},{3,7},{4,0},{5,1},{6,2},{7,3},{8,12},{9,13},{10,... | collective-permute-start | bytes 294920 | tf_op jit(solution)/shard_map/ppermute | solution.py:58
  522.7 21.4 %collective-permute-start.65 = (bf16[128,384]{1,0:T(8,128)(2,1)S(1)}, bf16[128,384]{1,0:T(8,128)(2,1)S(1)}, u32[]{:S(2)}, u32[]{:S(2)}) collective-permute-start(bf16[128,384]{1,0:T(8,128)(2,1)S(1)} %copy-done.73), channel_id=1, source_target_pairs={{0,6},{1,7},{2,4},{3,5},{4,2},{5,3},{6,0},{7,1},{8,14},{9,15},{10,... | collective-permute-start | bytes 294920 | tf_op jit(solution)/shard_map/ppermute | solution.py:58
  557.8 8.1 %collective-permute-start.72 = (f32[1,16,128]{2,1,0:T(8,128)S(1)}, f32[1,16,128]{2,1,0:T(8,128)S(1)}, u32[]{:S(2)}, u32[]{:S(2)}) collective-permute-start(f32[1,16,128]{2,1,0:T(8,128)S(1)} %bitcast.133), channel_id=1, source_target_pairs={{0,6},{1,7},{2,4},{3,5},{4,2},{5,3},{6,0},{7,1},{8,14},{9,15},{10,... | collective-permute-start | bytes 24584 | tf_op jit(solution)/shard_map/ppermute | solution.py:58
  557.8 8.1 %collective-permute-start.71 = (f32[1,16,128]{2,1,0:T(8,128)S(1)}, f32[1,16,128]{2,1,0:T(8,128)S(1)}, u32[]{:S(2)}, u32[]{:S(2)}) collective-permute-start(f32[1,16,128]{2,1,0:T(8,128)S(1)} %bitcast.134), channel_id=1, source_target_pairs={{0,4},{1,5},{2,6},{3,7},{4,0},{5,1},{6,2},{7,3},{8,12},{9,13},{10,... | collective-permute-start | bytes 24584 | tf_op jit(solution)/shard_map/ppermute | solution.py:58
  560.6 12.9 %collective-permute-start.84 = (bf16[128,1024]{1,0:T(8,128)(2,1)S(1)}, bf16[128,1024]{1,0:T(8,128)(2,1)}, u32[]{:S(2)}, u32[]{:S(2)}) collective-permute-start(bf16[128,1024]{1,0:T(8,128)(2,1)S(1)} %copy-done.30), channel_id=1, source_target_pairs={{0,8},{1,9},{2,10},{3,11},{4,12},{5,13},{6,14},{7,15},{8,0},{9,1},... | collective-permute-start | bytes 786440 | tf_op jit(solution)/shard_map/ppermute | solution.py:58
  565.8 7.6 %collective-permute-start.85 = (bf16[128,1024]{1,0:T(8,128)(2,1)S(1)}, bf16[128,1024]{1,0:T(8,128)(2,1)}, u32[]{:S(2)}, u32[]{:S(2)}) collective-permute-start(bf16[128,1024]{1,0:T(8,128)(2,1)S(1)} %collective-permute-done.61.refs_1_), channel_id=1, source_target_pairs={{0,8},{1,9},{2,10},{3,11},{4,12},{5,13},{6,14},{7,15},{8,0},{9,1},... | collective-permute-start | bytes 786440 | tf_op jit(solution)/shard_map/ppermute | solution.py:58
  566.0 22.5 %collective-permute-start.73 = (f32[4,1,16,128]{3,2,1,0:T(8,128)S(1)}, f32[4,1,16,128]{3,2,1,0:T(8,128)S(1)}, u32[]{:S(2)}, u32[]{:S(2)}) collective-permute-start(f32[4,1,16,128]{3,2,1,0:T(8,128)S(1)} %get-tuple-element.406), channel_id=1, source_target_pairs={{0,1},{1,0},{2,3},{3,2},{4,5},{5,4},{6,7},{7,6},{8,9},{9,8},{10,11... | collective-permute-start | bytes 98312 | tf_op jit(solution)/shard_map/ppermute | solution.py:58
  580.4 19.8 %collective-permute-start.77 = (bf16[512,384]{1,0:T(8,128)(2,1)}, bf16[512,384]{1,0:T(8,128)(2,1)S(1)}, u32[]{:S(2)}, u32[]{:S(2)}) collective-permute-start(bf16[512,384]{1,0:T(8,128)(2,1)} %second_sums.9), channel_id=1, source_target_pairs={{0,16},{1,17},{2,18},{3,19},{4,20},{5,21},{6,22},{7,23},{8,24},{9,... | collective-permute-start | bytes 1179656 | tf_op jit(solution)/shard_map/ppermute | solution.py:58
  584.3 14.2 %collective-permute-start.76 = (bf16[16,7296]{1,0:T(8,128)(2,1)S(1)}, bf16[16,7296]{1,0:T(8,128)(2,1)S(1)}, u32[]{:S(2)}, u32[]{:S(2)}) collective-permute-start(bf16[16,7296]{1,0:T(8,128)(2,1)S(1)} %reshape.109), channel_id=1, source_target_pairs={{0,24},{1,25},{2,26},{3,27},{4,28},{5,29},{6,30},{7,31},{8,16},{9,... | collective-permute-start | bytes 700424 | tf_op jit(solution)/shard_map/ppermute | solution.py:58
  587.2 12.5 %collective-permute-start.75 = (bf16[16,7296]{1,0:T(8,128)(2,1)S(1)}, bf16[16,7296]{1,0:T(8,128)(2,1)S(1)}, u32[]{:S(2)}, u32[]{:S(2)}) collective-permute-start(bf16[16,7296]{1,0:T(8,128)(2,1)S(1)} %reshape.109), channel_id=1, source_target_pairs={{0,16},{1,17},{2,18},{3,19},{4,20},{5,21},{6,22},{7,23},{8,24},{9,... | collective-permute-start | bytes 700424 | tf_op jit(solution)/shard_map/ppermute | solution.py:58
  588.4 11.3 %collective-permute-start.74 = (bf16[16,7296]{1,0:T(8,128)(2,1)S(1)}, bf16[16,7296]{1,0:T(8,128)(2,1)S(1)}, u32[]{:S(2)}, u32[]{:S(2)}) collective-permute-start(bf16[16,7296]{1,0:T(8,128)(2,1)S(1)} %reshape.109), channel_id=1, source_target_pairs={{0,8},{1,9},{2,10},{3,11},{4,12},{5,13},{6,14},{7,15},{8,0},{9,1},... | collective-permute-start | bytes 700424 | tf_op jit(solution)/shard_map/ppermute | solution.py:58
  606.1 8.4 %collective-permute-start.80 = (bf16[128,384]{1,0:T(8,128)(2,1)}, bf16[128,384]{1,0:T(8,128)(2,1)S(1)}, u32[]{:S(2)}, u32[]{:S(2)}) collective-permute-start(bf16[128,384]{1,0:T(8,128)(2,1)} %get-tuple-element.338), channel_id=1, source_target_pairs={{0,6},{1,7},{2,4},{3,5},{4,2},{5,3},{6,0},{7,1},{8,14},{9,15},{10,... | collective-permute-start | bytes 294920 | tf_op jit(solution)/shard_map/ppermute | solution.py:58
  618.7 9.4 %collective-permute-start.83 = (bf16[128,1024]{1,0:T(8,128)(2,1)S(1)}, bf16[128,1024]{1,0:T(8,128)(2,1)S(1)}, u32[]{:S(2)}, u32[]{:S(2)}) collective-permute-start(bf16[128,1024]{1,0:T(8,128)(2,1)S(1)} %pad_maximum_fusion.5.refs_0_), channel_id=1, source_target_pairs={{0,24},{1,25},{2,26},{3,27},{4,28},{5,29},{6,30},{7,31},{8,16},{9,... | collective-permute-start | bytes 786440 | tf_op jit(solution)/shard_map/ppermute | solution.py:58
  621.4 12.5 %collective-permute-start.81 = (bf16[128,1024]{1,0:T(8,128)(2,1)S(1)}, bf16[128,1024]{1,0:T(8,128)(2,1)S(1)}, u32[]{:S(2)}, u32[]{:S(2)}) collective-permute-start(bf16[128,1024]{1,0:T(8,128)(2,1)S(1)} %pad_maximum_fusion.5.refs_0_), channel_id=1, source_target_pairs={{0,16},{1,17},{2,18},{3,19},{4,20},{5,21},{6,22},{7,23},{8,24},{9,... | collective-permute-start | bytes 786440 | tf_op jit(solution)/shard_map/ppermute | solution.py:58
  (104 other events, 1014.9 us)
Sparse Core Ops, SparseCore 0:
  75.9 86.0 all-gather.1

commit v3 on v2

--- a/solution.py
+++ b/solution.py
@@ -93,8 +93,9 @@
 
 def weight_copies(place_ref, pieces, sources, buffer, sem):
     copies = []
-    if sources is None:
-        return [pltpu.make_async_copy(pieces[0], buffer, sem.at[0])]
+    if len(pieces) == 1:
+        window = pieces[0].at[:, pl.ds(sources, buffer.shape[1])]
+        return [pltpu.make_async_copy(window, buffer, sem.at[0])]
     for column_from, quarter, rows, column_to in sources:
         for number in range(10):
             core, kind = number // 5, number % 5
@@ -120,51 +121,61 @@
     return left.astype(WIDE) + right.astype(WIDE)
 
 
-def add_blocks(place, steps, block, outs, name):
-    arrays, specs, plan = [], [], []
-    for _, _, terms in outs:
-        entry = []
-        for array, where, when in terms:
-            entry.append((len(arrays), when))
-            arrays.append(array)
-            specs.append(pl.BlockSpec(block, functools.partial(lambda where, n, p: where(n, p), where)))
-        plan.append(entry)
+def add_blocks(place, jobs, name):
+    arrays, in_specs, out_specs, out_shapes, plan = [], [], [], [], []
+
+    def block_spec(block, where, steps):
+        return pl.BlockSpec(block, lambda n, p: where(jnp.minimum(n, steps - 1), p))
+
+    for steps, outs in jobs:
+        for blocks, block, where_out, terms in outs:
+            entry = []
+            for array, where, when in terms:
+                entry.append((len(arrays), when))
+                arrays.append(array)
+                in_specs.append(block_spec(block, where, steps))
+            out_specs.append(block_spec(block, where_out, steps))
+            out_shapes.append(jax.ShapeDtypeStruct((blocks[0] * block[0], blocks[1] * block[1]), LOW))
+            plan.append((steps, entry))
 
     def body(place_ref, *refs):
         step = pl.program_id(0)
-        for entry, out_ref in zip(plan, refs[len(arrays) :]):
-            total = None
-            for number, when in entry:
-                value = refs[number][...].astype(WIDE)
-                if when is not None:
-                    value = jnp.where(when(step, place_ref), value, 0.0)
-                total = value if total is None else total + value
-            out_ref[...] = total.astype(LOW)
-
-    return pl.pallas_call(
+        for (steps, entry), out_ref in zip(plan, refs[len(arrays) :]):
+
+            @pl.when(step < steps)
+            def _():
+                total = None
+                for number, when in entry:
+                    value = refs[number][...].astype(WIDE)
+                    if when is not None:
+                        value = jnp.where(when(step, place_ref), value, 0.0)
+                    total = value if total is None else total + value
+                out_ref[...] = total.astype(LOW)
+
+    results = pl.pallas_call(
         body,
         grid_spec=pltpu.PrefetchScalarGridSpec(
             num_scalar_prefetch=1,
-            grid=(steps,),
-            in_specs=specs,
-            out_specs=[
-                pl.BlockSpec(block, functools.partial(lambda where, n, p: where(n, p), where))
-                for _, where, _ in outs
-            ],
+            grid=(max(steps for steps, _ in jobs),),
+            in_specs=in_specs,
+            out_specs=out_specs,
         ),
-        out_shape=[
-            jax.ShapeDtypeStruct((blocks[0] * block[0], blocks[1] * block[1]), LOW) for blocks, _, _ in outs
-        ],
+        out_shape=out_shapes,
         compiler_params=pltpu.CompilerParams(vmem_limit_bytes=VMEM_LIMIT),
         cost_estimate=LIGHT,
         name=name,
     )(place.table, *arrays)
+    grouped, cursor = [], 0
+    for _, outs in jobs:
+        grouped.append(list(results[cursor : cursor + len(outs)]))
+        cursor += len(outs)
+    return grouped
 
 
 class RowSum:
-    def __init__(self, place, keep, arrived, rows, order):
-        self.place, self.base = place, [keep, arrived]
-        self.block = (rows, keep.shape[1] // 2)
+    def __init__(self, keep, arrived, rows, order):
+        self.base = [keep, arrived]
+        self.rows, self.width = rows, keep.shape[1] // 2
         self.streams = (
             [{"z": 0, "count": 2, "order": "yx"}, {"z": 2, "count": 2, "order": "xy"}]
             if order == "mixed"
@@ -172,19 +183,24 @@
         )
 
     def first(self):
-        outs, steps = [], 2 * self.streams[0]["count"]
+        outs = []
         for stream in self.streams:
             start, count = stream["z"], stream["count"]
             if stream["order"] == "yx":
-                where = lambda n, p, start=start: (2 * start + n, 1 - p[0])
-                outs.append(((2 * count, 1), lambda n, p: (n, 0), [(t, where, None) for t in self.base]))
+                block, blocks = (count * self.rows, self.width), (2, 1)
+                where = lambda n, p: (jnp.minimum(n, 1), 1 - p[0])
+                out = lambda n, p: (jnp.minimum(n, 1), 0)
             else:
-                where = lambda n, p, start=start: (2 * (start + n // 2) + 1 - p[3], n % 2)
-                outs.append(((count, 2), lambda n, p: (n // 2, n % 2), [(t, where, None) for t in self.base]))
-        sent = add_blocks(self.place, steps, self.block, outs, "first_sums")
-        return [(v, {"d" + s["order"][0]: 1}) for v, s in zip(sent, self.streams)]
+                block, blocks = (self.rows, 2 * self.width), (count, 1)
+                where = lambda n, p, start=start: (2 * (start + n) + 1 - p[3], 0)
+                out = lambda n, p: (n, 0)
+            outs.append((blocks, block, out, [(t, where, None) for t in self.base]))
+        steps = 2 if self.streams[0]["order"] == "yx" else self.streams[0]["count"]
+        self.axes = [{"d" + stream["order"][0]: 1} for stream in self.streams]
+        return steps, outs
 
     def second(self, arrived):
+        block = (self.rows, self.width)
         outs, steps = [], self.streams[0]["count"]
         for stream, value in zip(self.streams, arrived):
             stream["first"] = value
@@ -195,9 +211,11 @@
             else:
                 where = lambda n, p, start=start: (2 * (start + n) + p[3], 1 - p[0])
                 terms = [(value, lambda n, p: (n, 1 - p[0]), None)]
-            outs.append(((count, 1), lambda n, p: (n, 0), [(t, where, None) for t in self.base] + terms))
-        sent = add_blocks(self.place, steps, self.block, outs, "second_sums")
-        return [(v, {"d" + s["order"][1]: 1}) for v, s in zip(sent, self.streams)]
+            outs.append(
+                ((count, 1), block, lambda n, p: (n, 0), [(t, where, None) for t in self.base] + terms)
+            )
+        self.axes = [{"d" + stream["order"][1]: 1} for stream in self.streams]
+        return steps, outs
 
     def terms(self, flip):
         out = [(t, lambda n, p: (2 * (p[2] ^ flip) + p[3], p[0]), None) for t in self.base]
@@ -217,13 +235,16 @@
     def third(self, arrived):
         for stream, value in zip(self.streams, arrived):
             stream["second"] = value
-        outs = [((1, 1), lambda n, p: (0, 0), self.terms(k)) for k in (1, 2, 3)]
-        sent = add_blocks(self.place, 1, self.block, outs, "third_sums")
-        return [(v, {"dz": k}) for v, k in zip(sent, (1, 2, 3))]
-
-    def finish(self, arrived):
+        self.axes = [{"dz": k} for k in (1, 2, 3)]
+        block = (self.rows, self.width)
+        return 1, [((1, 1), block, lambda n, p: (0, 0), self.terms(k)) for k in (1, 2, 3)]
+
+    def last(self, arrived):
         terms = self.terms(0) + [(v, lambda n, p: (0, 0), None) for v in arrived]
-        return add_blocks(self.place, 1, self.block, [((1, 1), lambda n, p: (0, 0), terms)], "last_sums")[0]
+        return 1, [((1, 1), (self.rows, self.width), lambda n, p: (0, 0), terms)]
+
+    def moves(self, sums):
+        return list(zip(sums, self.axes))
 
 
 def beside(kernel, operand, moves):
@@ -236,22 +257,22 @@
     return (results[0] if len(results) == 1 else results), arrived
 
 
-def lay_out_kernel(layout, place_ref, *refs):
-    quarters, outs = refs[:4], refs[4:]
+def lay_out_kernel(layouts, place_ref, *refs):
+    quarters, outs = refs[: 4 * len(layouts)], refs[4 * len(layouts) :]
     here = place_ref[1] * 2 + place_ref[0]
-    for apart, ref in enumerate(quarters):
-        index = here ^ apart
-        for number, column, width, row, to, stride in layout:
+    for number, ref in enumerate(quarters):
+        index = here ^ (number % 4)
+        for number, column, width, row, to, stride in layouts[number // 4]:
             rows = ref.shape[0]
             start = pl.multiple_of(to + index * stride, 128)
             outs[number][pl.ds(row, rows), pl.ds(start, width)] = ref[:, column : column + width].astype(WIDE)
 
 
-def lay_out(place, quarters, layout, shapes, name):
+def lay_out(place, quarters, layouts, shapes, name):
     vmem = pl.BlockSpec(memory_space=pltpu.VMEM)
     return pl.pallas_call(
-        functools.partial(lay_out_kernel, layout),
-        in_specs=[pl.BlockSpec(memory_space=pltpu.SMEM)] + [vmem] * 4,
+        functools.partial(lay_out_kernel, layouts),
+        in_specs=[pl.BlockSpec(memory_space=pltpu.SMEM)] + [vmem] * len(quarters),
         out_specs=[vmem] * len(shapes),
         out_shape=[jax.ShapeDtypeStruct(shape, WIDE) for shape in shapes],
         compiler_params=pltpu.CompilerParams(vmem_limit_bytes=VMEM_LIMIT),
@@ -490,7 +511,7 @@
         parts.extend(pieces)
         where.append((start, len(pieces), sources))
     shapes = [weight[2] for weight in weights]
-    counts = [1 if sources is None else 32 * len(sources) for _, _, sources in where]
+    counts = [1 if count == 1 else 32 * len(sources) for _, count, sources in where]
     blocked_count, full_count, out_count, weight_count = len(blocked), len(full), len(outs), len(weights)
 
     def body(place_ref, lengths_ref, *refs):
@@ -541,9 +562,9 @@
         + [pl.BlockSpec(v.shape, lambda i: (0, 0)) for v in full]
         + [any_space] * len(parts),
         out_specs=[pl.BlockSpec((block_rows, width), lambda i: (i, 0)) for width, _ in outs]
-        + [pl.BlockSpec((8, 1024), lambda i: (0, 0))] * sums,
+        + [pl.BlockSpec((16, 1024), lambda i: (0, 0))] * sums,
         out_shape=[jax.ShapeDtypeStruct((rows, width), kind) for width, kind in outs]
-        + [jax.ShapeDtypeStruct((8, 1024), WIDE)] * sums,
+        + [jax.ShapeDtypeStruct((16, 1024), WIDE)] * sums,
         scratch_shapes=[pltpu.VMEM(shape, LOW) for shape in shapes]
         + [pltpu.SemaphoreType.DMA((count,)) for count in counts],
         compiler_params=pltpu.CompilerParams(vmem_limit_bytes=VMEM_LIMIT),
@@ -576,81 +597,57 @@
         qkv_ref[:, start + 256 : start + 384] = raw[:, 256:].astype(LOW)
 
 
-def branch_kernel(second, real, tokens, full, ready, outs, sums):
-    attended_ref, x_ref = tokens
-    gamma, scale, shift = full
-    attn_ref, h_ref, act_ref, slope_ref = outs
+def block_kernel(second, real, tokens, full, ready, outs, sums):
+    attended_ref, x_ref, cot_ref = tokens
+    gamma_one_ref, gamma_two_ref, scale_ref, shift_ref = full
+    out_ref, h_ref, act_ref, mlp_grad_ref, hidden_grad_ref, middle_ref, attn_grad_ref, attended_grad_ref = outs
     (sum_ref,) = sums
-    attn = dot(attended_ref[...], ready(0)[...]).astype(LOW)
-    attn_ref[...] = attn
-    branch = jnp.where(real, per_row(gamma, second) * attn.astype(WIDE), 0.0)
-    add_sums(sum_ref, 0, second, branch * branch)
-    unit, _ = normalize(x_ref[...].astype(WIDE) + branch)
-    hidden = (unit * (1.0 + per_row(scale, second)) + per_row(shift, second)).astype(LOW)
+    gate_one, gate_two = per_row(gamma_one_ref, second), per_row(gamma_two_ref, second)
+    scale = 1.0 + per_row(scale_ref, second)
+    upstream = cot_ref[...].astype(WIDE)
+    mlp_grad = jnp.where(real, gate_two * upstream, 0.0).astype(LOW)
+    mlp_grad_ref[...] = mlp_grad
+    proj = ready(0)
+    attn = dot(attended_ref[...], proj[...])
+    branch_one = jnp.where(real, gate_one * attn, 0.0)
+    middle = x_ref[...].astype(WIDE) + branch_one
+    unit, root = normalize(middle)
+    hidden = (unit * scale + per_row(shift_ref, second)).astype(LOW)
     h_ref[...] = hidden
-    width = 512
-    fc1 = ready(1)
+    mlp, grad = 0.0, 0.0
+    width = 1024
+    fc1, fc2 = ready(1), ready(2)
     for start in range(0, fc1.shape[1], width):
         span = slice(start, start + width)
         wide = dot(hidden, fc1[:, span])
+        act_grad = dot(mlp_grad, fc2[span, :], NT)
         square = wide * wide
         lift = 0.5 + 0.5 * jnp.tanh(wide * (GELU_COEF + (GELU_COEF * 0.044715) * square))
-        act_ref[:, span] = (wide * lift).astype(LOW)
+        act = (wide * lift).astype(LOW)
+        act_ref[:, span] = act
         bend = wide * (2.0 * GELU_COEF + (6.0 * 0.044715 * GELU_COEF) * square)
-        slope_ref[:, span] = (lift * (1.0 + bend * (1.0 - lift))).astype(LOW)
-
-
-def stream_kernel(second, real, tokens, full, ready, outs, sums):
-    act_ref, x_ref, attn_ref, cot_ref = tokens
-    gamma_one, gamma_two = full
-    out_ref, grad_ref = outs
-    (sum_ref,) = sums
-    mlp = dot(act_ref[...], ready(0)[...])
-    branch_one = jnp.where(real, per_row(gamma_one, second) * attn_ref[...].astype(WIDE), 0.0)
-    gate = per_row(gamma_two, second)
-    branch_two = jnp.where(real, gate * mlp, 0.0)
-    stream = x_ref[...].astype(WIDE) + branch_one + branch_two
+        hidden_grad = (act_grad * (lift * (1.0 + bend * (1.0 - lift)))).astype(LOW)
+        hidden_grad_ref[:, span] = hidden_grad
+        mlp = mlp + dot(act, fc2[span, :])
+        grad = grad + dot(hidden_grad, fc1[:, span], NT)
+    branch_two = jnp.where(real, gate_two * mlp, 0.0)
+    stream = middle + branch_two
     out_ref[...] = stream.astype(LOW)
-    upstream = cot_ref[...].astype(WIDE)
-    grad_ref[...] = jnp.where(real, gate * upstream, 0.0).astype(LOW)
+    scaled = grad * scale
+    middle_grad = upstream + root * (
+        scaled - jnp.mean(scaled, -1, keepdims=True) - unit * jnp.mean(scaled * unit, -1, keepdims=True)
+    )
+    middle_ref[...] = middle_grad.astype(LOW)
+    attn_grad = jnp.where(real, gate_one * middle_grad, 0.0).astype(LOW)
+    attn_grad_ref[...] = attn_grad
+    attended_grad_ref[...] = dot(attn_grad, proj[...], NT).astype(LOW)
     add_sums(sum_ref, 0, second, jnp.where(real, stream * stream, 0.0))
-    add_sums(sum_ref, 2, second, branch_two * branch_two)
-    add_sums(sum_ref, 4, second, jnp.where(real, mlp * upstream, 0.0))
-
-
-def hidden_back_kernel(second, real, tokens, full, ready, outs, sums):
-    grad_ref, slope_ref = tokens
-    (out_ref,) = outs
-    grad = grad_ref[...]
-    width = 512
-    fc2 = ready(0)
-    for start in range(0, fc2.shape[0], width):
-        span = slice(start, start + width)
-        out_ref[:, span] = (
-            dot(grad, fc2[span, :], NT) * slope_ref[:, span].astype(WIDE)
-        ).astype(LOW)
-
-
-def middle_back_kernel(second, real, tokens, full, ready, outs, sums):
-    grad_ref, x_ref, attn_ref, cot_ref = tokens
-    gamma, scale = full
-    middle_ref, attn_grad_ref, attended_grad_ref = outs
-    (sum_ref,) = sums
-    grad = dot(grad_ref[...], ready(0)[...], NT)
-    attn = attn_ref[...].astype(WIDE)
-    gate = per_row(gamma, second)
-    unit, root = normalize(x_ref[...].astype(WIDE) + jnp.where(real, gate * attn, 0.0))
-    add_sums(sum_ref, 0, second, grad * unit)
-    add_sums(sum_ref, 2, second, grad)
-    scaled = grad * (1.0 + per_row(scale, second))
-    middle = cot_ref[...].astype(WIDE) + root * (
-        scaled - jnp.mean(scaled, -1, keepdims=True) - unit * jnp.mean(scaled * unit, -1, keepdims=True)
-    )
-    middle_ref[...] = middle.astype(LOW)
-    add_sums(sum_ref, 4, second, jnp.where(real, attn * middle, 0.0))
-    attn_grad = jnp.where(real, gate * middle, 0.0).astype(LOW)
-    attn_grad_ref[...] = attn_grad
-    attended_grad_ref[...] = dot(attn_grad, ready(1)[...], NT).astype(LOW)
+    add_sums(sum_ref, 2, second, branch_one * branch_one)
+    add_sums(sum_ref, 4, second, branch_two * branch_two)
+    add_sums(sum_ref, 6, second, jnp.where(real, mlp * upstream, 0.0))
+    add_sums(sum_ref, 8, second, jnp.where(real, attn * middle_grad, 0.0))
+    add_sums(sum_ref, 10, second, grad * unit)
+    add_sums(sum_ref, 12, second, grad)
 
 
 def token_back_kernel(second, real, tokens, full, ready, outs, sums):
@@ -677,10 +674,9 @@
     out_ref[...] = dot(left_ref[...], right_ref[...], TN).astype(LOW)
 
 
-def outer(left, right, half=None):
+def outer(left, right, half):
     count, height = left.shape
-    width = right.shape[1] if half is None else right.shape[1] // 2
-    half = jnp.zeros((1,), jnp.int32) if half is None else half.reshape(1).astype(jnp.int32)
+    width = right.shape[1] // 2
     tall = min(height, 1024)
     wide = min(width, 1024 if width % 1024 == 0 else 768 if width % 768 == 0 else 512)
     steps = width // wide
@@ -699,7 +695,33 @@
         compiler_params=pltpu.CompilerParams(vmem_limit_bytes=VMEM_LIMIT),
         cost_estimate=LIGHT,
         name="outer",
-    )(half, left, right)
+    )(half.reshape(1).astype(jnp.int32), left, right)
+
+
+def outer_pair(left, right, other_left, other_right, half):
+    count, height = left.shape
+    widths = (right.shape[1] // 4, other_right.shape[1] // 4)
+    total = sum(widths)
+    whole = lambda v: pl.BlockSpec(v.shape, lambda j, h: (0, 0))
+    part = lambda width: pl.BlockSpec((count, width), lambda j, h: (0, 2 * h[0] + j))
+
+    def body(half_ref, left_ref, right_ref, other_left_ref, other_right_ref, out_ref):
+        out_ref[:, : widths[0]] = dot(left_ref[...], right_ref[...], TN).astype(LOW)
+        out_ref[:, widths[0] :] = dot(other_left_ref[...], other_right_ref[...], TN).astype(LOW)
+
+    return pl.pallas_call(
+        body,
+        grid_spec=pltpu.PrefetchScalarGridSpec(
+            num_scalar_prefetch=1,
+            grid=(2,),
+            in_specs=[whole(left), part(widths[0]), whole(other_left), part(widths[1])],
+            out_specs=pl.BlockSpec((height, total), lambda j, h: (0, j)),
+        ),
+        out_shape=jax.ShapeDtypeStruct((height, 2 * total), LOW),
+        compiler_params=pltpu.CompilerParams(vmem_limit_bytes=VMEM_LIMIT),
+        cost_estimate=LIGHT,
+        name="outer_pair",
+    )(half.reshape(1).astype(jnp.int32), left, right, other_left, other_right)
 
 
 def plain_sum(place, keep, send):
@@ -753,8 +775,7 @@
         rest.over_z()
         qkv.over_both()
         qkv.over_core_first()
-        out = tie(rest.stack, *qkv.from_both)
-        rest.stack, qkv.from_both = out[0], list(out[1:])
+        rest.stack, *qkv.from_both = tie(rest.stack, *qkv.from_both)
         rest.over_xy()
         qkv_parts = qkv.over_core()
         piece = w_fc2.shape[0] // place.dp_count
@@ -763,10 +784,10 @@
         fc2_full = lax.all_gather(fc2_piece, ("fsdp", "dp"), axis=0, tiled=True)
         quarter = half // 2
         qkv_weight = (qkv_parts, [(0, quarter, unit_rows, 0)], (width, 2 * half))
-        fc2_weight = ([fc2_full], None, (hidden_width, width))
+        fc2_weight = ([fc2_full], 0, (hidden_width, width))
     else:
         qkv_weight, proj_weight, fc1_weight, fc2_weight = (
-            ([lax.all_gather(w, "fsdp", axis=0, tiled=True)], None, (w.shape[0] * place.fsdp_count, w.shape[1]))
+            ([lax.all_gather(w, "fsdp", axis=0, tiled=True)], 0, (w.shape[0] * place.fsdp_count, w.shape[1]))
             for w in (paired, w_proj, w_fc1, w_fc2)
         )
         modulation = lax.psum_scatter(
@@ -790,22 +811,20 @@
     query_mask, key_mask = mask_tables(length)
     attended, extra = attend(projected, query_mask, key_mask)
     if place.grouped:
-        out = tie(attended, *rest.from_both)
-        attended, rest.from_both = out[0], list(out[1:])
+        attended, *rest.from_both = tie(attended, *rest.from_both)
         rest_parts = rest.over_core()
         proj_weight = (rest_parts, [(0, width // 4, unit_rows, 0)], (width, width))
         fc1_weight = (
             rest_parts, [(width // 4, hidden_width // 4, unit_rows, 0)], (width, hidden_width)
         )
     flat_attended = attended.reshape(rows, width)
-    attn, normed_two, act, slope, sum_one = token_call(
-        branch_kernel, place, rows, length, lengths, [flat_attended, tokens],
-        [gamma_one, scale_two, shift_two], [proj_weight, fc1_weight],
-        [(width, LOW), (width, LOW), (hidden_width, LOW), (hidden_width, LOW)], 1, "branch",
-    )
-    result, grad_mlp, sum_two = token_call(
-        stream_kernel, place, rows, length, lengths, [act, tokens, attn, cotangent],
-        [gamma_one, gamma_two], [fc2_weight], [(width, LOW), (width, LOW)], 1, "stream",
+    (
+        result, normed_two, act, grad_mlp, grad_hidden, grad_middle, grad_attn, grad_attended, sum_one,
+    ) = token_call(
+        block_kernel, place, rows, length, lengths, [flat_attended, tokens, cotangent],
+        [gamma_one, gamma_two, scale_two, shift_two], [proj_weight, fc1_weight, fc2_weight],
+        [(width, LOW), (width, LOW), (hidden_width, LOW), (width, LOW), (hidden_width, LOW)]
+        + [(width, LOW)] * 3, 1, "block",
     )
 
     def send_part(left, right):
@@ -813,18 +832,6 @@
 
     def keep_part(left, right):
         return outer(left, right, place.c)
-
-    def hidden_back(grad):
-        return token_call(
-            hidden_back_kernel, place, rows, length, lengths, [grad, slope], [], [fc2_weight],
-            [(hidden_width, LOW)], 0, "hidden_back",
-        )[0]
-
-    def middle_back(grad):
-        return token_call(
-            middle_back_kernel, place, rows, length, lengths, [grad, tokens, attn, cotangent],
-            [gamma_one, scale_two], [fc1_weight, proj_weight], [(width, LOW)] * 3, 1, "middle_back",
-        )
 
     def heads_back(grad, first):
         out, sums = attend_back(
@@ -839,83 +846,88 @@
         )
 
     if place.grouped:
-        fc2_rows = w_fc2.shape[0]
+        quarter = width // 4
         fc2_send = send_part(act, grad_mlp)
         fc2_keep, arrived = beside(lambda g: keep_part(act, g), grad_mlp, [(fc2_send, {"dc": 1})])
-        fc2_sum = RowSum(place, fc2_keep, arrived[0], fc2_rows, "mixed")
-        grad_hidden, arrived = beside(hidden_back, grad_mlp, fc2_sum.first())
-        fc1_send, arrived = beside(lambda g: send_part(normed_two, g), grad_hidden, fc2_sum.second(arrived))
-        fc2_moves = fc2_sum.third(arrived)
-        fc1_keep, arrived = beside(lambda g: keep_part(normed_two, g), grad_hidden, [(fc1_send, {"dc": 1})])
-        fc1_sum = RowSum(place, fc1_keep, arrived[0], unit_rows, "mixed")
-        out, arrived = beside(middle_back, grad_hidden, fc1_sum.first() + fc2_moves)
-        grad_middle, grad_attn, grad_attended, sum_three = out
-        fc2_own = fc2_sum.finish(arrived[2:])
-        fc1_moves = fc1_sum.second(arrived[:2])
-        grad_attn, *tied = tie(grad_attn, fc2_own, *(v for v, _ in fc1_moves))
-        fc2_own, fc1_moves = tied[0], [(v, axes) for v, (_, axes) in zip(tied[1:], fc1_moves)]
-        proj_send = send_part(flat_attended, grad_attn)
-        proj_keep, arrived = beside(lambda g: keep_part(flat_attended, g), grad_attn, [(proj_send, {"dc": 1})])
-        proj_sum = RowSum(place, proj_keep, arrived[0], unit_rows, "yx")
-        out, arrived = beside(
-            lambda g: heads_back(g, 0), grad_attended, fc1_moves + proj_sum.first() + [(fc2_own, {"dy": 1})]
-        )
-        grad_first, heads_first = out
-        fc1_moves = fc1_sum.third(arrived[:2])
-        proj_moves = proj_sum.second(arrived[2:3])
-        fc2_y = arrived[3]
-        first_send, fc2_core = beside(
-            lambda g: send_part(normed_one, g), grad_first, [(fc2_own, {"dc": 1}), (fc2_y, {"dc": 1})]
-        )
-        first_keep, arrived = beside(lambda g: keep_part(normed_one, g), grad_first, [(first_send, {"dc": 1})])
-        first_sum = RowSum(place, first_keep, arrived[0], unit_rows, "yx")
-        out, arrived = beside(
-            lambda g: heads_back(g, pairs // 2), grad_attended, fc1_moves + first_sum.first() + proj_moves
-        )
-        grad_second, heads_second = out
-        fc1_own = fc1_sum.finish(arrived[:3])
-        first_moves = first_sum.second(arrived[3:4])
-        proj_moves = proj_sum.third(arrived[4:])
-        second_send, arrived = beside(
-            lambda g: send_part(normed_one, g), grad_second, proj_moves + first_moves
-        )
-        proj_own = proj_sum.finish(arrived[:3])
-        first_moves = first_sum.third(arrived[3:])
+        fc2 = RowSum(fc2_keep, arrived[0], w_fc2.shape[0], "mixed")
+        (sums,) = add_blocks(place, [fc2.first()], "sums_a")
+
+        (grad_first, heads_first), arrived = beside(
+            lambda g: heads_back(g, 0), grad_attended, fc2.moves(sums)
+        )
+        (sums,) = add_blocks(place, [fc2.second(arrived)], "sums_b")
+
+        first_pair = functools.partial(outer_pair, normed_one, grad_first, flat_attended)
+        first_send, fc2_arrived = beside(
+            lambda g: first_pair(g, 1 - place.c), tie(grad_attn, grad_first)[0], fc2.moves(sums)
+        )
+        first_keep, arrived = beside(lambda g: first_pair(g, place.c), grad_attn, [(first_send, {"dc": 1})])
+        first = RowSum(first_keep, arrived[0], unit_rows, "mixed")
+        first_sums, fc2_sums = add_blocks(place, [first.first(), fc2.third(fc2_arrived)], "sums_c")
+        fc2_moves = fc2.moves(fc2_sums)
+
+        fc1_send, arrived = beside(lambda g: send_part(normed_two, g), grad_hidden, first.moves(first_sums))
+        (first_sums,) = add_blocks(place, [first.second(arrived)], "sums_d")
+        fc1_keep, arrived = beside(
+            lambda g: keep_part(normed_two, g), grad_hidden, [(fc1_send, {"dc": 1})] + first.moves(first_sums)
+        )
+        fc1 = RowSum(fc1_keep, arrived[0], unit_rows, "mixed")
+        fc1_sums, first_sums = add_blocks(place, [fc1.first(), first.third(arrived[1:])], "sums_e")
+        first_moves = first.moves(first_sums)
+
+        (grad_second, heads_second), arrived = beside(
+            lambda g: heads_back(g, pairs // 2), grad_attended, fc1.moves(fc1_sums) + fc2_moves
+        )
+        fc1_sums, (fc2_own,) = add_blocks(
+            place, [fc1.second(arrived[:2]), fc2.last(arrived[2:])], "sums_f"
+        )
+        second_send, fc1_arrived = beside(
+            lambda g: send_part(normed_one, g), grad_second, fc1.moves(fc1_sums)
+        )
         second_keep, arrived = beside(
-            lambda g: keep_part(normed_one, g), grad_second, [(second_send, {"dc": 1}), (fc1_own, {"dy": 1})]
-        )
-        fc1_y = arrived[1]
-        second_sum = RowSum(place, second_keep, arrived[0], unit_rows, "xy")
-        out, arrived = beside(
-            lambda g: token_back(grad_first, g), grad_second, second_sum.first() + first_moves
-        )
-        grad_tokens, sum_four = out
-        second_moves = second_sum.second(arrived[:1])
-        first_own = first_sum.finish(arrived[1:])
-        second_moves = second_sum.third([hop(v, **axes) for v, axes in second_moves])
-        second_own = second_sum.finish([hop(v, **axes) for v, axes in second_moves])
-        quarter = width // 4
+            lambda g: keep_part(normed_one, g), grad_second,
+            [(second_send, {"dc": 1}), (fc2_own, {"dy": 1})] + first_moves,
+        )
+        fc2_y = arrived[1]
+        second = RowSum(second_keep, arrived[0], unit_rows, "mixed")
+        second_sums, fc1_sums, (first_own,) = add_blocks(
+            place, [second.first(), fc1.third(fc1_arrived), first.last(arrived[2:])], "sums_g"
+        )
+        (grad_tokens, sum_four), arrived = beside(
+            lambda g: token_back(grad_first, g), grad_second, second.moves(second_sums) + fc1.moves(fc1_sums)
+        )
+        second_sums, (fc1_own,) = add_blocks(
+            place, [second.second(arrived[:2]), fc1.last(arrived[2:])], "sums_h"
+        )
+        second_moves = second.moves(second_sums)
+        sum_four = tie(sum_four, *second_sums)[0]
+        second_arrived = [hop(v, **axes) for v, axes in second_moves]
+        (second_sums,) = add_blocks(place, [second.third(second_arrived)], "sums_i")
+        fc2_core = [hop(fc2_own, dc=1), hop(fc2_y, dc=1)]
+        others = jnp.concatenate([fc1_own, first_own], 1)
+        others_y = hop(others, dy=1)
+        others_core = [hop(others, dc=1), hop(others_y, dc=1)]
+        ((second_own,),) = add_blocks(
+            place, [second.last([hop(v, **axes) for v, axes in second.moves(second_sums)])], "sums_j"
+        )
+        second_all = spread(second_own)
         (grad_fc2,) = lay_out(
-            place, [fc2_own, fc2_y] + fc2_core, [(0, 0, quarter, 0, 0, quarter)], [w_fc2.shape], "lay_out_fc2"
-        )
-        (grad_fc1,) = lay_out(
-            place, [fc1_own, fc1_y, hop(fc1_own, dc=1), hop(fc1_y, dc=1)],
-            [(0, 0, hidden_width // 4, 0, 0, hidden_width // 4)], [w_fc1.shape], "lay_out_fc1",
-        )
-        late = spread(jnp.concatenate([first_own, second_own, proj_own], 1))
-        layout = [
-            (0, 384 * side + 128 * n, 128, 0, n * width + 512 * side, 128) for side in range(2) for n in range(3)
-        ]
-        layout.append((1, 768, quarter, 0, 0, quarter))
-        grad_qkv, grad_proj = lay_out(place, late, layout, [w_qkv.shape, w_proj.shape], "lay_out_late")
+            place, [fc2_own, fc2_y] + fc2_core, [[(0, 0, quarter, 0, 0, quarter)]], [w_fc2.shape], "lay_out_fc2"
+        )
+        wide = hidden_width // 4
+        layout = [(0, 0, wide, 0, 0, wide), (1, wide + 384, quarter, 0, 0, quarter)]
+        layout += [(2, wide + 128 * n, 128, 0, n * width, 128) for n in range(3)]
+        layout_two = [(2, 128 * n, 128, 0, n * width + 512, 128) for n in range(3)]
+        grad_fc1, grad_proj, grad_qkv = lay_out(
+            place, [others, others_y] + others_core + second_all, [layout, layout_two],
+            [w_fc1.shape, w_proj.shape, w_qkv.shape], "lay_out_others",
+        )
     else:
         def whole_sum(left, right):
             return plain_sum(place, keep_part(left, right), send_part(left, right))
 
         grad_fc2 = whole_sum(act, grad_mlp)
-        grad_hidden = hidden_back(grad_mlp)
         grad_fc1 = whole_sum(normed_two, grad_hidden)
-        grad_middle, grad_attn, grad_attended, sum_three = middle_back(grad_hidden)
         grad_proj = whole_sum(flat_attended, grad_attn)
         grad_first, heads_first = heads_back(grad_attended, 0)
         grad_second, heads_second = heads_back(grad_attended, pairs // 2)
@@ -927,7 +939,7 @@
     head_terms = jnp.concatenate([heads_first, heads_second], 2).reshape(items, heads, width // heads).sum(2)
     head_parts = jnp.concatenate([*two_parts(head_terms), jnp.zeros((items, 128 - 2 * heads), LOW)], 1)
     grad_modulation = jnp.concatenate(
-        [sum_three[4:6], sum_two[4:6], sum_four[0:2], sum_three[0:2], sum_four[2:4], sum_three[2:4]], 1
+        [sum_one[8:10], sum_one[6:8], sum_four[0:2], sum_one[10:12], sum_four[2:4], sum_one[12:14]], 1
     ).astype(LOW)
     group = gather_small(place, jnp.concatenate([grad_modulation, head_parts, silu_cond], 1), False)
     grad_columns = dot(group[:, : 6 * width], w_ada, NT)
@@ -948,7 +960,7 @@
 
     counted = (lengths * width).astype(WIDE)
     squares = jnp.stack(
-        [sum_two[0:2].sum(1), sum_one[0:2].sum(1), sum_two[2:4].sum(1)], 1
+        [sum_one[0:2].sum(1), sum_one[2:4].sum(1), sum_one[4:6].sum(1)], 1
     )
     rms_rows = jnp.sqrt(squares / counted[:, None] + EPS)
     return (

time: 652 us -> 584 us (0.90)
  Pallas kernels: 413 us -> 339 us
  waiting for transfers between devices: 78.1 us -> 89.4 us
  starting transfers between devices: 97.1 us -> 87.9 us
    pallas_call x6 -> x3, Pallas kernels: 161 us -> 125 us  [token_call(): pl.pallas_call(body, grid=(grid,), in_specs=[smem, smem] + [pl.BlockSpec(...]
    pallas_call x20 -> x10, Pallas kernels: 78.5 us -> 45.7 us  [add_blocks(): pl.pallas_call(body, grid_spec=pltpu.PrefetchScalarGridSpec(num_scalar_pr...]
    pallas_call x10 -> x6, Pallas kernels: 78.9 us -> 56.2 us  [outer(): pl.pallas_call(outer_kernel, grid_spec=pltpu.PrefetchScalarGridSpec(num_s...]
    pallas_call x3 -> x4, Pallas kernels: 8.08 us -> 25.5 us  [the longest x2 19 us: outer_pair(): pl.pallas_call(body, grid_spec=pltpu.PrefetchScalarGridSpec(num_scalar_pr...]
    ppermute x86 -> x84, starting transfers between devices: 97.1 us -> 87.9 us  [hop(): return lax.ppermute(values, AXES, pairs)]
    all_gather x1, waiting for transfers between devices: 0.02 us -> 8.47 us  [shards(): fc2_full = lax.all_gather(fc2_piece, ('fsdp', 'dp'), axis=0, tiled=True)]
    unnamed x185 -> x156, local copies, waits for them, and re-layouts: 17.4 us -> 20.5 us
    ppermute x86 -> x84, waiting for transfers between devices: 78.1 us -> 80.9 us  [hop(): return lax.ppermute(values, AXES, pairs)]
  transfers between devices with their start and end apart: 87 -> 85, of which waited for: 24 -> 23; matrix products, arithmetic and copies ran while one was open for 3% -> 4% of each run, Pallas kernels for 49% -> 36%
where the time goes in v3:
time: 584 us; the launch traced here: 572 us
  Pallas kernels  339 us (58%)
  waiting for transfers between devices  89.4 us (15%)
  starting transfers between devices  87.9 us (15%)
  local copies, waits for them, and re-layouts  29 us (5%)
  between operations  15.8 us (3%)
  other arithmetic  8.73 us (1%)
    pallas_call x3, Pallas kernels, token_call(): pl.pallas_call(body, grid=(grid,), in_specs=[smem, smem] + [pl.BlockSpec(...  125 us
    ppermute x84, starting transfers between devices, hop(): return lax.ppermute(values, AXES, pairs)  87.9 us
    ppermute x84, waiting for transfers between devices, hop(): return lax.ppermute(values, AXES, pairs)  80.9 us
    pallas_call x2, Pallas kernels, attend_back(): pl.pallas_call(attend_back_kernel, grid=(items, pairs), in_specs=[pl.Bloc...  59.8 us
    pallas_call x6, Pallas kernels, outer(): pl.pallas_call(outer_kernel, grid_spec=pltpu.PrefetchScalarGridSpec(num_s...  56.2 us
    pallas_call x10, Pallas kernels, add_blocks(): pl.pallas_call(body, grid_spec=pltpu.PrefetchScalarGridSpec(num_scalar_pr...  45.7 us
    pallas_call x1, Pallas kernels, attend(): pl.pallas_call(attend_kernel, grid=(items, pairs), in_specs=[pl.BlockSpec...  25.8 us
    unnamed x156, local copies, waits for them, and re-layouts  20.5 us
  transfers between devices with their start and end apart: 85, of which 23 were waited for; matrix products, arithmetic and copies ran while one was open for 4% of the time, Pallas kernels for 36%

profile of v3, /device:TPU:9, one launch (start us, length us, event | category | flops | bytes accessed | tf_op | source)
XLA Modules:
  0.0 572.5 jit_solution(15562878379511788560)
XLA Ops:
  9.4 2.2 collective-permute-start
  12.4 1.5 copy.38
  17.4 1.6 collective-permute-start.4
  22.1 4.5 collective-permute-done.4
  27.3 8.4 %collective-permute-done.5 = bf16[128,768]{1,0:T(8,128)(2,1)} collective-permute-done((bf16[128,768]{1,0:T(8,128)(2,1)S(1)}, bf16[128,768]{1,0:T(8,128)(2,1)}, u32[]{:S(2)}, u32[]{:S(2)}) %collective-permute-start.5) | collective-permute-done | bytes 196640 | tf_op jit(solution)/shard_map/ppermute | solution.py:58
  36.9 2.0 collective-permute-start.10
  42.8 2.5 collective-permute-start.11
  46.5 8.9 %collective-permute-done.14.refs_5_.refs_6_ = bf16[512,768]{1,0:T(8,128)(2,1)S(1)} collective-permute-done((bf16[512,768]{1,0:T(8,128)(2,1)S(1)}, bf16[512,768]{1,0:T(8,128)(2,1)S(1)}, u32[]{:S(2)}, u32[]{:S(2)}) %collective-permute-start.14) | collective-permute-done | bytes 786464 | tf_op jit(solution)/shard_map/ppermute | solution.py:58
  57.6 15.7 %collective-permute-done.13 = bf16[128,1280]{1,0:T(8,128)(2,1)S(1)} collective-permute-done((bf16[128,1280]{1,0:T(8,128)(2,1)S(1)}, bf16[128,1280]{1,0:T(8,128)(2,1)S(1)}, u32[]{:S(2)}, u32[]{:S(2)}) %collective-permute-start.13) | collective-permute-done | bytes 327712 | tf_op jit(solution)/shard_map/ppermute | solution.py:58
  74.4 3.0 collective-permute-start.24
  77.4 1.7 constant_dynamic-slice_fusion.13
  82.2 1.7 collective-permute-done.20.refs_9_.refs_10_
  87.0 23.2 %project.1 = (bf16[1360,1024]{1,0:T(8,128)(2,1)}, bf16[1360,3072]{1,0:T(8,128)(2,1)}, bf16[1360,1024]{1,0:T(8,128)(2,1)}) custom-call(s32[4]{0:T(128)} %pad_add_fusion.place_ref, s32[2]{0:T(128)} %fusion.19.lengths_ref, bf16[1360,1024]{1,0:T(8,128)(2,1)} %refs_2_.3, f32[2,1024]{1,0:T(2,128)} %get-tuple-element.371.refs_1_.refs_4_, ...), custom_call_target="tpu_custom_call" | custom-call | flops 1024 | bytes 1024 | tf_op jit(solution)/shard_map/project/pallas_call | solution.py:557
  110.2 4.3 collective-permute-done.18.refs_8_.refs_18_
  115.7 1.6 collective-permute-start.25
  119.7 2.2 collective-permute-start.27
  122.4 25.8 %attend.1 = (bf16[2,680,1024]{2,1,0:T(8,128)(2,1)}, bf16[2,680,1024]{2,1,0:T(8,128)(2,1)}) custom-call(bf16[2,680,3072]{2,1,0:T(8,128)(2,1)} %bitcast.76, bf16[680,128]{1,0:T(8,128)(2,1)} %constant.112.clone.qm_ref, bf16[680,128]{1,0:T(8,128)(2,1)} %constant.113.clone.km_ref), custom_call_target="tpu_custom_call" | custom-call | flops 1024 | bytes 1024 | tf_op jit(solution)/shard_map/attend/pallas_call | solution.py:380
  148.8 1.9 collective-permute-done.30.refs_15_.refs_25_
  151.7 8.5 %all-gather.2.cloned.1.call-done.refs_27_ = bf16[4096,1024]{1,0:T(8,128)(2,1)} async-done(((bf16[128,1024]{1,0:T(8,128)(2,1)}), bf16[4096,1024]{1,0:T(8,128)(2,1)}) %all-gather.2.cloned.1.call-update) | async-done | bytes 8388624 | tf_op jit(solution)/shard_map/all_gather | solution.py:784
  160.2 82.1 %block.1 = (bf16[1360,1024]{1,0:T(8,128)(2,1)}, bf16[1360,1024]{1,0:T(8,128)(2,1)}, bf16[1360,4096]{1,0:T(8,128)(2,1)}, bf16[1360,1024]{1,0:T(8,128)(2,1)}, bf16...) custom-call(s32[4]{0:T(128)} %pad_add_fusion.place_ref, ...), custom_call_target="tpu_custom_call" | custom-call | flops 1024 | bytes 1024 | tf_op jit(solution)/shard_map/block/pallas_call | solution.py:557
  242.3 11.0 %outer.6 = bf16[4096,512]{1,0:T(8,128)(2,1)} custom-call(s32[1]{0:T(128)} %bitcast.22.half_ref, bf16[1360,4096]{1,0:T(8,128)(2,1)} %get-tuple-element.184.left_ref, bf16[1360,1024]{1,0:T(8,128)(2,1)} %get-tuple-element.186.right_ref), custom_call_target="tpu_custom_call" | custom-call | flops 1024 | bytes 1024 | tf_op jit(solution)/shard_map/outer/pallas_call | solution.py:683
  253.6 10.9 %outer.7.refs_0_.refs_2_.refs_3_.refs_4_.refs_10_.refs_16_.refs_6_ = bf16[4096,512]{1,0:T(8,128)(2,1)} custom-call(s32[1]{0:T(128)} %bitcast.1.half_ref, bf16[1360,4096]{1,0:T(8,128)(2,1)} %get-tuple-element.184.left_ref, bf16[1360,1024]{1,0:T(8,128)(2,1)} %get-tuple-element.186.right_ref), custom_call_target="tpu_custom_call" | custom-call | flops 1024 | bytes 1024 | tf_op jit(solution)/shard_map/outer/pallas_call | solution.py:683
  264.5 2.0 copy-done.1
  266.4 4.1 sums_a.1
  272.0 29.8 %attend_back.2 = (bf16[2,680,1536]{2,1,0:T(8,128)(2,1)}, f32[2,1,512]{2,1,0:T(1,128)}) custom-call(bf16[2,680,3072]{2,1,0:T(8,128)(2,1)} %bitcast.77, bf16[2,680,1024]{2,1,0:T(8,128)(2,1)} %get-tuple-element.182.extra_ref, bf16[680,128]{1,0:T(8,128)(2,1)} %constant.113.clone.km_ref, bf16[2,680,1024]{2,1,0:T(8,128)(2,1)} %get-tuple-element.177.out_ref, ...), custom_call_target="tpu_custom_call" | custom-call | flops 1024 | bytes 1024 | tf_op jit(solution)/shard_map/attend_back/pallas_call | solution.py:459
  303.1 3.5 sums_b.1
  308.1 9.5 %outer_pair.2 = bf16[1024,1280]{1,0:T(8,128)(2,1)} custom-call(s32[1]{0:T(128)} %bitcast.22.half_ref, bf16[1360,1024]{1,0:T(8,128)(2,1)} %get-tuple-element.201.left_ref, bf16[1360,1536]{1,0:T(8,128)(2,1)} %bitcast.85, bf16[1360,1024]{1,0:T(8,128)(2,1)} %bitcast.80, bf16[1360,1024]{1,0:T(8,128)(2,1)} %get-tuple-element.212.other_right_ref), custom_call_target="tpu_custom_call" | custom-call | flops 1024 | bytes 1024 | tf_op jit(solution)/shard_map/outer_pair/pallas_call | solution.py:712
  317.6 1.9 collective-permute-done.35.refs_7_.refs_13_.refs_19_.refs_9_
  320.3 2.0 collective-permute-start.37
  322.3 9.5 %outer_pair.3.refs_0_.refs_2_.refs_3_.refs_4_.refs_10_.refs_16_.refs_22_ = bf16[1024,1280]{1,0:T(8,128)(2,1)} custom-call(s32[1]{0:T(128)} %bitcast.1.half_ref, bf16[1360,1024]{1,0:T(8,128)(2,1)} %get-tuple-element.201.left_ref, bf16[1360,1536]{1,0:T(8,128)(2,1)} %bitcast.86, bf16[1360,1024]{1,0:T(8,128)(2,1)} %bitcast.81, ...), custom_call_target="tpu_custom_call" | custom-call | flops 1024 | bytes 1024 | tf_op jit(solution)/shard_map/outer_pair/pallas_call | solution.py:712
  333.4 6.7 %sums_c.1 = (bf16[512,640]{1,0:T(8,128)(2,1)}, bf16[256,1280]{1,0:T(8,128)(2,1)}, bf16[512,256]{1,0:T(8,128)(2,1)}, bf16[512,256]{1,0:T(8,128)(2,1)}, bf16[512,256]{1,0:T(8,128)(2,1)}) custom-call(s32[4]{0:T(128)} %pad_add_fusion.place_ref, bf16[1024,1280]{1,0:T(8,128)(2,1)} %outer_pair.3.refs_0_.refs_2_.refs_3_.refs_4_.refs_10_.refs_16_.refs_22_, ...), custom_call_target="tpu_custom_call" | custom-call | flops 1024 | bytes 1024 | tf_op jit(solution)/shard_map/sums_c/pallas_call | solution.py:155
  341.4 11.0 %outer.8 = bf16[1024,2048]{1,0:T(8,128)(2,1)} custom-call(s32[1]{0:T(128)} %bitcast.22.half_ref, bf16[1360,1024]{1,0:T(8,128)(2,1)} %get-tuple-element.199.left_ref, bf16[1360,4096]{1,0:T(8,128)(2,1)} %get-tuple-element.228.right_ref), custom_call_target="tpu_custom_call" | custom-call | flops 1024 | bytes 1024 | tf_op jit(solution)/shard_map/outer/pallas_call | solution.py:683
  352.4 4.1 collective-permute-done.38.refs_2_.refs_6_.refs_12_.refs_18_.refs_24_
  358.2 3.1 sums_d.1
  363.6 10.9 %outer.9.refs_0_.refs_2_.refs_3_.refs_4_.refs_10_.refs_16_.refs_6_ = bf16[1024,2048]{1,0:T(8,128)(2,1)} custom-call(s32[1]{0:T(128)} %bitcast.1.half_ref, bf16[1360,1024]{1,0:T(8,128)(2,1)} %get-tuple-element.199.left_ref, bf16[1360,4096]{1,0:T(8,128)(2,1)} %get-tuple-element.228.right_ref), custom_call_target="tpu_custom_call" | custom-call | flops 1024 | bytes 1024 | tf_op jit(solution)/shard_map/outer/pallas_call | solution.py:683
  375.4 2.0 copy-done.2
  377.4 6.2 %sums_e.1 = (bf16[512,1024]{1,0:T(8,128)(2,1)}, bf16[256,2048]{1,0:T(8,128)(2,1)}, bf16[128,640]{1,0:T(8,128)(2,1)}, bf16[128,640]{1,0:T(8,128)(2,1)}, bf16[128,640]{1,0:T(8,128)(2,1)}) custom-call(s32[4]{0:T(128)} %pad_add_fusion.place_ref, bf16[1024,2048]{1,0:T(8,128)(2,1)} %outer.9.refs_0_.refs_2_.refs_3_.refs_4_.refs_10_.refs_16_.refs_6_, ...), custom_call_target="tpu_custom_call" | custom-call | flops 1024 | bytes 1024 | tf_op jit(solution)/shard_map/sums_e/pallas_call | solution.py:155
  385.3 2.4 collective-permute-start.45
  389.0 30.0 %attend_back.3 = (bf16[2,680,1536]{2,1,0:T(8,128)(2,1)}, f32[2,1,512]{2,1,0:T(1,128)}) custom-call(bf16[2,680,3072]{2,1,0:T(8,128)(2,1)} %bitcast.78, bf16[2,680,1024]{2,1,0:T(8,128)(2,1)} %get-tuple-element.182.extra_ref, bf16[680,128]{1,0:T(8,128)(2,1)} %constant.113.clone.km_ref, bf16[2,680,1024]{2,1,0:T(8,128)(2,1)} %get-tuple-element.177.out_ref, ...), custom_call_target="tpu_custom_call" | custom-call | flops 1024 | bytes 1024 | tf_op jit(solution)/shard_map/attend_back/pallas_call | solution.py:459
  420.5 5.0 sums_f.1
  427.6 6.3 %outer.10 = bf16[1024,768]{1,0:T(8,128)(2,1)} custom-call(s32[1]{0:T(128)} %bitcast.22.half_ref, bf16[1360,1024]{1,0:T(8,128)(2,1)} %get-tuple-element.201.left_ref, bf16[1360,1536]{1,0:T(8,128)(2,1)} %bitcast.82), custom_call_target="tpu_custom_call" | custom-call | flops 1024 | bytes 1024 | tf_op jit(solution)/shard_map/outer/pallas_call | solution.py:683
  433.9 3.6 collective-permute-done.48.refs_7_.refs_13_.refs_19_.refs_9_
  438.5 2.9 collective-permute-start.50
  442.2 2.3 collective-permute-start.52
  445.7 6.3 %outer.11.refs_0_.refs_2_.refs_3_.refs_6_.refs_12_ = bf16[1024,768]{1,0:T(8,128)(2,1)} custom-call(s32[1]{0:T(128)} %bitcast.1.half_ref, bf16[1360,1024]{1,0:T(8,128)(2,1)} %get-tuple-element.201.left_ref, bf16[1360,1536]{1,0:T(8,128)(2,1)} %bitcast.83), custom_call_target="tpu_custom_call" | custom-call | flops 1024 | bytes 1024 | tf_op jit(solution)/shard_map/outer/pallas_call | solution.py:683
  452.1 8.2 %collective-permute-done.54.refs_30_ = bf16[128,640]{1,0:T(8,128)(2,1)S(1)} collective-permute-done((bf16[128,640]{1,0:T(8,128)(2,1)S(1)}, bf16[128,640]{1,0:T(8,128)(2,1)S(1)}, u32[]{:S(2)}, u32[]{:S(2)}) %collective-permute-start.54) | collective-permute-done | bytes 163872 | tf_op jit(solution)/shard_map/ppermute | solution.py:58
  462.1 6.8 %sums_g.1 = (bf16[512,384]{1,0:T(8,128)(2,1)}, bf16[256,768]{1,0:T(8,128)(2,1)}, bf16[128,1024]{1,0:T(8,128)(2,1)}, bf16[128,1024]{1,0:T(8,128)(2,1)}, bf16[128,...) custom-call(s32[4]{0:T(128)} %pad_add_fusion.place_ref, bf16[1024,768]{1,0:T(8,128)(2,1)} %outer.11.refs_0_.refs_2_.refs_3_.refs_6_.refs_12_, ...), custom_call_target="tpu_custom_call" | custom-call | flops 1024 | bytes 1024 | tf_op jit(solution)/shard_map/sums_g/pallas_call | solution.py:155
  473.1 20.1 %token_back.1 = (bf16[1360,1024]{1,0:T(8,128)(2,1)}, f32[16,1024]{1,0:T(8,128)}) custom-call(s32[4]{0:T(128)} %pad_add_fusion.place_ref, s32[2]{0:T(128)} %fusion.19.lengths_ref, bf16[1360,1536]{1,0:T(8,128)(2,1)} %bitcast.87, bf16[1360,1536]{1,0:T(8,128)(2,1)} %bitcast.84, bf16[1360,1024]{1,0:T(8,128)(2,1)} %refs_2_.3, ...), custom_call_target="tpu_custom_call" | custom-call | flops 1024 | bytes 1024 | tf_op jit(solution)/shard_map/token_back/pallas_call | solution.py:557
  493.2 2.6 collective-permute-start.82
  497.0 4.5 sums_h.1
  505.1 2.7 lay_out_fc2.1
  510.4 4.5 collective-permute-done.63
  516.4 2.3 collective-permute-start.64
  519.9 2.2 collective-permute-done.65
  523.3 3.9 collective-permute-start.68
  528.1 2.1 collective-permute-start.70
  531.8 3.1 sums_i.1
  534.9 2.5 collective-permute-start.76
  538.5 3.3 collective-permute-done.76.refs_6_
  544.4 1.7 collective-permute-done.78.refs_8_
  547.2 2.7 sums_j.1.refs_4_
  554.6 2.2 collective-permute-start.73
  556.8 2.3 fusion
  561.3 3.9 lay_out_others.1
  (355 shorter events, 85.1 us)
Async XLA Ops:
  7.2 153.0 %all-gather.2.cloned.1.call-start = ((), (), s32[]{:S(2)}) async-start(), calls=%async_computation | async-start | bytes 8650752 | tf_op jit(solution)/shard_map/all_gather | solution.py:784
  8.1 6.1 %collective-permute-start.2 = (bf16[2,1024]{1,0:T(2,128)(2,1)S(1)}, bf16[2,1024]{1,0:T(2,128)(2,1)S(1)}, u32[]{:S(2)}, u32[]{:S(2)}) collective-permute-start(bf16[2,1024]{1,0:T(2,128)(2,1)S(1)} %fusion.12), channel_id=1, source_target_pairs={{0,6},{1,7},{2,4},{3,5},{4,2},{5,3},{6,0},{7,1},{8,14},{9,15},{10,... | collective-permute-start | bytes 12296 | tf_op jit(solution)/shard_map/ppermute | solution.py:58
  17.4 9.2 %collective-permute-start.4 = (bf16[128,768]{1,0:T(8,128)(2,1)S(1)}, bf16[128,768]{1,0:T(8,128)(2,1)S(1)}, u32[]{:S(2)}, u32[]{:S(2)}) collective-permute-start(bf16[128,768]{1,0:T(8,128)(2,1)S(1)} %copy.46), channel_id=1, source_target_pairs={{0,4},{1,5},{2,6},{3,7},{4,0},{5,1},{6,2},{7,3},{8,12},{9,13},{10,... | collective-permute-start | bytes 589832 | tf_op jit(solution)/shard_map/ppermute | solution.py:58
  19.1 16.6 %collective-permute-start.5 = (bf16[128,768]{1,0:T(8,128)(2,1)S(1)}, bf16[128,768]{1,0:T(8,128)(2,1)}, u32[]{:S(2)}, u32[]{:S(2)}) collective-permute-start(bf16[128,768]{1,0:T(8,128)(2,1)S(1)} %copy.46), channel_id=1, source_target_pairs={{0,6},{1,7},{2,4},{3,5},{4,2},{5,3},{6,0},{7,1},{8,14},{9,15},{10,... | collective-permute-start | bytes 589832 | tf_op jit(solution)/shard_map/ppermute | solution.py:58
  21.0 15.8 %collective-permute-start.7 = (f32[4,2,6144]{2,1,0:T(2,128)S(1)}, f32[4,2,6144]{2,1,0:T(2,128)S(1)}, u32[]{:S(2)}, u32[]{:S(2)}) collective-permute-start(f32[4,2,6144]{2,1,0:T(2,128)S(1)} %dynamic-slice_bitcast_fusion), channel_id=1, source_target_pairs={{0,1},{1,0},{2,3},{3,2},{4,5},{5,4},{6,7},{7,6},{8,9},{9,8},{10,11... | collective-permute-start | bytes 589832 | tf_op jit(solution)/shard_map/ppermute | solution.py:58
  40.2 15.2 %collective-permute-start.14 = (bf16[512,768]{1,0:T(8,128)(2,1)S(1)}, bf16[512,768]{1,0:T(8,128)(2,1)S(1)}, u32[]{:S(2)}, u32[]{:S(2)}) collective-permute-start(bf16[512,768]{1,0:T(8,128)(2,1)S(1)} %pad_maximum_fusion.3.refs_4_.refs_5_), channel_id=1, source_target_pairs={{0,1},{1,0},{2,3},{3,2},{4,5},{5,4},{6,7},{7,6},{8,9},{9,8},{10,11... | collective-permute-start | bytes 2359304 | tf_op jit(solution)/shard_map/ppermute | solution.py:58
  40.5 16.2 %collective-permute-start.16 = (bf16[512,768]{1,0:T(8,128)(2,1)S(1)}, bf16[512,768]{1,0:T(8,128)(2,1)S(1)}, u32[]{:S(2)}, u32[]{:S(2)}) collective-permute-start(bf16[512,768]{1,0:T(8,128)(2,1)S(1)} %pad_maximum_fusion.3.refs_4_.refs_5_), channel_id=1, source_target_pairs={{0,16},{1,17},{2,18},{3,19},{4,20},{5,21},{6,22},{7,23},{8,24},{9,... | collective-permute-start | bytes 2359304 | tf_op jit(solution)/shard_map/ppermute | solution.py:58
  42.8 14.4 %collective-permute-start.11 = (bf16[128,1280]{1,0:T(8,128)(2,1)S(1)}, bf16[128,1280]{1,0:T(8,128)(2,1)S(1)}, u32[]{:S(2)}, u32[]{:S(2)}) collective-permute-start(bf16[128,1280]{1,0:T(8,128)(2,1)S(1)} %pad_maximum_fusion.4), channel_id=1, source_target_pairs={{0,2},{1,3},{2,0},{3,1},{4,6},{5,7},{6,4},{7,5},{8,10},{9,11},{10,... | collective-permute-start | bytes 983048 | tf_op jit(solution)/shard_map/ppermute | solution.py:58
  45.2 11.9 %collective-permute-start.12 = (bf16[128,1280]{1,0:T(8,128)(2,1)S(1)}, bf16[128,1280]{1,0:T(8,128)(2,1)S(1)}, u32[]{:S(2)}, u32[]{:S(2)}) collective-permute-start(bf16[128,1280]{1,0:T(8,128)(2,1)S(1)} %pad_maximum_fusion.4), channel_id=1, source_target_pairs={{0,4},{1,5},{2,6},{3,7},{4,0},{5,1},{6,2},{7,3},{8,12},{9,13},{10,... | collective-permute-start | bytes 983048 | tf_op jit(solution)/shard_map/ppermute | solution.py:58
  45.2 28.1 %collective-permute-start.13 = (bf16[128,1280]{1,0:T(8,128)(2,1)S(1)}, bf16[128,1280]{1,0:T(8,128)(2,1)S(1)}, u32[]{:S(2)}, u32[]{:S(2)}) collective-permute-start(bf16[128,1280]{1,0:T(8,128)(2,1)S(1)} %pad_maximum_fusion.4), channel_id=1, source_target_pairs={{0,6},{1,7},{2,4},{3,5},{4,2},{5,3},{6,0},{7,1},{8,14},{9,15},{10,... | collective-permute-start | bytes 983048 | tf_op jit(solution)/shard_map/ppermute | solution.py:58
  55.5 19.0 %collective-permute-start.15 = (bf16[256,768]{1,0:T(8,128)(2,1)S(1)}, bf16[256,768]{1,0:T(8,128)(2,1)S(1)}, u32[]{:S(2)}, u32[]{:S(2)}) collective-permute-start(bf16[256,768]{1,0:T(8,128)(2,1)S(1)} %slice.102), channel_id=1, source_target_pairs={{0,16},{1,17},{2,18},{3,19},{4,20},{5,21},{6,22},{7,23},{8,24},{9,... | collective-permute-start | bytes 1179656 | tf_op jit(solution)/shard_map/ppermute | solution.py:58
  56.8 17.6 %collective-permute-start.17 = (bf16[256,768]{1,0:T(8,128)(2,1)S(1)}, bf16[256,768]{1,0:T(8,128)(2,1)}, u32[]{:S(2)}, u32[]{:S(2)}) collective-permute-start(bf16[256,768]{1,0:T(8,128)(2,1)S(1)} %slice.103), channel_id=1, source_target_pairs={{0,1},{1,0},{2,3},{3,2},{4,5},{5,4},{6,7},{7,6},{8,9},{9,8},{10,11... | collective-permute-start | bytes 1179656 | tf_op jit(solution)/shard_map/ppermute | solution.py:58
  79.1 35.4 %collective-permute-start.18 = (bf16[512,1280]{1,0:T(8,128)(2,1)S(1)}, bf16[512,1280]{1,0:T(8,128)(2,1)}, u32[]{:S(2)}, u32[]{:S(2)}) collective-permute-start(bf16[512,1280]{1,0:T(8,128)(2,1)S(1)} %pad_maximum_fusion.refs_7_.refs_17_), channel_id=1, source_target_pairs={{0,1},{1,0},{2,3},{3,2},{4,5},{5,4},{6,7},{7,6},{8,9},{9,8},{10,11... | collective-permute-start | bytes 3932168 | tf_op jit(solution)/shard_map/ppermute | solution.py:58
  79.5 35.1 %collective-permute-start.19 = (bf16[512,1280]{1,0:T(8,128)(2,1)S(1)}, bf16[512,1280]{1,0:T(8,128)(2,1)}, u32[]{:S(2)}, u32[]{:S(2)}) collective-permute-start(bf16[512,1280]{1,0:T(8,128)(2,1)S(1)} %pad_maximum_fusion.refs_7_.refs_17_), channel_id=1, source_target_pairs={{0,16},{1,17},{2,18},{3,19},{4,20},{5,21},{6,22},{7,23},{8,24},{9,... | collective-permute-start | bytes 3932168 | tf_op jit(solution)/shard_map/ppermute | solution.py:58
  115.7 32.6 %collective-permute-start.25 = (bf16[256,1280]{1,0:T(8,128)(2,1)S(1)}, bf16[256,1280]{1,0:T(8,128)(2,1)S(1)}, u32[]{:S(2)}, u32[]{:S(2)}) collective-permute-start(bf16[256,1280]{1,0:T(8,128)(2,1)S(1)} %slice.82), channel_id=1, source_target_pairs={{0,16},{1,17},{2,18},{3,19},{4,20},{5,21},{6,22},{7,23},{8,24},{9,... | collective-permute-start | bytes 1966088 | tf_op jit(solution)/shard_map/ppermute | solution.py:58
  118.5 29.8 %collective-permute-start.26 = (bf16[256,1280]{1,0:T(8,128)(2,1)S(1)}, bf16[256,1280]{1,0:T(8,128)(2,1)}, u32[]{:S(2)}, u32[]{:S(2)}) collective-permute-start(bf16[256,1280]{1,0:T(8,128)(2,1)S(1)} %slice.83), channel_id=1, source_target_pairs={{0,1},{1,0},{2,3},{3,2},{4,5},{5,4},{6,7},{7,6},{8,9},{9,8},{10,11... | collective-permute-start | bytes 1966088 | tf_op jit(solution)/shard_map/ppermute | solution.py:58
  119.7 29.1 %collective-permute-start.27 = (bf16[512,1280]{1,0:T(8,128)(2,1)S(1)}, bf16[512,1280]{1,0:T(8,128)(2,1)}, u32[]{:S(2)}, u32[]{:S(2)}) collective-permute-start(bf16[512,1280]{1,0:T(8,128)(2,1)S(1)} %pad_maximum_fusion.refs_7_.refs_17_), channel_id=1, source_target_pairs={{0,8},{1,9},{2,10},{3,11},{4,12},{5,13},{6,14},{7,15},{8,0},{9,1},... | collective-permute-start | bytes 3932168 | tf_op jit(solution)/shard_map/ppermute | solution.py:58
  121.9 29.8 %collective-permute-start.28 = (bf16[512,1280]{1,0:T(8,128)(2,1)}, bf16[512,1280]{1,0:T(8,128)(2,1)}, u32[]{:S(2)}, u32[]{:S(2)}) collective-permute-start(bf16[512,1280]{1,0:T(8,128)(2,1)} %collective-permute-done.18.refs_8_.refs_18_), channel_id=1, source_target_pairs={{0,8},{1,9},{2,10},{3,11},{4,12},{5,13},{6,14},{7,15},{8,0},{9,1},... | collective-permute-start | bytes 3932168 | tf_op jit(solution)/shard_map/ppermute | solution.py:58
  121.9 29.8 %collective-permute-start.29 = (bf16[512,1280]{1,0:T(8,128)(2,1)}, bf16[512,1280]{1,0:T(8,128)(2,1)}, u32[]{:S(2)}, u32[]{:S(2)}) collective-permute-start(bf16[512,1280]{1,0:T(8,128)(2,1)} %collective-permute-done.19.refs_9_.refs_19_), channel_id=1, source_target_pairs={{0,8},{1,9},{2,10},{3,11},{4,12},{5,13},{6,14},{7,15},{8,0},{9,1},... | collective-permute-start | bytes 3932168 | tf_op jit(solution)/shard_map/ppermute | solution.py:58
  253.3 11.2 %collective-permute-start.32 = (bf16[4096,512]{1,0:T(8,128)(2,1)}, bf16[4096,512]{1,0:T(8,128)(2,1)S(1)}, u32[]{:S(2)}, u32[]{:S(2)}) collective-permute-start(bf16[4096,512]{1,0:T(8,128)(2,1)} %outer.6), channel_id=1, source_target_pairs={{0,8},{1,9},{2,10},{3,11},{4,12},{5,13},{6,14},{7,15},{8,0},{9,1},... | collective-permute-start | bytes 12582920 | tf_op jit(solution)/shard_map/ppermute | solution.py:58
  270.5 31.3 %collective-permute-start.33 = (bf16[2048,256]{1,0:T(8,128)(2,1)}, bf16[2048,256]{1,0:T(8,128)(2,1)S(1)}, u32[]{:S(2)}, u32[]{:S(2)}) collective-permute-start(bf16[2048,256]{1,0:T(8,128)(2,1)} %get-tuple-element.196), channel_id=1, source_target_pairs={{0,16},{1,17},{2,18},{3,19},{4,20},{5,21},{6,22},{7,23},{8,24},{9,... | collective-permute-start | bytes 3145736 | tf_op jit(solution)/shard_map/ppermute | solution.py:58
  271.6 30.1 %collective-permute-start.34 = (bf16[1024,512]{1,0:T(8,128)(2,1)}, bf16[1024,512]{1,0:T(8,128)(2,1)S(1)}, u32[]{:S(2)}, u32[]{:S(2)}) collective-permute-start(bf16[1024,512]{1,0:T(8,128)(2,1)} %get-tuple-element.197), channel_id=1, source_target_pairs={{0,1},{1,0},{2,3},{3,2},{4,5},{5,4},{6,7},{7,6},{8,9},{9,8},{10,11... | collective-permute-start | bytes 3145736 | tf_op jit(solution)/shard_map/ppermute | solution.py:58
  306.6 12.9 %collective-permute-start.35 = (bf16[1024,256]{1,0:T(8,128)(2,1)}, bf16[1024,256]{1,0:T(8,128)(2,1)S(1)}, u32[]{:S(2)}, u32[]{:S(2)}) collective-permute-start(bf16[1024,256]{1,0:T(8,128)(2,1)} %get-tuple-element.209), channel_id=1, source_target_pairs={{0,1},{1,0},{2,3},{3,2},{4,5},{5,4},{6,7},{7,6},{8,9},{9,8},{10,11... | collective-permute-start | bytes 1572872 | tf_op jit(solution)/shard_map/ppermute | solution.py:58
  307.8 12.5 %collective-permute-start.36 = (bf16[1024,256]{1,0:T(8,128)(2,1)}, bf16[1024,256]{1,0:T(8,128)(2,1)S(1)}, u32[]{:S(2)}, u32[]{:S(2)}) collective-permute-start(bf16[1024,256]{1,0:T(8,128)(2,1)} %get-tuple-element.210), channel_id=1, source_target_pairs={{0,16},{1,17},{2,18},{3,19},{4,20},{5,21},{6,22},{7,23},{8,24},{9,... | collective-permute-start | bytes 1572872 | tf_op jit(solution)/shard_map/ppermute | solution.py:58
  320.3 11.6 %collective-permute-start.37 = (bf16[1024,1280]{1,0:T(8,128)(2,1)}, bf16[1024,1280]{1,0:T(8,128)(2,1)S(1)}, u32[]{:S(2)}, u32[]{:S(2)}) collective-permute-start(bf16[1024,1280]{1,0:T(8,128)(2,1)} %outer_pair.2), channel_id=1, source_target_pairs={{0,8},{1,9},{2,10},{3,11},{4,12},{5,13},{6,14},{7,15},{8,0},{9,1},... | collective-permute-start | bytes 7864328 | tf_op jit(solution)/shard_map/ppermute | solution.py:58
  340.0 16.4 %collective-permute-start.38 = (bf16[512,640]{1,0:T(8,128)(2,1)}, bf16[512,640]{1,0:T(8,128)(2,1)S(1)}, u32[]{:S(2)}, u32[]{:S(2)}) collective-permute-start(bf16[512,640]{1,0:T(8,128)(2,1)} %get-tuple-element.221), channel_id=1, source_target_pairs={{0,16},{1,17},{2,18},{3,19},{4,20},{5,21},{6,22},{7,23},{8,24},{9,... | collective-permute-start | bytes 1966088 | tf_op jit(solution)/shard_map/ppermute | solution.py:58
  340.3 16.2 %collective-permute-start.39 = (bf16[256,1280]{1,0:T(8,128)(2,1)}, bf16[256,1280]{1,0:T(8,128)(2,1)S(1)}, u32[]{:S(2)}, u32[]{:S(2)}) collective-permute-start(bf16[256,1280]{1,0:T(8,128)(2,1)} %get-tuple-element.222), channel_id=1, source_target_pairs={{0,1},{1,0},{2,3},{3,2},{4,5},{5,4},{6,7},{7,6},{8,9},{9,8},{10,11... | collective-permute-start | bytes 1966088 | tf_op jit(solution)/shard_map/ppermute | solution.py:58
  361.3 13.2 %collective-permute-start.40 = (bf16[1024,2048]{1,0:T(8,128)(2,1)}, bf16[1024,2048]{1,0:T(8,128)(2,1)S(1)}, u32[]{:S(2)}, u32[]{:S(2)}) collective-permute-start(bf16[1024,2048]{1,0:T(8,128)(2,1)} %outer.8), channel_id=1, source_target_pairs={{0,8},{1,9},{2,10},{3,11},{4,12},{5,13},{6,14},{7,15},{8,0},{9,1},... | collective-permute-start | bytes 12582920 | tf_op jit(solution)/shard_map/ppermute | solution.py:58
  362.3 12.2 %collective-permute-start.41 = (bf16[256,640]{1,0:T(8,128)(2,1)}, bf16[256,640]{1,0:T(8,128)(2,1)S(1)}, u32[]{:S(2)}, u32[]{:S(2)}) collective-permute-start(bf16[256,640]{1,0:T(8,128)(2,1)} %get-tuple-element.230), channel_id=1, source_target_pairs={{0,1},{1,0},{2,3},{3,2},{4,5},{5,4},{6,7},{7,6},{8,9},{9,8},{10,11... | collective-permute-start | bytes 983048 | tf_op jit(solution)/shard_map/ppermute | solution.py:58
  362.8 11.8 %collective-permute-start.42 = (bf16[256,640]{1,0:T(8,128)(2,1)}, bf16[256,640]{1,0:T(8,128)(2,1)S(1)}, u32[]{:S(2)}, u32[]{:S(2)}) collective-permute-start(bf16[256,640]{1,0:T(8,128)(2,1)} %get-tuple-element.231), channel_id=1, source_target_pairs={{0,16},{1,17},{2,18},{3,19},{4,20},{5,21},{6,22},{7,23},{8,24},{9,... | collective-permute-start | bytes 983048 | tf_op jit(solution)/shard_map/ppermute | solution.py:58
  383.7 35.3 %collective-permute-start.43 = (bf16[512,1024]{1,0:T(8,128)(2,1)}, bf16[512,1024]{1,0:T(8,128)(2,1)S(1)}, u32[]{:S(2)}, u32[]{:S(2)}) collective-permute-start(bf16[512,1024]{1,0:T(8,128)(2,1)} %get-tuple-element.244), channel_id=1, source_target_pairs={{0,16},{1,17},{2,18},{3,19},{4,20},{5,21},{6,22},{7,23},{8,24},{9,... | collective-permute-start | bytes 3145736 | tf_op jit(solution)/shard_map/ppermute | solution.py:58
  384.5 34.5 %collective-permute-start.44 = (bf16[256,2048]{1,0:T(8,128)(2,1)}, bf16[256,2048]{1,0:T(8,128)(2,1)S(1)}, u32[]{:S(2)}, u32[]{:S(2)}) collective-permute-start(bf16[256,2048]{1,0:T(8,128)(2,1)} %get-tuple-element.245), channel_id=1, source_target_pairs={{0,1},{1,0},{2,3},{3,2},{4,5},{5,4},{6,7},{7,6},{8,9},{9,8},{10,11... | collective-permute-start | bytes 3145736 | tf_op jit(solution)/shard_map/ppermute | solution.py:58
  385.3 33.6 %collective-permute-start.45 = (bf16[512,256]{1,0:T(8,128)(2,1)S(1)}, bf16[512,256]{1,0:T(8,128)(2,1)S(1)}, u32[]{:S(2)}, u32[]{:S(2)}) collective-permute-start(bf16[512,256]{1,0:T(8,128)(2,1)S(1)} %copy-done.59), channel_id=1, source_target_pairs={{0,2},{1,3},{2,0},{3,1},{4,6},{5,7},{6,4},{7,5},{8,10},{9,11},{10,... | collective-permute-start | bytes 786440 | tf_op jit(solution)/shard_map/ppermute | solution.py:58
  387.7 31.2 %collective-permute-start.46 = (bf16[512,256]{1,0:T(8,128)(2,1)S(1)}, bf16[512,256]{1,0:T(8,128)(2,1)S(1)}, u32[]{:S(2)}, u32[]{:S(2)}) collective-permute-start(bf16[512,256]{1,0:T(8,128)(2,1)S(1)} %copy-done.58), channel_id=1, source_target_pairs={{0,4},{1,5},{2,6},{3,7},{4,0},{5,1},{6,2},{7,3},{8,12},{9,13},{10,... | collective-permute-start | bytes 786440 | tf_op jit(solution)/shard_map/ppermute | solution.py:58
  387.7 31.2 %collective-permute-start.47 = (bf16[512,256]{1,0:T(8,128)(2,1)S(1)}, bf16[512,256]{1,0:T(8,128)(2,1)S(1)}, u32[]{:S(2)}, u32[]{:S(2)}) collective-permute-start(bf16[512,256]{1,0:T(8,128)(2,1)S(1)} %copy-done.57), channel_id=1, source_target_pairs={{0,6},{1,7},{2,4},{3,5},{4,2},{5,3},{6,0},{7,1},{8,14},{9,15},{10,... | collective-permute-start | bytes 786440 | tf_op jit(solution)/shard_map/ppermute | solution.py:58
  425.5 11.9 %collective-permute-start.48 = (bf16[256,1024]{1,0:T(8,128)(2,1)}, bf16[256,1024]{1,0:T(8,128)(2,1)S(1)}, u32[]{:S(2)}, u32[]{:S(2)}) collective-permute-start(bf16[256,1024]{1,0:T(8,128)(2,1)} %get-tuple-element.258), channel_id=1, source_target_pairs={{0,1},{1,0},{2,3},{3,2},{4,5},{5,4},{6,7},{7,6},{8,9},{9,8},{10,11... | collective-permute-start | bytes 1572872 | tf_op jit(solution)/shard_map/ppermute | solution.py:58
  426.9 11.6 %collective-permute-start.49 = (bf16[256,1024]{1,0:T(8,128)(2,1)}, bf16[256,1024]{1,0:T(8,128)(2,1)S(1)}, u32[]{:S(2)}, u32[]{:S(2)}) collective-permute-start(bf16[256,1024]{1,0:T(8,128)(2,1)} %get-tuple-element.259), channel_id=1, source_target_pairs={{0,16},{1,17},{2,18},{3,19},{4,20},{5,21},{6,22},{7,23},{8,24},{9,... | collective-permute-start | bytes 1572872 | tf_op jit(solution)/shard_map/ppermute | solution.py:58
  438.5 21.8 %collective-permute-start.50 = (bf16[1024,768]{1,0:T(8,128)(2,1)}, bf16[1024,768]{1,0:T(8,128)(2,1)S(1)}, u32[]{:S(2)}, u32[]{:S(2)}) collective-permute-start(bf16[1024,768]{1,0:T(8,128)(2,1)} %outer.10), channel_id=1, source_target_pairs={{0,8},{1,9},{2,10},{3,11},{4,12},{5,13},{6,14},{7,15},{8,0},{9,1},... | collective-permute-start | bytes 4718600 | tf_op jit(solution)/shard_map/ppermute | solution.py:58
  441.4 18.8 %collective-permute-start.51 = (bf16[512,256]{1,0:T(8,128)(2,1)S(1)}, bf16[512,256]{1,0:T(8,128)(2,1)}, u32[]{:S(2)}, u32[]{:S(2)}) collective-permute-start(bf16[512,256]{1,0:T(8,128)(2,1)S(1)} %copy-done.39), channel_id=1, source_target_pairs={{0,16},{1,17},{2,18},{3,19},{4,20},{5,21},{6,22},{7,23},{8,24},{9,... | collective-permute-start | bytes 786440 | tf_op jit(solution)/shard_map/ppermute | solution.py:58
  442.2 9.9 %collective-permute-start.52 = (bf16[128,640]{1,0:T(8,128)(2,1)S(1)}, bf16[128,640]{1,0:T(8,128)(2,1)S(1)}, u32[]{:S(2)}, u32[]{:S(2)}) collective-permute-start(bf16[128,640]{1,0:T(8,128)(2,1)S(1)} %copy-done.62), channel_id=1, source_target_pairs={{0,2},{1,3},{2,0},{3,1},{4,6},{5,7},{6,4},{7,5},{8,10},{9,11},{10,... | collective-permute-start | bytes 491528 | tf_op jit(solution)/shard_map/ppermute | solution.py:58
  444.5 7.6 %collective-permute-start.53 = (bf16[128,640]{1,0:T(8,128)(2,1)S(1)}, bf16[128,640]{1,0:T(8,128)(2,1)S(1)}, u32[]{:S(2)}, u32[]{:S(2)}) collective-permute-start(bf16[128,640]{1,0:T(8,128)(2,1)S(1)} %copy-done.61), channel_id=1, source_target_pairs={{0,4},{1,5},{2,6},{3,7},{4,0},{5,1},{6,2},{7,3},{8,12},{9,13},{10,... | collective-permute-start | bytes 491528 | tf_op jit(solution)/shard_map/ppermute | solution.py:58
  444.5 15.8 %collective-permute-start.54 = (bf16[128,640]{1,0:T(8,128)(2,1)S(1)}, bf16[128,640]{1,0:T(8,128)(2,1)S(1)}, u32[]{:S(2)}, u32[]{:S(2)}) collective-permute-start(bf16[128,640]{1,0:T(8,128)(2,1)S(1)} %copy-done.60), channel_id=1, source_target_pairs={{0,6},{1,7},{2,4},{3,5},{4,2},{5,3},{6,0},{7,1},{8,14},{9,15},{10,... | collective-permute-start | bytes 491528 | tf_op jit(solution)/shard_map/ppermute | solution.py:58
  468.9 27.1 %collective-permute-start.55 = (bf16[512,384]{1,0:T(8,128)(2,1)}, bf16[512,384]{1,0:T(8,128)(2,1)S(1)}, u32[]{:S(2)}, u32[]{:S(2)}) collective-permute-start(bf16[512,384]{1,0:T(8,128)(2,1)} %get-tuple-element.287), channel_id=1, source_target_pairs={{0,16},{1,17},{2,18},{3,19},{4,20},{5,21},{6,22},{7,23},{8,24},{9,... | collective-permute-start | bytes 1179656 | tf_op jit(solution)/shard_map/ppermute | solution.py:58
  469.7 26.3 %collective-permute-start.56 = (bf16[256,768]{1,0:T(8,128)(2,1)}, bf16[256,768]{1,0:T(8,128)(2,1)S(1)}, u32[]{:S(2)}, u32[]{:S(2)}) collective-permute-start(bf16[256,768]{1,0:T(8,128)(2,1)} %get-tuple-element.288), channel_id=1, source_target_pairs={{0,1},{1,0},{2,3},{3,2},{4,5},{5,4},{6,7},{7,6},{8,9},{9,8},{10,11... | collective-permute-start | bytes 1179656 | tf_op jit(solution)/shard_map/ppermute | solution.py:58
  470.0 23.1 %collective-permute-start.57 = (bf16[128,1024]{1,0:T(8,128)(2,1)}, bf16[128,1024]{1,0:T(8,128)(2,1)S(1)}, u32[]{:S(2)}, u32[]{:S(2)}) collective-permute-start(bf16[128,1024]{1,0:T(8,128)(2,1)} %get-tuple-element.289), channel_id=1, source_target_pairs={{0,2},{1,3},{2,0},{3,1},{4,6},{5,7},{6,4},{7,5},{8,10},{9,11},{10,... | collective-permute-start | bytes 786440 | tf_op jit(solution)/shard_map/ppermute | solution.py:58
  470.0 25.8 %collective-permute-start.58 = (bf16[128,1024]{1,0:T(8,128)(2,1)}, bf16[128,1024]{1,0:T(8,128)(2,1)S(1)}, u32[]{:S(2)}, u32[]{:S(2)}) collective-permute-start(bf16[128,1024]{1,0:T(8,128)(2,1)} %get-tuple-element.290), channel_id=1, source_target_pairs={{0,4},{1,5},{2,6},{3,7},{4,0},{5,1},{6,2},{7,3},{8,12},{9,13},{10,... | collective-permute-start | bytes 786440 | tf_op jit(solution)/shard_map/ppermute | solution.py:58
  471.3 24.6 %collective-permute-start.59 = (bf16[128,1024]{1,0:T(8,128)(2,1)}, bf16[128,1024]{1,0:T(8,128)(2,1)S(1)}, u32[]{:S(2)}, u32[]{:S(2)}) collective-permute-start(bf16[128,1024]{1,0:T(8,128)(2,1)} %get-tuple-element.291), channel_id=1, source_target_pairs={{0,6},{1,7},{2,4},{3,5},{4,2},{5,3},{6,0},{7,1},{8,14},{9,15},{10,... | collective-permute-start | bytes 786440 | tf_op jit(solution)/shard_map/ppermute | solution.py:58
  493.2 11.9 %collective-permute-start.82 = (bf16[512,256]{1,0:T(8,128)(2,1)S(1)}, bf16[512,256]{1,0:T(8,128)(2,1)}, u32[]{:S(2)}, u32[]{:S(2)}) collective-permute-start(bf16[512,256]{1,0:T(8,128)(2,1)S(1)} %copy-done.39), channel_id=1, source_target_pairs={{0,8},{1,9},{2,10},{3,11},{4,12},{5,13},{6,14},{7,15},{8,0},{9,1},... | collective-permute-start | bytes 786440 | tf_op jit(solution)/shard_map/ppermute | solution.py:58
  495.8 9.2 %collective-permute-start.83 = (bf16[512,256]{1,0:T(8,128)(2,1)}, bf16[512,256]{1,0:T(8,128)(2,1)}, u32[]{:S(2)}, u32[]{:S(2)}) collective-permute-start(bf16[512,256]{1,0:T(8,128)(2,1)} %collective-permute-done.51.refs_1_), channel_id=1, source_target_pairs={{0,8},{1,9},{2,10},{3,11},{4,12},{5,13},{6,14},{7,15},{8,0},{9,1},... | collective-permute-start | bytes 786440 | tf_op jit(solution)/shard_map/ppermute | solution.py:58
  501.7 7.9 %collective-permute-start.60 = (bf16[2,7296]{1,0:T(2,128)(2,1)S(1)}, bf16[2,7296]{1,0:T(2,128)(2,1)S(1)}, u32[]{:S(2)}, u32[]{:S(2)}) collective-permute-start(bf16[2,7296]{1,0:T(2,128)(2,1)S(1)} %concatenate.38), channel_id=1, source_target_pairs={{0,2},{1,3},{2,0},{3,1},{4,6},{5,7},{6,4},{7,5},{8,10},{9,11},{10,... | collective-permute-start | bytes 87560 | tf_op jit(solution)/shard_map/ppermute | solution.py:58
  502.4 7.2 %collective-permute-start.61 = (bf16[2,7296]{1,0:T(2,128)(2,1)S(1)}, bf16[2,7296]{1,0:T(2,128)(2,1)S(1)}, u32[]{:S(2)}, u32[]{:S(2)}) collective-permute-start(bf16[2,7296]{1,0:T(2,128)(2,1)S(1)} %concatenate.38), channel_id=1, source_target_pairs={{0,4},{1,5},{2,6},{3,7},{4,0},{5,1},{6,2},{7,3},{8,12},{9,13},{10,... | collective-permute-start | bytes 87560 | tf_op jit(solution)/shard_map/ppermute | solution.py:58
  503.0 6.6 %collective-permute-start.62 = (bf16[2,7296]{1,0:T(2,128)(2,1)S(1)}, bf16[2,7296]{1,0:T(2,128)(2,1)S(1)}, u32[]{:S(2)}, u32[]{:S(2)}) collective-permute-start(bf16[2,7296]{1,0:T(2,128)(2,1)S(1)} %concatenate.38), channel_id=1, source_target_pairs={{0,6},{1,7},{2,4},{3,5},{4,2},{5,3},{6,0},{7,1},{8,14},{9,15},{10,... | collective-permute-start | bytes 87560 | tf_op jit(solution)/shard_map/ppermute | solution.py:58
  507.7 22.7 %collective-permute-start.74 = (bf16[256,384]{1,0:T(8,128)(2,1)}, bf16[256,384]{1,0:T(8,128)(2,1)S(1)}, u32[]{:S(2)}, u32[]{:S(2)}) collective-permute-start(bf16[256,384]{1,0:T(8,128)(2,1)} %get-tuple-element.300), channel_id=1, source_target_pairs={{0,1},{1,0},{2,3},{3,2},{4,5},{5,4},{6,7},{7,6},{8,9},{9,8},{10,11... | collective-permute-start | bytes 589832 | tf_op jit(solution)/shard_map/ppermute | solution.py:58
  508.9 21.6 %collective-permute-start.75 = (bf16[256,384]{1,0:T(8,128)(2,1)}, bf16[256,384]{1,0:T(8,128)(2,1)S(1)}, u32[]{:S(2)}, u32[]{:S(2)}) collective-permute-start(bf16[256,384]{1,0:T(8,128)(2,1)} %get-tuple-element.301), channel_id=1, source_target_pairs={{0,16},{1,17},{2,18},{3,19},{4,20},{5,21},{6,22},{7,23},{8,24},{9,... | collective-permute-start | bytes 589832 | tf_op jit(solution)/shard_map/ppermute | solution.py:58
  523.3 26.6 %collective-permute-start.68 = (bf16[16,7296]{1,0:T(8,128)(2,1)S(1)}, bf16[16,7296]{1,0:T(8,128)(2,1)S(1)}, u32[]{:S(2)}, u32[]{:S(2)}) collective-permute-start(bf16[16,7296]{1,0:T(8,128)(2,1)S(1)} %reshape.107), channel_id=1, source_target_pairs={{0,8},{1,9},{2,10},{3,11},{4,12},{5,13},{6,14},{7,15},{8,0},{9,1},... | collective-permute-start | bytes 700424 | tf_op jit(solution)/shard_map/ppermute | solution.py:58
  527.2 23.4 %collective-permute-start.69 = (bf16[16,7296]{1,0:T(8,128)(2,1)S(1)}, bf16[16,7296]{1,0:T(8,128)(2,1)}, u32[]{:S(2)}, u32[]{:S(2)}) collective-permute-start(bf16[16,7296]{1,0:T(8,128)(2,1)S(1)} %reshape.107), channel_id=1, source_target_pairs={{0,16},{1,17},{2,18},{3,19},{4,20},{5,21},{6,22},{7,23},{8,24},{9,... | collective-permute-start | bytes 700424 | tf_op jit(solution)/shard_map/ppermute | solution.py:58
  528.1 23.4 %collective-permute-start.70 = (bf16[16,7296]{1,0:T(8,128)(2,1)S(1)}, bf16[16,7296]{1,0:T(8,128)(2,1)S(1)}, u32[]{:S(2)}, u32[]{:S(2)}) collective-permute-start(bf16[16,7296]{1,0:T(8,128)(2,1)S(1)} %reshape.107), channel_id=1, source_target_pairs={{0,24},{1,25},{2,26},{3,27},{4,28},{5,29},{6,30},{7,31},{8,16},{9,... | collective-permute-start | bytes 700424 | tf_op jit(solution)/shard_map/ppermute | solution.py:58
  534.9 6.8 %collective-permute-start.76 = (bf16[128,384]{1,0:T(8,128)(2,1)}, bf16[128,384]{1,0:T(8,128)(2,1)S(1)}, u32[]{:S(2)}, u32[]{:S(2)}) collective-permute-start(bf16[128,384]{1,0:T(8,128)(2,1)} %get-tuple-element.307), channel_id=1, source_target_pairs={{0,2},{1,3},{2,0},{3,1},{4,6},{5,7},{6,4},{7,5},{8,10},{9,11},{10,... | collective-permute-start | bytes 294920 | tf_op jit(solution)/shard_map/ppermute | solution.py:58
  537.5 6.2 %collective-permute-start.77 = (bf16[128,384]{1,0:T(8,128)(2,1)}, bf16[128,384]{1,0:T(8,128)(2,1)S(1)}, u32[]{:S(2)}, u32[]{:S(2)}) collective-permute-start(bf16[128,384]{1,0:T(8,128)(2,1)} %get-tuple-element.308), channel_id=1, source_target_pairs={{0,4},{1,5},{2,6},{3,7},{4,0},{5,1},{6,2},{7,3},{8,12},{9,13},{10,... | collective-permute-start | bytes 294920 | tf_op jit(solution)/shard_map/ppermute | solution.py:58
  543.7 10.9 %collective-permute-start.71 = (bf16[128,1664]{1,0:T(8,128)(2,1)S(1)}, bf16[128,1664]{1,0:T(8,128)(2,1)S(1)}, u32[]{:S(2)}, u32[]{:S(2)}) collective-permute-start(bf16[128,1664]{1,0:T(8,128)(2,1)S(1)} %constant_dynamic-update-slice_fusion.24.refs_0_), channel_id=1, source_target_pairs={{0,16},{1,17},{2,18},{3,19},{4,20},{5,21},{6,22},{7,23},{8,24},{9,... | collective-permute-start | bytes 1277960 | tf_op jit(solution)/shard_map/ppermute | solution.py:58
  546.1 13.6 %collective-permute-start.72 = (bf16[128,1664]{1,0:T(8,128)(2,1)S(1)}, bf16[128,1664]{1,0:T(8,128)(2,1)S(1)}, u32[]{:S(2)}, u32[]{:S(2)}) collective-permute-start(bf16[128,1664]{1,0:T(8,128)(2,1)S(1)} %constant_dynamic-update-slice_fusion.24.refs_0_), channel_id=1, source_target_pairs={{0,8},{1,9},{2,10},{3,11},{4,12},{5,13},{6,14},{7,15},{8,0},{9,1},... | collective-permute-start | bytes 1277960 | tf_op jit(solution)/shard_map/ppermute | solution.py:58
  549.9 9.8 %collective-permute-start.79 = (bf16[128,384]{1,0:T(8,128)(2,1)}, bf16[128,384]{1,0:T(8,128)(2,1)S(1)}, u32[]{:S(2)}, u32[]{:S(2)}) collective-permute-start(bf16[128,384]{1,0:T(8,128)(2,1)} %sums_j.1.refs_4_), channel_id=1, source_target_pairs={{0,16},{1,17},{2,18},{3,19},{4,20},{5,21},{6,22},{7,23},{8,24},{9,... | collective-permute-start | bytes 294920 | tf_op jit(solution)/shard_map/ppermute | solution.py:58
  550.6 9.1 %collective-permute-start.80 = (bf16[128,384]{1,0:T(8,128)(2,1)}, bf16[128,384]{1,0:T(8,128)(2,1)S(1)}, u32[]{:S(2)}, u32[]{:S(2)}) collective-permute-start(bf16[128,384]{1,0:T(8,128)(2,1)} %sums_j.1.refs_4_), channel_id=1, source_target_pairs={{0,8},{1,9},{2,10},{3,11},{4,12},{5,13},{6,14},{7,15},{8,0},{9,1},... | collective-permute-start | bytes 294920 | tf_op jit(solution)/shard_map/ppermute | solution.py:58
  551.5 8.2 %collective-permute-start.81 = (bf16[128,384]{1,0:T(8,128)(2,1)}, bf16[128,384]{1,0:T(8,128)(2,1)S(1)}, u32[]{:S(2)}, u32[]{:S(2)}) collective-permute-start(bf16[128,384]{1,0:T(8,128)(2,1)} %sums_j.1.refs_4_), channel_id=1, source_target_pairs={{0,24},{1,25},{2,26},{3,27},{4,28},{5,29},{6,30},{7,31},{8,16},{9,... | collective-permute-start | bytes 294920 | tf_op jit(solution)/shard_map/ppermute | solution.py:58
  (87 other events, 715.3 us)
Sparse Core Ops, SparseCore 0:
  79.3 80.8 all-gather.1

commit v4 on v3

--- a/solution.py
+++ b/solution.py
@@ -24,6 +24,10 @@
 
 def dot(left, right, dims=NN):
     return lax.dot_general(left, right, dims, preferred_element_type=WIDE)
+
+
+def far(values):
+    return pltpu.with_memory_space_constraint(values, pltpu.HBM)
 
 
 def two_parts(values):
@@ -161,7 +165,7 @@
             out_specs=out_specs,
         ),
         out_shape=out_shapes,
-        compiler_params=pltpu.CompilerParams(vmem_limit_bytes=VMEM_LIMIT),
+        compiler_params=pltpu.CompilerParams(vmem_limit_bytes=20 << 20),
         cost_estimate=LIGHT,
         name=name,
     )(place.table, *arrays)
@@ -175,6 +179,7 @@
 class RowSum:
     def __init__(self, keep, arrived, rows, order):
         self.base = [keep, arrived]
+        self.rest = [far(keep), far(arrived)]
         self.rows, self.width = rows, keep.shape[1] // 2
         self.streams = (
             [{"z": 0, "count": 2, "order": "yx"}, {"z": 2, "count": 2, "order": "xy"}]
@@ -212,13 +217,13 @@
                 where = lambda n, p, start=start: (2 * (start + n) + p[3], 1 - p[0])
                 terms = [(value, lambda n, p: (n, 1 - p[0]), None)]
             outs.append(
-                ((count, 1), block, lambda n, p: (n, 0), [(t, where, None) for t in self.base] + terms)
+                ((count, 1), block, lambda n, p: (n, 0), [(t, where, None) for t in self.rest] + terms)
             )
         self.axes = [{"d" + stream["order"][1]: 1} for stream in self.streams]
         return steps, outs
 
     def terms(self, flip):
-        out = [(t, lambda n, p: (2 * (p[2] ^ flip) + p[3], p[0]), None) for t in self.base]
+        out = [(t, lambda n, p: (2 * (p[2] ^ flip) + p[3], p[0]), None) for t in self.rest]
         for stream in self.streams:
             mask = stream["count"] - 1
             when = None
@@ -275,7 +280,7 @@
         in_specs=[pl.BlockSpec(memory_space=pltpu.SMEM)] + [vmem] * len(quarters),
         out_specs=[vmem] * len(shapes),
         out_shape=[jax.ShapeDtypeStruct(shape, WIDE) for shape in shapes],
-        compiler_params=pltpu.CompilerParams(vmem_limit_bytes=VMEM_LIMIT),
+        compiler_params=pltpu.CompilerParams(vmem_limit_bytes=20 << 20),
         cost_estimate=LIGHT,
         name=name,
     )(place.table, *quarters)
@@ -383,10 +388,10 @@
         in_specs=[pl.BlockSpec((1, length, 384), lambda i, p: (i, 0, p)), table, table],
         out_specs=[block, block],
         out_shape=[jax.ShapeDtypeStruct((items, length, 128 * pairs), LOW)] * 2,
-        compiler_params=pltpu.CompilerParams(vmem_limit_bytes=VMEM_LIMIT),
+        compiler_params=pltpu.CompilerParams(vmem_limit_bytes=24 << 20),
         cost_estimate=LIGHT,
         name="attend",
-    )(qkv, query_mask, key_mask)
+    )(far(qkv), query_mask, key_mask)
 
 
 def side_table(cross, size=128):
@@ -474,10 +479,10 @@
             pltpu.VMEM((2, length, 128), WIDE),
             pltpu.VMEM((length, 128), WIDE),
         ],
-        compiler_params=pltpu.CompilerParams(vmem_limit_bytes=VMEM_LIMIT),
+        compiler_params=pltpu.CompilerParams(vmem_limit_bytes=24 << 20),
         cost_estimate=LIGHT,
         name="attend_back",
-    )(qkv, extra, key_mask, out, grad, roots, gain)
+    )(far(qkv), far(extra), key_mask, far(out), far(grad), far(roots), gain)
 
 
 def row_facts(lengths_ref, block_rows, length):
@@ -491,9 +496,24 @@
     return jnp.where(second, ref[1:2, :], ref[0:1, :])
 
 
-def add_sums(ref, start, second, values):
-    ref[start : start + 1, :] += jnp.sum(jnp.where(second, 0.0, values), 0, keepdims=True)
-    ref[start + 1 : start + 2, :] += jnp.sum(jnp.where(second, values, 0.0), 0, keepdims=True)
+def add_sums(ref, second, values):
+    count = values[0].shape[0]
+    flags = pl.program_id(0) * count
+    half = count * pl.num_programs(0) // 2
+    split = (flags < half) & (flags + count > half)
+
+    @pl.when(jnp.logical_not(split))
+    def _():
+        for number, value in enumerate(values):
+            row = 2 * number + jnp.where(flags >= half, 1, 0)
+            ref[pl.ds(row, 1), :] += jnp.sum(value, 0, keepdims=True)
+
+    @pl.when(split)
+    def _():
+        for number, value in enumerate(values):
+            later = jnp.sum(jnp.where(second, value, 0.0), 0, keepdims=True)
+            ref[2 * number : 2 * number + 1, :] += jnp.sum(value, 0, keepdims=True) - later
+            ref[2 * number + 1 : 2 * number + 2, :] += later
 
 
 def normalize(values):
@@ -570,7 +590,7 @@
         compiler_params=pltpu.CompilerParams(vmem_limit_bytes=VMEM_LIMIT),
         cost_estimate=LIGHT,
         name=name,
-    )(place.table, lengths, *blocked, *full, *parts)
+    )(place.table, lengths, *map(far, blocked), *full, *parts)
 
 
 def project_kernel(second, real, tokens, full, ready, outs, sums):
@@ -641,13 +661,19 @@
     attn_grad = jnp.where(real, gate_one * middle_grad, 0.0).astype(LOW)
     attn_grad_ref[...] = attn_grad
     attended_grad_ref[...] = dot(attn_grad, proj[...], NT).astype(LOW)
-    add_sums(sum_ref, 0, second, jnp.where(real, stream * stream, 0.0))
-    add_sums(sum_ref, 2, second, branch_one * branch_one)
-    add_sums(sum_ref, 4, second, branch_two * branch_two)
-    add_sums(sum_ref, 6, second, jnp.where(real, mlp * upstream, 0.0))
-    add_sums(sum_ref, 8, second, jnp.where(real, attn * middle_grad, 0.0))
-    add_sums(sum_ref, 10, second, grad * unit)
-    add_sums(sum_ref, 12, second, grad)
+    add_sums(
+        sum_ref,
+        second,
+        [
+            jnp.where(real, stream * stream, 0.0),
+            branch_one * branch_one,
+            branch_two * branch_two,
+            jnp.where(real, mlp * upstream, 0.0),
+            jnp.where(real, attn * middle_grad, 0.0),
+            grad * unit,
+            grad,
+        ],
+    )
 
 
 def token_back_kernel(second, real, tokens, full, ready, outs, sums):
@@ -661,8 +687,7 @@
         grad = grad + dot(ref[...], weight[:, column : column + ref.shape[1]], NT)
         column += ref.shape[1]
     unit, root = normalize(x_ref[...].astype(WIDE))
-    add_sums(sum_ref, 0, second, grad * unit)
-    add_sums(sum_ref, 2, second, grad)
+    add_sums(sum_ref, second, [grad * unit, grad])
     scaled = grad * (1.0 + per_row(scale, second))
     total = middle_ref[...].astype(WIDE) + root * (
         scaled - jnp.mean(scaled, -1, keepdims=True) - unit * jnp.mean(scaled * unit, -1, keepdims=True)
@@ -692,36 +717,41 @@
             out_specs=pl.BlockSpec((tall, wide), lambda i, j, h: (i, j)),
         ),
         out_shape=jax.ShapeDtypeStruct((height, width), LOW),
-        compiler_params=pltpu.CompilerParams(vmem_limit_bytes=VMEM_LIMIT),
+        compiler_params=pltpu.CompilerParams(vmem_limit_bytes=28 << 20),
         cost_estimate=LIGHT,
         name="outer",
-    )(half.reshape(1).astype(jnp.int32), left, right)
-
-
-def outer_pair(left, right, other_left, other_right, half):
+    )(half.reshape(1).astype(jnp.int32), far(left), far(right))
+
+
+def outer_joint(left, rights, other_left, other_right, half):
     count, height = left.shape
-    widths = (right.shape[1] // 4, other_right.shape[1] // 4)
+    rights = [*rights, other_right]
+    widths = [right.shape[1] // 4 for right in rights]
     total = sum(widths)
     whole = lambda v: pl.BlockSpec(v.shape, lambda j, h: (0, 0))
     part = lambda width: pl.BlockSpec((count, width), lambda j, h: (0, 2 * h[0] + j))
 
-    def body(half_ref, left_ref, right_ref, other_left_ref, other_right_ref, out_ref):
-        out_ref[:, : widths[0]] = dot(left_ref[...], right_ref[...], TN).astype(LOW)
-        out_ref[:, widths[0] :] = dot(other_left_ref[...], other_right_ref[...], TN).astype(LOW)
+    def body(half_ref, left_ref, other_ref, *refs):
+        *right_refs, out_ref = refs
+        column = 0
+        for number, (ref, width) in enumerate(zip(right_refs, widths)):
+            source = other_ref if number == len(widths) - 1 else left_ref
+            out_ref[:, column : column + width] = dot(source[...], ref[...], TN).astype(LOW)
+            column += width
 
     return pl.pallas_call(
         body,
         grid_spec=pltpu.PrefetchScalarGridSpec(
             num_scalar_prefetch=1,
             grid=(2,),
-            in_specs=[whole(left), part(widths[0]), whole(other_left), part(widths[1])],
+            in_specs=[whole(left), whole(other_left)] + [part(width) for width in widths],
             out_specs=pl.BlockSpec((height, total), lambda j, h: (0, j)),
         ),
         out_shape=jax.ShapeDtypeStruct((height, 2 * total), LOW),
-        compiler_params=pltpu.CompilerParams(vmem_limit_bytes=VMEM_LIMIT),
+        compiler_params=pltpu.CompilerParams(vmem_limit_bytes=40 << 20),
         cost_estimate=LIGHT,
-        name="outer_pair",
-    )(half.reshape(1).astype(jnp.int32), left, right, other_left, other_right)
+        name="outer_joint",
+    )(half.reshape(1).astype(jnp.int32), far(left), far(other_left), *map(far, rights))
 
 
 def plain_sum(place, keep, send):
@@ -827,6 +857,14 @@
         + [(width, LOW)] * 3, 1, "block",
     )
 
+    def small_group(sum_four):
+        head_terms = jnp.concatenate([heads_first, heads_second], 2).reshape(items, heads, width // heads).sum(2)
+        head_parts = jnp.concatenate([*two_parts(head_terms), jnp.zeros((items, 128 - 2 * heads), LOW)], 1)
+        grad_modulation = jnp.concatenate(
+            [sum_one[8:10], sum_one[6:8], sum_four[0:2], sum_one[10:12], sum_four[2:4], sum_one[12:14]], 1
+        ).astype(LOW)
+        return jnp.concatenate([grad_modulation, head_parts, silu_cond], 1)
+
     def send_part(left, right):
         return outer(left, right, 1 - place.c)
 
@@ -857,70 +895,63 @@
         )
         (sums,) = add_blocks(place, [fc2.second(arrived)], "sums_b")
 
-        first_pair = functools.partial(outer_pair, normed_one, grad_first, flat_attended)
-        first_send, fc2_arrived = beside(
-            lambda g: first_pair(g, 1 - place.c), tie(grad_attn, grad_first)[0], fc2.moves(sums)
-        )
-        first_keep, arrived = beside(lambda g: first_pair(g, place.c), grad_attn, [(first_send, {"dc": 1})])
-        first = RowSum(first_keep, arrived[0], unit_rows, "mixed")
-        first_sums, fc2_sums = add_blocks(place, [first.first(), fc2.third(fc2_arrived)], "sums_c")
-        fc2_moves = fc2.moves(fc2_sums)
-
-        fc1_send, arrived = beside(lambda g: send_part(normed_two, g), grad_hidden, first.moves(first_sums))
-        (first_sums,) = add_blocks(place, [first.second(arrived)], "sums_d")
-        fc1_keep, arrived = beside(
-            lambda g: keep_part(normed_two, g), grad_hidden, [(fc1_send, {"dc": 1})] + first.moves(first_sums)
-        )
+        fc1_send, fc2_arrived = beside(
+            lambda g: send_part(normed_two, g), tie(grad_hidden, grad_first)[0], fc2.moves(sums)
+        )
+        fc1_keep, arrived = beside(lambda g: keep_part(normed_two, g), grad_hidden, [(fc1_send, {"dc": 1})])
         fc1 = RowSum(fc1_keep, arrived[0], unit_rows, "mixed")
-        fc1_sums, first_sums = add_blocks(place, [fc1.first(), first.third(arrived[1:])], "sums_e")
-        first_moves = first.moves(first_sums)
+        fc1_sums, fc2_sums = add_blocks(place, [fc1.first(), fc2.third(fc2_arrived)], "sums_c")
 
         (grad_second, heads_second), arrived = beside(
-            lambda g: heads_back(g, pairs // 2), grad_attended, fc1.moves(fc1_sums) + fc2_moves
+            lambda g: heads_back(g, pairs // 2), grad_attended, fc1.moves(fc1_sums) + fc2.moves(fc2_sums)
         )
         fc1_sums, (fc2_own,) = add_blocks(
-            place, [fc1.second(arrived[:2]), fc2.last(arrived[2:])], "sums_f"
-        )
-        second_send, fc1_arrived = beside(
-            lambda g: send_part(normed_one, g), grad_second, fc1.moves(fc1_sums)
-        )
-        second_keep, arrived = beside(
-            lambda g: keep_part(normed_one, g), grad_second,
-            [(second_send, {"dc": 1}), (fc2_own, {"dy": 1})] + first_moves,
-        )
-        fc2_y = arrived[1]
-        second = RowSum(second_keep, arrived[0], unit_rows, "mixed")
-        second_sums, fc1_sums, (first_own,) = add_blocks(
-            place, [second.first(), fc1.third(fc1_arrived), first.last(arrived[2:])], "sums_g"
-        )
+            place, [fc1.second(arrived[:2]), fc2.last(arrived[2:])], "sums_d"
+        )
+        joint = functools.partial(outer_joint, normed_one, [grad_first, grad_second], flat_attended)
+        last_send, (*fc1_arrived, fc2_y, fc2_c) = beside(
+            lambda g: joint(g, 1 - place.c),
+            tie(grad_attn, grad_second)[0],
+            fc1.moves(fc1_sums) + [(fc2_own, {"dy": 1}), (fc2_own, {"dc": 1})],
+        )
+        last_keep, (arrived, fc2_both) = beside(
+            lambda g: joint(g, place.c), grad_attn, [(last_send, {"dc": 1}), (fc2_y, {"dc": 1})]
+        )
+        last = RowSum(last_keep, arrived, unit_rows, "mixed")
+        fc1_sums, last_sums = add_blocks(place, [fc1.third(fc1_arrived), last.first()], "sums_e")
+
         (grad_tokens, sum_four), arrived = beside(
-            lambda g: token_back(grad_first, g), grad_second, second.moves(second_sums) + fc1.moves(fc1_sums)
-        )
-        second_sums, (fc1_own,) = add_blocks(
-            place, [second.second(arrived[:2]), fc1.last(arrived[2:])], "sums_h"
-        )
-        second_moves = second.moves(second_sums)
-        sum_four = tie(sum_four, *second_sums)[0]
-        second_arrived = [hop(v, **axes) for v, axes in second_moves]
-        (second_sums,) = add_blocks(place, [second.third(second_arrived)], "sums_i")
-        fc2_core = [hop(fc2_own, dc=1), hop(fc2_y, dc=1)]
-        others = jnp.concatenate([fc1_own, first_own], 1)
-        others_y = hop(others, dy=1)
-        others_core = [hop(others, dc=1), hop(others_y, dc=1)]
-        ((second_own,),) = add_blocks(
-            place, [second.last([hop(v, **axes) for v, axes in second.moves(second_sums)])], "sums_j"
-        )
-        second_all = spread(second_own)
+            lambda g: token_back(grad_first, g), grad_second, last.moves(last_sums) + fc1.moves(fc1_sums)
+        )
+        last_sums, (fc1_own,) = add_blocks(place, [last.second(arrived[:2]), fc1.last(arrived[2:])], "sums_f")
+        group = small_group(sum_four)
+        moves = last.moves(last_sums)
+        sent, group = tie(tuple(v for v, _ in moves), group)
+        arrived = [hop(v, **axes) for v, (_, axes) in zip(sent, moves)]
+        group_stack = small_over_z(group)
+        arrived, group_stack = tie(arrived, group_stack)
+        (last_sums,) = add_blocks(place, [last.third(arrived)], "sums_g")
+        sent, group_stack = tie(tuple(last_sums), group_stack)
+        arrived = [hop(v, **axes) for v, axes in last.moves(sent)]
+        group = small_over_x(place, group_stack)
+        fc1_y = hop(fc1_own, dy=1)
+        ((last_own,),) = add_blocks(place, [last.last(arrived)], "sums_h")
+        last_all = spread(last_own)
+        fc1_core = [hop(fc1_own, dc=1), hop(fc1_y, dc=1)]
         (grad_fc2,) = lay_out(
-            place, [fc2_own, fc2_y] + fc2_core, [[(0, 0, quarter, 0, 0, quarter)]], [w_fc2.shape], "lay_out_fc2"
+            place, [fc2_own, fc2_y, fc2_c, fc2_both], [[(0, 0, quarter, 0, 0, quarter)]], [w_fc2.shape],
+            "lay_out_fc2",
         )
         wide = hidden_width // 4
-        layout = [(0, 0, wide, 0, 0, wide), (1, wide + 384, quarter, 0, 0, quarter)]
-        layout += [(2, wide + 128 * n, 128, 0, n * width, 128) for n in range(3)]
-        layout_two = [(2, 128 * n, 128, 0, n * width + 512, 128) for n in range(3)]
-        grad_fc1, grad_proj, grad_qkv = lay_out(
-            place, [others, others_y] + others_core + second_all, [layout, layout_two],
-            [w_fc1.shape, w_proj.shape, w_qkv.shape], "lay_out_others",
+        (grad_fc1,) = lay_out(
+            place, [fc1_own, fc1_y] + fc1_core, [[(0, 0, wide, 0, 0, wide)]], [w_fc1.shape], "lay_out_fc1"
+        )
+        layout = [
+            (0, 384 * side + 128 * n, 128, 0, n * width + 512 * side, 128) for side in range(2) for n in range(3)
+        ]
+        layout.append((1, 768, quarter, 0, 0, quarter))
+        grad_qkv, grad_proj = lay_out(
+            place, last_all, [layout], [w_qkv.shape, w_proj.shape], "lay_out_last"
         )
     else:
         def whole_sum(left, right):
@@ -935,13 +966,8 @@
             jnp.concatenate([whole_sum(normed_one, grad_first), whole_sum(normed_one, grad_second)], 1)
         )
         grad_tokens, sum_four = token_back(grad_first, grad_second)
-
-    head_terms = jnp.concatenate([heads_first, heads_second], 2).reshape(items, heads, width // heads).sum(2)
-    head_parts = jnp.concatenate([*two_parts(head_terms), jnp.zeros((items, 128 - 2 * heads), LOW)], 1)
-    grad_modulation = jnp.concatenate(
-        [sum_one[8:10], sum_one[6:8], sum_four[0:2], sum_one[10:12], sum_four[2:4], sum_one[12:14]], 1
-    ).astype(LOW)
-    group = gather_small(place, jnp.concatenate([grad_modulation, head_parts, silu_cond], 1), False)
+        group = gather_small(place, small_group(sum_four), False)
+
     grad_columns = dot(group[:, : 6 * width], w_ada, NT)
     everything = over_dp(place, group)
     all_heads = everything[:, 6 * width : 6 * width + 2 * heads].astype(WIDE)

time: 584 us -> 545 us (0.933)
  Pallas kernels: 339 us -> 305 us
  waiting for transfers between devices: 89.4 us -> 81.8 us
    pallas_call x10 -> x8, Pallas kernels: 45.7 us -> 28.2 us  [add_blocks(): pl.pallas_call(body, grid_spec=pltpu.PrefetchScalarGridSpec(num_scalar_pr...]
    pallas_call x6 -> x4, Pallas kernels: 56.2 us -> 38.8 us  [outer(): pl.pallas_call(outer_kernel, grid_spec=pltpu.PrefetchScalarGridSpec(num_s...]
    pallas_call x2, Pallas kernels: 19 us -> 25.2 us  [outer_joint(): pl.pallas_call(body, grid_spec=pltpu.PrefetchScalarGridSpec(num_scalar_pr...]
    ppermute x84 -> x76, waiting for transfers between devices: 80.9 us -> 76.8 us  [hop(): return lax.ppermute(values, AXES, pairs)]
    ppermute x84 -> x76, starting transfers between devices: 87.9 us -> 86.1 us  [hop(): return lax.ppermute(values, AXES, pairs)]
    unnamed x156 -> x113, local copies, waits for them, and re-layouts: 20.5 us -> 20.6 us
  transfers between devices with their start and end apart: 85 -> 77, of which waited for: 23 -> 22; matrix products, arithmetic and copies ran while one was open for 4% -> 6% of each run, Pallas kernels for 36% -> 35%
where the time goes in v4:
time: 545 us; the launch traced here: 536 us
  Pallas kernels  305 us (56%)
  starting transfers between devices  86.1 us (16%)
  waiting for transfers between devices  81.8 us (15%)
  local copies, waits for them, and re-layouts  33.6 us (6%)
  between operations  15.5 us (3%)
  other arithmetic  10.1 us (2%)
    pallas_call x3, Pallas kernels, token_call(): pl.pallas_call(body, grid=(grid,), in_specs=[smem, smem] + [pl.BlockSpec(...  123 us
    ppermute x76, starting transfers between devices, hop(): return lax.ppermute(values, AXES, pairs)  86.1 us
    ppermute x76, waiting for transfers between devices, hop(): return lax.ppermute(values, AXES, pairs)  76.8 us
    pallas_call x2, Pallas kernels, attend_back(): pl.pallas_call(attend_back_kernel, grid=(items, pairs), in_specs=[pl.Bloc...  58 us
    pallas_call x4, Pallas kernels, outer(): pl.pallas_call(outer_kernel, grid_spec=pltpu.PrefetchScalarGridSpec(num_s...  38.8 us
    pallas_call x8, Pallas kernels, add_blocks(): pl.pallas_call(body, grid_spec=pltpu.PrefetchScalarGridSpec(num_scalar_pr...  28.2 us
    pallas_call x1, Pallas kernels, attend(): pl.pallas_call(attend_kernel, grid=(items, pairs), in_specs=[pl.BlockSpec...  25.9 us
    pallas_call x2, Pallas kernels, outer_joint(): pl.pallas_call(body, grid_spec=pltpu.PrefetchScalarGridSpec(num_scalar_pr...  25.2 us
  transfers between devices with their start and end apart: 77, of which 22 were waited for; matrix products, arithmetic and copies ran while one was open for 6% of the time, Pallas kernels for 35%

profile of v4, /device:TPU:9, one launch (start us, length us, event | category | flops | bytes accessed | tf_op | source)
XLA Modules:
  0.0 536.4 jit_solution(17704549376785415029)
XLA Ops:
  9.4 2.2 collective-permute-start
  12.4 1.5 copy.38
  17.4 1.6 collective-permute-start.4
  22.1 4.5 collective-permute-done.4
  27.3 8.4 %collective-permute-done.5 = bf16[128,768]{1,0:T(8,128)(2,1)} collective-permute-done((bf16[128,768]{1,0:T(8,128)(2,1)S(1)}, bf16[128,768]{1,0:T(8,128)(2,1)}, u32[]{:S(2)}, u32[]{:S(2)}) %collective-permute-start.5) | collective-permute-done | bytes 196640 | tf_op jit(solution)/shard_map/ppermute | solution.py:62
  36.9 2.0 collective-permute-start.10
  42.8 2.5 collective-permute-start.11
  46.5 8.9 %collective-permute-done.14.refs_5_.refs_6_ = bf16[512,768]{1,0:T(8,128)(2,1)S(1)} collective-permute-done((bf16[512,768]{1,0:T(8,128)(2,1)S(1)}, bf16[512,768]{1,0:T(8,128)(2,1)S(1)}, u32[]{:S(2)}, u32[]{:S(2)}) %collective-permute-start.14) | collective-permute-done | bytes 786464 | tf_op jit(solution)/shard_map/ppermute | solution.py:62
  57.6 15.7 %collective-permute-done.13 = bf16[128,1280]{1,0:T(8,128)(2,1)S(1)} collective-permute-done((bf16[128,1280]{1,0:T(8,128)(2,1)S(1)}, bf16[128,1280]{1,0:T(8,128)(2,1)S(1)}, u32[]{:S(2)}, u32[]{:S(2)}) %collective-permute-start.13) | collective-permute-done | bytes 327712 | tf_op jit(solution)/shard_map/ppermute | solution.py:62
  74.4 3.0 collective-permute-start.24
  77.4 1.7 constant_dynamic-slice_fusion.13
  82.2 1.7 collective-permute-done.20.refs_9_.refs_10_
  88.3 23.2 %project.1 = (bf16[1360,1024]{1,0:T(8,128)(2,1)}, bf16[1360,3072]{1,0:T(8,128)(2,1)}, bf16[1360,1024]{1,0:T(8,128)(2,1)}) custom-call(s32[4]{0:T(128)} %pad_add_fusion.place_ref, s32[2]{0:T(128)} %fusion.19.lengths_ref, bf16[1360,1024]{1,0:T(8,128)(2,1)} %refs_2_.3, f32[2,1024]{1,0:T(2,128)} %get-tuple-element.341.refs_1_.refs_4_, ...), custom_call_target="tpu_custom_call" | custom-call | flops 1024 | bytes 1024 | tf_op jit(solution)/shard_map/project/pallas_call | solution.py:577
  111.6 3.0 collective-permute-done.18.refs_8_.refs_18_
  115.7 1.6 collective-permute-start.25
  119.7 2.2 collective-permute-start.27
  122.4 25.9 %attend.1 = (bf16[2,680,1024]{2,1,0:T(8,128)(2,1)S(1)}, bf16[2,680,1024]{2,1,0:T(8,128)(2,1)S(1)}) custom-call(bf16[2,680,3072]{2,1,0:T(8,128)(2,1)} %bitcast.84, bf16[680,128]{1,0:T(8,128)(2,1)S(1)} %copy-done.28, bf16[680,128]{1,0:T(8,128)(2,1)S(1)} %copy-done.19), custom_call_target="tpu_custom_call" | custom-call | flops 1024 | bytes 1024 | tf_op jit(solution)/shard_map/attend/pallas_call | solution.py:385
  148.3 1.5 copy-done.7
  149.9 1.5 copy-done.14
  151.9 2.3 collective-permute-done.30.refs_15_.refs_25_
  155.1 5.0 all-gather.2.cloned.1.call-done.refs_27_
  160.1 78.6 %block.1 = (bf16[1360,1024]{1,0:T(8,128)(2,1)}, bf16[1360,1024]{1,0:T(8,128)(2,1)}, bf16[1360,4096]{1,0:T(8,128)(2,1)}, bf16[1360,1024]{1,0:T(8,128)(2,1)}, bf16...) custom-call(s32[4]{0:T(128)} %pad_add_fusion.place_ref, ...), custom_call_target="tpu_custom_call" | custom-call | flops 1024 | bytes 1024 | tf_op jit(solution)/shard_map/block/pallas_call | solution.py:577
  238.7 9.6 %outer.4 = bf16[4096,512]{1,0:T(8,128)(2,1)S(1)} custom-call(s32[1]{0:T(128)} %bitcast.22.half_ref, bf16[1360,4096]{1,0:T(8,128)(2,1)} %get-tuple-element.169.left_ref, bf16[1360,1024]{1,0:T(8,128)(2,1)} %get-tuple-element.171.right_ref), custom_call_target="tpu_custom_call" | custom-call | flops 1024 | bytes 1024 | tf_op jit(solution)/shard_map/outer/pallas_call | solution.py:708
  248.6 9.6 %outer.5.refs_0_.refs_2_.refs_3_.refs_4_.refs_10_.refs_16_.refs_6_ = bf16[4096,512]{1,0:T(8,128)(2,1)S(1)} custom-call(s32[1]{0:T(128)} %bitcast.1.half_ref, bf16[1360,4096]{1,0:T(8,128)(2,1)} %get-tuple-element.169.left_ref, bf16[1360,1024]{1,0:T(8,128)(2,1)} %get-tuple-element.171.right_ref), custom_call_target="tpu_custom_call" | custom-call | flops 1024 | bytes 1024 | tf_op jit(solution)/shard_map/outer/pallas_call | solution.py:708
  263.0 29.0 %attend_back.2 = (bf16[2,680,1536]{2,1,0:T(8,128)(2,1)S(1)}, f32[2,1,512]{2,1,0:T(1,128)S(1)}) custom-call(bf16[2,680,3072]{2,1,0:T(8,128)(2,1)} %bitcast.85, bf16[2,680,1024]{2,1,0:T(8,128)(2,1)} %copy-done.14, bf16[680,128]{1,0:T(8,128)(2,1)S(1)} %copy-done.19, bf16[2,680,1024]{2,1,0:T(8,128)(2,1)} %copy-done.7, bf16[2,680,1024]{2,1,0:T(8,128)(2,1)} %bitcast.89, ...), custom_call_target="tpu_custom_call" | custom-call | flops 1024 | bytes 1024 | tf_op jit(solution)/shard_map/attend_back/pallas_call | solution.py:464
  292.1 3.2 sums_b.1
  296.8 9.8 %outer.6 = bf16[1024,2048]{1,0:T(8,128)(2,1)S(1)} custom-call(s32[1]{0:T(128)} %bitcast.22.half_ref, bf16[1360,1024]{1,0:T(8,128)(2,1)} %get-tuple-element.184.left_ref, bf16[1360,4096]{1,0:T(8,128)(2,1)} %get-tuple-element.195.right_ref), custom_call_target="tpu_custom_call" | custom-call | flops 1024 | bytes 1024 | tf_op jit(solution)/shard_map/outer/pallas_call | solution.py:708
  308.8 2.0 collective-permute-start.37
  310.9 9.8 %outer.7.refs_0_.refs_2_.refs_3_.refs_6_.refs_12_ = bf16[1024,2048]{1,0:T(8,128)(2,1)S(1)} custom-call(s32[1]{0:T(128)} %bitcast.1.half_ref, bf16[1360,1024]{1,0:T(8,128)(2,1)} %get-tuple-element.184.left_ref, bf16[1360,4096]{1,0:T(8,128)(2,1)} %get-tuple-element.195.right_ref), custom_call_target="tpu_custom_call" | custom-call | flops 1024 | bytes 1024 | tf_op jit(solution)/shard_map/outer/pallas_call | solution.py:708
  320.7 5.1 sums_c.1
  327.3 2.9 collective-permute-start.40
  331.4 29.0 %attend_back.3 = (bf16[2,680,1536]{2,1,0:T(8,128)(2,1)S(1)}, f32[2,1,512]{2,1,0:T(1,128)S(1)}) custom-call(bf16[2,680,3072]{2,1,0:T(8,128)(2,1)} %bitcast.86, bf16[2,680,1024]{2,1,0:T(8,128)(2,1)} %copy-done.14, bf16[680,128]{1,0:T(8,128)(2,1)S(1)} %copy-done.19, bf16[2,680,1024]{2,1,0:T(8,128)(2,1)} %copy-done.7, bf16[2,680,1024]{2,1,0:T(8,128)(2,1)} %bitcast.90, ...), custom_call_target="tpu_custom_call" | custom-call | flops 1024 | bytes 1024 | tf_op jit(solution)/shard_map/attend_back/pallas_call | solution.py:464
  360.4 1.9 copy-done.9
  362.4 2.9 sums_d.1
  365.9 1.4 collective-permute-start.45
  367.2 2.0 collective-permute-start.46
  369.2 12.5 %outer_joint.2 = bf16[1024,2048]{1,0:T(8,128)(2,1)S(1)} custom-call(s32[1]{0:T(128)} %bitcast.22.half_ref, bf16[1360,1024]{1,0:T(8,128)(2,1)} %get-tuple-element.216.left_ref, bf16[1360,1024]{1,0:T(8,128)(2,1)} %bitcast.76, bf16[1360,1536]{1,0:T(8,128)(2,1)} %bitcast.78, bf16[1360,1536]{1,0:T(8,128)(2,1)} %bitcast.81, ...), custom_call_target="tpu_custom_call" | custom-call | flops 1024 | bytes 1024 | tf_op jit(solution)/shard_map/outer_joint/pallas_call | solution.py:742
  381.7 1.7 collective-permute-done.45.refs_1_
  383.4 2.4 collective-permute-start.47
  385.9 12.7 %outer_joint.3.refs_18_.refs_20_.refs_0_.refs_3_.refs_6_.refs_12_ = bf16[1024,2048]{1,0:T(8,128)(2,1)S(1)} custom-call(s32[1]{0:T(128)} %bitcast.1.half_ref, bf16[1360,1024]{1,0:T(8,128)(2,1)} %get-tuple-element.216.left_ref, bf16[1360,1024]{1,0:T(8,128)(2,1)} %bitcast.77, bf16[1360,1536]{1,0:T(8,128)(2,1)} %bitcast.79, bf16[1360,1536]{1,0:T(8,128)(2,1)} %bitcast.82, ...), custom_call_target="tpu_custom_call" | custom-call | flops 1024 | bytes 1024 | tf_op jit(solution)/shard_map/outer_joint/pallas_call | solution.py:742
  398.7 5.9 %sums_e.1 = (bf16[128,1024]{1,0:T(8,128)(2,1)}, bf16[128,1024]{1,0:T(8,128)(2,1)}, bf16[128,1024]{1,0:T(8,128)(2,1)}, bf16[512,1024]{1,0:T(8,128)(2,1)}, bf16[256,2048]{1,0:T(8,128)(2,1)}) custom-call(s32[4]{0:T(128)S(1)} %copy-done.29, bf16[1024,2048]{1,0:T(8,128)(2,1)} %copy-done.3, bf16[1024,2048]{1,0:T(8,128)(2,1)} %copy-done.6, ...), custom_call_target="tpu_custom_call" | custom-call | flops 1024 | bytes 1024 | tf_op jit(solution)/shard_map/sums_e/pallas_call | solution.py:159
  405.9 2.4 collective-permute-start.51
  409.7 20.7 %token_back.1 = (bf16[1360,1024]{1,0:T(8,128)(2,1)}, f32[16,1024]{1,0:T(8,128)}) custom-call(s32[4]{0:T(128)} %pad_add_fusion.place_ref, s32[2]{0:T(128)} %fusion.19.lengths_ref, bf16[1360,1536]{1,0:T(8,128)(2,1)} %bitcast.80, bf16[1360,1536]{1,0:T(8,128)(2,1)} %bitcast.83, bf16[1360,1024]{1,0:T(8,128)(2,1)} %refs_2_.3, ...), custom_call_target="tpu_custom_call" | custom-call | flops 1024 | bytes 1024 | tf_op jit(solution)/shard_map/token_back/pallas_call | solution.py:577
  430.5 1.6 collective-permute-done.53.refs_14_
  433.0 4.0 sums_f.1
  443.5 8.8 %collective-permute-done.54.refs_3_.refs_9_.refs_15_ = bf16[256,1024]{1,0:T(8,128)(2,1)S(1)} collective-permute-done((bf16[256,1024]{1,0:T(8,128)(2,1)}, bf16[256,1024]{1,0:T(8,128)(2,1)S(1)}, u32[]{:S(2)}, u32[]{:S(2)}) %collective-permute-start.54) | collective-permute-done | bytes 524320 | tf_op jit(solution)/shard_map/ppermute | solution.py:62
  452.4 3.6 sums_g.1
  465.3 1.7 reshape.105
  467.1 1.4 fusion.2
  468.5 1.7 collective-permute-start.60
  471.6 5.7 %collective-permute-start.74 = (bf16[128,1024]{1,0:T(8,128)(2,1)}, bf16[128,1024]{1,0:T(8,128)(2,1)}, u32[]{:S(2)}, u32[]{:S(2)}) collective-permute-start(bf16[128,1024]{1,0:T(8,128)(2,1)} %get-tuple-element.281.refs_0_), channel_id=1, source_target_pairs={{0,8},{1,9},{2,10},{3,11},{4,12},{5,13},{6,14},{7,15},{8,0},{9,1},... | collective-permute-start | bytes 786440 | tf_op jit(solution)/shard_map/ppermute | solution.py:62
  482.1 2.0 lay_out_fc2.1
  484.1 2.6 collective-permute-start.67
  487.8 2.7 lay_out_fc1.1
  490.5 3.5 collective-permute-start.64
  494.0 1.7 stack_reshape.3
  497.3 4.3 collective-permute-start.66
  502.3 8.0 %collective-permute-done.69.refs_8_ = bf16[128,1024]{1,0:T(8,128)(2,1)} collective-permute-done((bf16[128,1024]{1,0:T(8,128)(2,1)}, bf16[128,1024]{1,0:T(8,128)(2,1)}, u32[]{:S(2)}, u32[]{:S(2)}) %collective-permute-start.69) | collective-permute-done | bytes 262176 | tf_op jit(solution)/shard_map/ppermute | solution.py:62
  511.3 2.2 sums_h.1.refs_0_
  513.5 1.4 collective-permute-start.70
  514.9 2.4 collective-permute-start.71
  519.3 2.3 fusion
  521.6 5.7 %collective-permute-done.72.refs_3_ = bf16[128,1024]{1,0:T(8,128)(2,1)S(1)} collective-permute-done((bf16[128,1024]{1,0:T(8,128)(2,1)S(1)}, bf16[128,1024]{1,0:T(8,128)(2,1)S(1)}, u32[]{:S(2)}, u32[]{:S(2)}) %collective-permute-start.72) | collective-permute-done | bytes 262176 | tf_op jit(solution)/shard_map/ppermute | solution.py:62
  527.2 2.1 lay_out_last.1
  (291 shorter events, 76.6 us)
Async XLA Ops:
  7.2 152.9 %all-gather.2.cloned.1.call-start = ((), (), s32[]{:S(2)}) async-start(), calls=%async_computation | async-start | bytes 8650752 | tf_op jit(solution)/shard_map/all_gather | solution.py:814
  8.1 6.1 %collective-permute-start.2 = (bf16[2,1024]{1,0:T(2,128)(2,1)S(1)}, bf16[2,1024]{1,0:T(2,128)(2,1)S(1)}, u32[]{:S(2)}, u32[]{:S(2)}) collective-permute-start(bf16[2,1024]{1,0:T(2,128)(2,1)S(1)} %fusion.12), channel_id=1, source_target_pairs={{0,6},{1,7},{2,4},{3,5},{4,2},{5,3},{6,0},{7,1},{8,14},{9,15},{10,... | collective-permute-start | bytes 12296 | tf_op jit(solution)/shard_map/ppermute | solution.py:62
  15.0 5.1 collective-permute-start.6
  17.3 4.8 collective-permute-start.3
  17.4 9.2 %collective-permute-start.4 = (bf16[128,768]{1,0:T(8,128)(2,1)S(1)}, bf16[128,768]{1,0:T(8,128)(2,1)S(1)}, u32[]{:S(2)}, u32[]{:S(2)}) collective-permute-start(bf16[128,768]{1,0:T(8,128)(2,1)S(1)} %copy.46), channel_id=1, source_target_pairs={{0,4},{1,5},{2,6},{3,7},{4,0},{5,1},{6,2},{7,3},{8,12},{9,13},{10,... | collective-permute-start | bytes 589832 | tf_op jit(solution)/shard_map/ppermute | solution.py:62
  19.1 16.6 %collective-permute-start.5 = (bf16[128,768]{1,0:T(8,128)(2,1)S(1)}, bf16[128,768]{1,0:T(8,128)(2,1)}, u32[]{:S(2)}, u32[]{:S(2)}) collective-permute-start(bf16[128,768]{1,0:T(8,128)(2,1)S(1)} %copy.46), channel_id=1, source_target_pairs={{0,6},{1,7},{2,4},{3,5},{4,2},{5,3},{6,0},{7,1},{8,14},{9,15},{10,... | collective-permute-start | bytes 589832 | tf_op jit(solution)/shard_map/ppermute | solution.py:62
  21.0 15.8 %collective-permute-start.7 = (f32[4,2,6144]{2,1,0:T(2,128)S(1)}, f32[4,2,6144]{2,1,0:T(2,128)S(1)}, u32[]{:S(2)}, u32[]{:S(2)}) collective-permute-start(f32[4,2,6144]{2,1,0:T(2,128)S(1)} %dynamic-slice_bitcast_fusion), channel_id=1, source_target_pairs={{0,1},{1,0},{2,3},{3,2},{4,5},{5,4},{6,7},{7,6},{8,9},{9,8},{10,11... | collective-permute-start | bytes 589832 | tf_op jit(solution)/shard_map/ppermute | solution.py:62
  36.9 4.8 collective-permute-start.10
  40.2 15.2 %collective-permute-start.14 = (bf16[512,768]{1,0:T(8,128)(2,1)S(1)}, bf16[512,768]{1,0:T(8,128)(2,1)S(1)}, u32[]{:S(2)}, u32[]{:S(2)}) collective-permute-start(bf16[512,768]{1,0:T(8,128)(2,1)S(1)} %pad_maximum_fusion.3.refs_4_.refs_5_), channel_id=1, source_target_pairs={{0,1},{1,0},{2,3},{3,2},{4,5},{5,4},{6,7},{7,6},{8,9},{9,8},{10,11... | collective-permute-start | bytes 2359304 | tf_op jit(solution)/shard_map/ppermute | solution.py:62
  40.5 16.2 %collective-permute-start.16 = (bf16[512,768]{1,0:T(8,128)(2,1)S(1)}, bf16[512,768]{1,0:T(8,128)(2,1)S(1)}, u32[]{:S(2)}, u32[]{:S(2)}) collective-permute-start(bf16[512,768]{1,0:T(8,128)(2,1)S(1)} %pad_maximum_fusion.3.refs_4_.refs_5_), channel_id=1, source_target_pairs={{0,16},{1,17},{2,18},{3,19},{4,20},{5,21},{6,22},{7,23},{8,24},{9,... | collective-permute-start | bytes 2359304 | tf_op jit(solution)/shard_map/ppermute | solution.py:62
  42.8 14.3 %collective-permute-start.11 = (bf16[128,1280]{1,0:T(8,128)(2,1)S(1)}, bf16[128,1280]{1,0:T(8,128)(2,1)S(1)}, u32[]{:S(2)}, u32[]{:S(2)}) collective-permute-start(bf16[128,1280]{1,0:T(8,128)(2,1)S(1)} %pad_maximum_fusion.4), channel_id=1, source_target_pairs={{0,2},{1,3},{2,0},{3,1},{4,6},{5,7},{6,4},{7,5},{8,10},{9,11},{10,... | collective-permute-start | bytes 983048 | tf_op jit(solution)/shard_map/ppermute | solution.py:62
  45.2 11.9 %collective-permute-start.12 = (bf16[128,1280]{1,0:T(8,128)(2,1)S(1)}, bf16[128,1280]{1,0:T(8,128)(2,1)S(1)}, u32[]{:S(2)}, u32[]{:S(2)}) collective-permute-start(bf16[128,1280]{1,0:T(8,128)(2,1)S(1)} %pad_maximum_fusion.4), channel_id=1, source_target_pairs={{0,4},{1,5},{2,6},{3,7},{4,0},{5,1},{6,2},{7,3},{8,12},{9,13},{10,... | collective-permute-start | bytes 983048 | tf_op jit(solution)/shard_map/ppermute | solution.py:62
  45.2 28.1 %collective-permute-start.13 = (bf16[128,1280]{1,0:T(8,128)(2,1)S(1)}, bf16[128,1280]{1,0:T(8,128)(2,1)S(1)}, u32[]{:S(2)}, u32[]{:S(2)}) collective-permute-start(bf16[128,1280]{1,0:T(8,128)(2,1)S(1)} %pad_maximum_fusion.4), channel_id=1, source_target_pairs={{0,6},{1,7},{2,4},{3,5},{4,2},{5,3},{6,0},{7,1},{8,14},{9,15},{10,... | collective-permute-start | bytes 983048 | tf_op jit(solution)/shard_map/ppermute | solution.py:62
  55.4 19.0 %collective-permute-start.15 = (bf16[256,768]{1,0:T(8,128)(2,1)S(1)}, bf16[256,768]{1,0:T(8,128)(2,1)S(1)}, u32[]{:S(2)}, u32[]{:S(2)}) collective-permute-start(bf16[256,768]{1,0:T(8,128)(2,1)S(1)} %slice.102), channel_id=1, source_target_pairs={{0,16},{1,17},{2,18},{3,19},{4,20},{5,21},{6,22},{7,23},{8,24},{9,... | collective-permute-start | bytes 1179656 | tf_op jit(solution)/shard_map/ppermute | solution.py:62
  56.8 17.7 %collective-permute-start.17 = (bf16[256,768]{1,0:T(8,128)(2,1)S(1)}, bf16[256,768]{1,0:T(8,128)(2,1)}, u32[]{:S(2)}, u32[]{:S(2)}) collective-permute-start(bf16[256,768]{1,0:T(8,128)(2,1)S(1)} %slice.103), channel_id=1, source_target_pairs={{0,1},{1,0},{2,3},{3,2},{4,5},{5,4},{6,7},{7,6},{8,9},{9,8},{10,11... | collective-permute-start | bytes 1179656 | tf_op jit(solution)/shard_map/ppermute | solution.py:62
  79.1 35.5 %collective-permute-start.18 = (bf16[512,1280]{1,0:T(8,128)(2,1)S(1)}, bf16[512,1280]{1,0:T(8,128)(2,1)}, u32[]{:S(2)}, u32[]{:S(2)}) collective-permute-start(bf16[512,1280]{1,0:T(8,128)(2,1)S(1)} %pad_maximum_fusion.refs_7_.refs_17_), channel_id=1, source_target_pairs={{0,1},{1,0},{2,3},{3,2},{4,5},{5,4},{6,7},{7,6},{8,9},{9,8},{10,11... | collective-permute-start | bytes 3932168 | tf_op jit(solution)/shard_map/ppermute | solution.py:62
  79.5 35.1 %collective-permute-start.19 = (bf16[512,1280]{1,0:T(8,128)(2,1)S(1)}, bf16[512,1280]{1,0:T(8,128)(2,1)}, u32[]{:S(2)}, u32[]{:S(2)}) collective-permute-start(bf16[512,1280]{1,0:T(8,128)(2,1)S(1)} %pad_maximum_fusion.refs_7_.refs_17_), channel_id=1, source_target_pairs={{0,16},{1,17},{2,18},{3,19},{4,20},{5,21},{6,22},{7,23},{8,24},{9,... | collective-permute-start | bytes 3932168 | tf_op jit(solution)/shard_map/ppermute | solution.py:62
  81.6 6.7 %collective-permute-start.21 = (bf16[512,768]{1,0:T(8,128)(2,1)}, bf16[512,768]{1,0:T(8,128)(2,1)}, u32[]{:S(2)}, u32[]{:S(2)}) collective-permute-start(bf16[512,768]{1,0:T(8,128)(2,1)} %copy-done.36), channel_id=1, source_target_pairs={{0,8},{1,9},{2,10},{3,11},{4,12},{5,13},{6,14},{7,15},{8,0},{9,1},... | collective-permute-start | bytes 2359304 | tf_op jit(solution)/shard_map/ppermute | solution.py:62
  81.6 6.7 %collective-permute-start.22 = (bf16[512,768]{1,0:T(8,128)(2,1)}, bf16[512,768]{1,0:T(8,128)(2,1)}, u32[]{:S(2)}, u32[]{:S(2)}) collective-permute-start(bf16[512,768]{1,0:T(8,128)(2,1)} %copy-done.37), channel_id=1, source_target_pairs={{0,8},{1,9},{2,10},{3,11},{4,12},{5,13},{6,14},{7,15},{8,0},{9,1},... | collective-permute-start | bytes 2359304 | tf_op jit(solution)/shard_map/ppermute | solution.py:62
  115.7 35.6 %collective-permute-start.25 = (bf16[256,1280]{1,0:T(8,128)(2,1)S(1)}, bf16[256,1280]{1,0:T(8,128)(2,1)}, u32[]{:S(2)}, u32[]{:S(2)}) collective-permute-start(bf16[256,1280]{1,0:T(8,128)(2,1)S(1)} %slice.82), channel_id=1, source_target_pairs={{0,16},{1,17},{2,18},{3,19},{4,20},{5,21},{6,22},{7,23},{8,24},{9,... | collective-permute-start | bytes 1966088 | tf_op jit(solution)/shard_map/ppermute | solution.py:62
  118.5 32.9 %collective-permute-start.26 = (bf16[256,1280]{1,0:T(8,128)(2,1)S(1)}, bf16[256,1280]{1,0:T(8,128)(2,1)}, u32[]{:S(2)}, u32[]{:S(2)}) collective-permute-start(bf16[256,1280]{1,0:T(8,128)(2,1)S(1)} %slice.83), channel_id=1, source_target_pairs={{0,1},{1,0},{2,3},{3,2},{4,5},{5,4},{6,7},{7,6},{8,9},{9,8},{10,11... | collective-permute-start | bytes 1966088 | tf_op jit(solution)/shard_map/ppermute | solution.py:62
  119.7 32.2 %collective-permute-start.27 = (bf16[512,1280]{1,0:T(8,128)(2,1)S(1)}, bf16[512,1280]{1,0:T(8,128)(2,1)}, u32[]{:S(2)}, u32[]{:S(2)}) collective-permute-start(bf16[512,1280]{1,0:T(8,128)(2,1)S(1)} %pad_maximum_fusion.refs_7_.refs_17_), channel_id=1, source_target_pairs={{0,8},{1,9},{2,10},{3,11},{4,12},{5,13},{6,14},{7,15},{8,0},{9,1},... | collective-permute-start | bytes 3932168 | tf_op jit(solution)/shard_map/ppermute | solution.py:62
  121.9 33.2 %collective-permute-start.28 = (bf16[512,1280]{1,0:T(8,128)(2,1)}, bf16[512,1280]{1,0:T(8,128)(2,1)}, u32[]{:S(2)}, u32[]{:S(2)}) collective-permute-start(bf16[512,1280]{1,0:T(8,128)(2,1)} %collective-permute-done.18.refs_8_.refs_18_), channel_id=1, source_target_pairs={{0,8},{1,9},{2,10},{3,11},{4,12},{5,13},{6,14},{7,15},{8,0},{9,1},... | collective-permute-start | bytes 3932168 | tf_op jit(solution)/shard_map/ppermute | solution.py:62
  121.9 33.2 %collective-permute-start.29 = (bf16[512,1280]{1,0:T(8,128)(2,1)}, bf16[512,1280]{1,0:T(8,128)(2,1)}, u32[]{:S(2)}, u32[]{:S(2)}) collective-permute-start(bf16[512,1280]{1,0:T(8,128)(2,1)} %collective-permute-done.19.refs_9_.refs_19_), channel_id=1, source_target_pairs={{0,8},{1,9},{2,10},{3,11},{4,12},{5,13},{6,14},{7,15},{8,0},{9,1},... | collective-permute-start | bytes 3932168 | tf_op jit(solution)/shard_map/ppermute | solution.py:62
  248.3 9.9 %collective-permute-start.32 = (bf16[4096,512]{1,0:T(8,128)(2,1)S(1)}, bf16[4096,512]{1,0:T(8,128)(2,1)S(1)}, u32[]{:S(2)}, u32[]{:S(2)}) collective-permute-start(bf16[4096,512]{1,0:T(8,128)(2,1)S(1)} %outer.4), channel_id=1, source_target_pairs={{0,8},{1,9},{2,10},{3,11},{4,12},{5,13},{6,14},{7,15},{8,0},{9,1},... | collective-permute-start | bytes 12582920 | tf_op jit(solution)/shard_map/ppermute | solution.py:62
  261.6 30.5 %collective-permute-start.33 = (bf16[2048,256]{1,0:T(8,128)(2,1)S(1)}, bf16[2048,256]{1,0:T(8,128)(2,1)S(1)}, u32[]{:S(2)}, u32[]{:S(2)}) collective-permute-start(bf16[2048,256]{1,0:T(8,128)(2,1)S(1)} %get-tuple-element.181), channel_id=1, source_target_pairs={{0,16},{1,17},{2,18},{3,19},{4,20},{5,21},{6,22},{7,23},{8,24},{9,... | collective-permute-start | bytes 3145736 | tf_op jit(solution)/shard_map/ppermute | solution.py:62
  262.8 29.3 %collective-permute-start.34 = (bf16[1024,512]{1,0:T(8,128)(2,1)S(1)}, bf16[1024,512]{1,0:T(8,128)(2,1)S(1)}, u32[]{:S(2)}, u32[]{:S(2)}) collective-permute-start(bf16[1024,512]{1,0:T(8,128)(2,1)S(1)} %get-tuple-element.182), channel_id=1, source_target_pairs={{0,1},{1,0},{2,3},{3,2},{4,5},{5,4},{6,7},{7,6},{8,9},{9,8},{10,11... | collective-permute-start | bytes 3145736 | tf_op jit(solution)/shard_map/ppermute | solution.py:62
  295.3 12.7 %collective-permute-start.35 = (bf16[1024,256]{1,0:T(8,128)(2,1)S(1)}, bf16[1024,256]{1,0:T(8,128)(2,1)S(1)}, u32[]{:S(2)}, u32[]{:S(2)}) collective-permute-start(bf16[1024,256]{1,0:T(8,128)(2,1)S(1)} %get-tuple-element.192), channel_id=1, source_target_pairs={{0,1},{1,0},{2,3},{3,2},{4,5},{5,4},{6,7},{7,6},{8,9},{9,8},{10,11... | collective-permute-start | bytes 1572872 | tf_op jit(solution)/shard_map/ppermute | solution.py:62
  296.5 12.3 %collective-permute-start.36 = (bf16[1024,256]{1,0:T(8,128)(2,1)S(1)}, bf16[1024,256]{1,0:T(8,128)(2,1)S(1)}, u32[]{:S(2)}, u32[]{:S(2)}) collective-permute-start(bf16[1024,256]{1,0:T(8,128)(2,1)S(1)} %get-tuple-element.193), channel_id=1, source_target_pairs={{0,16},{1,17},{2,18},{3,19},{4,20},{5,21},{6,22},{7,23},{8,24},{9,... | collective-permute-start | bytes 1572872 | tf_op jit(solution)/shard_map/ppermute | solution.py:62
  308.8 11.9 %collective-permute-start.37 = (bf16[1024,2048]{1,0:T(8,128)(2,1)S(1)}, bf16[1024,2048]{1,0:T(8,128)(2,1)S(1)}, u32[]{:S(2)}, u32[]{:S(2)}) collective-permute-start(bf16[1024,2048]{1,0:T(8,128)(2,1)S(1)} %outer.6), channel_id=1, source_target_pairs={{0,8},{1,9},{2,10},{3,11},{4,12},{5,13},{6,14},{7,15},{8,0},{9,1},... | collective-permute-start | bytes 12582920 | tf_op jit(solution)/shard_map/ppermute | solution.py:62
  325.8 36.6 %collective-permute-start.38 = (bf16[512,1024]{1,0:T(8,128)(2,1)S(1)}, bf16[512,1024]{1,0:T(8,128)(2,1)S(1)}, u32[]{:S(2)}, u32[]{:S(2)}) collective-permute-start(bf16[512,1024]{1,0:T(8,128)(2,1)S(1)} %get-tuple-element.209), channel_id=1, source_target_pairs={{0,16},{1,17},{2,18},{3,19},{4,20},{5,21},{6,22},{7,23},{8,24},{9,... | collective-permute-start | bytes 3145736 | tf_op jit(solution)/shard_map/ppermute | solution.py:62
  326.2 36.2 %collective-permute-start.39 = (bf16[256,2048]{1,0:T(8,128)(2,1)S(1)}, bf16[256,2048]{1,0:T(8,128)(2,1)S(1)}, u32[]{:S(2)}, u32[]{:S(2)}) collective-permute-start(bf16[256,2048]{1,0:T(8,128)(2,1)S(1)} %get-tuple-element.210), channel_id=1, source_target_pairs={{0,1},{1,0},{2,3},{3,2},{4,5},{5,4},{6,7},{7,6},{8,9},{9,8},{10,11... | collective-permute-start | bytes 3145736 | tf_op jit(solution)/shard_map/ppermute | solution.py:62
  327.3 35.1 %collective-permute-start.40 = (bf16[512,256]{1,0:T(8,128)(2,1)S(1)}, bf16[512,256]{1,0:T(8,128)(2,1)S(1)}, u32[]{:S(2)}, u32[]{:S(2)}) collective-permute-start(bf16[512,256]{1,0:T(8,128)(2,1)S(1)} %get-tuple-element.211), channel_id=1, source_target_pairs={{0,2},{1,3},{2,0},{3,1},{4,6},{5,7},{6,4},{7,5},{8,10},{9,11},{10,... | collective-permute-start | bytes 786440 | tf_op jit(solution)/shard_map/ppermute | solution.py:62
  330.2 32.2 %collective-permute-start.41 = (bf16[512,256]{1,0:T(8,128)(2,1)S(1)}, bf16[512,256]{1,0:T(8,128)(2,1)S(1)}, u32[]{:S(2)}, u32[]{:S(2)}) collective-permute-start(bf16[512,256]{1,0:T(8,128)(2,1)S(1)} %get-tuple-element.212), channel_id=1, source_target_pairs={{0,4},{1,5},{2,6},{3,7},{4,0},{5,1},{6,2},{7,3},{8,12},{9,13},{10,... | collective-permute-start | bytes 786440 | tf_op jit(solution)/shard_map/ppermute | solution.py:62
  330.2 32.2 %collective-permute-start.42 = (bf16[512,256]{1,0:T(8,128)(2,1)S(1)}, bf16[512,256]{1,0:T(8,128)(2,1)S(1)}, u32[]{:S(2)}, u32[]{:S(2)}) collective-permute-start(bf16[512,256]{1,0:T(8,128)(2,1)S(1)} %get-tuple-element.213), channel_id=1, source_target_pairs={{0,6},{1,7},{2,4},{3,5},{4,2},{5,3},{6,0},{7,1},{8,14},{9,15},{10,... | collective-permute-start | bytes 786440 | tf_op jit(solution)/shard_map/ppermute | solution.py:62
  365.4 18.0 %collective-permute-start.43 = (bf16[256,1024]{1,0:T(8,128)(2,1)S(1)}, bf16[256,1024]{1,0:T(8,128)(2,1)S(1)}, u32[]{:S(2)}, u32[]{:S(2)}) collective-permute-start(bf16[256,1024]{1,0:T(8,128)(2,1)S(1)} %get-tuple-element.227), channel_id=1, source_target_pairs={{0,1},{1,0},{2,3},{3,2},{4,5},{5,4},{6,7},{7,6},{8,9},{9,8},{10,11... | collective-permute-start | bytes 1572872 | tf_op jit(solution)/shard_map/ppermute | solution.py:62
  365.8 17.6 %collective-permute-start.44 = (bf16[256,1024]{1,0:T(8,128)(2,1)S(1)}, bf16[256,1024]{1,0:T(8,128)(2,1)S(1)}, u32[]{:S(2)}, u32[]{:S(2)}) collective-permute-start(bf16[256,1024]{1,0:T(8,128)(2,1)S(1)} %get-tuple-element.228), channel_id=1, source_target_pairs={{0,16},{1,17},{2,18},{3,19},{4,20},{5,21},{6,22},{7,23},{8,24},{9,... | collective-permute-start | bytes 1572872 | tf_op jit(solution)/shard_map/ppermute | solution.py:62
  365.9 17.5 %collective-permute-start.45 = (bf16[512,256]{1,0:T(8,128)(2,1)S(1)}, bf16[512,256]{1,0:T(8,128)(2,1)S(1)}, u32[]{:S(2)}, u32[]{:S(2)}) collective-permute-start(bf16[512,256]{1,0:T(8,128)(2,1)S(1)} %get-tuple-element.230.refs_0_), channel_id=1, source_target_pairs={{0,16},{1,17},{2,18},{3,19},{4,20},{5,21},{6,22},{7,23},{8,24},{9,... | collective-permute-start | bytes 786440 | tf_op jit(solution)/shard_map/ppermute | solution.py:62
  367.2 16.2 %collective-permute-start.46 = (bf16[512,256]{1,0:T(8,128)(2,1)S(1)}, bf16[512,256]{1,0:T(8,128)(2,1)S(1)}, u32[]{:S(2)}, u32[]{:S(2)}) collective-permute-start(bf16[512,256]{1,0:T(8,128)(2,1)S(1)} %get-tuple-element.230.refs_0_), channel_id=1, source_target_pairs={{0,8},{1,9},{2,10},{3,11},{4,12},{5,13},{6,14},{7,15},{8,0},{9,1},... | collective-permute-start | bytes 786440 | tf_op jit(solution)/shard_map/ppermute | solution.py:62
  383.4 15.2 %collective-permute-start.47 = (bf16[1024,2048]{1,0:T(8,128)(2,1)S(1)}, bf16[1024,2048]{1,0:T(8,128)(2,1)S(1)}, u32[]{:S(2)}, u32[]{:S(2)}) collective-permute-start(bf16[1024,2048]{1,0:T(8,128)(2,1)S(1)} %outer_joint.2), channel_id=1, source_target_pairs={{0,8},{1,9},{2,10},{3,11},{4,12},{5,13},{6,14},{7,15},{8,0},{9,1},... | collective-permute-start | bytes 12582920 | tf_op jit(solution)/shard_map/ppermute | solution.py:62
  385.8 12.8 %collective-permute-start.48 = (bf16[512,256]{1,0:T(8,128)(2,1)S(1)}, bf16[512,256]{1,0:T(8,128)(2,1)S(1)}, u32[]{:S(2)}, u32[]{:S(2)}) collective-permute-start(bf16[512,256]{1,0:T(8,128)(2,1)S(1)} %collective-permute-done.45.refs_1_), channel_id=1, source_target_pairs={{0,8},{1,9},{2,10},{3,11},{4,12},{5,13},{6,14},{7,15},{8,0},{9,1},... | collective-permute-start | bytes 786440 | tf_op jit(solution)/shard_map/ppermute | solution.py:62
  404.6 27.4 %collective-permute-start.49 = (bf16[512,1024]{1,0:T(8,128)(2,1)}, bf16[512,1024]{1,0:T(8,128)(2,1)S(1)}, u32[]{:S(2)}, u32[]{:S(2)}) collective-permute-start(bf16[512,1024]{1,0:T(8,128)(2,1)} %get-tuple-element.249), channel_id=1, source_target_pairs={{0,16},{1,17},{2,18},{3,19},{4,20},{5,21},{6,22},{7,23},{8,24},{9,... | collective-permute-start | bytes 3145736 | tf_op jit(solution)/shard_map/ppermute | solution.py:62
  404.8 27.3 %collective-permute-start.50 = (bf16[256,2048]{1,0:T(8,128)(2,1)}, bf16[256,2048]{1,0:T(8,128)(2,1)}, u32[]{:S(2)}, u32[]{:S(2)}) collective-permute-start(bf16[256,2048]{1,0:T(8,128)(2,1)} %get-tuple-element.250), channel_id=1, source_target_pairs={{0,1},{1,0},{2,3},{3,2},{4,5},{5,4},{6,7},{7,6},{8,9},{9,8},{10,11... | collective-permute-start | bytes 3145736 | tf_op jit(solution)/shard_map/ppermute | solution.py:62
  405.9 24.5 %collective-permute-start.51 = (bf16[128,1024]{1,0:T(8,128)(2,1)}, bf16[128,1024]{1,0:T(8,128)(2,1)S(1)}, u32[]{:S(2)}, u32[]{:S(2)}) collective-permute-start(bf16[128,1024]{1,0:T(8,128)(2,1)} %get-tuple-element.251), channel_id=1, source_target_pairs={{0,2},{1,3},{2,0},{3,1},{4,6},{5,7},{6,4},{7,5},{8,10},{9,11},{10,... | collective-permute-start | bytes 786440 | tf_op jit(solution)/shard_map/ppermute | solution.py:62
  408.3 22.2 %collective-permute-start.52 = (bf16[128,1024]{1,0:T(8,128)(2,1)}, bf16[128,1024]{1,0:T(8,128)(2,1)}, u32[]{:S(2)}, u32[]{:S(2)}) collective-permute-start(bf16[128,1024]{1,0:T(8,128)(2,1)} %get-tuple-element.252), channel_id=1, source_target_pairs={{0,4},{1,5},{2,6},{3,7},{4,0},{5,1},{6,2},{7,3},{8,12},{9,13},{10,... | collective-permute-start | bytes 786440 | tf_op jit(solution)/shard_map/ppermute | solution.py:62
  408.3 23.8 %collective-permute-start.53 = (bf16[128,1024]{1,0:T(8,128)(2,1)}, bf16[128,1024]{1,0:T(8,128)(2,1)}, u32[]{:S(2)}, u32[]{:S(2)}) collective-permute-start(bf16[128,1024]{1,0:T(8,128)(2,1)} %get-tuple-element.253), channel_id=1, source_target_pairs={{0,6},{1,7},{2,4},{3,5},{4,2},{5,3},{6,0},{7,1},{8,14},{9,15},{10,... | collective-permute-start | bytes 786440 | tf_op jit(solution)/shard_map/ppermute | solution.py:62
  441.4 10.9 %collective-permute-start.54 = (bf16[256,1024]{1,0:T(8,128)(2,1)}, bf16[256,1024]{1,0:T(8,128)(2,1)S(1)}, u32[]{:S(2)}, u32[]{:S(2)}) collective-permute-start(bf16[256,1024]{1,0:T(8,128)(2,1)} %copy-done.33), channel_id=1, source_target_pairs={{0,1},{1,0},{2,3},{3,2},{4,5},{5,4},{6,7},{7,6},{8,9},{9,8},{10,11... | collective-permute-start | bytes 1572872 | tf_op jit(solution)/shard_map/ppermute | solution.py:62
  441.7 10.6 %collective-permute-start.55 = (bf16[256,1024]{1,0:T(8,128)(2,1)}, bf16[256,1024]{1,0:T(8,128)(2,1)S(1)}, u32[]{:S(2)}, u32[]{:S(2)}) collective-permute-start(bf16[256,1024]{1,0:T(8,128)(2,1)} %copy-done.32), channel_id=1, source_target_pairs={{0,16},{1,17},{2,18},{3,19},{4,20},{5,21},{6,22},{7,23},{8,24},{9,... | collective-permute-start | bytes 1572872 | tf_op jit(solution)/shard_map/ppermute | solution.py:62
  457.2 20.0 %collective-permute-start.73 = (bf16[128,1024]{1,0:T(8,128)(2,1)}, bf16[128,1024]{1,0:T(8,128)(2,1)}, u32[]{:S(2)}, u32[]{:S(2)}) collective-permute-start(bf16[128,1024]{1,0:T(8,128)(2,1)} %get-tuple-element.281.refs_0_), channel_id=1, source_target_pairs={{0,16},{1,17},{2,18},{3,19},{4,20},{5,21},{6,22},{7,23},{8,24},{9,... | collective-permute-start | bytes 786440 | tf_op jit(solution)/shard_map/ppermute | solution.py:62
  468.5 8.9 %collective-permute-start.60 = (f32[1,16,128]{2,1,0:T(8,128)S(1)}, f32[1,16,128]{2,1,0:T(8,128)S(1)}, u32[]{:S(2)}, u32[]{:S(2)}) collective-permute-start(f32[1,16,128]{2,1,0:T(8,128)S(1)} %bitcast.125), channel_id=1, source_target_pairs={{0,2},{1,3},{2,0},{3,1},{4,6},{5,7},{6,4},{7,5},{8,10},{9,11},{10,... | collective-permute-start | bytes 24584 | tf_op jit(solution)/shard_map/ppermute | solution.py:62
  470.2 7.2 %collective-permute-start.61 = (f32[1,16,128]{2,1,0:T(8,128)S(1)}, f32[1,16,128]{2,1,0:T(8,128)S(1)}, u32[]{:S(2)}, u32[]{:S(2)}) collective-permute-start(f32[1,16,128]{2,1,0:T(8,128)S(1)} %bitcast.126), channel_id=1, source_target_pairs={{0,4},{1,5},{2,6},{3,7},{4,0},{5,1},{6,2},{7,3},{8,12},{9,13},{10,... | collective-permute-start | bytes 24584 | tf_op jit(solution)/shard_map/ppermute | solution.py:62
  470.2 7.2 %collective-permute-start.62 = (f32[1,16,128]{2,1,0:T(8,128)S(1)}, f32[1,16,128]{2,1,0:T(8,128)S(1)}, u32[]{:S(2)}, u32[]{:S(2)}) collective-permute-start(f32[1,16,128]{2,1,0:T(8,128)S(1)} %bitcast.127), channel_id=1, source_target_pairs={{0,6},{1,7},{2,4},{3,5},{4,2},{5,3},{6,0},{7,1},{8,14},{9,15},{10,... | collective-permute-start | bytes 24584 | tf_op jit(solution)/shard_map/ppermute | solution.py:62
  471.6 15.1 %collective-permute-start.74 = (bf16[128,1024]{1,0:T(8,128)(2,1)}, bf16[128,1024]{1,0:T(8,128)(2,1)}, u32[]{:S(2)}, u32[]{:S(2)}) collective-permute-start(bf16[128,1024]{1,0:T(8,128)(2,1)} %get-tuple-element.281.refs_0_), channel_id=1, source_target_pairs={{0,8},{1,9},{2,10},{3,11},{4,12},{5,13},{6,14},{7,15},{8,0},{9,1},... | collective-permute-start | bytes 786440 | tf_op jit(solution)/shard_map/ppermute | solution.py:62
  477.3 10.6 %collective-permute-start.75 = (bf16[128,1024]{1,0:T(8,128)(2,1)}, bf16[128,1024]{1,0:T(8,128)(2,1)}, u32[]{:S(2)}, u32[]{:S(2)}) collective-permute-start(bf16[128,1024]{1,0:T(8,128)(2,1)} %collective-permute-done.73.refs_1_), channel_id=1, source_target_pairs={{0,8},{1,9},{2,10},{3,11},{4,12},{5,13},{6,14},{7,15},{8,0},{9,1},... | collective-permute-start | bytes 786440 | tf_op jit(solution)/shard_map/ppermute | solution.py:62
  477.4 18.4 %collective-permute-start.63 = (f32[4,1,16,128]{3,2,1,0:T(8,128)S(1)}, f32[4,1,16,128]{3,2,1,0:T(8,128)S(1)}, u32[]{:S(2)}, u32[]{:S(2)}) collective-permute-start(f32[4,1,16,128]{3,2,1,0:T(8,128)S(1)} %get-tuple-element.343), channel_id=1, source_target_pairs={{0,1},{1,0},{2,3},{3,2},{4,5},{5,4},{6,7},{7,6},{8,9},{9,8},{10,11... | collective-permute-start | bytes 98312 | tf_op jit(solution)/shard_map/ppermute | solution.py:62
  484.1 13.2 %collective-permute-start.67 = (bf16[128,1024]{1,0:T(8,128)(2,1)}, bf16[128,1024]{1,0:T(8,128)(2,1)S(1)}, u32[]{:S(2)}, u32[]{:S(2)}) collective-permute-start(bf16[128,1024]{1,0:T(8,128)(2,1)} %get-tuple-element.276), channel_id=1, source_target_pairs={{0,2},{1,3},{2,0},{3,1},{4,6},{5,7},{6,4},{7,5},{8,10},{9,11},{10,... | collective-permute-start | bytes 786440 | tf_op jit(solution)/shard_map/ppermute | solution.py:62
  486.6 15.6 %collective-permute-start.68 = (bf16[128,1024]{1,0:T(8,128)(2,1)}, bf16[128,1024]{1,0:T(8,128)(2,1)}, u32[]{:S(2)}, u32[]{:S(2)}) collective-permute-start(bf16[128,1024]{1,0:T(8,128)(2,1)} %get-tuple-element.277), channel_id=1, source_target_pairs={{0,4},{1,5},{2,6},{3,7},{4,0},{5,1},{6,2},{7,3},{8,12},{9,13},{10,... | collective-permute-start | bytes 786440 | tf_op jit(solution)/shard_map/ppermute | solution.py:62
  486.7 23.6 %collective-permute-start.69 = (bf16[128,1024]{1,0:T(8,128)(2,1)}, bf16[128,1024]{1,0:T(8,128)(2,1)}, u32[]{:S(2)}, u32[]{:S(2)}) collective-permute-start(bf16[128,1024]{1,0:T(8,128)(2,1)} %get-tuple-element.278), channel_id=1, source_target_pairs={{0,6},{1,7},{2,4},{3,5},{4,2},{5,3},{6,0},{7,1},{8,14},{9,15},{10,... | collective-permute-start | bytes 786440 | tf_op jit(solution)/shard_map/ppermute | solution.py:62
  490.5 26.8 %collective-permute-start.64 = (bf16[16,7296]{1,0:T(8,128)(2,1)}, bf16[16,7296]{1,0:T(8,128)(2,1)}, u32[]{:S(2)}, u32[]{:S(2)}) collective-permute-start(bf16[16,7296]{1,0:T(8,128)(2,1)} %reshape.105), channel_id=1, source_target_pairs={{0,8},{1,9},{2,10},{3,11},{4,12},{5,13},{6,14},{7,15},{8,0},{9,1},... | collective-permute-start | bytes 700424 | tf_op jit(solution)/shard_map/ppermute | solution.py:62
  495.8 21.6 %collective-permute-start.65 = (bf16[16,7296]{1,0:T(8,128)(2,1)}, bf16[16,7296]{1,0:T(8,128)(2,1)S(1)}, u32[]{:S(2)}, u32[]{:S(2)}) collective-permute-start(bf16[16,7296]{1,0:T(8,128)(2,1)} %reshape.105), channel_id=1, source_target_pairs={{0,16},{1,17},{2,18},{3,19},{4,20},{5,21},{6,22},{7,23},{8,24},{9,... | collective-permute-start | bytes 700424 | tf_op jit(solution)/shard_map/ppermute | solution.py:62
  497.3 20.0 %collective-permute-start.66 = (bf16[16,7296]{1,0:T(8,128)(2,1)}, bf16[16,7296]{1,0:T(8,128)(2,1)S(1)}, u32[]{:S(2)}, u32[]{:S(2)}) collective-permute-start(bf16[16,7296]{1,0:T(8,128)(2,1)} %reshape.105), channel_id=1, source_target_pairs={{0,24},{1,25},{2,26},{3,27},{4,28},{5,29},{6,30},{7,31},{8,16},{9,... | collective-permute-start | bytes 700424 | tf_op jit(solution)/shard_map/ppermute | solution.py:62
  513.5 8.0 %collective-permute-start.70 = (bf16[128,1024]{1,0:T(8,128)(2,1)S(1)}, bf16[128,1024]{1,0:T(8,128)(2,1)S(1)}, u32[]{:S(2)}, u32[]{:S(2)}) collective-permute-start(bf16[128,1024]{1,0:T(8,128)(2,1)S(1)} %sums_h.1.refs_0_), channel_id=1, source_target_pairs={{0,16},{1,17},{2,18},{3,19},{4,20},{5,21},{6,22},{7,23},{8,24},{9,... | collective-permute-start | bytes 786440 | tf_op jit(solution)/shard_map/ppermute | solution.py:62
  514.9 6.7 %collective-permute-start.71 = (bf16[128,1024]{1,0:T(8,128)(2,1)S(1)}, bf16[128,1024]{1,0:T(8,128)(2,1)S(1)}, u32[]{:S(2)}, u32[]{:S(2)}) collective-permute-start(bf16[128,1024]{1,0:T(8,128)(2,1)S(1)} %sums_h.1.refs_0_), channel_id=1, source_target_pairs={{0,8},{1,9},{2,10},{3,11},{4,12},{5,13},{6,14},{7,15},{8,0},{9,1},... | collective-permute-start | bytes 786440 | tf_op jit(solution)/shard_map/ppermute | solution.py:62
  517.3 9.9 %collective-permute-start.72 = (bf16[128,1024]{1,0:T(8,128)(2,1)S(1)}, bf16[128,1024]{1,0:T(8,128)(2,1)S(1)}, u32[]{:S(2)}, u32[]{:S(2)}) collective-permute-start(bf16[128,1024]{1,0:T(8,128)(2,1)S(1)} %sums_h.1.refs_0_), channel_id=1, source_target_pairs={{0,24},{1,25},{2,26},{3,27},{4,28},{5,29},{6,30},{7,31},{8,16},{9,... | collective-permute-start | bytes 786440 | tf_op jit(solution)/shard_map/ppermute | solution.py:62
  (58 other events, 547.8 us)
Sparse Core Ops, SparseCore 0:
  79.3 80.8 all-gather.1

commit v5 on v4

--- a/solution.py
+++ b/solution.py
@@ -33,11 +33,6 @@
 def two_parts(values):
     high = values.astype(LOW)
     return high, (values - high.astype(WIDE)).astype(LOW)
-
-
-def split_dot(values, table):
-    high, rest = two_parts(values)
-    return dot(high, table) + dot(rest, table)
 
 
 class Place:
@@ -347,8 +342,8 @@
     return jnp.asarray(query_side, LOW), jnp.asarray(key_side, LOW)
 
 
-FORWARD_BLOCKS = ((0, 240, 256), (240, 416, 512), (416, 680, 680))
-BACKWARD_BLOCKS = ((424, 680, 680), (240, 424, 432), (0, 240, 256))
+FORWARD_BLOCKS = ((416, 680, 680), (0, 416, 512))
+BACKWARD_BLOCKS = ((424, 680, 680), (0, 424, 432))
 
 
 def attend_kernel(qkv_ref, qm_ref, km_ref, out_ref, extra_ref):
@@ -409,7 +404,7 @@
     lane = lax.broadcasted_iota(jnp.int32, query.shape, 1)
     even = lane < 64
     spare = lane & 63
-    centre = split_dot(grad.astype(WIDE) * out_ref[0].astype(WIDE), side_table(True))
+    centre = dot((grad.astype(WIDE) * out_ref[0].astype(WIDE)).astype(LOW), side_table(True))
     high, rest = two_parts(-centre)
     grad_extra = jnp.where(spare == 0, high, jnp.where(spare == 1, rest, jnp.zeros_like(high)))
     ones = jnp.ones_like(value)
@@ -420,9 +415,9 @@
         (jnp.where(even, extra, query), jnp.where(even, key_mask, key),
          jnp.where(even, ones, value), jnp.where(even, grad_extra, grad)),
     )
-    for head, (query_head, key_head, value_head, grad_head) in enumerate(heads):
-        head_rows = key_rows[64 * head : 64 * head + 64]
-        for number, (start, stop, keys) in enumerate(BACKWARD_BLOCKS):
+    for number, (start, stop, keys) in enumerate(BACKWARD_BLOCKS):
+        for head, (query_head, key_head, value_head, grad_head) in enumerate(heads):
+            head_rows = key_rows[64 * head : 64 * head + 64]
             probs = jnp.exp(dot(key_head[:keys], query_head[start:stop], NT))
             grad_probs = dot(value_head[:keys], grad_head[start:stop], NT)
             grad_scores = (probs * grad_probs).astype(LOW)
@@ -447,12 +442,12 @@
     product = unit_query * grad_query
     head_ref[0] = jnp.sum(product, 0, keepdims=True)
     grad_qkv_ref[0, :, :128] = (
-        root_query * (grad_query - unit_query * split_dot(product, same))
+        root_query * (grad_query - unit_query * dot(product.astype(LOW), same))
     ).astype(LOW)
     grad_key = jnp.where(even, key_sum[0], key_sum[1])
     unit_key = key.astype(WIDE)
     grad_qkv_ref[0, :, 128:256] = (
-        root_key * (grad_key - unit_key * split_dot(unit_key * grad_key, same))
+        root_key * (grad_key - unit_key * dot((unit_key * grad_key).astype(LOW), same))
     ).astype(LOW)
     grad_qkv_ref[0, :, 256:] = jnp.where(even, value_sum[0], value_sum[1]).astype(LOW)
 
@@ -681,12 +676,13 @@
     (scale,) = full
     (out_ref,) = outs
     (sum_ref,) = sums
+    unit, root = normalize(x_ref[...].astype(WIDE))
     weight = ready(0)
-    grad, column = 0.0, 0
+    grad, column = None, 0
     for ref in grad_refs:
-        grad = grad + dot(ref[...], weight[:, column : column + ref.shape[1]], NT)
+        part = dot(ref[...], weight[:, column : column + ref.shape[1]], NT)
+        grad = part if grad is None else grad + part
         column += ref.shape[1]
-    unit, root = normalize(x_ref[...].astype(WIDE))
     add_sums(sum_ref, second, [grad * unit, grad])
     scaled = grad * (1.0 + per_row(scale, second))
     total = middle_ref[...].astype(WIDE) + root * (
@@ -806,11 +802,11 @@
         qkv.over_both()
         qkv.over_core_first()
         rest.stack, *qkv.from_both = tie(rest.stack, *qkv.from_both)
-        rest.over_xy()
         qkv_parts = qkv.over_core()
         piece = w_fc2.shape[0] // place.dp_count
         fc2_piece = lax.dynamic_slice(w_fc2, (place.dp_index * piece, 0), (piece, width))
-        fc2_piece, qkv_parts[-1] = tie(fc2_piece, qkv_parts[-1])
+        fc2_piece, rest.stack = tie(fc2_piece, rest.stack)
+        rest.over_xy()
         fc2_full = lax.all_gather(fc2_piece, ("fsdp", "dp"), axis=0, tiled=True)
         quarter = half // 2
         qkv_weight = (qkv_parts, [(0, quarter, unit_rows, 0)], (width, 2 * half))

time: 545 us -> 539 us (0.989)
  Pallas kernels: 305 us -> 295 us
    pallas_call x2, Pallas kernels: 58 us -> 50.1 us  [attend_back(): pl.pallas_call(attend_back_kernel, grid=(items, pairs), in_specs=[pl.Bloc...]
    unnamed x113 -> x119, local copies, waits for them, and re-layouts: 20.6 us -> 20.9 us
  transfers between devices with their start and end apart: 77 -> 77, of which waited for: 22 -> 22; matrix products, arithmetic and copies ran while one was open for 6% -> 7% of each run, Pallas kernels for 35% -> 34%
where the time goes in v5:
time: 539 us; the launch traced here: 530 us
  Pallas kernels  295 us (55%)
  starting transfers between devices  84.7 us (16%)
  waiting for transfers between devices  83.6 us (16%)
  local copies, waits for them, and re-layouts  35.7 us (7%)
  between operations  15.7 us (3%)
  other arithmetic  11.9 us (2%)
    pallas_call x3, Pallas kernels, token_call(): pl.pallas_call(body, grid=(grid,), in_specs=[smem, smem] + [pl.BlockSpec(...  124 us
    ppermute x76, starting transfers between devices, hop(): return lax.ppermute(values, AXES, pairs)  84.7 us
    ppermute x76, waiting for transfers between devices, hop(): return lax.ppermute(values, AXES, pairs)  74.7 us
    pallas_call x2, Pallas kernels, attend_back(): pl.pallas_call(attend_back_kernel, grid=(items, pairs), in_specs=[pl.Bloc...  50.1 us
    pallas_call x4, Pallas kernels, outer(): pl.pallas_call(outer_kernel, grid_spec=pltpu.PrefetchScalarGridSpec(num_s...  38.8 us
    pallas_call x8, Pallas kernels, add_blocks(): pl.pallas_call(body, grid_spec=pltpu.PrefetchScalarGridSpec(num_scalar_pr...  28 us
    pallas_call x2, Pallas kernels, outer_joint(): pl.pallas_call(body, grid_spec=pltpu.PrefetchScalarGridSpec(num_scalar_pr...  25.2 us
    pallas_call x1, Pallas kernels, attend(): pl.pallas_call(attend_kernel, grid=(items, pairs), in_specs=[pl.BlockSpec...  22.3 us
  transfers between devices with their start and end apart: 77, of which 22 were waited for; matrix products, arithmetic and copies ran while one was open for 7% of the time, Pallas kernels for 34%

profile of v5, /device:TPU:9, one launch (start us, length us, event | category | flops | bytes accessed | tf_op | source)
XLA Modules:
  0.0 530.3 jit_solution(3785371710352265045)
XLA Ops:
  9.4 2.2 collective-permute-start
  12.4 1.5 copy.38
  17.4 1.6 collective-permute-start.4
  22.1 4.5 collective-permute-done.4
  27.3 8.4 %collective-permute-done.5 = bf16[128,768]{1,0:T(8,128)(2,1)} collective-permute-done((bf16[128,768]{1,0:T(8,128)(2,1)S(1)}, bf16[128,768]{1,0:T(8,128)(2,1)}, u32[]{:S(2)}, u32[]{:S(2)}) %collective-permute-start.5) | collective-permute-done | bytes 196640 | tf_op jit(solution)/shard_map/ppermute | solution.py:57
  36.9 2.0 collective-permute-start.10
  42.8 1.5 fusion.5
  44.3 2.3 collective-permute-start.11
  47.8 8.3 %collective-permute-done.14.refs_5_.refs_6_ = bf16[512,768]{1,0:T(8,128)(2,1)S(1)} collective-permute-done((bf16[512,768]{1,0:T(8,128)(2,1)S(1)}, bf16[512,768]{1,0:T(8,128)(2,1)S(1)}, u32[]{:S(2)}, u32[]{:S(2)}) %collective-permute-start.14) | collective-permute-done | bytes 786464 | tf_op jit(solution)/shard_map/ppermute | solution.py:57
  58.2 1.8 slice.103
  60.2 1.7 constant_dynamic-slice_fusion.25
  61.9 12.9 %collective-permute-done.13 = bf16[128,1280]{1,0:T(8,128)(2,1)} collective-permute-done((bf16[128,1280]{1,0:T(8,128)(2,1)}, bf16[128,1280]{1,0:T(8,128)(2,1)}, u32[]{:S(2)}, u32[]{:S(2)}) %collective-permute-start.13) | collective-permute-done | bytes 327712 | tf_op jit(solution)/shard_map/ppermute | solution.py:57
  76.2 3.2 collective-permute-start.20
  82.1 1.4 collective-permute-done.23.refs_12_.refs_13_
  87.4 23.2 %project.1 = (bf16[1360,1024]{1,0:T(8,128)(2,1)}, bf16[1360,3072]{1,0:T(8,128)(2,1)}, bf16[1360,1024]{1,0:T(8,128)(2,1)}) custom-call(s32[4]{0:T(128)} %pad_add_fusion.place_ref, s32[2]{0:T(128)} %fusion.19.lengths_ref, bf16[1360,1024]{1,0:T(8,128)(2,1)} %refs_2_.3, f32[2,1024]{1,0:T(2,128)} %get-tuple-element.341.refs_1_.refs_4_, ...), custom_call_target="tpu_custom_call" | custom-call | flops 1024 | bytes 1024 | tf_op jit(solution)/shard_map/project/pallas_call | solution.py:572
  110.6 5.3 collective-permute-done.18.refs_8_.refs_18_
  120.3 1.8 collective-permute-start.27
  122.7 22.3 %attend.1 = (bf16[2,680,1024]{2,1,0:T(8,128)(2,1)S(1)}, bf16[2,680,1024]{2,1,0:T(8,128)(2,1)S(1)}) custom-call(bf16[2,680,3072]{2,1,0:T(8,128)(2,1)} %bitcast.84, bf16[680,128]{1,0:T(8,128)(2,1)S(1)} %copy-done.28, bf16[680,128]{1,0:T(8,128)(2,1)S(1)} %copy-done.19), custom_call_target="tpu_custom_call" | custom-call | flops 1024 | bytes 1024 | tf_op jit(solution)/shard_map/attend/pallas_call | solution.py:380
  144.9 1.5 copy-done.7
  146.4 1.5 copy-done.14
  148.5 2.0 collective-permute-done.30.refs_15_.refs_25_
  151.5 8.9 %all-gather.2.cloned.1.call-done.refs_27_ = bf16[4096,1024]{1,0:T(8,128)(2,1)} async-done(((bf16[128,1024]{1,0:T(8,128)(2,1)}), bf16[4096,1024]{1,0:T(8,128)(2,1)}) %all-gather.2.cloned.1.call-update) | async-done | bytes 8388624 | tf_op jit(solution)/shard_map/all_gather | solution.py:810
  160.4 78.8 %block.1 = (bf16[1360,1024]{1,0:T(8,128)(2,1)}, bf16[1360,1024]{1,0:T(8,128)(2,1)}, bf16[1360,4096]{1,0:T(8,128)(2,1)}, bf16[1360,1024]{1,0:T(8,128)(2,1)}, bf16...) custom-call(s32[4]{0:T(128)} %pad_add_fusion.place_ref, ...), custom_call_target="tpu_custom_call" | custom-call | flops 1024 | bytes 1024 | tf_op jit(solution)/shard_map/block/pallas_call | solution.py:572
  239.2 9.6 %outer.4 = bf16[4096,512]{1,0:T(8,128)(2,1)S(1)} custom-call(s32[1]{0:T(128)} %bitcast.22.half_ref, bf16[1360,4096]{1,0:T(8,128)(2,1)} %get-tuple-element.169.left_ref, bf16[1360,1024]{1,0:T(8,128)(2,1)} %get-tuple-element.171.right_ref), custom_call_target="tpu_custom_call" | custom-call | flops 1024 | bytes 1024 | tf_op jit(solution)/shard_map/outer/pallas_call | solution.py:704
  249.1 9.6 %outer.5.refs_0_.refs_2_.refs_3_.refs_4_.refs_10_.refs_16_.refs_6_ = bf16[4096,512]{1,0:T(8,128)(2,1)S(1)} custom-call(s32[1]{0:T(128)} %bitcast.1.half_ref, bf16[1360,4096]{1,0:T(8,128)(2,1)} %get-tuple-element.169.left_ref, bf16[1360,1024]{1,0:T(8,128)(2,1)} %get-tuple-element.171.right_ref), custom_call_target="tpu_custom_call" | custom-call | flops 1024 | bytes 1024 | tf_op jit(solution)/shard_map/outer/pallas_call | solution.py:704
  263.5 25.0 %attend_back.2 = (bf16[2,680,1536]{2,1,0:T(8,128)(2,1)S(1)}, f32[2,1,512]{2,1,0:T(1,128)S(1)}) custom-call(bf16[2,680,3072]{2,1,0:T(8,128)(2,1)} %bitcast.85, bf16[2,680,1024]{2,1,0:T(8,128)(2,1)} %copy-done.14, bf16[680,128]{1,0:T(8,128)(2,1)S(1)} %copy-done.19, bf16[2,680,1024]{2,1,0:T(8,128)(2,1)} %copy-done.7, bf16[2,680,1024]{2,1,0:T(8,128)(2,1)} %bitcast.89, ...), custom_call_target="tpu_custom_call" | custom-call | flops 1024 | bytes 1024 | tf_op jit(solution)/shard_map/attend_back/pallas_call | solution.py:459
  288.6 3.2 sums_b.1
  293.3 9.8 %outer.6 = bf16[1024,2048]{1,0:T(8,128)(2,1)S(1)} custom-call(s32[1]{0:T(128)} %bitcast.22.half_ref, bf16[1360,1024]{1,0:T(8,128)(2,1)} %get-tuple-element.184.left_ref, bf16[1360,4096]{1,0:T(8,128)(2,1)} %get-tuple-element.195.right_ref), custom_call_target="tpu_custom_call" | custom-call | flops 1024 | bytes 1024 | tf_op jit(solution)/shard_map/outer/pallas_call | solution.py:704
  305.4 2.0 collective-permute-start.37
  307.4 9.8 %outer.7.refs_0_.refs_2_.refs_3_.refs_6_.refs_12_ = bf16[1024,2048]{1,0:T(8,128)(2,1)S(1)} custom-call(s32[1]{0:T(128)} %bitcast.1.half_ref, bf16[1360,1024]{1,0:T(8,128)(2,1)} %get-tuple-element.184.left_ref, bf16[1360,4096]{1,0:T(8,128)(2,1)} %get-tuple-element.195.right_ref), custom_call_target="tpu_custom_call" | custom-call | flops 1024 | bytes 1024 | tf_op jit(solution)/shard_map/outer/pallas_call | solution.py:704
  317.3 4.8 sums_c.1
  323.6 3.5 collective-permute-start.40
  328.3 25.1 %attend_back.3 = (bf16[2,680,1536]{2,1,0:T(8,128)(2,1)S(1)}, f32[2,1,512]{2,1,0:T(1,128)S(1)}) custom-call(bf16[2,680,3072]{2,1,0:T(8,128)(2,1)} %bitcast.86, bf16[2,680,1024]{2,1,0:T(8,128)(2,1)} %copy-done.14, bf16[680,128]{1,0:T(8,128)(2,1)S(1)} %copy-done.19, bf16[2,680,1024]{2,1,0:T(8,128)(2,1)} %copy-done.7, bf16[2,680,1024]{2,1,0:T(8,128)(2,1)} %bitcast.90, ...), custom_call_target="tpu_custom_call" | custom-call | flops 1024 | bytes 1024 | tf_op jit(solution)/shard_map/attend_back/pallas_call | solution.py:459
  353.4 2.0 copy-done.9
  355.4 2.9 sums_d.1
  360.4 2.0 collective-permute-start.46
  362.4 12.5 %outer_joint.2 = bf16[1024,2048]{1,0:T(8,128)(2,1)S(1)} custom-call(s32[1]{0:T(128)} %bitcast.22.half_ref, bf16[1360,1024]{1,0:T(8,128)(2,1)} %get-tuple-element.216.left_ref, bf16[1360,1024]{1,0:T(8,128)(2,1)} %bitcast.76, bf16[1360,1536]{1,0:T(8,128)(2,1)} %bitcast.78, bf16[1360,1536]{1,0:T(8,128)(2,1)} %bitcast.81, ...), custom_call_target="tpu_custom_call" | custom-call | flops 1024 | bytes 1024 | tf_op jit(solution)/shard_map/outer_joint/pallas_call | solution.py:738
  374.9 1.7 collective-permute-done.45.refs_1_
  376.6 2.4 collective-permute-start.47
  379.1 12.7 %outer_joint.3.refs_18_.refs_20_.refs_0_.refs_3_.refs_6_.refs_12_ = bf16[1024,2048]{1,0:T(8,128)(2,1)S(1)} custom-call(s32[1]{0:T(128)} %bitcast.1.half_ref, bf16[1360,1024]{1,0:T(8,128)(2,1)} %get-tuple-element.216.left_ref, bf16[1360,1024]{1,0:T(8,128)(2,1)} %bitcast.77, bf16[1360,1536]{1,0:T(8,128)(2,1)} %bitcast.79, bf16[1360,1536]{1,0:T(8,128)(2,1)} %bitcast.82, ...), custom_call_target="tpu_custom_call" | custom-call | flops 1024 | bytes 1024 | tf_op jit(solution)/shard_map/outer_joint/pallas_call | solution.py:738
  391.9 5.9 %sums_e.1 = (bf16[128,1024]{1,0:T(8,128)(2,1)}, bf16[128,1024]{1,0:T(8,128)(2,1)}, bf16[128,1024]{1,0:T(8,128)(2,1)}, bf16[512,1024]{1,0:T(8,128)(2,1)}, bf16[256,2048]{1,0:T(8,128)(2,1)}) custom-call(s32[4]{0:T(128)S(1)} %copy-done.29, bf16[1024,2048]{1,0:T(8,128)(2,1)} %copy-done.3, bf16[1024,2048]{1,0:T(8,128)(2,1)} %copy-done.6, ...), custom_call_target="tpu_custom_call" | custom-call | flops 1024 | bytes 1024 | tf_op jit(solution)/shard_map/sums_e/pallas_call | solution.py:154
  399.1 2.4 collective-permute-start.51
  402.9 21.6 %token_back.1 = (bf16[1360,1024]{1,0:T(8,128)(2,1)}, f32[16,1024]{1,0:T(8,128)}) custom-call(s32[4]{0:T(128)} %pad_add_fusion.place_ref, s32[2]{0:T(128)} %fusion.19.lengths_ref, bf16[1360,1536]{1,0:T(8,128)(2,1)} %bitcast.80, bf16[1360,1536]{1,0:T(8,128)(2,1)} %bitcast.83, bf16[1360,1024]{1,0:T(8,128)(2,1)} %refs_2_.3, ...), custom_call_target="tpu_custom_call" | custom-call | flops 1024 | bytes 1024 | tf_op jit(solution)/shard_map/token_back/pallas_call | solution.py:572
  426.2 4.0 sums_f.1
  431.9 1.7 collective-permute-start.56
  437.6 8.4 %collective-permute-done.54.refs_3_.refs_9_.refs_15_ = bf16[256,1024]{1,0:T(8,128)(2,1)S(1)} collective-permute-done((bf16[256,1024]{1,0:T(8,128)(2,1)}, bf16[256,1024]{1,0:T(8,128)(2,1)S(1)}, u32[]{:S(2)}, u32[]{:S(2)}) %collective-permute-start.54) | collective-permute-done | bytes 524320 | tf_op jit(solution)/shard_map/ppermute | solution.py:57
  446.4 3.6 sums_g.1
  452.1 1.6 collective-permute-done.59
  459.3 1.7 reshape.105
  461.0 1.4 fusion.2
  462.4 2.1 collective-permute-start.60
  465.9 5.6 %collective-permute-start.74 = (bf16[128,1024]{1,0:T(8,128)(2,1)}, bf16[128,1024]{1,0:T(8,128)(2,1)}, u32[]{:S(2)}, u32[]{:S(2)}) collective-permute-start(bf16[128,1024]{1,0:T(8,128)(2,1)} %get-tuple-element.281.refs_0_), channel_id=1, source_target_pairs={{0,8},{1,9},{2,10},{3,11},{4,12},{5,13},{6,14},{7,15},{8,0},{9,1},... | collective-permute-start | bytes 786440 | tf_op jit(solution)/shard_map/ppermute | solution.py:57
  476.0 2.0 lay_out_fc2.1
  478.1 2.6 collective-permute-start.67
  481.9 2.7 lay_out_fc1.1
  484.5 3.6 collective-permute-start.64
  488.1 1.7 stack_reshape.3
  491.3 3.8 collective-permute-start.66
  495.7 8.2 %collective-permute-done.69.refs_8_ = bf16[128,1024]{1,0:T(8,128)(2,1)} collective-permute-done((bf16[128,1024]{1,0:T(8,128)(2,1)}, bf16[128,1024]{1,0:T(8,128)(2,1)}, u32[]{:S(2)}, u32[]{:S(2)}) %collective-permute-start.69) | collective-permute-done | bytes 262176 | tf_op jit(solution)/shard_map/ppermute | solution.py:57
  504.9 2.2 sums_h.1.refs_0_
  508.4 2.8 collective-permute-start.71
  513.2 2.3 fusion
  515.5 5.4 %collective-permute-done.72.refs_3_ = bf16[128,1024]{1,0:T(8,128)(2,1)S(1)} collective-permute-done((bf16[128,1024]{1,0:T(8,128)(2,1)S(1)}, bf16[128,1024]{1,0:T(8,128)(2,1)S(1)}, u32[]{:S(2)}, u32[]{:S(2)}) %collective-permute-start.72) | collective-permute-done | bytes 262176 | tf_op jit(solution)/shard_map/ppermute | solution.py:57
  520.9 2.1 lay_out_last.1
  (297 shorter events, 78.2 us)
Async XLA Ops:
  7.2 153.2 %all-gather.2.cloned.1.call-start = ((), (), s32[]{:S(2)}) async-start(), calls=%async_computation | async-start | bytes 8650752 | tf_op jit(solution)/shard_map/all_gather | solution.py:810
  8.1 6.1 %collective-permute-start.2 = (bf16[2,1024]{1,0:T(2,128)(2,1)S(1)}, bf16[2,1024]{1,0:T(2,128)(2,1)S(1)}, u32[]{:S(2)}, u32[]{:S(2)}) collective-permute-start(bf16[2,1024]{1,0:T(2,128)(2,1)S(1)} %fusion.12), channel_id=1, source_target_pairs={{0,6},{1,7},{2,4},{3,5},{4,2},{5,3},{6,0},{7,1},{8,14},{9,15},{10,... | collective-permute-start | bytes 12296 | tf_op jit(solution)/shard_map/ppermute | solution.py:57
  15.0 5.1 collective-permute-start.6
  17.4 9.2 %collective-permute-start.4 = (bf16[128,768]{1,0:T(8,128)(2,1)S(1)}, bf16[128,768]{1,0:T(8,128)(2,1)S(1)}, u32[]{:S(2)}, u32[]{:S(2)}) collective-permute-start(bf16[128,768]{1,0:T(8,128)(2,1)S(1)} %copy.46), channel_id=1, source_target_pairs={{0,4},{1,5},{2,6},{3,7},{4,0},{5,1},{6,2},{7,3},{8,12},{9,13},{10,... | collective-permute-start | bytes 589832 | tf_op jit(solution)/shard_map/ppermute | solution.py:57
  19.1 16.6 %collective-permute-start.5 = (bf16[128,768]{1,0:T(8,128)(2,1)S(1)}, bf16[128,768]{1,0:T(8,128)(2,1)}, u32[]{:S(2)}, u32[]{:S(2)}) collective-permute-start(bf16[128,768]{1,0:T(8,128)(2,1)S(1)} %copy.46), channel_id=1, source_target_pairs={{0,6},{1,7},{2,4},{3,5},{4,2},{5,3},{6,0},{7,1},{8,14},{9,15},{10,... | collective-permute-start | bytes 589832 | tf_op jit(solution)/shard_map/ppermute | solution.py:57
  21.0 15.8 %collective-permute-start.7 = (f32[4,2,6144]{2,1,0:T(2,128)S(1)}, f32[4,2,6144]{2,1,0:T(2,128)S(1)}, u32[]{:S(2)}, u32[]{:S(2)}) collective-permute-start(f32[4,2,6144]{2,1,0:T(2,128)S(1)} %dynamic-slice_bitcast_fusion), channel_id=1, source_target_pairs={{0,1},{1,0},{2,3},{3,2},{4,5},{5,4},{6,7},{7,6},{8,9},{9,8},{10,11... | collective-permute-start | bytes 589832 | tf_op jit(solution)/shard_map/ppermute | solution.py:57
  36.9 5.5 %collective-permute-start.10 = (f32[2,6144]{1,0:T(2,128)S(1)}, f32[2,6144]{1,0:T(2,128)S(1)}, u32[]{:S(2)}, u32[]{:S(2)}) collective-permute-start(f32[2,6144]{1,0:T(2,128)S(1)} %get-tuple-element.334), channel_id=1, source_target_pairs={{0,6},{1,7},{2,4},{3,5},{4,2},{5,3},{6,0},{7,1},{8,14},{9,15},{10,... | collective-permute-start | bytes 147464 | tf_op jit(solution)/shard_map/ppermute | solution.py:57
  40.9 15.3 %collective-permute-start.14 = (bf16[512,768]{1,0:T(8,128)(2,1)S(1)}, bf16[512,768]{1,0:T(8,128)(2,1)S(1)}, u32[]{:S(2)}, u32[]{:S(2)}) collective-permute-start(bf16[512,768]{1,0:T(8,128)(2,1)S(1)} %pad_maximum_fusion.3.refs_4_.refs_5_), channel_id=1, source_target_pairs={{0,1},{1,0},{2,3},{3,2},{4,5},{5,4},{6,7},{7,6},{8,9},{9,8},{10,11... | collective-permute-start | bytes 2359304 | tf_op jit(solution)/shard_map/ppermute | solution.py:57
  41.1 17.1 %collective-permute-start.16 = (bf16[512,768]{1,0:T(8,128)(2,1)S(1)}, bf16[512,768]{1,0:T(8,128)(2,1)}, u32[]{:S(2)}, u32[]{:S(2)}) collective-permute-start(bf16[512,768]{1,0:T(8,128)(2,1)S(1)} %pad_maximum_fusion.3.refs_4_.refs_5_), channel_id=1, source_target_pairs={{0,16},{1,17},{2,18},{3,19},{4,20},{5,21},{6,22},{7,23},{8,24},{9,... | collective-permute-start | bytes 2359304 | tf_op jit(solution)/shard_map/ppermute | solution.py:57
  44.3 17.6 %collective-permute-start.11 = (bf16[128,1280]{1,0:T(8,128)(2,1)}, bf16[128,1280]{1,0:T(8,128)(2,1)}, u32[]{:S(2)}, u32[]{:S(2)}) collective-permute-start(bf16[128,1280]{1,0:T(8,128)(2,1)} %pad_maximum_fusion.4), channel_id=1, source_target_pairs={{0,2},{1,3},{2,0},{3,1},{4,6},{5,7},{6,4},{7,5},{8,10},{9,11},{10,... | collective-permute-start | bytes 983048 | tf_op jit(solution)/shard_map/ppermute | solution.py:57
  46.7 15.2 %collective-permute-start.12 = (bf16[128,1280]{1,0:T(8,128)(2,1)}, bf16[128,1280]{1,0:T(8,128)(2,1)}, u32[]{:S(2)}, u32[]{:S(2)}) collective-permute-start(bf16[128,1280]{1,0:T(8,128)(2,1)} %pad_maximum_fusion.4), channel_id=1, source_target_pairs={{0,4},{1,5},{2,6},{3,7},{4,0},{5,1},{6,2},{7,3},{8,12},{9,13},{10,... | collective-permute-start | bytes 983048 | tf_op jit(solution)/shard_map/ppermute | solution.py:57
  46.7 28.2 %collective-permute-start.13 = (bf16[128,1280]{1,0:T(8,128)(2,1)}, bf16[128,1280]{1,0:T(8,128)(2,1)}, u32[]{:S(2)}, u32[]{:S(2)}) collective-permute-start(bf16[128,1280]{1,0:T(8,128)(2,1)} %pad_maximum_fusion.4), channel_id=1, source_target_pairs={{0,6},{1,7},{2,4},{3,5},{4,2},{5,3},{6,0},{7,1},{8,14},{9,15},{10,... | collective-permute-start | bytes 983048 | tf_op jit(solution)/shard_map/ppermute | solution.py:57
  56.9 19.2 %collective-permute-start.15 = (bf16[256,768]{1,0:T(8,128)(2,1)}, bf16[256,768]{1,0:T(8,128)(2,1)S(1)}, u32[]{:S(2)}, u32[]{:S(2)}) collective-permute-start(bf16[256,768]{1,0:T(8,128)(2,1)} %slice.102), channel_id=1, source_target_pairs={{0,16},{1,17},{2,18},{3,19},{4,20},{5,21},{6,22},{7,23},{8,24},{9,... | collective-permute-start | bytes 1179656 | tf_op jit(solution)/shard_map/ppermute | solution.py:57
  60.0 16.3 %collective-permute-start.17 = (bf16[256,768]{1,0:T(8,128)(2,1)}, bf16[256,768]{1,0:T(8,128)(2,1)}, u32[]{:S(2)}, u32[]{:S(2)}) collective-permute-start(bf16[256,768]{1,0:T(8,128)(2,1)} %slice.103), channel_id=1, source_target_pairs={{0,1},{1,0},{2,3},{3,2},{4,5},{5,4},{6,7},{7,6},{8,9},{9,8},{10,11... | collective-permute-start | bytes 1179656 | tf_op jit(solution)/shard_map/ppermute | solution.py:57
  76.2 5.4 %collective-permute-start.20 = (bf16[512,768]{1,0:T(8,128)(2,1)}, bf16[512,768]{1,0:T(8,128)(2,1)}, u32[]{:S(2)}, u32[]{:S(2)}) collective-permute-start(bf16[512,768]{1,0:T(8,128)(2,1)} %copy-done.35), channel_id=1, source_target_pairs={{0,8},{1,9},{2,10},{3,11},{4,12},{5,13},{6,14},{7,15},{8,0},{9,1},... | collective-permute-start | bytes 2359304 | tf_op jit(solution)/shard_map/ppermute | solution.py:57
  79.4 36.5 %collective-permute-start.18 = (bf16[512,1280]{1,0:T(8,128)(2,1)S(1)}, bf16[512,1280]{1,0:T(8,128)(2,1)}, u32[]{:S(2)}, u32[]{:S(2)}) collective-permute-start(bf16[512,1280]{1,0:T(8,128)(2,1)S(1)} %pad_maximum_fusion.refs_7_.refs_17_), channel_id=1, source_target_pairs={{0,1},{1,0},{2,3},{3,2},{4,5},{5,4},{6,7},{7,6},{8,9},{9,8},{10,11... | collective-permute-start | bytes 3932168 | tf_op jit(solution)/shard_map/ppermute | solution.py:57
  79.7 36.2 %collective-permute-start.19 = (bf16[512,1280]{1,0:T(8,128)(2,1)S(1)}, bf16[512,1280]{1,0:T(8,128)(2,1)}, u32[]{:S(2)}, u32[]{:S(2)}) collective-permute-start(bf16[512,1280]{1,0:T(8,128)(2,1)S(1)} %pad_maximum_fusion.refs_7_.refs_17_), channel_id=1, source_target_pairs={{0,16},{1,17},{2,18},{3,19},{4,20},{5,21},{6,22},{7,23},{8,24},{9,... | collective-permute-start | bytes 3932168 | tf_op jit(solution)/shard_map/ppermute | solution.py:57
  81.6 5.8 %collective-permute-start.21 = (bf16[512,768]{1,0:T(8,128)(2,1)}, bf16[512,768]{1,0:T(8,128)(2,1)}, u32[]{:S(2)}, u32[]{:S(2)}) collective-permute-start(bf16[512,768]{1,0:T(8,128)(2,1)} %copy-done.36), channel_id=1, source_target_pairs={{0,8},{1,9},{2,10},{3,11},{4,12},{5,13},{6,14},{7,15},{8,0},{9,1},... | collective-permute-start | bytes 2359304 | tf_op jit(solution)/shard_map/ppermute | solution.py:57
  81.7 5.7 %collective-permute-start.22 = (bf16[512,768]{1,0:T(8,128)(2,1)}, bf16[512,768]{1,0:T(8,128)(2,1)}, u32[]{:S(2)}, u32[]{:S(2)}) collective-permute-start(bf16[512,768]{1,0:T(8,128)(2,1)} %collective-permute-done.16.refs_6_.refs_7_), channel_id=1, source_target_pairs={{0,8},{1,9},{2,10},{3,11},{4,12},{5,13},{6,14},{7,15},{8,0},{9,1},... | collective-permute-start | bytes 2359304 | tf_op jit(solution)/shard_map/ppermute | solution.py:57
  117.0 30.9 %collective-permute-start.25 = (bf16[256,1280]{1,0:T(8,128)(2,1)S(1)}, bf16[256,1280]{1,0:T(8,128)(2,1)}, u32[]{:S(2)}, u32[]{:S(2)}) collective-permute-start(bf16[256,1280]{1,0:T(8,128)(2,1)S(1)} %slice.82), channel_id=1, source_target_pairs={{0,16},{1,17},{2,18},{3,19},{4,20},{5,21},{6,22},{7,23},{8,24},{9,... | collective-permute-start | bytes 1966088 | tf_op jit(solution)/shard_map/ppermute | solution.py:57
  119.5 28.4 %collective-permute-start.26 = (bf16[256,1280]{1,0:T(8,128)(2,1)S(1)}, bf16[256,1280]{1,0:T(8,128)(2,1)}, u32[]{:S(2)}, u32[]{:S(2)}) collective-permute-start(bf16[256,1280]{1,0:T(8,128)(2,1)S(1)} %slice.83), channel_id=1, source_target_pairs={{0,1},{1,0},{2,3},{3,2},{4,5},{5,4},{6,7},{7,6},{8,9},{9,8},{10,11... | collective-permute-start | bytes 1966088 | tf_op jit(solution)/shard_map/ppermute | solution.py:57
  120.3 28.2 %collective-permute-start.27 = (bf16[512,1280]{1,0:T(8,128)(2,1)S(1)}, bf16[512,1280]{1,0:T(8,128)(2,1)}, u32[]{:S(2)}, u32[]{:S(2)}) collective-permute-start(bf16[512,1280]{1,0:T(8,128)(2,1)S(1)} %pad_maximum_fusion.refs_7_.refs_17_), channel_id=1, source_target_pairs={{0,8},{1,9},{2,10},{3,11},{4,12},{5,13},{6,14},{7,15},{8,0},{9,1},... | collective-permute-start | bytes 3932168 | tf_op jit(solution)/shard_map/ppermute | solution.py:57
  122.1 29.3 %collective-permute-start.28 = (bf16[512,1280]{1,0:T(8,128)(2,1)}, bf16[512,1280]{1,0:T(8,128)(2,1)}, u32[]{:S(2)}, u32[]{:S(2)}) collective-permute-start(bf16[512,1280]{1,0:T(8,128)(2,1)} %collective-permute-done.18.refs_8_.refs_18_), channel_id=1, source_target_pairs={{0,8},{1,9},{2,10},{3,11},{4,12},{5,13},{6,14},{7,15},{8,0},{9,1},... | collective-permute-start | bytes 3932168 | tf_op jit(solution)/shard_map/ppermute | solution.py:57
  122.1 29.3 %collective-permute-start.29 = (bf16[512,1280]{1,0:T(8,128)(2,1)}, bf16[512,1280]{1,0:T(8,128)(2,1)}, u32[]{:S(2)}, u32[]{:S(2)}) collective-permute-start(bf16[512,1280]{1,0:T(8,128)(2,1)} %collective-permute-done.19.refs_9_.refs_19_), channel_id=1, source_target_pairs={{0,8},{1,9},{2,10},{3,11},{4,12},{5,13},{6,14},{7,15},{8,0},{9,1},... | collective-permute-start | bytes 3932168 | tf_op jit(solution)/shard_map/ppermute | solution.py:57
  248.8 9.9 %collective-permute-start.32 = (bf16[4096,512]{1,0:T(8,128)(2,1)S(1)}, bf16[4096,512]{1,0:T(8,128)(2,1)S(1)}, u32[]{:S(2)}, u32[]{:S(2)}) collective-permute-start(bf16[4096,512]{1,0:T(8,128)(2,1)S(1)} %outer.4), channel_id=1, source_target_pairs={{0,8},{1,9},{2,10},{3,11},{4,12},{5,13},{6,14},{7,15},{8,0},{9,1},... | collective-permute-start | bytes 12582920 | tf_op jit(solution)/shard_map/ppermute | solution.py:57
  262.0 26.5 %collective-permute-start.33 = (bf16[2048,256]{1,0:T(8,128)(2,1)S(1)}, bf16[2048,256]{1,0:T(8,128)(2,1)S(1)}, u32[]{:S(2)}, u32[]{:S(2)}) collective-permute-start(bf16[2048,256]{1,0:T(8,128)(2,1)S(1)} %get-tuple-element.181), channel_id=1, source_target_pairs={{0,16},{1,17},{2,18},{3,19},{4,20},{5,21},{6,22},{7,23},{8,24},{9,... | collective-permute-start | bytes 3145736 | tf_op jit(solution)/shard_map/ppermute | solution.py:57
  263.3 25.3 %collective-permute-start.34 = (bf16[1024,512]{1,0:T(8,128)(2,1)S(1)}, bf16[1024,512]{1,0:T(8,128)(2,1)S(1)}, u32[]{:S(2)}, u32[]{:S(2)}) collective-permute-start(bf16[1024,512]{1,0:T(8,128)(2,1)S(1)} %get-tuple-element.182), channel_id=1, source_target_pairs={{0,1},{1,0},{2,3},{3,2},{4,5},{5,4},{6,7},{7,6},{8,9},{9,8},{10,11... | collective-permute-start | bytes 3145736 | tf_op jit(solution)/shard_map/ppermute | solution.py:57
  291.8 12.7 %collective-permute-start.35 = (bf16[1024,256]{1,0:T(8,128)(2,1)S(1)}, bf16[1024,256]{1,0:T(8,128)(2,1)S(1)}, u32[]{:S(2)}, u32[]{:S(2)}) collective-permute-start(bf16[1024,256]{1,0:T(8,128)(2,1)S(1)} %get-tuple-element.192), channel_id=1, source_target_pairs={{0,1},{1,0},{2,3},{3,2},{4,5},{5,4},{6,7},{7,6},{8,9},{9,8},{10,11... | collective-permute-start | bytes 1572872 | tf_op jit(solution)/shard_map/ppermute | solution.py:57
  293.1 12.3 %collective-permute-start.36 = (bf16[1024,256]{1,0:T(8,128)(2,1)S(1)}, bf16[1024,256]{1,0:T(8,128)(2,1)S(1)}, u32[]{:S(2)}, u32[]{:S(2)}) collective-permute-start(bf16[1024,256]{1,0:T(8,128)(2,1)S(1)} %get-tuple-element.193), channel_id=1, source_target_pairs={{0,16},{1,17},{2,18},{3,19},{4,20},{5,21},{6,22},{7,23},{8,24},{9,... | collective-permute-start | bytes 1572872 | tf_op jit(solution)/shard_map/ppermute | solution.py:57
  305.4 11.9 %collective-permute-start.37 = (bf16[1024,2048]{1,0:T(8,128)(2,1)S(1)}, bf16[1024,2048]{1,0:T(8,128)(2,1)S(1)}, u32[]{:S(2)}, u32[]{:S(2)}) collective-permute-start(bf16[1024,2048]{1,0:T(8,128)(2,1)S(1)} %outer.6), channel_id=1, source_target_pairs={{0,8},{1,9},{2,10},{3,11},{4,12},{5,13},{6,14},{7,15},{8,0},{9,1},... | collective-permute-start | bytes 12582920 | tf_op jit(solution)/shard_map/ppermute | solution.py:57
  322.1 33.2 %collective-permute-start.38 = (bf16[512,1024]{1,0:T(8,128)(2,1)S(1)}, bf16[512,1024]{1,0:T(8,128)(2,1)S(1)}, u32[]{:S(2)}, u32[]{:S(2)}) collective-permute-start(bf16[512,1024]{1,0:T(8,128)(2,1)S(1)} %get-tuple-element.209), channel_id=1, source_target_pairs={{0,16},{1,17},{2,18},{3,19},{4,20},{5,21},{6,22},{7,23},{8,24},{9,... | collective-permute-start | bytes 3145736 | tf_op jit(solution)/shard_map/ppermute | solution.py:57
  322.5 32.9 %collective-permute-start.39 = (bf16[256,2048]{1,0:T(8,128)(2,1)S(1)}, bf16[256,2048]{1,0:T(8,128)(2,1)S(1)}, u32[]{:S(2)}, u32[]{:S(2)}) collective-permute-start(bf16[256,2048]{1,0:T(8,128)(2,1)S(1)} %get-tuple-element.210), channel_id=1, source_target_pairs={{0,1},{1,0},{2,3},{3,2},{4,5},{5,4},{6,7},{7,6},{8,9},{9,8},{10,11... | collective-permute-start | bytes 3145736 | tf_op jit(solution)/shard_map/ppermute | solution.py:57
  323.6 31.7 %collective-permute-start.40 = (bf16[512,256]{1,0:T(8,128)(2,1)S(1)}, bf16[512,256]{1,0:T(8,128)(2,1)S(1)}, u32[]{:S(2)}, u32[]{:S(2)}) collective-permute-start(bf16[512,256]{1,0:T(8,128)(2,1)S(1)} %get-tuple-element.211), channel_id=1, source_target_pairs={{0,2},{1,3},{2,0},{3,1},{4,6},{5,7},{6,4},{7,5},{8,10},{9,11},{10,... | collective-permute-start | bytes 786440 | tf_op jit(solution)/shard_map/ppermute | solution.py:57
  327.1 28.2 %collective-permute-start.41 = (bf16[512,256]{1,0:T(8,128)(2,1)S(1)}, bf16[512,256]{1,0:T(8,128)(2,1)S(1)}, u32[]{:S(2)}, u32[]{:S(2)}) collective-permute-start(bf16[512,256]{1,0:T(8,128)(2,1)S(1)} %get-tuple-element.212), channel_id=1, source_target_pairs={{0,4},{1,5},{2,6},{3,7},{4,0},{5,1},{6,2},{7,3},{8,12},{9,13},{10,... | collective-permute-start | bytes 786440 | tf_op jit(solution)/shard_map/ppermute | solution.py:57
  327.2 28.1 %collective-permute-start.42 = (bf16[512,256]{1,0:T(8,128)(2,1)S(1)}, bf16[512,256]{1,0:T(8,128)(2,1)S(1)}, u32[]{:S(2)}, u32[]{:S(2)}) collective-permute-start(bf16[512,256]{1,0:T(8,128)(2,1)S(1)} %get-tuple-element.213), channel_id=1, source_target_pairs={{0,6},{1,7},{2,4},{3,5},{4,2},{5,3},{6,0},{7,1},{8,14},{9,15},{10,... | collective-permute-start | bytes 786440 | tf_op jit(solution)/shard_map/ppermute | solution.py:57
  358.3 18.2 %collective-permute-start.43 = (bf16[256,1024]{1,0:T(8,128)(2,1)S(1)}, bf16[256,1024]{1,0:T(8,128)(2,1)S(1)}, u32[]{:S(2)}, u32[]{:S(2)}) collective-permute-start(bf16[256,1024]{1,0:T(8,128)(2,1)S(1)} %get-tuple-element.227), channel_id=1, source_target_pairs={{0,1},{1,0},{2,3},{3,2},{4,5},{5,4},{6,7},{7,6},{8,9},{9,8},{10,11... | collective-permute-start | bytes 1572872 | tf_op jit(solution)/shard_map/ppermute | solution.py:57
  358.9 17.6 %collective-permute-start.44 = (bf16[256,1024]{1,0:T(8,128)(2,1)S(1)}, bf16[256,1024]{1,0:T(8,128)(2,1)S(1)}, u32[]{:S(2)}, u32[]{:S(2)}) collective-permute-start(bf16[256,1024]{1,0:T(8,128)(2,1)S(1)} %get-tuple-element.228), channel_id=1, source_target_pairs={{0,16},{1,17},{2,18},{3,19},{4,20},{5,21},{6,22},{7,23},{8,24},{9,... | collective-permute-start | bytes 1572872 | tf_op jit(solution)/shard_map/ppermute | solution.py:57
  359.3 17.2 %collective-permute-start.45 = (bf16[512,256]{1,0:T(8,128)(2,1)S(1)}, bf16[512,256]{1,0:T(8,128)(2,1)S(1)}, u32[]{:S(2)}, u32[]{:S(2)}) collective-permute-start(bf16[512,256]{1,0:T(8,128)(2,1)S(1)} %get-tuple-element.230.refs_0_), channel_id=1, source_target_pairs={{0,16},{1,17},{2,18},{3,19},{4,20},{5,21},{6,22},{7,23},{8,24},{9,... | collective-permute-start | bytes 786440 | tf_op jit(solution)/shard_map/ppermute | solution.py:57
  360.4 16.2 %collective-permute-start.46 = (bf16[512,256]{1,0:T(8,128)(2,1)S(1)}, bf16[512,256]{1,0:T(8,128)(2,1)S(1)}, u32[]{:S(2)}, u32[]{:S(2)}) collective-permute-start(bf16[512,256]{1,0:T(8,128)(2,1)S(1)} %get-tuple-element.230.refs_0_), channel_id=1, source_target_pairs={{0,8},{1,9},{2,10},{3,11},{4,12},{5,13},{6,14},{7,15},{8,0},{9,1},... | collective-permute-start | bytes 786440 | tf_op jit(solution)/shard_map/ppermute | solution.py:57
  376.6 15.3 %collective-permute-start.47 = (bf16[1024,2048]{1,0:T(8,128)(2,1)S(1)}, bf16[1024,2048]{1,0:T(8,128)(2,1)S(1)}, u32[]{:S(2)}, u32[]{:S(2)}) collective-permute-start(bf16[1024,2048]{1,0:T(8,128)(2,1)S(1)} %outer_joint.2), channel_id=1, source_target_pairs={{0,8},{1,9},{2,10},{3,11},{4,12},{5,13},{6,14},{7,15},{8,0},{9,1},... | collective-permute-start | bytes 12582920 | tf_op jit(solution)/shard_map/ppermute | solution.py:57
  379.0 12.8 %collective-permute-start.48 = (bf16[512,256]{1,0:T(8,128)(2,1)S(1)}, bf16[512,256]{1,0:T(8,128)(2,1)S(1)}, u32[]{:S(2)}, u32[]{:S(2)}) collective-permute-start(bf16[512,256]{1,0:T(8,128)(2,1)S(1)} %collective-permute-done.45.refs_1_), channel_id=1, source_target_pairs={{0,8},{1,9},{2,10},{3,11},{4,12},{5,13},{6,14},{7,15},{8,0},{9,1},... | collective-permute-start | bytes 786440 | tf_op jit(solution)/shard_map/ppermute | solution.py:57
  397.8 27.4 %collective-permute-start.49 = (bf16[512,1024]{1,0:T(8,128)(2,1)}, bf16[512,1024]{1,0:T(8,128)(2,1)S(1)}, u32[]{:S(2)}, u32[]{:S(2)}) collective-permute-start(bf16[512,1024]{1,0:T(8,128)(2,1)} %get-tuple-element.249), channel_id=1, source_target_pairs={{0,16},{1,17},{2,18},{3,19},{4,20},{5,21},{6,22},{7,23},{8,24},{9,... | collective-permute-start | bytes 3145736 | tf_op jit(solution)/shard_map/ppermute | solution.py:57
  398.3 27.0 %collective-permute-start.50 = (bf16[256,2048]{1,0:T(8,128)(2,1)}, bf16[256,2048]{1,0:T(8,128)(2,1)}, u32[]{:S(2)}, u32[]{:S(2)}) collective-permute-start(bf16[256,2048]{1,0:T(8,128)(2,1)} %get-tuple-element.250), channel_id=1, source_target_pairs={{0,1},{1,0},{2,3},{3,2},{4,5},{5,4},{6,7},{7,6},{8,9},{9,8},{10,11... | collective-permute-start | bytes 3145736 | tf_op jit(solution)/shard_map/ppermute | solution.py:57
  399.1 25.4 %collective-permute-start.51 = (bf16[128,1024]{1,0:T(8,128)(2,1)}, bf16[128,1024]{1,0:T(8,128)(2,1)S(1)}, u32[]{:S(2)}, u32[]{:S(2)}) collective-permute-start(bf16[128,1024]{1,0:T(8,128)(2,1)} %get-tuple-element.251), channel_id=1, source_target_pairs={{0,2},{1,3},{2,0},{3,1},{4,6},{5,7},{6,4},{7,5},{8,10},{9,11},{10,... | collective-permute-start | bytes 786440 | tf_op jit(solution)/shard_map/ppermute | solution.py:57
  401.4 23.0 %collective-permute-start.52 = (bf16[128,1024]{1,0:T(8,128)(2,1)}, bf16[128,1024]{1,0:T(8,128)(2,1)}, u32[]{:S(2)}, u32[]{:S(2)}) collective-permute-start(bf16[128,1024]{1,0:T(8,128)(2,1)} %get-tuple-element.252), channel_id=1, source_target_pairs={{0,4},{1,5},{2,6},{3,7},{4,0},{5,1},{6,2},{7,3},{8,12},{9,13},{10,... | collective-permute-start | bytes 786440 | tf_op jit(solution)/shard_map/ppermute | solution.py:57
  401.5 23.7 %collective-permute-start.53 = (bf16[128,1024]{1,0:T(8,128)(2,1)}, bf16[128,1024]{1,0:T(8,128)(2,1)}, u32[]{:S(2)}, u32[]{:S(2)}) collective-permute-start(bf16[128,1024]{1,0:T(8,128)(2,1)} %get-tuple-element.253), channel_id=1, source_target_pairs={{0,6},{1,7},{2,4},{3,5},{4,2},{5,3},{6,0},{7,1},{8,14},{9,15},{10,... | collective-permute-start | bytes 786440 | tf_op jit(solution)/shard_map/ppermute | solution.py:57
  434.8 11.2 %collective-permute-start.54 = (bf16[256,1024]{1,0:T(8,128)(2,1)}, bf16[256,1024]{1,0:T(8,128)(2,1)S(1)}, u32[]{:S(2)}, u32[]{:S(2)}) collective-permute-start(bf16[256,1024]{1,0:T(8,128)(2,1)} %copy-done.33), channel_id=1, source_target_pairs={{0,1},{1,0},{2,3},{3,2},{4,5},{5,4},{6,7},{7,6},{8,9},{9,8},{10,11... | collective-permute-start | bytes 1572872 | tf_op jit(solution)/shard_map/ppermute | solution.py:57
  435.5 10.9 %collective-permute-start.55 = (bf16[256,1024]{1,0:T(8,128)(2,1)}, bf16[256,1024]{1,0:T(8,128)(2,1)S(1)}, u32[]{:S(2)}, u32[]{:S(2)}) collective-permute-start(bf16[256,1024]{1,0:T(8,128)(2,1)} %copy-done.32), channel_id=1, source_target_pairs={{0,16},{1,17},{2,18},{3,19},{4,20},{5,21},{6,22},{7,23},{8,24},{9,... | collective-permute-start | bytes 1572872 | tf_op jit(solution)/shard_map/ppermute | solution.py:57
  450.9 20.7 %collective-permute-start.73 = (bf16[128,1024]{1,0:T(8,128)(2,1)}, bf16[128,1024]{1,0:T(8,128)(2,1)}, u32[]{:S(2)}, u32[]{:S(2)}) collective-permute-start(bf16[128,1024]{1,0:T(8,128)(2,1)} %get-tuple-element.281.refs_0_), channel_id=1, source_target_pairs={{0,16},{1,17},{2,18},{3,19},{4,20},{5,21},{6,22},{7,23},{8,24},{9,... | collective-permute-start | bytes 786440 | tf_op jit(solution)/shard_map/ppermute | solution.py:57
  462.4 9.2 %collective-permute-start.60 = (f32[1,16,128]{2,1,0:T(8,128)S(1)}, f32[1,16,128]{2,1,0:T(8,128)S(1)}, u32[]{:S(2)}, u32[]{:S(2)}) collective-permute-start(f32[1,16,128]{2,1,0:T(8,128)S(1)} %bitcast.125), channel_id=1, source_target_pairs={{0,2},{1,3},{2,0},{3,1},{4,6},{5,7},{6,4},{7,5},{8,10},{9,11},{10,... | collective-permute-start | bytes 24584 | tf_op jit(solution)/shard_map/ppermute | solution.py:57
  464.5 7.1 %collective-permute-start.61 = (f32[1,16,128]{2,1,0:T(8,128)S(1)}, f32[1,16,128]{2,1,0:T(8,128)S(1)}, u32[]{:S(2)}, u32[]{:S(2)}) collective-permute-start(f32[1,16,128]{2,1,0:T(8,128)S(1)} %bitcast.126), channel_id=1, source_target_pairs={{0,4},{1,5},{2,6},{3,7},{4,0},{5,1},{6,2},{7,3},{8,12},{9,13},{10,... | collective-permute-start | bytes 24584 | tf_op jit(solution)/shard_map/ppermute | solution.py:57
  465.0 6.7 %collective-permute-start.62 = (f32[1,16,128]{2,1,0:T(8,128)S(1)}, f32[1,16,128]{2,1,0:T(8,128)S(1)}, u32[]{:S(2)}, u32[]{:S(2)}) collective-permute-start(f32[1,16,128]{2,1,0:T(8,128)S(1)} %bitcast.127), channel_id=1, source_target_pairs={{0,6},{1,7},{2,4},{3,5},{4,2},{5,3},{6,0},{7,1},{8,14},{9,15},{10,... | collective-permute-start | bytes 24584 | tf_op jit(solution)/shard_map/ppermute | solution.py:57
  465.9 14.9 %collective-permute-start.74 = (bf16[128,1024]{1,0:T(8,128)(2,1)}, bf16[128,1024]{1,0:T(8,128)(2,1)}, u32[]{:S(2)}, u32[]{:S(2)}) collective-permute-start(bf16[128,1024]{1,0:T(8,128)(2,1)} %get-tuple-element.281.refs_0_), channel_id=1, source_target_pairs={{0,8},{1,9},{2,10},{3,11},{4,12},{5,13},{6,14},{7,15},{8,0},{9,1},... | collective-permute-start | bytes 786440 | tf_op jit(solution)/shard_map/ppermute | solution.py:57
  471.5 10.3 %collective-permute-start.75 = (bf16[128,1024]{1,0:T(8,128)(2,1)}, bf16[128,1024]{1,0:T(8,128)(2,1)}, u32[]{:S(2)}, u32[]{:S(2)}) collective-permute-start(bf16[128,1024]{1,0:T(8,128)(2,1)} %collective-permute-done.73.refs_1_), channel_id=1, source_target_pairs={{0,8},{1,9},{2,10},{3,11},{4,12},{5,13},{6,14},{7,15},{8,0},{9,1},... | collective-permute-start | bytes 786440 | tf_op jit(solution)/shard_map/ppermute | solution.py:57
  471.7 18.2 %collective-permute-start.63 = (f32[4,1,16,128]{3,2,1,0:T(8,128)S(1)}, f32[4,1,16,128]{3,2,1,0:T(8,128)S(1)}, u32[]{:S(2)}, u32[]{:S(2)}) collective-permute-start(f32[4,1,16,128]{3,2,1,0:T(8,128)S(1)} %get-tuple-element.343), channel_id=1, source_target_pairs={{0,1},{1,0},{2,3},{3,2},{4,5},{5,4},{6,7},{7,6},{8,9},{9,8},{10,11... | collective-permute-start | bytes 98312 | tf_op jit(solution)/shard_map/ppermute | solution.py:57
  478.1 13.2 %collective-permute-start.67 = (bf16[128,1024]{1,0:T(8,128)(2,1)}, bf16[128,1024]{1,0:T(8,128)(2,1)S(1)}, u32[]{:S(2)}, u32[]{:S(2)}) collective-permute-start(bf16[128,1024]{1,0:T(8,128)(2,1)} %get-tuple-element.276), channel_id=1, source_target_pairs={{0,2},{1,3},{2,0},{3,1},{4,6},{5,7},{6,4},{7,5},{8,10},{9,11},{10,... | collective-permute-start | bytes 786440 | tf_op jit(solution)/shard_map/ppermute | solution.py:57
  480.7 15.0 %collective-permute-start.68 = (bf16[128,1024]{1,0:T(8,128)(2,1)}, bf16[128,1024]{1,0:T(8,128)(2,1)}, u32[]{:S(2)}, u32[]{:S(2)}) collective-permute-start(bf16[128,1024]{1,0:T(8,128)(2,1)} %get-tuple-element.277), channel_id=1, source_target_pairs={{0,4},{1,5},{2,6},{3,7},{4,0},{5,1},{6,2},{7,3},{8,12},{9,13},{10,... | collective-permute-start | bytes 786440 | tf_op jit(solution)/shard_map/ppermute | solution.py:57
  480.8 23.1 %collective-permute-start.69 = (bf16[128,1024]{1,0:T(8,128)(2,1)}, bf16[128,1024]{1,0:T(8,128)(2,1)}, u32[]{:S(2)}, u32[]{:S(2)}) collective-permute-start(bf16[128,1024]{1,0:T(8,128)(2,1)} %get-tuple-element.278), channel_id=1, source_target_pairs={{0,6},{1,7},{2,4},{3,5},{4,2},{5,3},{6,0},{7,1},{8,14},{9,15},{10,... | collective-permute-start | bytes 786440 | tf_op jit(solution)/shard_map/ppermute | solution.py:57
  484.5 26.6 %collective-permute-start.64 = (bf16[16,7296]{1,0:T(8,128)(2,1)}, bf16[16,7296]{1,0:T(8,128)(2,1)}, u32[]{:S(2)}, u32[]{:S(2)}) collective-permute-start(bf16[16,7296]{1,0:T(8,128)(2,1)} %reshape.105), channel_id=1, source_target_pairs={{0,8},{1,9},{2,10},{3,11},{4,12},{5,13},{6,14},{7,15},{8,0},{9,1},... | collective-permute-start | bytes 700424 | tf_op jit(solution)/shard_map/ppermute | solution.py:57
  489.9 21.4 %collective-permute-start.65 = (bf16[16,7296]{1,0:T(8,128)(2,1)}, bf16[16,7296]{1,0:T(8,128)(2,1)S(1)}, u32[]{:S(2)}, u32[]{:S(2)}) collective-permute-start(bf16[16,7296]{1,0:T(8,128)(2,1)} %reshape.105), channel_id=1, source_target_pairs={{0,16},{1,17},{2,18},{3,19},{4,20},{5,21},{6,22},{7,23},{8,24},{9,... | collective-permute-start | bytes 700424 | tf_op jit(solution)/shard_map/ppermute | solution.py:57
  491.3 20.0 %collective-permute-start.66 = (bf16[16,7296]{1,0:T(8,128)(2,1)}, bf16[16,7296]{1,0:T(8,128)(2,1)S(1)}, u32[]{:S(2)}, u32[]{:S(2)}) collective-permute-start(bf16[16,7296]{1,0:T(8,128)(2,1)} %reshape.105), channel_id=1, source_target_pairs={{0,24},{1,25},{2,26},{3,27},{4,28},{5,29},{6,30},{7,31},{8,16},{9,... | collective-permute-start | bytes 700424 | tf_op jit(solution)/shard_map/ppermute | solution.py:57
  507.1 8.4 %collective-permute-start.70 = (bf16[128,1024]{1,0:T(8,128)(2,1)S(1)}, bf16[128,1024]{1,0:T(8,128)(2,1)S(1)}, u32[]{:S(2)}, u32[]{:S(2)}) collective-permute-start(bf16[128,1024]{1,0:T(8,128)(2,1)S(1)} %sums_h.1.refs_0_), channel_id=1, source_target_pairs={{0,16},{1,17},{2,18},{3,19},{4,20},{5,21},{6,22},{7,23},{8,24},{9,... | collective-permute-start | bytes 786440 | tf_op jit(solution)/shard_map/ppermute | solution.py:57
  508.4 7.1 %collective-permute-start.71 = (bf16[128,1024]{1,0:T(8,128)(2,1)S(1)}, bf16[128,1024]{1,0:T(8,128)(2,1)S(1)}, u32[]{:S(2)}, u32[]{:S(2)}) collective-permute-start(bf16[128,1024]{1,0:T(8,128)(2,1)S(1)} %sums_h.1.refs_0_), channel_id=1, source_target_pairs={{0,8},{1,9},{2,10},{3,11},{4,12},{5,13},{6,14},{7,15},{8,0},{9,1},... | collective-permute-start | bytes 786440 | tf_op jit(solution)/shard_map/ppermute | solution.py:57
  511.1 9.8 %collective-permute-start.72 = (bf16[128,1024]{1,0:T(8,128)(2,1)S(1)}, bf16[128,1024]{1,0:T(8,128)(2,1)S(1)}, u32[]{:S(2)}, u32[]{:S(2)}) collective-permute-start(bf16[128,1024]{1,0:T(8,128)(2,1)S(1)} %sums_h.1.refs_0_), channel_id=1, source_target_pairs={{0,24},{1,25},{2,26},{3,27},{4,28},{5,29},{6,30},{7,31},{8,16},{9,... | collective-permute-start | bytes 786440 | tf_op jit(solution)/shard_map/ppermute | solution.py:57
  (61 other events, 683.6 us)
Sparse Core Ops, SparseCore 0:
  76.4 83.9 all-gather.1
